TPU v7x, 32 devices: a whole 2x2x4 slice. The times are simulated.
32 devices in a mesh: row: 4 (over z), col: 8 (over y, x, core).
Axes of the slice: x: 2, y: 2, z: 4, core: 2. Of those that a mesh axis runs over, the one named last changes fastest.
Arguments:
- inputs: float32 [8192, 768], P(('row', 'col')), may hold values from -4 to 4
- rho: float32 [8192], P(('row', 'col')), may hold values from 38.243683 to 40.18358
- sigma: float32 [8192], P(('row', 'col')), may hold values from 0.4 to 2
- embed: float32 [64, 8192], P(None, ('row', 'col')), may hold values from -0.72 to 0.72
- knn_blocks: int32 [4, 8, 8, 4, 2], P('row', 'col'), may hold values from 0 to 1, as said below
- knn_seeds: int32 [4, 8, 8, 4], P('row', 'col'), may hold values from 0 to 8388607
- neg_rows: int32 [4, 8, 48], P('row', 'col'), may hold values from 0 to 15
- neg_cols: int32 [4, 8, 48], P('row', 'col'), may hold values from 0 to 7
- neg_count: int32 [4, 8], P('row', 'col'), may hold values from 1 to 48, as said below
Outputs:
- embedding: float32 [64, 8192], P(None, ('row', 'col'))
- last_force: float32 [64, 8192], P(None, ('row', 'col'))
Inputs may be any that keep to these rules, and one draw needn't show every extreme that they name: `knn_blocks`: if tile (r, c, a, s) lists blocks (u, v), tile (s, a, c, r) lists blocks (v, u); where both name the same span, u = v. `neg_count`: one device's list is full, 48 live slots.
All inputs are finite; a program needn't handle non-finite values.
Results may differ from a plain program's by a relative error of at most 0.0003.
Values sent between devices are 32-bit elements; how exact they have to be, the bound alone decides.
No kernel may reach another device: no remote copies, remote signals or barrier semaphores. Data moves between devices by JAX's collectives and lax.ppermute only.
A program may use at most 128 MiB of HBM per device.

v0:
```python
import jax
import jax.numpy as jnp
from jax import lax
from jax.sharding import PartitionSpec as P

D_IN = 768
D_EMB = 64
BLK = 128
CB = 2
NEG_DEV = 48
STEPS = 2


STEP_SIZE = 0.0005
REPULSION = 2.0
FORCE_SCALE = 0.015625
FULL_PRECISION = lax.Precision.HIGHEST


def hash_bits(salt_value, first, second):
    mixed = first * 1103515245 + salt_value
    mixed = (mixed ^ second * 747796405) * 277803737
    return (mixed >> 17 & 1).astype(jnp.float32)


def conditional(distance, offset, spread, mask):
    return mask * jnp.exp(-jnp.maximum(distance - offset, 0.0) / spread)


def pair_kernel(left, right):
    gram = jnp.einsum("dsi,dsj->sij", left, right, precision=FULL_PRECISION)
    total = (
        jnp.sum(left * left, axis=0)[:, :, None]
        + jnp.sum(right * right, axis=0)[:, None, :]
        - 2.0 * gram
    )
    return 1.0 / (1.0 + total)


def shards(inputs, rho, sigma, embed, knn_blocks, knn_seeds, neg_rows, neg_cols, neg_count):
    row_count = lax.axis_size("row")
    col_count = lax.axis_size("col")
    listing = knn_blocks.reshape(col_count, row_count, 2)
    seeds = knn_seeds.reshape(col_count, row_count)
    row_list = neg_rows.reshape(NEG_DEV)
    col_list = neg_cols.reshape(NEG_DEV)
    live_count = neg_count[0, 0]
    own_squares = jnp.sum(inputs * inputs, axis=1)
    params = jnp.stack([rho, sigma, own_squares])
    row_x, row_params = (
        lax.all_gather(inputs, "col", axis=0, tiled=True),
        lax.all_gather(params, "col", axis=1, tiled=True),
    )
    row_blocks = row_x.reshape(col_count, CB, BLK, D_IN)
    row_params = row_params.reshape(3, col_count, CB, BLK)
    positions = jnp.arange(BLK, dtype=jnp.int32)
    chosen = jnp.arange(row_count, dtype=jnp.int32)
    groups = jnp.arange(col_count, dtype=jnp.int32)

    def distances(col_blocks, col_squares, group):
        row_pick = listing[group, :, 0]
        col_pick = listing[group, :, 1]
        left = row_blocks[group][row_pick]
        right = col_blocks[chosen, col_pick]
        gram = jnp.einsum("sid,sjd->sij", left, right, precision=FULL_PRECISION)
        total = (
            row_params[2, group][row_pick][:, :, None]
            + col_squares[chosen, col_pick][:, None, :]
            - 2.0 * gram
        )
        distance = jnp.sqrt(jnp.maximum(total, 1.0))
        mask = hash_bits(
            seeds[group][:, None, None], positions[None, :, None], positions[None, None, :]
        )
        forward = conditional(
            distance,
            row_params[0, group][row_pick][:, :, None],
            row_params[1, group][row_pick][:, :, None],
            mask,
        )
        return (distance, forward, col_pick)

    col_x, col_squares = (
        lax.all_gather(inputs, "row", axis=0, tiled=True),
        lax.all_gather(own_squares[None], "row", axis=1, tiled=True),
    )
    col_blocks = col_x.reshape(row_count, CB, BLK, D_IN)
    col_squares = col_squares.reshape(row_count, CB, BLK)

    def forward_group(group):
        return distances(col_blocks, col_squares, group)[1]

    forward = lax.map(forward_group, groups)
    backward = lax.all_to_all(
        lax.all_to_all(forward, "row", split_axis=1, concat_axis=1, tiled=True),
        "col",
        split_axis=0,
        concat_axis=0,
        tiled=True,
    )
    backward = jnp.swapaxes(backward, 2, 3)
    weights = (forward + backward - forward * backward).astype(jnp.bfloat16)
    block_ids = jnp.arange(CB, dtype=jnp.int32)
    row_slots = jnp.arange(col_count * CB, dtype=jnp.int32)
    col_slots = jnp.arange(row_count * CB, dtype=jnp.int32)
    force = jnp.zeros_like(embed)
    for step in range(STEPS):
        row_y = lax.all_gather(embed, "col", axis=1, tiled=True).reshape(D_EMB, col_count, CB, BLK)
        col_y = lax.all_gather(embed, "row", axis=1, tiled=True).reshape(D_EMB, row_count, CB, BLK)

        def attract_group(group):
            row_pick = listing[group, :, 0]
            col_pick = listing[group, :, 1]
            left = row_y[:, group][:, row_pick]
            right = col_y[:, chosen, col_pick]
            pull_weight = weights[group].astype(jnp.float32) * pair_kernel(left, right)
            pull = (
                jnp.einsum("dsj,sij->dsi", right, pull_weight, precision=FULL_PRECISION)
                - left * jnp.sum(pull_weight, axis=2)[None]
            )
            onehot = (row_pick[:, None] == block_ids[None, :]).astype(jnp.float32)
            return jnp.einsum("sb,dsi->dbi", onehot, pull, precision=FULL_PRECISION)

        attract = lax.map(attract_group, groups)
        row_force = jnp.transpose(attract, (1, 0, 2, 3)).reshape(D_EMB, col_count * CB, BLK)
        row_flat = row_y.reshape(D_EMB, col_count * CB, BLK)
        col_flat = col_y.reshape(D_EMB, row_count * CB, BLK)
        live = (jnp.arange(NEG_DEV, dtype=jnp.int32) < live_count).astype(jnp.float32)
        left = row_flat[:, row_list]
        right = col_flat[:, col_list]
        kernel = pair_kernel(left, right)
        push = REPULSION * kernel * kernel * live[:, None, None]
        row_push = left * jnp.sum(push, axis=2)[None] - jnp.einsum(
            "dkj,kij->dki", right, push, precision=FULL_PRECISION
        )
        col_push = right * jnp.sum(push, axis=1)[None] - jnp.einsum(
            "dki,kij->dkj", left, push, precision=FULL_PRECISION
        )
        row_hot = (row_list[:, None] == row_slots[None, :]).astype(jnp.float32)
        col_hot = (col_list[:, None] == col_slots[None, :]).astype(jnp.float32)
        row_force = row_force + jnp.einsum(
            "ku,dki->dui", row_hot, row_push, precision=FULL_PRECISION
        )
        col_force = jnp.einsum("kv,dkj->dvj", col_hot, col_push, precision=FULL_PRECISION)
        row_total = lax.psum_scatter(
            row_force.reshape(D_EMB, col_count * CB * BLK), "col", scatter_dimension=1, tiled=True
        )
        col_total = lax.psum_scatter(
            col_force.reshape(D_EMB, row_count * CB * BLK), "row", scatter_dimension=1, tiled=True
        )
        force = row_total + col_total
        embed = embed + STEP_SIZE * force
    return (embed, force * FORCE_SCALE)


def solution(mesh):
    in_specs = (
        P(("row", "col"), None),
        P(("row", "col")),
        P(("row", "col")),
        P(None, ("row", "col")),
        P("row", "col", None, None, None),
        P("row", "col", None, None),
        P("row", "col", None),
        P("row", "col", None),
        P("row", "col"),
    )
    out_specs = (P(None, ("row", "col")), P(None, ("row", "col")))
    return jax.shard_map(shards, mesh=mesh, in_specs=in_specs, out_specs=out_specs, check_vma=False)
```

profile of v0, /device:TPU:0, one launch (start us, length us, event | category | flops | bytes accessed | tf_op | source)
XLA Modules:
  0.0 566.8 jit_solution(9662285046951404984)
XLA Ops:
  9.0 10.5 %all_gather.24 = f32[3,2048]{1,0:T(4,128)S(1)} all-gather(f32[3,256]{1,0:T(4,128)S(1)} %pad_maximum_fusion), channel_id=1, replica_groups=mesh['row'=4,'col'=8] {'col'}, dimensions={1}, use_global_device_ids=true | all-gather | bytes 27648 | tf_op jit(solution)/shard_map/all_gather | solution.py:52
  19.6 11.3 %all-gather.1 = f32[4,1,256]{2,1,0:T(1,128)S(1)} all-gather(f32[1,1,256]{2,1,0:T(1,128)S(1)} %bitcast.400), channel_id=2, replica_groups=mesh['row'=4,'col'=8] {'row'}, dimensions={0}, use_global_device_ids=true | all-gather | bytes 5120 | tf_op jit(solution)/shard_map/all_gather | solution.py:85
  30.9 44.9 %all-gather.7.cloned.1.call-done = f32[1024,768]{1,0:T(8,128)} async-done(((f32[256,768]{1,0:T(8,128)}), f32[1024,768]{1,0:T(8,128)}) %all-gather.7.cloned.1.call-update) | async-done | bytes 3145744 | tf_op jit(solution)/shard_map/all_gather | solution.py:84
  75.9 46.1 %all-gather.5.cloned.1.call-done = f32[2048,768]{1,0:T(8,128)} async-done(((f32[256,768]{1,0:T(8,128)}), f32[2048,768]{1,0:T(8,128)}) %all-gather.5.cloned.1.call-update) | async-done | bytes 6291472 | tf_op jit(solution)/shard_map/all_gather | solution.py:51
  122.0 93.7 %while.36 = (s32[]{:T(128)}, f32[8,4,128,128]{3,2,1,0:T(8,128)}, s32[8]{0:T(128)S(1)}, s32[8,4]{1,0:T(8,128)S(1)}, f32[3,8,2,128]{3,2,1,0:T(2,128)S(1)}, /*index...) while((s32[]{:T(128)}, f32[8,4,128,128]{3,2,1,0:T(8,128)}, ...), condition=%wide.region_2.3_spmd.clone.clone, body=%wide.region_1.2_spmd.clone.clone.sunk | while | flops 604899136 | bytes 11313599 | solution.py:93
  126.4 2.5 gather_fusion.5
  138.1 2.5 gather_fusion.5
  149.8 2.5 gather_fusion.5
  161.5 2.5 gather_fusion.5
  173.3 2.5 gather_fusion.5
  185.0 2.5 gather_fusion.5
  196.7 2.5 gather_fusion.5
  215.7 3.1 copy.105
  218.8 4.7 all-to-all-start
  224.2 9.8 %all_gather.28 = f32[64,2048]{1,0:T(8,128)S(1)} all-gather(f32[64,256]{1,0:T(8,128)S(1)} %copy-done.8), channel_id=1, replica_groups=mesh['row'=4,'col'=8] {'col'}, dimensions={1}, use_global_device_ids=true | all-gather | bytes 589824 | tf_op jit(solution)/shard_map/all_gather | solution.py:108
  235.6 44.3 %all_gather.29 = f32[64,1024]{1,0:T(8,128)S(1)} all-gather(f32[64,256]{1,0:T(8,128)S(1)} %copy-done.8), channel_id=1, replica_groups=mesh['row'=4,'col'=8] {'row'}, dimensions={1}, use_global_device_ids=true | all-gather | bytes 327680 | tf_op jit(solution)/shard_map/all_gather | solution.py:109
  281.8 3.2 copy.106
  285.0 4.4 all-to-all-start.1
  289.6 6.9 %fusion.138 = (f32[48,128]{1,0:T(8,128)S(1)}, f32[48,128]{1,0:T(8,128)S(1)}, f32[48,128,128]{2,1,0:T(8,128)S(1)}) fusion(f32[48]{0:T(128)S(1)} %compare_convert_fusion, f32[48,64,128]{2,1,0:T(8,128)S(1)} %gather_fusion.11, f32[48,64,128]{2,1,0:T(8,128)S(1)} %gather_fusion.10, f32[48,128]{1,0:T(8,128)S(1)} %get-tuple-element.426, ...), kind=kOutput, calls=%fused_computation.206 | convolution fusion | flops 611831808 | bytes 6389952 | tf_op jit(solution)/shard_map/dsi,dsj->sij/dot_general | solution.py:31
  296.5 2.8 bitcast_subtract_fusion.2
  306.2 8.6 %bitcast_subtract_fusion.3 = f32[64,48,128]{2,0,1:T(8,128)} fusion(f32[48,64,128]{2,1,0:T(8,128)S(1)} %gather_fusion.10, f32[48,128,128]{2,1,0:T(8,128)} %copy-done, f32[48,64,128]{2,1,0:T(8,128)S(1)} %gather_fusion.11, f32[48,128]{1,0:T(8,128)S(1)} %get-tuple-element.358), kind=kOutput, calls=%fused_computation.151 | convolution fusion | flops 604766208 | bytes 7888896 | tf_op jit(solution)/shard_map/dkj,kij->dki/dot_general | solution.py:133
  316.8 3.0 fusion.80
  319.9 53.4 %while.34 = (s32[]{:T(128)}, f32[8,64,2,128]{3,2,1,0:T(2,128)S(1)}, s32[8]{0:T(128)S(1)}, bf16[8,4,128,128]{2,3,1,0:T(8,128)(2,1)}, f32[64,8,2,128]{3,2,1,0:T(2,...) while((s32[]{:T(128)}, f32[8,64,2,128]{3,2,1,0:T(2,128)S(1)}, ...), condition=%wide.region_7.8_spmd.clone, body=%wide.region_3.7_spmd.clone.sunk | while | flops 102170168 | bytes 2573135 | solution.py:124
  376.0 34.7 %reduce-scatter.5.cloned.1.call-done = f32[64,256]{1,0:T(8,128)} async-done(((f32[64,2048]{1,0:T(8,128)}), f32[64,256]{1,0:T(8,128)}) %reduce-scatter.5.cloned.1.call-update) | async-done | bytes 65552 | tf_op jit(solution)/shard_map/reduce_scatter | solution.py:145
  411.6 9.8 %all_gather.30 = f32[64,2048]{1,0:T(8,128)S(1)} all-gather(f32[64,256]{1,0:T(8,128)S(1)} %multiply_add_fusion.1), channel_id=1, replica_groups=mesh['row'=4,'col'=8] {'col'}, dimensions={1}, use_global_device_ids=true | all-gather | bytes 589824 | tf_op jit(solution)/shard_map/all_gather | solution.py:108
  421.4 14.0 %all_gather.31 = f32[64,1024]{1,0:T(8,128)S(1)} all-gather(f32[64,256]{1,0:T(8,128)S(1)} %multiply_add_fusion.1), channel_id=1, replica_groups=mesh['row'=4,'col'=8] {'row'}, dimensions={1}, use_global_device_ids=true | all-gather | bytes 327680 | tf_op jit(solution)/shard_map/all_gather | solution.py:109
  436.3 50.7 %while.35 = (s32[]{:T(128)}, f32[8,64,2,128]{3,2,1,0:T(2,128)S(1)}, s32[8]{0:T(128)S(1)}, bf16[8,4,128,128]{2,3,1,0:T(8,128)(2,1)}, f32[64,8,2,128]{3,2,1,0:T(2,...) while((s32[]{:T(128)}, f32[8,64,2,128]{3,2,1,0:T(2,128)S(1)}, ...), condition=%wide.region_18.19_spmd.clone, body=%wide.region_14.18_spmd.clone.sunk | while | flops 102170168 | bytes 2573135 | solution.py:124
  490.0 6.9 %fusion.137 = (f32[48,128]{1,0:T(8,128)S(1)}, f32[48,128]{1,0:T(8,128)S(1)}, f32[48,128,128]{2,1,0:T(8,128)S(1)}) fusion(f32[48]{0:T(128)S(1)} %copy-done.18, f32[48,64,128]{2,1,0:T(8,128)S(1)} %gather_fusion.13, f32[48,64,128]{2,1,0:T(8,128)S(1)} %gather_fusion.12, f32[48,128]{1,0:T(8,128)S(1)} %fusion.84, f32[48,128]{1,0:T(8,128)S(1)} %fusion.88), kind=kOutput, calls=%fused_computation.205 | convolution fusion | flops 611831808 | bytes 6389952 | tf_op jit(solution)/shard_map/dsi,dsj->sij/dot_general | solution.py:31
  496.9 2.8 bitcast_subtract_fusion
  502.2 8.1 %bitcast_subtract_fusion.1 = f32[64,48,128]{2,0,1:T(8,128)S(1)} fusion(f32[48,64,128]{2,1,0:T(8,128)S(1)} %gather_fusion.12, f32[48,128,128]{2,1,0:T(8,128)} %copy-done.1, f32[48,64,128]{2,1,0:T(8,128)S(1)} %gather_fusion.13, f32[48,128]{1,0:T(8,128)S(1)} %get-tuple-element.356), kind=kOutput, calls=%fused_computation.137 | convolution fusion | flops 604766208 | bytes 7888896 | tf_op jit(solution)/shard_map/dkj,kij->dki/dot_general | solution.py:133
  512.9 9.7 %reduce-scatter.11.cloned.1.call-done = f32[64,256]{1,0:T(8,128)} async-done(((f32[64,1024]{1,0:T(8,128)}), f32[64,256]{1,0:T(8,128)}) %reduce-scatter.11.cloned.1.call-update) | async-done | bytes 65552 | tf_op jit(solution)/shard_map/reduce_scatter | solution.py:148
  522.6 35.6 %reduce-scatter.9.cloned.1.call-done = f32[64,256]{1,0:T(8,128)} async-done(((f32[64,2048]{1,0:T(8,128)}), f32[64,256]{1,0:T(8,128)}) %reduce-scatter.9.cloned.1.call-update) | async-done | bytes 65552 | tf_op jit(solution)/shard_map/reduce_scatter | solution.py:145
  (413 shorter events, 160.1 us)
Async XLA Ops:
  7.2 1.6 copy-start.2
  7.2 1.5 copy-start.10
  7.2 1.8 copy-start.15
  7.2 1.7 copy-start.16
  7.2 12.3 %copy-start.9 = (s32[1,1,8,4,2]{2,4,3,1,0:T(2,128)S(1)}, s32[1,1,8,4,2]{2,4,3,1,0:T(2,128)}, u32[]{:S(2)}) copy-start(s32[1,1,8,4,2]{2,4,3,1,0:T(2,128)} %param.19) | copy-start | bytes 772
  7.2 68.7 %all-gather.7.cloned.1.call-start = ((), (), s32[]{:S(2)}) async-start(), calls=%async_computation.7 | async-start | bytes 3932160 | tf_op jit(solution)/shard_map/all_gather | solution.py:84
  7.9 114.0 %all-gather.5.cloned.1.call-start = ((), (), s32[]{:S(2)}) async-start(), calls=%async_computation.6 | async-start | bytes 7077888 | tf_op jit(solution)/shard_map/all_gather | solution.py:51
  218.8 5.4 copy-start.13
  218.8 5.4 copy-start.8
  218.8 63.0 %all-to-all-start = ((f32[8,4,128,128]{3,2,0,1:T(8,128)}), f32[8,4,128,128]{3,2,0,1:T(8,128)}, u32[]{:S(2)}, u32[]{:S(2)}) async-start(f32[8,4,128,128]{3,2,0,1:T(8,128)} %copy.105), calls=%async_computation | async-start | bytes 4194304 | tf_op jit(solution)/shard_map/all_to_all | solution.py:95
  234.1 0.8 copy-start.4
  234.9 45.0 %copy-start.11 = (s32[1,1,48]{2,1,0:T(1,128)S(1)}, s32[1,1,48]{2,1,0:T(1,128)}, u32[]{:S(2)}) copy-start(s32[1,1,48]{2,1,0:T(1,128)} %param.22) | copy-start | bytes 580
  279.9 0.7 copy-start.5
  285.0 31.7 %all-to-all-start.1 = ((f32[8,4,128,128]{3,2,1,0:T(8,128)}), f32[8,4,128,128]{3,2,1,0:T(8,128)}, u32[]{:S(2)}, u32[]{:S(2)}) async-start(f32[8,4,128,128]{3,2,1,0:T(8,128)} %copy.106), calls=%async_computation.1 | async-start | bytes 4194304 | tf_op jit(solution)/shard_map/all_to_all | solution.py:94
  289.4 86.6 %reduce-scatter.7.cloned.1.call-start = ((), (), s32[]{:S(2)}) async-start(), calls=%async_computation.9 | async-start | bytes 327680 | tf_op jit(solution)/shard_map/reduce_scatter | solution.py:148
  289.6 6.9 %copy-start.17 = (f32[48]{0:T(128)}, f32[48]{0:T(128)S(1)}, u32[]{:S(2)}) copy-start(f32[48]{0:T(128)S(1)} %compare_convert_fusion) | copy-start | bytes 580
  296.5 2.8 copy-start
  299.4 4.9 copy-start.6
  301.7 109.1 %reduce-scatter.5.cloned.1.call-start = ((), (), s32[]{:S(2)}) async-start(), calls=%async_computation.8 | async-start | bytes 589824 | tf_op jit(solution)/shard_map/reduce_scatter | solution.py:145
  319.9 53.6 %copy-start.3 = (f32[64,48,128]{2,0,1:T(8,128)S(1)}, f32[64,48,128]{2,0,1:T(8,128)}, u32[]{:S(2)}) copy-start(f32[64,48,128]{2,0,1:T(8,128)} %bitcast_subtract_fusion.3) | copy-start | bytes 4718596
  375.9 146.6 %reduce-scatter.11.cloned.1.call-start = ((), (), s32[]{:S(2)}) async-start(), calls=%async_computation.11 | async-start | bytes 327680 | tf_op jit(solution)/shard_map/reduce_scatter | solution.py:148
  489.3 0.7 copy-start.18
  496.8 2.9 copy-start.1
  496.9 2.9 copy-start.12
  502.2 56.0 %reduce-scatter.9.cloned.1.call-start = ((), (), s32[]{:S(2)}) async-start(), calls=%async_computation.10 | async-start | bytes 589824 | tf_op jit(solution)/shard_map/reduce_scatter | solution.py:145
  502.2 8.1 %copy-start.7 = (f32[64,8,2,128]{3,2,1,0:T(2,128)S(1)}, f32[64,8,2,128]{3,2,1,0:T(2,128)}, u32[]{:S(2)}) copy-start(f32[64,8,2,128]{3,2,1,0:T(2,128)} %copy.120) | copy-start | bytes 1572868
  502.2 8.1 %copy-start.14 = (s32[1,1,48]{2,1,0:T(1,128)S(1)}, s32[1,1,48]{2,1,0:T(1,128)}, u32[]{:S(2)}) copy-start(s32[1,1,48]{2,1,0:T(1,128)} %param.21) | copy-start | bytes 580
Sparse Core Ops, SparseCore 0:
  9.6 66.2 all-gather.6
  77.8 44.1 all-gather.4
  301.8 20.0 reduce-scatter.6
  376.1 34.6 reduce-scatter.4
  502.3 20.2 reduce-scatter.10
  525.8 32.3 reduce-scatter.8
where the time goes:
time: 574 us; the launch traced here: 567 us
  waiting for transfers between devices  173 us (30%)
  local copies, waits for them, and re-layouts  116 us (20%)
  blocking collectives  99.7 us (17%)
  matrix products  97.1 us (17%)
  loops' own time  48.1 us (8%)
  between operations  15.5 us (3%)
  starting transfers between devices  9.72 us (2%)
  other arithmetic  8.21 us (1%)
    reduce_scatter x2, waiting for transfers between devices, shards(): lax.psum_scatter(row_force.reshape(D_EMB, col_count * CB * BLK), 'col', s...  70.3 us
    all_gather x2, blocking collectives, shards(): lax.all_gather(embed, 'row', axis=1, tiled=True)  58.3 us
    all_gather x1, waiting for transfers between devices, shards(): lax.all_gather(inputs, 'col', axis=0, tiled=True)  46.1 us
    all_gather x1, waiting for transfers between devices, shards(): lax.all_gather(inputs, 'row', axis=0, tiled=True)  44.9 us
    dot_general x18, matrix products, pair_kernel(): gram = jnp.einsum('dsi,dsj->sij', left, right, precision=FULL_PRECISION)  38.4 us
    another operation x2, loops' own time, shards(): attract = lax.map(attract_group, groups)  32.1 us
    gather x8, local copies, waits for them, and re-layouts, distances(): right = col_blocks[chosen, col_pick]  20.3 us
    all_gather x2, blocking collectives, shards(): lax.all_gather(embed, 'col', axis=1, tiled=True)  19.6 us
  transfers between devices with their start and end apart: 8, of which 5 were waited for; matrix products, arithmetic and copies ran while one was open for 15% of the time, Pallas kernels for 0%

commit v1 on v0

v1 whole, which is shorter than its diff:
```python
import functools

import jax
import jax.numpy as jnp
from jax import lax
from jax.experimental import pallas as pl
from jax.experimental.pallas import tpu as pltpu
from jax.sharding import PartitionSpec as P

D_EMB = 64
BLK = 128
CB = 2
SPAN = CB * BLK
STEPS = 2

STEP_SIZE = 0.0005
REPULSION = 2.0
FORCE_SCALE = 0.015625

RHO, SIGMA, SQUARES, SEEDS = D_EMB, D_EMB + 1, D_EMB + 2, D_EMB + 3
PACK = 72
STACK = 4 * D_EMB
PULL = 2 * D_EMB + 16
UNROLL = 4
F32, BF16, I32 = jnp.float32, jnp.bfloat16, jnp.int32
VMEM_LIMIT = 56 * 2**20


def split(value):
    high = value.astype(BF16)
    return high, (value - high.astype(F32)).astype(BF16)


def nt_dot(left, right):
    return lax.dot_general(left, right, (((1,), (1,)), ((), ())), preferred_element_type=F32)


def nn_dot(left, right):
    return lax.dot_general(left, right, (((1,), (0,)), ((), ())), preferred_element_type=F32)


def hash_bits(salt_value, first, second):
    mixed = first * 1103515245 + salt_value
    mixed = (mixed ^ second * 747796405) * 277803737
    return (mixed >> 17 & 1).astype(F32)


def takes_shift(shift, row, row_count):
    if 2 * shift != row_count:
        return True
    half = row_count // 2
    return jnp.where(row < half, row % 2 == 0, (row - half) % 2 == 1)


def weights_kernel(row_count, col_count, meta, listing, seeds, seeds_back, row_x, row_pack, *rest):
    shifts = row_count // 2 + 1
    col_x, col_pack = rest[:shifts], rest[shifts : 2 * shifts]
    out, high_c, low_c, col_params = rest[2 * shifts :]
    group = pl.program_id(0)
    row, col = meta[0], meta[1]

    @pl.when(group == 0)
    def _():
        for shift in range(shifts):
            high, low = split(col_x[shift][...])
            high_c[shift], low_c[shift] = high, low
            for block in range(CB):
                params = col_pack[shift][RHO : RHO + 8, block * BLK : (block + 1) * BLK]
                col_params[shift, block] = params.T

    high_r, low_r = split(row_x[0])
    high_r = high_r.reshape(CB, BLK, high_r.shape[1])
    low_r = low_r.reshape(CB, BLK, low_r.shape[1])
    positions_j = lax.broadcasted_iota(I32, (BLK, BLK), 0)
    positions_i = lax.broadcasted_iota(I32, (BLK, BLK), 1)

    for shift in range(shifts):
        if shift == 0:
            offset = lax.rem(group - col + col_count, col_count)
            active = (2 * offset < col_count) | ((2 * offset == col_count) & (2 * col < col_count))
        else:
            active = takes_shift(shift, row, row_count)
        other = lax.rem(row + shift, row_count)
        entry = (group * row_count + other) * 2
        row_pick, col_pick = listing[entry], listing[entry + 1]

        @pl.when(jnp.logical_not(active))
        def _():
            out[0, shift] = jnp.zeros((BLK, BLK), BF16)

        for pick in range(CB):

            @pl.when(active & (row_pick == pick))
            def _():
                start = pl.multiple_of(col_pick * BLK, BLK)
                left_high = high_c[shift, pl.ds(start, BLK), :]
                left_low = low_c[shift, pl.ds(start, BLK), :]
                gram = (
                    nt_dot(left_high, low_r[pick])
                    + nt_dot(left_low, high_r[pick])
                    + nt_dot(left_high, high_r[pick])
                )
                lanes = slice(pick * BLK, (pick + 1) * BLK)
                rho_i = row_pack[0, RHO - D_EMB : RHO - D_EMB + 1, lanes]
                sigma_i = row_pack[0, SIGMA - D_EMB : SIGMA - D_EMB + 1, lanes]
                square_i = row_pack[0, SQUARES - D_EMB : SQUARES - D_EMB + 1, lanes]
                params_j = col_params[shift, col_pick]
                rho_j, sigma_j, square_j = params_j[:, 0:1], params_j[:, 1:2], params_j[:, 2:3]
                total = square_j + square_i - 2.0 * gram
                distance = jnp.sqrt(jnp.maximum(total, 1.0))
                seed = seeds[group * row_count + other]
                seed_back = seeds_back[shift * col_count + group]
                ahead = hash_bits(seed, positions_i, positions_j) * jnp.exp(
                    jnp.maximum(distance - rho_i, 0.0) * (-1.0 / sigma_i)
                )
                behind = hash_bits(seed_back, positions_j, positions_i) * jnp.exp(
                    jnp.maximum(distance - rho_j, 0.0) * (-1.0 / sigma_j)
                )
                weights = (ahead + behind - ahead * behind).astype(BF16)
                if shift == 0:
                    weights = (weights.astype(F32) * jnp.where(group == col, 0.5, 1.0)).astype(BF16)
                out[0, shift] = weights


def pair_weights(row_count, col_count, meta, listing, seeds, seeds_back, row_x, row_pack, col_x, col_pack):
    shifts = row_count // 2 + 1
    depth = row_x.shape[-1]
    smem = pl.BlockSpec(memory_space=pltpu.SMEM)
    vmem = pl.BlockSpec(memory_space=pltpu.VMEM)
    tiles = col_count * shifts
    return pl.pallas_call(
        functools.partial(weights_kernel, row_count, col_count),
        grid=(col_count,),
        in_specs=[smem] * 4
        + [
            pl.BlockSpec((1, SPAN, depth), lambda a: (a, 0, 0)),
            pl.BlockSpec((1, 8, SPAN), lambda a: (a, D_EMB // 8, 0)),
        ]
        + [vmem] * (2 * shifts),
        out_specs=pl.BlockSpec((1, shifts, BLK, BLK), lambda a: (a, 0, 0, 0)),
        out_shape=jax.ShapeDtypeStruct((col_count, shifts, BLK, BLK), BF16),
        scratch_shapes=[
            pltpu.VMEM((shifts, SPAN, depth), BF16),
            pltpu.VMEM((shifts, SPAN, depth), BF16),
            pltpu.VMEM((shifts, CB, BLK, 8), F32),
        ],
        compiler_params=pltpu.CompilerParams(vmem_limit_bytes=VMEM_LIMIT),
        cost_estimate=pl.CostEstimate(
            flops=tiles * 6 * BLK * BLK * depth,
            bytes_accessed=(col_count + shifts) * SPAN * depth * 4,
            transcendentals=tiles * 3 * BLK * BLK,
        ),
        name="weights",
    )(meta, listing, seeds, seeds_back, row_x, row_pack, *col_x, *col_pack)


def force_kernel(row_count, col_count, meta, listing, neg_rows, neg_cols, weights, row_y, *rest):
    shifts = row_count // 2 + 1
    col_y = rest[:row_count]
    row_force, col_force = rest[row_count], rest[row_count + 1 : 2 * row_count + 1]
    left_gram, right_gram, left_pull, right_pull, left_acc, right_acc = rest[2 * row_count + 1 :]
    row, col, live = meta[0], meta[1], meta[2]
    iota = lax.broadcasted_iota(I32, (D_EMB, BLK), 0)
    ones = jnp.ones((16, BLK), BF16)
    blank = jnp.zeros((D_EMB, BLK), BF16)

    def norm_rows(value, first):
        norm = jnp.sum(value * value, axis=0, keepdims=True)
        high, rest_ = split(norm)
        left_over = norm - high.astype(F32) - rest_.astype(F32)
        high, middle = high.astype(F32), rest_.astype(F32)
        return jnp.where(
            iota == first,
            high,
            jnp.where(iota == first + 1, middle, jnp.where(iota == first + 2, left_over, 0.0)),
        )

    def pulls(high, low):
        top = jnp.concatenate([high, ones, low], axis=0)
        bottom = jnp.concatenate([high, ones, blank], axis=0)
        return jnp.concatenate([top, bottom], axis=1)

    def left_block(index, value):
        high, low = split(value)
        extra = norm_rows(value, 0) + jnp.where((iota >= 3) & (iota < 7), 1.0, 0.0)
        left_gram[index] = jnp.concatenate([high, low, high, extra.astype(BF16)], axis=0)
        left_pull[index] = pulls(high, low)
        left_acc[index] = jnp.zeros((PULL, BLK), F32)

    def right_block(index, value):
        high, low = split(value)
        extra = norm_rows(value, 3) + jnp.where((iota < 3) | (iota == 6), 1.0, 0.0)
        twice_high, twice_low = -2.0 * high.astype(F32), -2.0 * low.astype(F32)
        stack = jnp.concatenate([twice_high, twice_high, twice_low, extra], axis=0)
        right_gram[index] = stack.T.astype(BF16)
        right_pull[index] = pulls(high, low)
        right_acc[index] = jnp.zeros((PULL, BLK), F32)

    @pl.loop(0, col_count)
    def _(group):
        for block in range(CB):
            left_block(group * CB + block, row_y[group, :D_EMB, block * BLK : (block + 1) * BLK])

    for shift in range(row_count):
        for block in range(CB):
            right_block(shift * CB + block, col_y[shift][:D_EMB, block * BLK : (block + 1) * BLK])

    def kernel_of(left, right):
        return 1.0 / nn_dot(right_gram[right], left_gram[left])

    def apply(left, right, coefficient):
        high, low = split(coefficient)
        left_part = nn_dot(right_pull[right], jnp.concatenate([high, low], axis=0))
        right_part = nt_dot(left_pull[left], jnp.concatenate([high, low], axis=1))
        left_acc[left] += left_part
        right_acc[right] += right_part

    near = col_count // 2 + 1
    tiles = near + col_count * (shifts - 1)
    spare = lax.rem(col + col_count - 1, col_count) * shifts
    last = jnp.where(takes_shift(shifts - 1, row, row_count), tiles, tiles - col_count)

    @pl.loop(0, lax.div(last + UNROLL - 1, UNROLL))
    def _(step):
        for lane in range(UNROLL):
            index = step * UNROLL + lane
            far = jnp.maximum(index - near, 0)
            shift = jnp.where(index < near, 0, 1 + lax.div(far, col_count))
            group = jnp.where(index < near, lax.rem(col + index, col_count), lax.rem(far, col_count))
            inside = index < last
            shift = jnp.where(inside, shift, 0)
            slot = jnp.where(inside, group * shifts + shift, spare)
            entry = (group * row_count + lax.rem(row + shift, row_count)) * 2
            left = group * CB + listing[entry]
            right = shift * CB + listing[entry + 1]
            apply(left, right, weights[slot].astype(F32) * kernel_of(left, right))

    @pl.loop(0, lax.div(live + UNROLL - 1, UNROLL))
    def _(step):
        for lane in range(UNROLL):
            index = step * UNROLL + lane
            strength = jnp.where(index < live, -REPULSION, 0.0)
            place = jnp.minimum(index, live - 1)
            left = neg_rows[place]
            other = neg_cols[place]
            shift = lax.rem(lax.div(other, CB) - row + row_count, row_count)
            right = shift * CB + lax.rem(other, CB)
            kernel = kernel_of(left, right)
            apply(left, right, strength * kernel * kernel)

    def force_of(acc, value):
        return acc[:D_EMB] + acc[D_EMB + 16 :] - value * acc[D_EMB : D_EMB + 1]

    @pl.loop(0, col_count)
    def _(group):
        for block in range(CB):
            lanes = slice(block * BLK, (block + 1) * BLK)
            row_force[group, :, lanes] = force_of(left_acc[group * CB + block], row_y[group, :D_EMB, lanes])

    for shift in range(row_count):
        for block in range(CB):
            lanes = slice(block * BLK, (block + 1) * BLK)
            col_force[shift][:, lanes] = force_of(right_acc[shift * CB + block], col_y[shift][:D_EMB, lanes])


def pair_forces(row_count, col_count, meta, listing, neg_rows, neg_cols, weights, row_y, col_y):
    smem = pl.BlockSpec(memory_space=pltpu.SMEM)
    vmem = pl.BlockSpec(memory_space=pltpu.VMEM)
    lefts, rights = col_count * CB, row_count * CB
    tiles = col_count * 2 + 48
    weights = weights.reshape(-1, BLK, BLK)
    outs = pl.pallas_call(
        functools.partial(force_kernel, row_count, col_count),
        in_specs=[smem] * 4 + [vmem] * (2 + row_count),
        out_specs=[vmem] * (1 + row_count),
        out_shape=[jax.ShapeDtypeStruct((col_count, D_EMB, SPAN), F32)]
        + [jax.ShapeDtypeStruct((D_EMB, SPAN), F32)] * row_count,
        scratch_shapes=[
            pltpu.VMEM((lefts, STACK, BLK), BF16),
            pltpu.VMEM((rights, BLK, STACK), BF16),
            pltpu.VMEM((lefts, PULL, 2 * BLK), BF16),
            pltpu.VMEM((rights, PULL, 2 * BLK), BF16),
            pltpu.VMEM((lefts, PULL, BLK), F32),
            pltpu.VMEM((rights, PULL, BLK), F32),
        ],
        compiler_params=pltpu.CompilerParams(vmem_limit_bytes=VMEM_LIMIT),
        cost_estimate=pl.CostEstimate(
            flops=tiles * 2 * BLK * BLK * (STACK + 4 * PULL),
            bytes_accessed=4 * D_EMB * SPAN * 2 * (col_count + row_count),
            transcendentals=tiles * BLK * BLK,
        ),
        name="forces",
    )(meta, listing, neg_rows, neg_cols, weights, row_y, *col_y)
    return outs[0], outs[1:]


def shards(inputs, rho, sigma, embed, knn_blocks, knn_seeds, neg_rows, neg_cols, neg_count):
    row_count = lax.axis_size("row")
    col_count = lax.axis_size("col")
    shifts = row_count // 2 + 1
    row, col = lax.axis_index("row"), lax.axis_index("col")
    listing = knn_blocks.reshape(-1)
    seeds = knn_seeds.reshape(-1)
    row_list, col_list = neg_rows.reshape(-1), neg_cols.reshape(-1)
    meta = jnp.stack([row, col, neg_count[0, 0]]).astype(I32)

    def from_shift(value, shift):
        pairs = [((r + shift) % row_count, r) for r in range(row_count)]
        return lax.ppermute(value, "row", pairs)

    def from_half(value):
        half = row_count // 2
        pairs = [(r + half, r) if r % 2 == 0 else (r, r + half) for r in range(half)]
        return lax.ppermute(value, "row", pairs)

    def to_shift(value, shift):
        pairs = [(r, (r + shift) % row_count) for r in range(row_count)]
        return lax.ppermute(value, "row", pairs)

    row_x = lax.all_gather(inputs, "col", axis=0, tiled=False)
    col_x = [inputs]
    for shift in range(1, shifts):
        col_x.append(from_half(inputs) if 2 * shift == row_count else from_shift(inputs, shift))

    squares = jnp.sum(inputs * inputs, axis=1)
    seed_row = jnp.zeros((SPAN,), F32).at[: seeds.shape[0]].set(seeds.astype(F32))
    params = jnp.stack([rho, sigma, squares, seed_row])
    pack = jnp.concatenate([embed, params, jnp.zeros((PACK - D_EMB - 4, SPAN), F32)], axis=0)
    row_pack = lax.all_gather(pack, "col", axis=0, tiled=False)
    col_pack = [pack] + [from_shift(pack, shift) for shift in range(1, row_count)]

    plane_seeds = row_pack[:, SEEDS, : seeds.shape[0]].reshape(col_count, col_count, row_count)
    own_column = lax.dynamic_index_in_dim(plane_seeds, col, 1, keepdims=False)
    seeds_back = []
    for shift in range(shifts):
        wanted = lax.dynamic_index_in_dim(own_column, (row - shift) % row_count, 1, keepdims=False)
        seeds_back.append(from_shift(wanted, shift) if shift else wanted)
    seeds_back = jnp.concatenate(seeds_back).astype(I32)

    weights = pair_weights(
        row_count, col_count, meta, listing, seeds, seeds_back, row_x, row_pack, col_x, col_pack[:shifts]
    )

    row_y, col_y = row_pack, col_pack
    for step in range(STEPS):
        if step:
            row_y = lax.all_gather(embed, "col", axis=0, tiled=False)
            col_y = [embed] + [from_shift(embed, shift) for shift in range(1, row_count)]
        row_force, col_force = pair_forces(
            row_count, col_count, meta, listing, row_list, col_list, weights, row_y, col_y
        )
        row_parts = lax.all_to_all(row_force, "col", split_axis=0, concat_axis=0, tiled=True)
        force = jnp.sum(row_parts, axis=0) + col_force[0]
        for shift in range(1, row_count):
            force = force + to_shift(col_force[shift], shift)
        embed = embed + STEP_SIZE * force
    return (embed, force * FORCE_SCALE)


def solution(mesh):
    in_specs = (
        P(("row", "col"), None),
        P(("row", "col")),
        P(("row", "col")),
        P(None, ("row", "col")),
        P("row", "col", None, None, None),
        P("row", "col", None, None),
        P("row", "col", None),
        P("row", "col", None),
        P("row", "col"),
    )
    out_specs = (P(None, ("row", "col")), P(None, ("row", "col")))
    return jax.shard_map(shards, mesh=mesh, in_specs=in_specs, out_specs=out_specs, check_vma=False)
```

time: 574 us -> 165 us (0.29); the launches traced: 567 us -> 167 us
  waiting for transfers between devices: 173 us -> 17 us
  local copies, waits for them, and re-layouts: 116 us -> 6.01 us
  matrix products: 97.1 us -> 0 us
  blocking collectives: 99.7 us -> 22.8 us
  loops' own time: 48.1 us -> 0 us
  starting transfers between devices: 9.72 us -> 55.8 us
  Pallas kernels: 0 us -> 43.3 us
    dot_general x66 -> x0, matrix products: 97.1 us -> none  [the longest x18 38.4 us: pair_kernel(): gram = jnp.einsum('dsi,dsj->sij', left, right, precision=FULL_PRECISION)]
    all_gather x2 -> x1, waiting for transfers between devices: 91 us -> 3.37 us  [shards(): row_x = lax.all_gather(inputs, 'col', axis=0, tiled=False)]
    reduce_scatter x4 -> x0, waiting for transfers between devices: 80 us -> none  [the longest x2 70.3 us: shards(): lax.psum_scatter(row_force.reshape(D_EMB, col_count * CB * BLK), 'col', s...]
    all_gather x6 -> x2, blocking collectives: 99.7 us -> 22.8 us  [the longest x1 12.8 us: shards(): row_pack = lax.all_gather(pack, 'col', axis=0, tiled=False)]
    gather x84 -> x0, local copies, waits for them, and re-layouts: 64 us -> none  [the longest x8 20.3 us: distances(): right = col_blocks[chosen, col_pick]]
    another operation x3 -> x0, loops' own time: 48.1 us -> none  [the longest x2 32.1 us: shards(): attract = lax.map(attract_group, groups)]
    pallas_call x0 -> x3, Pallas kernels: none -> 43.3 us  [the longest x2 29.9 us: pair_forces(): pl.pallas_call(functools.partial(force_kernel, row_count, col_count), in_...]
    ppermute x0 -> x16, starting transfers between devices: none -> 39.2 us  [the longest x9 29.3 us: from_shift(): return lax.ppermute(value, 'row', pairs)]
  transfers between devices with their start and end apart: 8 -> 19, of which waited for: 5 -> 6; matrix products, arithmetic and copies ran while one was open for 15% -> 5% of each run, Pallas kernels for 0% -> 8%
where the time goes in v1:
time: 165 us; the launch traced here: 167 us
  starting transfers between devices  55.8 us (34%)
  Pallas kernels  43.3 us (26%)
  blocking collectives  22.8 us (14%)
  waiting for transfers between devices  17 us (10%)
  between operations  14.9 us (9%)
  other arithmetic  7.03 us (4%)
  local copies, waits for them, and re-layouts  6.01 us (4%)
    pallas_call x2, Pallas kernels, pair_forces(): pl.pallas_call(functools.partial(force_kernel, row_count, col_count), in_...  29.9 us
    ppermute x9, starting transfers between devices, from_shift(): return lax.ppermute(value, 'row', pairs)  29.3 us
    all_to_all x2, starting transfers between devices, shards(): lax.all_to_all(row_force, 'col', split_axis=0, concat_axis=0, tiled=True)  16.6 us
    pallas_call x1, Pallas kernels, pair_weights(): pl.pallas_call(functools.partial(weights_kernel, row_count, col_count), g...  13.4 us
    all_gather x1, blocking collectives, shards(): row_pack = lax.all_gather(pack, 'col', axis=0, tiled=False)  12.8 us
    all_to_all x2, waiting for transfers between devices, shards(): lax.all_to_all(row_force, 'col', split_axis=0, concat_axis=0, tiled=True)  10.9 us
    all_gather x1, blocking collectives, shards(): row_y = lax.all_gather(embed, 'col', axis=0, tiled=False)  10 us
    ppermute x6, starting transfers between devices, to_shift(): return lax.ppermute(value, 'row', pairs)  8.61 us
  transfers between devices with their start and end apart: 19, of which 6 were waited for; matrix products, arithmetic and copies ran while one was open for 5% of the time, Pallas kernels for 8%

profile of v1, /device:TPU:0, one launch (start us, length us, event | category | flops | bytes accessed | tf_op | source)
XLA Modules:
  0.0 166.9 jit_solution(10898552243936182017)
XLA Ops:
  7.2 0.7 all-gather.5.cloned.1.call-update
  7.9 5.1 %collective-permute-start.2 = (f32[256,768]{1,0:T(8,128)}, f32[256,768]{1,0:T(8,128)S(1)}, u32[]{:S(2)}, u32[]{:S(2)}) collective-permute-start(f32[256,768]{1,0:T(8,128)} %rest_0_.1), channel_id=1, source_target_pairs={{8,0},{16,8},{24,16},{0,24},{9,1},{17,9},{25,17},{1,25},{10,2},{18... | collective-permute-start | bytes 2359304 | tf_op jit(solution)/shard_map/ppermute | solution.py:309
  13.0 1.3 collective-permute-start.3
  14.3 0.7 convert_element_type.14
  15.1 1.3 multiply_reduce_fusion
  16.4 1.6 concatenate.8.rest_3_.rest_0_
  18.5 3.2 %collective-permute-start.5 = (f32[72,256]{1,0:T(8,128)S(1)}, f32[72,256]{1,0:T(8,128)S(1)}, u32[]{:S(2)}, u32[]{:S(2)}) collective-permute-start(f32[72,256]{1,0:T(8,128)S(1)} %concatenate.8.rest_3_.rest_0_), channel_id=1, source_target_pairs={{16,0},{24,8},{0,16},{8,24},{17,1},{25,9},{1,17},{9,25},{18,2},{26... | collective-permute-start | bytes 221192 | tf_op jit(solution)/shard_map/ppermute | solution.py:309
  21.7 12.8 %all-gather = f32[576,256]{1,0:T(8,128)S(1)} all-gather(f32[72,256]{1,0:T(8,128)S(1)} %concatenate.8.rest_3_.rest_0_), channel_id=2, replica_groups=mesh['row'=4,'col'=8] {'col'}, dimensions={0}, use_global_device_ids=true | all-gather | bytes 663552 | tf_op jit(solution)/shard_map/all_gather | solution.py:329
  34.6 1.2 collective-permute-start
  35.9 0.8 copy.18
  37.3 0.8 copy.17
  38.1 0.7 reshape.59.listing
  38.8 0.7 reshape.62.seeds
  40.0 11.1 %collective-permute-start.1 = (f32[8]{0:T(128)S(1)}, f32[8]{0:T(128)S(1)}, u32[]{:S(2)}, u32[]{:S(2)}) collective-permute-start(f32[8]{0:T(128)S(1)} %get-tuple-element.37), channel_id=1, source_target_pairs={{16,0},{24,8},{0,16},{8,24},{17,1},{25,9},{1,17},{9,25},{18,2},{26... | collective-permute-start | bytes 104 | tf_op jit(solution)/shard_map/ppermute | solution.py:309
  51.1 1.5 collective-permute-done.1
  52.6 3.9 %collective-permute-start.6 = (f32[72,256]{1,0:T(8,128)S(1)}, f32[72,256]{1,0:T(8,128)S(1)}, u32[]{:S(2)}, u32[]{:S(2)}) collective-permute-start(f32[72,256]{1,0:T(8,128)S(1)} %concatenate.8.rest_3_.rest_0_), channel_id=1, source_target_pairs={{24,0},{0,8},{8,16},{16,24},{25,1},{1,9},{9,17},{17,25},{26,2},{2,... | collective-permute-start | bytes 221192 | tf_op jit(solution)/shard_map/ppermute | solution.py:309
  57.1 3.4 %all-gather.5.cloned.1.call-done = f32[2048,768]{1,0:T(8,128)} async-done(((f32[256,768]{1,0:T(8,128)}), f32[2048,768]{1,0:T(8,128)}) %all-gather.5.cloned.1.call-update) | async-done | bytes 6291472 | tf_op jit(solution)/shard_map/all_gather | solution.py:320
  60.5 13.4 %weights.1 = bf16[8,3,128,128]{3,2,1,0:T(8,128)(2,1)} custom-call(s32[3]{0:T(128)} %pad_add_fusion.meta, s32[64]{0:T(128)} %reshape.59.listing, s32[32]{0:T(128)} %reshape.62.seeds, s32[24]{0:T(128)} %maximum_convert_fusion.seeds_back, f32[8,256,768]{2,1,0:T(8,128)} %bitcast.24, f32[8,72,256]{2,1,0:T(8,128)} %bitcast.26, f32[256,768]{1,0:T(8,128)} %rest_0_.1, ...), custom_call_target="tpu_custom_call" | custom-call | flops 1811939328 | bytes 8650752 | tf_op jit(solution)/shard_map/weights/pallas_call | solution.py:131
  74.6 14.9 %forces.2 = (f32[8,64,256]{2,1,0:T(8,128)}, f32[64,256]{1,0:T(8,128)}, f32[64,256]{1,0:T(8,128)}, f32[64,256]{1,0:T(8,128)}, f32[64,256]{1,0:T(8,128)}) custom-call(s32[3]{0:T(128)} %pad_add_fusion.meta, s32[64]{0:T(128)} %reshape.59.listing, s32[48]{0:T(128)} %bitcast.35, s32[48]{0:T(128)} %bitcast.37, bf16[24,128,128]{2,1,0:T(8,128)(2,1)} %bitcast.28, ...), custom_call_target="tpu_custom_call" | custom-call | flops 1744830464 | bytes 1572864 | tf_op jit(solution)/shard_map/forces/pallas_call | solution.py:272
  89.6 8.1 %all-to-all-start = ((f32[8,64,256]{2,1,0:T(8,128)}), f32[8,64,256]{2,1,0:T(8,128)S(1)}, u32[]{:S(2)}, u32[]{:S(2)}) async-start(f32[8,64,256]{2,1,0:T(8,128)} %get-tuple-element.24), calls=%async_computation | async-start | bytes 1048576 | tf_op jit(solution)/shard_map/all_to_all | solution.py:352
  97.7 4.1 %collective-permute-start.8 = (f32[64,256]{1,0:T(8,128)}, f32[64,256]{1,0:T(8,128)S(1)}, u32[]{:S(2)}, u32[]{:S(2)}) collective-permute-start(f32[64,256]{1,0:T(8,128)} %get-tuple-element.27), channel_id=1, source_target_pairs={{0,16},{8,24},{16,0},{24,8},{1,17},{9,25},{17,1},{25,9},{2,18},{10... | collective-permute-start | bytes 196616 | tf_op jit(solution)/shard_map/ppermute | solution.py:318
  101.8 5.6 %all-to-all-done = f32[8,64,256]{2,1,0:T(8,128)S(1)} async-done(((f32[8,64,256]{2,1,0:T(8,128)}), f32[8,64,256]{2,1,0:T(8,128)S(1)}, u32[]{:S(2)}, u32[]{:S(2)}) %all-to-all-start) | async-done | bytes 524320 | tf_op jit(solution)/shard_map/all_to_all | solution.py:352
  107.5 0.9 multiply_add_fusion.1.rest_0_
  108.4 3.6 %collective-permute-start.10 = (f32[64,256]{1,0:T(8,128)S(1)}, f32[64,256]{1,0:T(8,128)S(1)}, u32[]{:S(2)}, u32[]{:S(2)}) collective-permute-start(f32[64,256]{1,0:T(8,128)S(1)} %multiply_add_fusion.1.rest_0_), channel_id=1, source_target_pairs={{8,0},{16,8},{24,16},{0,24},{9,1},{17,9},{25,17},{1,25},{10,2},{18... | collective-permute-start | bytes 196616 | tf_op jit(solution)/shard_map/ppermute | solution.py:309
  112.0 0.6 collective-permute-start.12
  112.6 10.0 %all-gather.2 = f32[512,256]{1,0:T(8,128)} all-gather(f32[64,256]{1,0:T(8,128)S(1)} %multiply_add_fusion.1.rest_0_), channel_id=4, replica_groups=mesh['row'=4,'col'=8] {'col'}, dimensions={0}, use_global_device_ids=true | all-gather | bytes 589824 | tf_op jit(solution)/shard_map/all_gather | solution.py:347
  123.3 14.9 %forces.3 = (f32[8,64,256]{2,1,0:T(8,128)}, f32[64,256]{1,0:T(8,128)}, f32[64,256]{1,0:T(8,128)}, f32[64,256]{1,0:T(8,128)}, f32[64,256]{1,0:T(8,128)}) custom-call(s32[3]{0:T(128)} %pad_add_fusion.meta, s32[64]{0:T(128)} %reshape.59.listing, s32[48]{0:T(128)} %bitcast.36, s32[48]{0:T(128)} %bitcast.38, bf16[24,128,128]{2,1,0:T(8,128)(2,1)} %bitcast.29, ...), custom_call_target="tpu_custom_call" | custom-call | flops 1744830464 | bytes 1572864 | tf_op jit(solution)/shard_map/forces/pallas_call | solution.py:272
  138.2 8.6 %all-to-all-start.1 = ((f32[8,64,256]{2,1,0:T(8,128)}), f32[8,64,256]{2,1,0:T(8,128)S(1)}, u32[]{:S(2)}, u32[]{:S(2)}) async-start(f32[8,64,256]{2,1,0:T(8,128)} %get-tuple-element.29), calls=%async_computation.1 | async-start | bytes 1048576 | tf_op jit(solution)/shard_map/all_to_all | solution.py:352
  146.8 4.5 %collective-permute-start.14 = (f32[64,256]{1,0:T(8,128)}, f32[64,256]{1,0:T(8,128)S(1)}, u32[]{:S(2)}, u32[]{:S(2)}) collective-permute-start(f32[64,256]{1,0:T(8,128)} %get-tuple-element.32), channel_id=1, source_target_pairs={{0,16},{8,24},{16,0},{24,8},{1,17},{9,25},{17,1},{25,9},{2,18},{10... | collective-permute-start | bytes 196616 | tf_op jit(solution)/shard_map/ppermute | solution.py:318
  151.3 5.3 %all-to-all-done.1 = f32[8,64,256]{2,1,0:T(8,128)S(1)} async-done(((f32[8,64,256]{2,1,0:T(8,128)}), f32[8,64,256]{2,1,0:T(8,128)S(1)}, u32[]{:S(2)}, u32[]{:S(2)}) %all-to-all-start.1) | async-done | bytes 524320 | tf_op jit(solution)/shard_map/all_to_all | solution.py:352
  157.1 1.5 broadcast_multiply_fusion
  158.6 1.5 multiply_add_fusion
  (57 shorter events, 3.9 us)
Async XLA Ops:
  7.2 53.3 %all-gather.5.cloned.1.call-start = ((), (), s32[]{:S(2)}) async-start(), calls=%async_computation.2 | async-start | bytes 7077888 | tf_op jit(solution)/shard_map/all_gather | solution.py:320
  7.9 49.2 %collective-permute-start.2 = (f32[256,768]{1,0:T(8,128)}, f32[256,768]{1,0:T(8,128)S(1)}, u32[]{:S(2)}, u32[]{:S(2)}) collective-permute-start(f32[256,768]{1,0:T(8,128)} %rest_0_.1), channel_id=1, source_target_pairs={{8,0},{16,8},{24,16},{0,24},{9,1},{17,9},{25,17},{1,25},{10,2},{18... | collective-permute-start | bytes 2359304 | tf_op jit(solution)/shard_map/ppermute | solution.py:309
  13.0 44.1 %collective-permute-start.3 = (f32[256,768]{1,0:T(8,128)}, f32[256,768]{1,0:T(8,128)S(1)}, u32[]{:S(2)}, u32[]{:S(2)}) collective-permute-start(f32[256,768]{1,0:T(8,128)} %rest_0_.1), channel_id=1, source_target_pairs={{16,0},{8,24},{17,1},{9,25},{18,2},{10,26},{19,3},{11,27},{20,4},{... | collective-permute-start | bytes 2359304 | tf_op jit(solution)/shard_map/ppermute | solution.py:314
  18.0 42.5 %copy-start.3 = (f32[72,256]{1,0:T(8,128)}, f32[72,256]{1,0:T(8,128)S(1)}, u32[]{:S(2)}) copy-start(f32[72,256]{1,0:T(8,128)S(1)} %concatenate.8.rest_3_.rest_0_) | copy-start | bytes 221188
  18.0 39.1 %collective-permute-start.4 = (f32[72,256]{1,0:T(8,128)S(1)}, f32[72,256]{1,0:T(8,128)S(1)}, u32[]{:S(2)}, u32[]{:S(2)}) collective-permute-start(f32[72,256]{1,0:T(8,128)S(1)} %concatenate.8.rest_3_.rest_0_), channel_id=1, source_target_pairs={{8,0},{16,8},{24,16},{0,24},{9,1},{17,9},{25,17},{1,25},{10,2},{18... | collective-permute-start | bytes 221192 | tf_op jit(solution)/shard_map/ppermute | solution.py:309
  18.5 38.6 %collective-permute-start.5 = (f32[72,256]{1,0:T(8,128)S(1)}, f32[72,256]{1,0:T(8,128)S(1)}, u32[]{:S(2)}, u32[]{:S(2)}) collective-permute-start(f32[72,256]{1,0:T(8,128)S(1)} %concatenate.8.rest_3_.rest_0_), channel_id=1, source_target_pairs={{16,0},{24,8},{0,16},{8,24},{17,1},{25,9},{1,17},{9,25},{18,2},{26... | collective-permute-start | bytes 221192 | tf_op jit(solution)/shard_map/ppermute | solution.py:309
  34.5 26.0 %copy-start = (f32[576,256]{1,0:T(8,128)}, f32[576,256]{1,0:T(8,128)S(1)}, u32[]{:S(2)}) copy-start(f32[576,256]{1,0:T(8,128)S(1)} %all-gather) | copy-start | bytes 1769476
  34.6 5.4 %collective-permute-start = (f32[8]{0:T(128)S(1)}, f32[8]{0:T(128)S(1)}, u32[]{:S(2)}, u32[]{:S(2)}) collective-permute-start(f32[8]{0:T(128)S(1)} %get-tuple-element.38), channel_id=1, source_target_pairs={{8,0},{16,8},{24,16},{0,24},{9,1},{17,9},{25,17},{1,25},{10,2},{18... | collective-permute-start | bytes 104 | tf_op jit(solution)/shard_map/ppermute | solution.py:309
  40.0 12.6 %collective-permute-start.1 = (f32[8]{0:T(128)S(1)}, f32[8]{0:T(128)S(1)}, u32[]{:S(2)}, u32[]{:S(2)}) collective-permute-start(f32[8]{0:T(128)S(1)} %get-tuple-element.37), channel_id=1, source_target_pairs={{16,0},{24,8},{0,16},{8,24},{17,1},{25,9},{1,17},{9,25},{18,2},{26... | collective-permute-start | bytes 104 | tf_op jit(solution)/shard_map/ppermute | solution.py:309
  52.6 21.4 %collective-permute-start.6 = (f32[72,256]{1,0:T(8,128)S(1)}, f32[72,256]{1,0:T(8,128)S(1)}, u32[]{:S(2)}, u32[]{:S(2)}) collective-permute-start(f32[72,256]{1,0:T(8,128)S(1)} %concatenate.8.rest_3_.rest_0_), channel_id=1, source_target_pairs={{24,0},{0,8},{8,16},{16,24},{25,1},{1,9},{9,17},{17,25},{26,2},{2,... | collective-permute-start | bytes 221192 | tf_op jit(solution)/shard_map/ppermute | solution.py:309
  57.1 3.4 %copy-start.6 = (f32[72,256]{1,0:T(8,128)}, f32[72,256]{1,0:T(8,128)S(1)}, u32[]{:S(2)}) copy-start(f32[72,256]{1,0:T(8,128)S(1)} %collective-permute-done.4.rest_4_.rest_1_) | copy-start | bytes 221188
  57.1 3.4 %copy-start.7 = (f32[72,256]{1,0:T(8,128)}, f32[72,256]{1,0:T(8,128)S(1)}, u32[]{:S(2)}) copy-start(f32[72,256]{1,0:T(8,128)S(1)} %collective-permute-done.5.rest_5_.rest_2_) | copy-start | bytes 221188
  57.1 3.4 %copy-start.1 = (f32[256,768]{1,0:T(8,128)}, f32[256,768]{1,0:T(8,128)S(1)}, u32[]{:S(2)}) copy-start(f32[256,768]{1,0:T(8,128)S(1)} %collective-permute-done.2.rest_1_) | copy-start | bytes 2359300
  57.1 3.4 %copy-start.2 = (f32[256,768]{1,0:T(8,128)}, f32[256,768]{1,0:T(8,128)S(1)}, u32[]{:S(2)}) copy-start(f32[256,768]{1,0:T(8,128)S(1)} %collective-permute-done.3.rest_2_) | copy-start | bytes 2359300
  74.0 33.5 %copy-start.5 = (f32[64,256]{1,0:T(8,128)S(1)}, f32[64,256]{1,0:T(8,128)}, u32[]{:S(2)}) copy-start(f32[64,256]{1,0:T(8,128)} %param.14) | copy-start | bytes 196612
  74.0 0.6 copy-start.8
  89.6 17.8 %all-to-all-start = ((f32[8,64,256]{2,1,0:T(8,128)}), f32[8,64,256]{2,1,0:T(8,128)S(1)}, u32[]{:S(2)}, u32[]{:S(2)}) async-start(f32[8,64,256]{2,1,0:T(8,128)} %get-tuple-element.24), calls=%async_computation | async-start | bytes 1048576 | tf_op jit(solution)/shard_map/all_to_all | solution.py:352
  97.6 9.8 %collective-permute-start.7 = (f32[64,256]{1,0:T(8,128)}, f32[64,256]{1,0:T(8,128)S(1)}, u32[]{:S(2)}, u32[]{:S(2)}) collective-permute-start(f32[64,256]{1,0:T(8,128)} %get-tuple-element.26), channel_id=1, source_target_pairs={{0,8},{8,16},{16,24},{24,0},{1,9},{9,17},{17,25},{25,1},{2,10},{10... | collective-permute-start | bytes 196616 | tf_op jit(solution)/shard_map/ppermute | solution.py:318
  97.7 9.8 %collective-permute-start.8 = (f32[64,256]{1,0:T(8,128)}, f32[64,256]{1,0:T(8,128)S(1)}, u32[]{:S(2)}, u32[]{:S(2)}) collective-permute-start(f32[64,256]{1,0:T(8,128)} %get-tuple-element.27), channel_id=1, source_target_pairs={{0,16},{8,24},{16,0},{24,8},{1,17},{9,25},{17,1},{25,9},{2,18},{10... | collective-permute-start | bytes 196616 | tf_op jit(solution)/shard_map/ppermute | solution.py:318
  101.8 5.7 %collective-permute-start.9 = (f32[64,256]{1,0:T(8,128)}, f32[64,256]{1,0:T(8,128)S(1)}, u32[]{:S(2)}, u32[]{:S(2)}) collective-permute-start(f32[64,256]{1,0:T(8,128)} %get-tuple-element.28), channel_id=1, source_target_pairs={{0,24},{8,0},{16,8},{24,16},{1,25},{9,1},{17,9},{25,17},{2,26},{10... | collective-permute-start | bytes 196616 | tf_op jit(solution)/shard_map/ppermute | solution.py:318
  108.4 14.3 %copy-start.4 = (f32[64,256]{1,0:T(8,128)}, f32[64,256]{1,0:T(8,128)S(1)}, u32[]{:S(2)}) copy-start(f32[64,256]{1,0:T(8,128)S(1)} %multiply_add_fusion.1.rest_0_) | copy-start | bytes 196612
  108.4 14.3 %collective-permute-start.10 = (f32[64,256]{1,0:T(8,128)S(1)}, f32[64,256]{1,0:T(8,128)S(1)}, u32[]{:S(2)}, u32[]{:S(2)}) collective-permute-start(f32[64,256]{1,0:T(8,128)S(1)} %multiply_add_fusion.1.rest_0_), channel_id=1, source_target_pairs={{8,0},{16,8},{24,16},{0,24},{9,1},{17,9},{25,17},{1,25},{10,2},{18... | collective-permute-start | bytes 196616 | tf_op jit(solution)/shard_map/ppermute | solution.py:309
  112.0 10.7 %collective-permute-start.11 = (f32[64,256]{1,0:T(8,128)S(1)}, f32[64,256]{1,0:T(8,128)S(1)}, u32[]{:S(2)}, u32[]{:S(2)}) collective-permute-start(f32[64,256]{1,0:T(8,128)S(1)} %multiply_add_fusion.1.rest_0_), channel_id=1, source_target_pairs={{16,0},{24,8},{0,16},{8,24},{17,1},{25,9},{1,17},{9,25},{18,2},{26... | collective-permute-start | bytes 196616 | tf_op jit(solution)/shard_map/ppermute | solution.py:309
  112.0 10.7 %collective-permute-start.12 = (f32[64,256]{1,0:T(8,128)S(1)}, f32[64,256]{1,0:T(8,128)S(1)}, u32[]{:S(2)}, u32[]{:S(2)}) collective-permute-start(f32[64,256]{1,0:T(8,128)S(1)} %multiply_add_fusion.1.rest_0_), channel_id=1, source_target_pairs={{24,0},{0,8},{8,16},{16,24},{25,1},{1,9},{9,17},{17,25},{26,2},{2,... | collective-permute-start | bytes 196616 | tf_op jit(solution)/shard_map/ppermute | solution.py:309
  122.6 0.6 copy-start.9
  122.6 0.6 copy-start.10
  122.7 0.6 copy-start.11
  138.2 18.3 %all-to-all-start.1 = ((f32[8,64,256]{2,1,0:T(8,128)}), f32[8,64,256]{2,1,0:T(8,128)S(1)}, u32[]{:S(2)}, u32[]{:S(2)}) async-start(f32[8,64,256]{2,1,0:T(8,128)} %get-tuple-element.29), calls=%async_computation.1 | async-start | bytes 1048576 | tf_op jit(solution)/shard_map/all_to_all | solution.py:352
  146.8 9.8 %collective-permute-start.13 = (f32[64,256]{1,0:T(8,128)}, f32[64,256]{1,0:T(8,128)S(1)}, u32[]{:S(2)}, u32[]{:S(2)}) collective-permute-start(f32[64,256]{1,0:T(8,128)} %get-tuple-element.31), channel_id=1, source_target_pairs={{0,8},{8,16},{16,24},{24,0},{1,9},{9,17},{17,25},{25,1},{2,10},{10... | collective-permute-start | bytes 196616 | tf_op jit(solution)/shard_map/ppermute | solution.py:318
  146.8 9.8 %collective-permute-start.14 = (f32[64,256]{1,0:T(8,128)}, f32[64,256]{1,0:T(8,128)S(1)}, u32[]{:S(2)}, u32[]{:S(2)}) collective-permute-start(f32[64,256]{1,0:T(8,128)} %get-tuple-element.32), channel_id=1, source_target_pairs={{0,16},{8,24},{16,0},{24,8},{1,17},{9,25},{17,1},{25,9},{2,18},{10... | collective-permute-start | bytes 196616 | tf_op jit(solution)/shard_map/ppermute | solution.py:318
  151.3 5.8 %collective-permute-start.15 = (f32[64,256]{1,0:T(8,128)}, f32[64,256]{1,0:T(8,128)S(1)}, u32[]{:S(2)}, u32[]{:S(2)}) collective-permute-start(f32[64,256]{1,0:T(8,128)} %get-tuple-element.33), channel_id=1, source_target_pairs={{0,24},{8,0},{16,8},{24,16},{1,25},{9,1},{17,9},{25,17},{2,26},{10... | collective-permute-start | bytes 196616 | tf_op jit(solution)/shard_map/ppermute | solution.py:318
Sparse Core Ops, SparseCore 0:
  9.9 50.5 all-gather.4

commit v2 on v1

--- a/solution.py
+++ b/solution.py
@@ -21,7 +21,7 @@
 PACK = 72
 STACK = 4 * D_EMB
 PULL = 2 * D_EMB + 16
-UNROLL = 4
+UNROLL = 12
 F32, BF16, I32 = jnp.float32, jnp.bfloat16, jnp.int32
 VMEM_LIMIT = 56 * 2**20
 
@@ -52,113 +52,103 @@
     return jnp.where(row < half, row % 2 == 0, (row - half) % 2 == 1)
 
 
-def weights_kernel(row_count, col_count, meta, listing, seeds, seeds_back, row_x, row_pack, *rest):
-    shifts = row_count // 2 + 1
-    col_x, col_pack = rest[:shifts], rest[shifts : 2 * shifts]
-    out, high_c, low_c, col_params = rest[2 * shifts :]
-    group = pl.program_id(0)
+def weights_kernel(sizes, plan, spans, meta, listing, seeds, seeds_back, *rest):
+    row_count, col_count = sizes
+    row_spans, col_spans = spans
+    count = len(row_spans) + len(col_spans)
+    arrays = rest[: len(rest) - 7 - count]
+    packs = rest[len(arrays) : len(arrays) + count]
+    out, raw, high, low, col_params, grams, sems = rest[len(arrays) + count :]
     row, col = meta[0], meta[1]
-
-    @pl.when(group == 0)
-    def _():
-        for shift in range(shifts):
-            high, low = split(col_x[shift][...])
-            high_c[shift], low_c[shift] = high, low
-            for block in range(CB):
-                params = col_pack[shift][RHO : RHO + 8, block * BLK : (block + 1) * BLK]
-                col_params[shift, block] = params.T
-
-    high_r, low_r = split(row_x[0])
-    high_r = high_r.reshape(CB, BLK, high_r.shape[1])
-    low_r = low_r.reshape(CB, BLK, low_r.shape[1])
+    places = col_spans + row_spans
+    copies = []
+    for place, (array, index) in enumerate(places):
+        source = arrays[array] if index is None else arrays[array].at[index]
+        copies.append(pltpu.make_async_copy(source, raw.at[place], sems.at[place]))
+        copies[-1].start()
+    for place in range(len(col_spans)):
+        for block in range(CB):
+            params = packs[place][RHO : RHO + 8, block * BLK : (block + 1) * BLK]
+            col_params[place, block] = params.T
     positions_j = lax.broadcasted_iota(I32, (BLK, BLK), 0)
     positions_i = lax.broadcasted_iota(I32, (BLK, BLK), 1)
 
-    for shift in range(shifts):
-        if shift == 0:
-            offset = lax.rem(group - col + col_count, col_count)
-            active = (2 * offset < col_count) | ((2 * offset == col_count) & (2 * col < col_count))
-        else:
-            active = takes_shift(shift, row, row_count)
-        other = lax.rem(row + shift, row_count)
-        entry = (group * row_count + other) * 2
-        row_pick, col_pick = listing[entry], listing[entry + 1]
-
-        @pl.when(jnp.logical_not(active))
-        def _():
-            out[0, shift] = jnp.zeros((BLK, BLK), BF16)
-
-        for pick in range(CB):
-
-            @pl.when(active & (row_pick == pick))
-            def _():
-                start = pl.multiple_of(col_pick * BLK, BLK)
-                left_high = high_c[shift, pl.ds(start, BLK), :]
-                left_low = low_c[shift, pl.ds(start, BLK), :]
-                gram = (
-                    nt_dot(left_high, low_r[pick])
-                    + nt_dot(left_low, high_r[pick])
-                    + nt_dot(left_high, high_r[pick])
-                )
-                lanes = slice(pick * BLK, (pick + 1) * BLK)
-                rho_i = row_pack[0, RHO - D_EMB : RHO - D_EMB + 1, lanes]
-                sigma_i = row_pack[0, SIGMA - D_EMB : SIGMA - D_EMB + 1, lanes]
-                square_i = row_pack[0, SQUARES - D_EMB : SQUARES - D_EMB + 1, lanes]
-                params_j = col_params[shift, col_pick]
-                rho_j, sigma_j, square_j = params_j[:, 0:1], params_j[:, 1:2], params_j[:, 2:3]
-                total = square_j + square_i - 2.0 * gram
-                distance = jnp.sqrt(jnp.maximum(total, 1.0))
-                seed = seeds[group * row_count + other]
-                seed_back = seeds_back[shift * col_count + group]
-                ahead = hash_bits(seed, positions_i, positions_j) * jnp.exp(
-                    jnp.maximum(distance - rho_i, 0.0) * (-1.0 / sigma_i)
-                )
-                behind = hash_bits(seed_back, positions_j, positions_i) * jnp.exp(
-                    jnp.maximum(distance - rho_j, 0.0) * (-1.0 / sigma_j)
-                )
-                weights = (ahead + behind - ahead * behind).astype(BF16)
-                if shift == 0:
-                    weights = (weights.astype(F32) * jnp.where(group == col, 0.5, 1.0)).astype(BF16)
-                out[0, shift] = weights
-
-
-def pair_weights(row_count, col_count, meta, listing, seeds, seeds_back, row_x, row_pack, col_x, col_pack):
-    shifts = row_count // 2 + 1
-    depth = row_x.shape[-1]
+    def take(place):
+        copies[place].wait()
+        high[place], low[place] = split(raw[place])
+
+    for place in range(len(col_spans)):
+        take(place)
+    for line in range(len(row_spans)):
+        place = len(col_spans) + line
+        take(place)
+        tiles = [(tile, entry) for tile, entry in enumerate(plan) if entry[0] == line]
+        picks = {}
+        for tile, (_, column, shift) in tiles:
+            group = meta[3 + line]
+            other = lax.rem(row + shift, row_count)
+            entry = (group * row_count + other) * 2
+            start_i = pl.multiple_of(listing[entry] * BLK, BLK)
+            start_j = pl.multiple_of(listing[entry + 1] * BLK, BLK)
+            picks[tile] = group, other, start_i, listing[entry + 1]
+            high_j, low_j = high[column, pl.ds(start_j, BLK), :], low[column, pl.ds(start_j, BLK), :]
+            high_i, low_i = high[place, pl.ds(start_i, BLK), :], low[place, pl.ds(start_i, BLK), :]
+            grams[tile] = nt_dot(high_j, low_i) + nt_dot(low_j, high_i) + nt_dot(high_j, high_i)
+        for tile, (_, column, shift) in tiles:
+            group, other, start_i, col_pick = picks[tile]
+            params_i = packs[place][RHO : RHO + 8, pl.ds(start_i, BLK)]
+            rho_i, sigma_i, square_i = params_i[0:1], params_i[1:2], params_i[2:3]
+            params_j = col_params[column, col_pick]
+            rho_j, sigma_j, square_j = params_j[:, 0:1], params_j[:, 1:2], params_j[:, 2:3]
+            total = square_j + square_i - 2.0 * grams[tile]
+            distance = jnp.sqrt(jnp.maximum(total, 1.0))
+            seed = seeds[group * row_count + other]
+            seed_back = seeds_back[shift * col_count + group]
+            ahead = hash_bits(seed, positions_i, positions_j) * jnp.exp(
+                jnp.maximum(distance - rho_i, 0.0) * (-1.0 / sigma_i)
+            )
+            behind = hash_bits(seed_back, positions_j, positions_i) * jnp.exp(
+                jnp.maximum(distance - rho_j, 0.0) * (-1.0 / sigma_j)
+            )
+            weights = (ahead + behind - ahead * behind).astype(BF16)
+            if shift == 0:
+                weights = (weights.astype(F32) * jnp.where(group == col, 0.5, 1.0)).astype(BF16)
+            out[tile] = weights
+
+
+def pair_weights(sizes, plan, row_spans, col_spans, meta, listing, seeds, seeds_back, arrays, packs):
+    depth = arrays[0].shape[-1]
     smem = pl.BlockSpec(memory_space=pltpu.SMEM)
     vmem = pl.BlockSpec(memory_space=pltpu.VMEM)
-    tiles = col_count * shifts
+    tiles, count = len(plan), len(row_spans) + len(col_spans)
     return pl.pallas_call(
-        functools.partial(weights_kernel, row_count, col_count),
-        grid=(col_count,),
-        in_specs=[smem] * 4
-        + [
-            pl.BlockSpec((1, SPAN, depth), lambda a: (a, 0, 0)),
-            pl.BlockSpec((1, 8, SPAN), lambda a: (a, D_EMB // 8, 0)),
-        ]
-        + [vmem] * (2 * shifts),
-        out_specs=pl.BlockSpec((1, shifts, BLK, BLK), lambda a: (a, 0, 0, 0)),
-        out_shape=jax.ShapeDtypeStruct((col_count, shifts, BLK, BLK), BF16),
+        functools.partial(weights_kernel, sizes, plan, (row_spans, col_spans)),
+        in_specs=[smem] * 4 + [pl.BlockSpec(memory_space=pl.ANY)] * len(arrays) + [vmem] * count,
+        out_specs=vmem,
+        out_shape=jax.ShapeDtypeStruct((tiles, BLK, BLK), BF16),
         scratch_shapes=[
-            pltpu.VMEM((shifts, SPAN, depth), BF16),
-            pltpu.VMEM((shifts, SPAN, depth), BF16),
-            pltpu.VMEM((shifts, CB, BLK, 8), F32),
+            pltpu.VMEM((count, SPAN, depth), F32),
+            pltpu.VMEM((count, SPAN, depth), BF16),
+            pltpu.VMEM((count, SPAN, depth), BF16),
+            pltpu.VMEM((len(col_spans), CB, BLK, 8), F32),
+            pltpu.VMEM((tiles, BLK, BLK), F32),
+            pltpu.SemaphoreType.DMA((count,)),
         ],
         compiler_params=pltpu.CompilerParams(vmem_limit_bytes=VMEM_LIMIT),
         cost_estimate=pl.CostEstimate(
             flops=tiles * 6 * BLK * BLK * depth,
-            bytes_accessed=(col_count + shifts) * SPAN * depth * 4,
+            bytes_accessed=count * SPAN * depth * 4,
             transcendentals=tiles * 3 * BLK * BLK,
         ),
         name="weights",
-    )(meta, listing, seeds, seeds_back, row_x, row_pack, *col_x, *col_pack)
+    )(meta, listing, seeds, seeds_back, *arrays, *packs)
 
 
 def force_kernel(row_count, col_count, meta, listing, neg_rows, neg_cols, weights, row_y, *rest):
     shifts = row_count // 2 + 1
     col_y = rest[:row_count]
     row_force, col_force = rest[row_count], rest[row_count + 1 : 2 * row_count + 1]
-    left_gram, right_gram, left_pull, right_pull, left_acc, right_acc = rest[2 * row_count + 1 :]
+    left_gram, right_gram, left_pull, right_pull, left_acc, right_acc, held_v, held_h = rest[2 * row_count + 1 :]
     row, col, live = meta[0], meta[1], meta[2]
     iota = lax.broadcasted_iota(I32, (D_EMB, BLK), 0)
     ones = jnp.ones((16, BLK), BF16)
@@ -208,20 +198,27 @@
     def kernel_of(left, right):
         return 1.0 / nn_dot(right_gram[right], left_gram[left])
 
-    def apply(left, right, coefficient):
-        high, low = split(coefficient)
-        left_part = nn_dot(right_pull[right], jnp.concatenate([high, low], axis=0))
-        right_part = nt_dot(left_pull[left], jnp.concatenate([high, low], axis=1))
-        left_acc[left] += left_part
-        right_acc[right] += right_part
+    def apply_all(tiles_):
+        for lane, (left, right, coefficient) in enumerate(tiles_):
+            high, low = split(coefficient())
+            held_v[lane, :BLK], held_v[lane, BLK:] = high, low
+            held_h[lane, :, :BLK], held_h[lane, :, BLK:] = high, low
+        for lane, (left, right, _) in enumerate(tiles_):
+            left_acc[left] += nn_dot(right_pull[right], held_v[lane])
+        for lane, (left, right, _) in enumerate(tiles_):
+            right_acc[right] += nt_dot(left_pull[left], held_h[lane])
+
+    def near_active(group):
+        offset = lax.rem(group - col + col_count, col_count)
+        return (2 * offset < col_count) | ((2 * offset == col_count) & (2 * col < col_count))
 
     near = col_count // 2 + 1
     tiles = near + col_count * (shifts - 1)
-    spare = lax.rem(col + col_count - 1, col_count) * shifts
     last = jnp.where(takes_shift(shifts - 1, row, row_count), tiles, tiles - col_count)
 
     @pl.loop(0, lax.div(last + UNROLL - 1, UNROLL))
     def _(step):
+        batch = []
         for lane in range(UNROLL):
             index = step * UNROLL + lane
             far = jnp.maximum(index - near, 0)
@@ -229,14 +226,21 @@
             group = jnp.where(index < near, lax.rem(col + index, col_count), lax.rem(far, col_count))
             inside = index < last
             shift = jnp.where(inside, shift, 0)
-            slot = jnp.where(inside, group * shifts + shift, spare)
+            inside &= (shift > 0) | near_active(group)
+            slot = shift * col_count + group
             entry = (group * row_count + lax.rem(row + shift, row_count)) * 2
             left = group * CB + listing[entry]
             right = shift * CB + listing[entry + 1]
-            apply(left, right, weights[slot].astype(F32) * kernel_of(left, right))
+
+            def pull(left=left, right=right, slot=slot, inside=inside):
+                return weights[slot].astype(F32) * (kernel_of(left, right) * jnp.where(inside, 1.0, 0.0))
+
+            batch.append((left, right, pull))
+        apply_all(batch)
 
     @pl.loop(0, lax.div(live + UNROLL - 1, UNROLL))
     def _(step):
+        batch = []
         for lane in range(UNROLL):
             index = step * UNROLL + lane
             strength = jnp.where(index < live, -REPULSION, 0.0)
@@ -245,8 +249,11 @@
             other = neg_cols[place]
             shift = lax.rem(lax.div(other, CB) - row + row_count, row_count)
             right = shift * CB + lax.rem(other, CB)
-            kernel = kernel_of(left, right)
-            apply(left, right, strength * kernel * kernel)
+            def push(left=left, right=right, strength=strength):
+                kernel = kernel_of(left, right)
+                return strength * kernel * kernel
+            batch.append((left, right, push))
+        apply_all(batch)
 
     def force_of(acc, value):
         return acc[:D_EMB] + acc[D_EMB + 16 :] - value * acc[D_EMB : D_EMB + 1]
@@ -268,7 +275,6 @@
     vmem = pl.BlockSpec(memory_space=pltpu.VMEM)
     lefts, rights = col_count * CB, row_count * CB
     tiles = col_count * 2 + 48
-    weights = weights.reshape(-1, BLK, BLK)
     outs = pl.pallas_call(
         functools.partial(force_kernel, row_count, col_count),
         in_specs=[smem] * 4 + [vmem] * (2 + row_count),
@@ -282,6 +288,8 @@
             pltpu.VMEM((rights, PULL, 2 * BLK), BF16),
             pltpu.VMEM((lefts, PULL, BLK), F32),
             pltpu.VMEM((rights, PULL, BLK), F32),
+            pltpu.VMEM((UNROLL, 2 * BLK, BLK), BF16),
+            pltpu.VMEM((UNROLL, BLK, 2 * BLK), BF16),
         ],
         compiler_params=pltpu.CompilerParams(vmem_limit_bytes=VMEM_LIMIT),
         cost_estimate=pl.CostEstimate(
@@ -337,8 +345,22 @@
         seeds_back.append(from_shift(wanted, shift) if shift else wanted)
     seeds_back = jnp.concatenate(seeds_back).astype(I32)
 
+    sizes = row_count, col_count
+    plan = [(group, shift, shift) for shift in range(shifts) for group in range(col_count)]
+    row_spans = [(0, group) for group in range(col_count)]
+    col_spans = [(1 + shift, None) for shift in range(shifts)]
+    row_packs = [row_pack[group] for group in range(col_count)]
     weights = pair_weights(
-        row_count, col_count, meta, listing, seeds, seeds_back, row_x, row_pack, col_x, col_pack[:shifts]
+        sizes,
+        plan,
+        row_spans,
+        col_spans,
+        jnp.concatenate([meta, jnp.arange(col_count, dtype=I32)]),
+        listing,
+        seeds,
+        seeds_back,
+        [row_x] + col_x,
+        col_pack[:shifts] + row_packs,
     )
 
     row_y, col_y = row_pack, col_pack

time: 165 us -> 143 us (0.87); the launches traced: 167 us -> 142 us
  starting transfers between devices: 55.8 us -> 36.3 us
  Pallas kernels: 43.3 us -> 25.2 us
  waiting for transfers between devices: 17 us -> 27.7 us
    pallas_call x2, Pallas kernels: 29.9 us -> 13.3 us  [pair_forces(): pl.pallas_call(functools.partial(force_kernel, row_count, col_count), in_...]
    ppermute x9, starting transfers between devices: 29.3 us -> 17.9 us  [from_shift(): return lax.ppermute(value, 'row', pairs)]
    ppermute x9, waiting for transfers between devices: 1.54 us -> 12.7 us  [from_shift(): return lax.ppermute(value, 'row', pairs)]
    all_to_all x2, starting transfers between devices: 16.6 us -> 8.65 us  [shards(): lax.all_to_all(row_force, 'col', split_axis=0, concat_axis=0, tiled=True)]
  transfers between devices with their start and end apart: 19 -> 19, of which waited for: 6 -> 6; matrix products, arithmetic and copies ran while one was open for 5% -> 7% of each run, Pallas kernels for 8% -> 8%
where the time goes in v2:
time: 143 us; the launch traced here: 142 us
  starting transfers between devices  36.3 us (25%)
  waiting for transfers between devices  27.7 us (19%)
  Pallas kernels  25.2 us (18%)
  blocking collectives  23.6 us (17%)
  between operations  14.9 us (10%)
  other arithmetic  7.59 us (5%)
  local copies, waits for them, and re-layouts  6.77 us (5%)
    ppermute x9, starting transfers between devices, from_shift(): return lax.ppermute(value, 'row', pairs)  17.9 us
    pallas_call x2, Pallas kernels, pair_forces(): pl.pallas_call(functools.partial(force_kernel, row_count, col_count), in_...  13.3 us
    all_gather x1, blocking collectives, shards(): row_pack = lax.all_gather(pack, 'col', axis=0, tiled=False)  12.8 us
    ppermute x9, waiting for transfers between devices, from_shift(): return lax.ppermute(value, 'row', pairs)  12.7 us
    pallas_call x1, Pallas kernels, pair_weights(): pl.pallas_call(functools.partial(weights_kernel, sizes, plan, (row_spans,...  11.9 us
    all_to_all x2, waiting for transfers between devices, shards(): lax.all_to_all(row_force, 'col', split_axis=0, concat_axis=0, tiled=True)  11.1 us
    all_gather x1, blocking collectives, shards(): row_y = lax.all_gather(embed, 'col', axis=0, tiled=False)  10.8 us
    all_to_all x2, starting transfers between devices, shards(): lax.all_to_all(row_force, 'col', split_axis=0, concat_axis=0, tiled=True)  8.65 us
  transfers between devices with their start and end apart: 19, of which 6 were waited for; matrix products, arithmetic and copies ran while one was open for 7% of the time, Pallas kernels for 8%

profile of v2, /device:TPU:0, one launch (start us, length us, event | category | flops | bytes accessed | tf_op | source)
XLA Modules:
  0.0 142.0 jit_solution(15698307012778473260)
XLA Ops:
  7.9 5.1 %collective-permute-start.2 = (f32[256,768]{1,0:T(8,128)}, f32[256,768]{1,0:T(8,128)S(1)}, u32[]{:S(2)}, u32[]{:S(2)}) collective-permute-start(f32[256,768]{1,0:T(8,128)} %rest_1_.1), channel_id=1, source_target_pairs={{8,0},{16,8},{24,16},{0,24},{9,1},{17,9},{25,17},{1,25},{10,2},{18... | collective-permute-start | bytes 2359304 | tf_op jit(solution)/shard_map/ppermute | solution.py:317
  13.0 1.3 collective-permute-start.3
  15.1 1.3 multiply_reduce_fusion
  16.4 1.6 %concatenate.13.rest_4_.rest_0_ = f32[72,256]{1,0:T(8,128)S(1)} concatenate(f32[64,256]{1,0:T(8,128)} %param.14, f32[1,256]{1,0:T(1,128)} %bitcast.30, f32[1,256]{1,0:T(1,128)} %bitcast.31, f32[1,256]{1,0:T(1,128)S(1)} %bitcast.29, f32[1,256]{1,0:T(1,128)S(1)} %scatter.4, f32[4,256]{1,0:T(4,128)S(1)} %broadcast_in_dim.4), dimensions={0} | concatenate | bytes 147456 | tf_op jit(solution)/shard_map/concatenate | solution.py:336
  18.5 3.2 %collective-permute-start.5 = (f32[72,256]{1,0:T(8,128)S(1)}, f32[72,256]{1,0:T(8,128)S(1)}, u32[]{:S(2)}, u32[]{:S(2)}) collective-permute-start(f32[72,256]{1,0:T(8,128)S(1)} %concatenate.13.rest_4_.rest_0_), channel_id=1, source_target_pairs={{16,0},{24,8},{0,16},{8,24},{17,1},{25,9},{1,17},{9,25},{18,2},{26... | collective-permute-start | bytes 221192 | tf_op jit(solution)/shard_map/ppermute | solution.py:317
  21.7 12.8 %all-gather = f32[576,256]{1,0:T(8,128)S(1)} all-gather(f32[72,256]{1,0:T(8,128)S(1)} %concatenate.13.rest_4_.rest_0_), channel_id=2, replica_groups=mesh['row'=4,'col'=8] {'col'}, dimensions={0}, use_global_device_ids=true | all-gather | bytes 663552 | tf_op jit(solution)/shard_map/all_gather | solution.py:337
  34.7 0.8 copy.18
  36.2 0.8 copy.17
  39.3 0.8 fusion.3
  40.2 11.4 %collective-permute-done.1 = f32[8]{0:T(128)S(1)} collective-permute-done((f32[8]{0:T(128)S(1)}, f32[8]{0:T(128)S(1)}, u32[]{:S(2)}, u32[]{:S(2)}) %collective-permute-start.1) | collective-permute-done | bytes 64 | tf_op jit(solution)/shard_map/ppermute | solution.py:317
  51.6 4.4 %collective-permute-start = (f32[8]{0:T(128)S(1)}, f32[8]{0:T(128)S(1)}, u32[]{:S(2)}, u32[]{:S(2)}) collective-permute-start(f32[8]{0:T(128)S(1)} %get-tuple-element.46), channel_id=1, source_target_pairs={{8,0},{16,8},{24,16},{0,24},{9,1},{17,9},{25,17},{1,25},{10,2},{18... | collective-permute-start | bytes 104 | tf_op jit(solution)/shard_map/ppermute | solution.py:317
  56.0 1.3 collective-permute-done
  57.9 2.6 %all-gather.5.cloned.1.call-done = f32[2048,768]{1,0:T(8,128)} async-done(((f32[256,768]{1,0:T(8,128)}), f32[2048,768]{1,0:T(8,128)}) %all-gather.5.cloned.1.call-update) | async-done | bytes 6291472 | tf_op jit(solution)/shard_map/all_gather | solution.py:328
  60.5 11.9 %weights.1 = bf16[24,128,128]{2,1,0:T(8,128)(2,1)} custom-call(s32[11]{0:T(128)} %pad_add_fusion.1.meta, s32[64]{0:T(128)} %reshape.55.listing, s32[32]{0:T(128)} %reshape.58.seeds, s32[24]{0:T(128)} %maximum_convert_fusion.seeds_back, f32[8,256,768]{2,1,0:T(8,128)} %bitcast.24, f32[256,768]{1,0:T(8,128)} %rest_1_.1, f32[256,768]{1,0:T(8,128)} %copy-done.1, ...), custom_call_target="tpu_custom_call" | custom-call | flops 1811939328 | bytes 8650752 | tf_op jit(solution)/shard_map/weights/pallas_call | solution.py:124
  73.1 6.6 %forces.2 = (f32[8,64,256]{2,1,0:T(8,128)}, f32[64,256]{1,0:T(8,128)}, f32[64,256]{1,0:T(8,128)}, f32[64,256]{1,0:T(8,128)}, f32[64,256]{1,0:T(8,128)}) custom-call(s32[3]{0:T(128)} %pad_add_fusion.meta, s32[64]{0:T(128)} %reshape.55.listing, s32[48]{0:T(128)} %bitcast.32, s32[48]{0:T(128)} %bitcast.34, bf16[24,128,128]{2,1,0:T(8,128)(2,1)} %weights.1, ...), custom_call_target="tpu_custom_call" | custom-call | flops 1744830464 | bytes 1572864 | tf_op jit(solution)/shard_map/forces/pallas_call | solution.py:278
  79.7 4.6 %all-to-all-start = ((f32[8,64,256]{2,1,0:T(8,128)}), f32[8,64,256]{2,1,0:T(8,128)S(1)}, u32[]{:S(2)}, u32[]{:S(2)}) async-start(f32[8,64,256]{2,1,0:T(8,128)} %get-tuple-element.24), calls=%async_computation | async-start | bytes 1048576 | tf_op jit(solution)/shard_map/all_to_all | solution.py:374
  84.3 2.3 %collective-permute-start.9 = (f32[64,256]{1,0:T(8,128)}, f32[64,256]{1,0:T(8,128)S(1)}, u32[]{:S(2)}, u32[]{:S(2)}) collective-permute-start(f32[64,256]{1,0:T(8,128)} %get-tuple-element.28), channel_id=1, source_target_pairs={{0,24},{8,0},{16,8},{24,16},{1,25},{9,1},{17,9},{25,17},{2,26},{10... | collective-permute-start | bytes 196616 | tf_op jit(solution)/shard_map/ppermute | solution.py:326
  86.6 0.8 collective-permute-start.8
  87.4 1.9 %collective-permute-start.7 = (f32[64,256]{1,0:T(8,128)}, f32[64,256]{1,0:T(8,128)S(1)}, u32[]{:S(2)}, u32[]{:S(2)}) collective-permute-start(f32[64,256]{1,0:T(8,128)} %get-tuple-element.26), channel_id=1, source_target_pairs={{0,8},{8,16},{16,24},{24,0},{1,9},{9,17},{17,25},{25,1},{2,10},{10... | collective-permute-start | bytes 196616 | tf_op jit(solution)/shard_map/ppermute | solution.py:326
  89.4 4.7 %all-to-all-done = f32[8,64,256]{2,1,0:T(8,128)S(1)} async-done(((f32[8,64,256]{2,1,0:T(8,128)}), f32[8,64,256]{2,1,0:T(8,128)S(1)}, u32[]{:S(2)}, u32[]{:S(2)}) %all-to-all-start) | async-done | bytes 524320 | tf_op jit(solution)/shard_map/all_to_all | solution.py:374
  94.7 0.9 multiply_add_fusion.1.rest_0_
  95.6 1.9 %collective-permute-start.10 = (f32[64,256]{1,0:T(8,128)S(1)}, f32[64,256]{1,0:T(8,128)S(1)}, u32[]{:S(2)}, u32[]{:S(2)}) collective-permute-start(f32[64,256]{1,0:T(8,128)S(1)} %multiply_add_fusion.1.rest_0_), channel_id=1, source_target_pairs={{8,0},{16,8},{24,16},{0,24},{9,1},{17,9},{25,17},{1,25},{10,2},{18... | collective-permute-start | bytes 196616 | tf_op jit(solution)/shard_map/ppermute | solution.py:317
  97.5 0.7 collective-permute-start.11
  98.2 1.9 %collective-permute-start.12 = (f32[64,256]{1,0:T(8,128)S(1)}, f32[64,256]{1,0:T(8,128)S(1)}, u32[]{:S(2)}, u32[]{:S(2)}) collective-permute-start(f32[64,256]{1,0:T(8,128)S(1)} %multiply_add_fusion.1.rest_0_), channel_id=1, source_target_pairs={{24,0},{0,8},{8,16},{16,24},{25,1},{1,9},{9,17},{17,25},{26,2},{2,... | collective-permute-start | bytes 196616 | tf_op jit(solution)/shard_map/ppermute | solution.py:317
  100.2 10.8 %all-gather.2 = f32[512,256]{1,0:T(8,128)} all-gather(f32[64,256]{1,0:T(8,128)S(1)} %multiply_add_fusion.1.rest_0_), channel_id=4, replica_groups=mesh['row'=4,'col'=8] {'col'}, dimensions={0}, use_global_device_ids=true | all-gather | bytes 589824 | tf_op jit(solution)/shard_map/all_gather | solution.py:369
  111.6 6.6 %forces.3 = (f32[8,64,256]{2,1,0:T(8,128)}, f32[64,256]{1,0:T(8,128)}, f32[64,256]{1,0:T(8,128)}, f32[64,256]{1,0:T(8,128)}, f32[64,256]{1,0:T(8,128)}) custom-call(s32[3]{0:T(128)} %pad_add_fusion.meta, s32[64]{0:T(128)} %reshape.55.listing, s32[48]{0:T(128)} %bitcast.33, s32[48]{0:T(128)} %bitcast.35, bf16[24,128,128]{2,1,0:T(8,128)(2,1)} %weights.1, ...), custom_call_target="tpu_custom_call" | custom-call | flops 1744830464 | bytes 1572864 | tf_op jit(solution)/shard_map/forces/pallas_call | solution.py:278
  118.3 4.1 %all-to-all-start.1 = ((f32[8,64,256]{2,1,0:T(8,128)}), f32[8,64,256]{2,1,0:T(8,128)S(1)}, u32[]{:S(2)}, u32[]{:S(2)}) async-start(f32[8,64,256]{2,1,0:T(8,128)} %get-tuple-element.29), calls=%async_computation.1 | async-start | bytes 1048576 | tf_op jit(solution)/shard_map/all_to_all | solution.py:374
  122.4 1.3 collective-permute-start.15
  123.7 1.5 %collective-permute-start.14 = (f32[64,256]{1,0:T(8,128)}, f32[64,256]{1,0:T(8,128)S(1)}, u32[]{:S(2)}, u32[]{:S(2)}) collective-permute-start(f32[64,256]{1,0:T(8,128)} %get-tuple-element.32), channel_id=1, source_target_pairs={{0,16},{8,24},{16,0},{24,8},{1,17},{9,25},{17,1},{25,9},{2,18},{10... | collective-permute-start | bytes 196616 | tf_op jit(solution)/shard_map/ppermute | solution.py:326
  125.7 6.4 %all-to-all-done.1 = f32[8,64,256]{2,1,0:T(8,128)S(1)} async-done(((f32[8,64,256]{2,1,0:T(8,128)}), f32[8,64,256]{2,1,0:T(8,128)S(1)}, u32[]{:S(2)}, u32[]{:S(2)}) %all-to-all-start.1) | async-done | bytes 524320 | tf_op jit(solution)/shard_map/all_to_all | solution.py:374
  132.2 1.5 %broadcast_multiply_fusion = (f32[64,256]{1,0:T(8,128)}, f32[64,256]{1,0:T(8,128)S(1)}) fusion(f32[64,256]{1,0:T(8,128)S(1)} %collective-permute-done.15, f32[64,256]{1,0:T(8,128)S(1)} %collective-permute-done.14, f32[64,256]{1,0:T(8,128)S(1)} %collective-permute-done.13, f32[64,256]{1,0:T(8,128)S(1)} %reduce_sum.29, f32[64,256]{1,0:T(8,128)} %get-tuple-element.30), kind=kLoop, calls=%fused_computation.4 | loop fusion | flops 81920 | bytes 458752 | tf_op jit(solution)/shard_map/mul | solution.py:379
  133.7 1.5 %multiply_add_fusion = f32[64,256]{1,0:T(8,128)} fusion(f32[64,256]{1,0:T(8,128)} %copy-done.4, f32[64,256]{1,0:T(8,128)S(1)} %get-tuple-element.35), kind=kLoop, calls=%fused_computation.1 | loop fusion | flops 32768 | bytes 196608 | tf_op jit(solution)/shard_map/add | solution.py:378
  (60 shorter events, 7.7 us)
Async XLA Ops:
  7.2 53.3 %all-gather.5.cloned.1.call-start = ((), (), s32[]{:S(2)}) async-start(), calls=%async_computation.2 | async-start | bytes 7077888 | tf_op jit(solution)/shard_map/all_gather | solution.py:328
  7.9 50.0 %collective-permute-start.2 = (f32[256,768]{1,0:T(8,128)}, f32[256,768]{1,0:T(8,128)S(1)}, u32[]{:S(2)}, u32[]{:S(2)}) collective-permute-start(f32[256,768]{1,0:T(8,128)} %rest_1_.1), channel_id=1, source_target_pairs={{8,0},{16,8},{24,16},{0,24},{9,1},{17,9},{25,17},{1,25},{10,2},{18... | collective-permute-start | bytes 2359304 | tf_op jit(solution)/shard_map/ppermute | solution.py:317
  13.0 44.9 %collective-permute-start.3 = (f32[256,768]{1,0:T(8,128)}, f32[256,768]{1,0:T(8,128)S(1)}, u32[]{:S(2)}, u32[]{:S(2)}) collective-permute-start(f32[256,768]{1,0:T(8,128)} %rest_1_.1), channel_id=1, source_target_pairs={{16,0},{8,24},{17,1},{9,25},{18,2},{10,26},{19,3},{11,27},{20,4},{... | collective-permute-start | bytes 2359304 | tf_op jit(solution)/shard_map/ppermute | solution.py:322
  18.0 42.5 %copy-start.3 = (f32[72,256]{1,0:T(8,128)}, f32[72,256]{1,0:T(8,128)S(1)}, u32[]{:S(2)}) copy-start(f32[72,256]{1,0:T(8,128)S(1)} %concatenate.13.rest_4_.rest_0_) | copy-start | bytes 221188
  18.0 39.9 %collective-permute-start.4 = (f32[72,256]{1,0:T(8,128)S(1)}, f32[72,256]{1,0:T(8,128)S(1)}, u32[]{:S(2)}, u32[]{:S(2)}) collective-permute-start(f32[72,256]{1,0:T(8,128)S(1)} %concatenate.13.rest_4_.rest_0_), channel_id=1, source_target_pairs={{8,0},{16,8},{24,16},{0,24},{9,1},{17,9},{25,17},{1,25},{10,2},{18... | collective-permute-start | bytes 221192 | tf_op jit(solution)/shard_map/ppermute | solution.py:317
  18.5 39.4 %collective-permute-start.5 = (f32[72,256]{1,0:T(8,128)S(1)}, f32[72,256]{1,0:T(8,128)S(1)}, u32[]{:S(2)}, u32[]{:S(2)}) collective-permute-start(f32[72,256]{1,0:T(8,128)S(1)} %concatenate.13.rest_4_.rest_0_), channel_id=1, source_target_pairs={{16,0},{24,8},{0,16},{8,24},{17,1},{25,9},{1,17},{9,25},{18,2},{26... | collective-permute-start | bytes 221192 | tf_op jit(solution)/shard_map/ppermute | solution.py:317
  34.5 37.9 %copy-start = (f32[576,256]{1,0:T(8,128)}, f32[576,256]{1,0:T(8,128)S(1)}, u32[]{:S(2)}) copy-start(f32[576,256]{1,0:T(8,128)S(1)} %all-gather) | copy-start | bytes 1769476
  34.6 16.9 %collective-permute-start.1 = (f32[8]{0:T(128)S(1)}, f32[8]{0:T(128)S(1)}, u32[]{:S(2)}, u32[]{:S(2)}) collective-permute-start(f32[8]{0:T(128)S(1)} %get-tuple-element.45), channel_id=1, source_target_pairs={{16,0},{24,8},{0,16},{8,24},{17,1},{25,9},{1,17},{9,25},{18,2},{26... | collective-permute-start | bytes 104 | tf_op jit(solution)/shard_map/ppermute | solution.py:317
  51.6 5.7 %collective-permute-start = (f32[8]{0:T(128)S(1)}, f32[8]{0:T(128)S(1)}, u32[]{:S(2)}, u32[]{:S(2)}) collective-permute-start(f32[8]{0:T(128)S(1)} %get-tuple-element.46), channel_id=1, source_target_pairs={{8,0},{16,8},{24,16},{0,24},{9,1},{17,9},{25,17},{1,25},{10,2},{18... | collective-permute-start | bytes 104 | tf_op jit(solution)/shard_map/ppermute | solution.py:317
  57.3 15.2 %collective-permute-start.6 = (f32[72,256]{1,0:T(8,128)S(1)}, f32[72,256]{1,0:T(8,128)S(1)}, u32[]{:S(2)}, u32[]{:S(2)}) collective-permute-start(f32[72,256]{1,0:T(8,128)S(1)} %concatenate.13.rest_4_.rest_0_), channel_id=1, source_target_pairs={{24,0},{0,8},{8,16},{16,24},{25,1},{1,9},{9,17},{17,25},{26,2},{2,... | collective-permute-start | bytes 221192 | tf_op jit(solution)/shard_map/ppermute | solution.py:317
  57.9 2.7 %copy-start.6 = (f32[72,256]{1,0:T(8,128)}, f32[72,256]{1,0:T(8,128)S(1)}, u32[]{:S(2)}) copy-start(f32[72,256]{1,0:T(8,128)S(1)} %collective-permute-done.4.rest_5_.rest_1_) | copy-start | bytes 221188
  57.9 2.7 %copy-start.7 = (f32[72,256]{1,0:T(8,128)}, f32[72,256]{1,0:T(8,128)S(1)}, u32[]{:S(2)}) copy-start(f32[72,256]{1,0:T(8,128)S(1)} %collective-permute-done.5.rest_6_.rest_2_) | copy-start | bytes 221188
  57.9 2.6 %copy-start.1 = (f32[256,768]{1,0:T(8,128)}, f32[256,768]{1,0:T(8,128)S(1)}, u32[]{:S(2)}) copy-start(f32[256,768]{1,0:T(8,128)S(1)} %collective-permute-done.2.rest_2_) | copy-start | bytes 2359300
  57.9 2.6 %copy-start.2 = (f32[256,768]{1,0:T(8,128)}, f32[256,768]{1,0:T(8,128)S(1)}, u32[]{:S(2)}) copy-start(f32[256,768]{1,0:T(8,128)S(1)} %collective-permute-done.3.rest_3_) | copy-start | bytes 2359300
  72.4 22.3 %copy-start.5 = (f32[64,256]{1,0:T(8,128)S(1)}, f32[64,256]{1,0:T(8,128)}, u32[]{:S(2)}) copy-start(f32[64,256]{1,0:T(8,128)} %param.14) | copy-start | bytes 196612
  72.5 0.6 copy-start.8
  79.7 14.3 %all-to-all-start = ((f32[8,64,256]{2,1,0:T(8,128)}), f32[8,64,256]{2,1,0:T(8,128)S(1)}, u32[]{:S(2)}, u32[]{:S(2)}) async-start(f32[8,64,256]{2,1,0:T(8,128)} %get-tuple-element.24), calls=%async_computation | async-start | bytes 1048576 | tf_op jit(solution)/shard_map/all_to_all | solution.py:374
  84.3 9.8 %collective-permute-start.9 = (f32[64,256]{1,0:T(8,128)}, f32[64,256]{1,0:T(8,128)S(1)}, u32[]{:S(2)}, u32[]{:S(2)}) collective-permute-start(f32[64,256]{1,0:T(8,128)} %get-tuple-element.28), channel_id=1, source_target_pairs={{0,24},{8,0},{16,8},{24,16},{1,25},{9,1},{17,9},{25,17},{2,26},{10... | collective-permute-start | bytes 196616 | tf_op jit(solution)/shard_map/ppermute | solution.py:326
  86.6 8.1 %collective-permute-start.8 = (f32[64,256]{1,0:T(8,128)}, f32[64,256]{1,0:T(8,128)S(1)}, u32[]{:S(2)}, u32[]{:S(2)}) collective-permute-start(f32[64,256]{1,0:T(8,128)} %get-tuple-element.27), channel_id=1, source_target_pairs={{0,16},{8,24},{16,0},{24,8},{1,17},{9,25},{17,1},{25,9},{2,18},{10... | collective-permute-start | bytes 196616 | tf_op jit(solution)/shard_map/ppermute | solution.py:326
  87.4 7.3 %collective-permute-start.7 = (f32[64,256]{1,0:T(8,128)}, f32[64,256]{1,0:T(8,128)S(1)}, u32[]{:S(2)}, u32[]{:S(2)}) collective-permute-start(f32[64,256]{1,0:T(8,128)} %get-tuple-element.26), channel_id=1, source_target_pairs={{0,8},{8,16},{16,24},{24,0},{1,9},{9,17},{17,25},{25,1},{2,10},{10... | collective-permute-start | bytes 196616 | tf_op jit(solution)/shard_map/ppermute | solution.py:326
  95.6 15.4 %copy-start.4 = (f32[64,256]{1,0:T(8,128)}, f32[64,256]{1,0:T(8,128)S(1)}, u32[]{:S(2)}) copy-start(f32[64,256]{1,0:T(8,128)S(1)} %multiply_add_fusion.1.rest_0_) | copy-start | bytes 196612
  95.6 15.4 %collective-permute-start.10 = (f32[64,256]{1,0:T(8,128)S(1)}, f32[64,256]{1,0:T(8,128)S(1)}, u32[]{:S(2)}, u32[]{:S(2)}) collective-permute-start(f32[64,256]{1,0:T(8,128)S(1)} %multiply_add_fusion.1.rest_0_), channel_id=1, source_target_pairs={{8,0},{16,8},{24,16},{0,24},{9,1},{17,9},{25,17},{1,25},{10,2},{18... | collective-permute-start | bytes 196616 | tf_op jit(solution)/shard_map/ppermute | solution.py:317
  97.5 13.5 %collective-permute-start.11 = (f32[64,256]{1,0:T(8,128)S(1)}, f32[64,256]{1,0:T(8,128)S(1)}, u32[]{:S(2)}, u32[]{:S(2)}) collective-permute-start(f32[64,256]{1,0:T(8,128)S(1)} %multiply_add_fusion.1.rest_0_), channel_id=1, source_target_pairs={{16,0},{24,8},{0,16},{8,24},{17,1},{25,9},{1,17},{9,25},{18,2},{26... | collective-permute-start | bytes 196616 | tf_op jit(solution)/shard_map/ppermute | solution.py:317
  98.2 12.7 %collective-permute-start.12 = (f32[64,256]{1,0:T(8,128)S(1)}, f32[64,256]{1,0:T(8,128)S(1)}, u32[]{:S(2)}, u32[]{:S(2)}) collective-permute-start(f32[64,256]{1,0:T(8,128)S(1)} %multiply_add_fusion.1.rest_0_), channel_id=1, source_target_pairs={{24,0},{0,8},{8,16},{16,24},{25,1},{1,9},{9,17},{17,25},{26,2},{2,... | collective-permute-start | bytes 196616 | tf_op jit(solution)/shard_map/ppermute | solution.py:317
  111.0 0.6 copy-start.9
  111.0 0.6 copy-start.10
  111.0 0.6 copy-start.11
  118.3 13.8 %all-to-all-start.1 = ((f32[8,64,256]{2,1,0:T(8,128)}), f32[8,64,256]{2,1,0:T(8,128)S(1)}, u32[]{:S(2)}, u32[]{:S(2)}) async-start(f32[8,64,256]{2,1,0:T(8,128)} %get-tuple-element.29), calls=%async_computation.1 | async-start | bytes 1048576 | tf_op jit(solution)/shard_map/all_to_all | solution.py:374
  122.4 9.8 %collective-permute-start.15 = (f32[64,256]{1,0:T(8,128)}, f32[64,256]{1,0:T(8,128)S(1)}, u32[]{:S(2)}, u32[]{:S(2)}) collective-permute-start(f32[64,256]{1,0:T(8,128)} %get-tuple-element.33), channel_id=1, source_target_pairs={{0,24},{8,0},{16,8},{24,16},{1,25},{9,1},{17,9},{25,17},{2,26},{10... | collective-permute-start | bytes 196616 | tf_op jit(solution)/shard_map/ppermute | solution.py:326
  123.7 8.4 %collective-permute-start.14 = (f32[64,256]{1,0:T(8,128)}, f32[64,256]{1,0:T(8,128)S(1)}, u32[]{:S(2)}, u32[]{:S(2)}) collective-permute-start(f32[64,256]{1,0:T(8,128)} %get-tuple-element.32), channel_id=1, source_target_pairs={{0,16},{8,24},{16,0},{24,8},{1,17},{9,25},{17,1},{25,9},{2,18},{10... | collective-permute-start | bytes 196616 | tf_op jit(solution)/shard_map/ppermute | solution.py:326
  125.2 6.9 %collective-permute-start.13 = (f32[64,256]{1,0:T(8,128)}, f32[64,256]{1,0:T(8,128)S(1)}, u32[]{:S(2)}, u32[]{:S(2)}) collective-permute-start(f32[64,256]{1,0:T(8,128)} %get-tuple-element.31), channel_id=1, source_target_pairs={{0,8},{8,16},{16,24},{24,0},{1,9},{9,17},{17,25},{25,1},{2,10},{10... | collective-permute-start | bytes 196616 | tf_op jit(solution)/shard_map/ppermute | solution.py:326
Sparse Core Ops, SparseCore 0:
  9.9 50.5 all-gather.4

commit v3 on v2

--- a/solution.py
+++ b/solution.py
@@ -23,7 +23,7 @@
 PULL = 2 * D_EMB + 16
 UNROLL = 12
 F32, BF16, I32 = jnp.float32, jnp.bfloat16, jnp.int32
-VMEM_LIMIT = 56 * 2**20
+VMEM_LIMIT = 44 * 2**20
 
 
 def split(value):
@@ -52,50 +52,40 @@
     return jnp.where(row < half, row % 2 == 0, (row - half) % 2 == 1)
 
 
-def weights_kernel(sizes, plan, spans, meta, listing, seeds, seeds_back, *rest):
+def weights_kernel(sizes, plan, spans, meta, listing, seeds, *rest):
     row_count, col_count = sizes
-    row_spans, col_spans = spans
-    count = len(row_spans) + len(col_spans)
-    arrays = rest[: len(rest) - 7 - count]
-    packs = rest[len(arrays) : len(arrays) + count]
-    out, raw, high, low, col_params, grams, sems = rest[len(arrays) + count :]
+    col_spans, row_spans = spans
+    count = row_spans + col_spans
+    arrays, packs = rest[:count], rest[count : 2 * count]
+    out, high, low, col_params, grams = rest[2 * count :]
     row, col = meta[0], meta[1]
-    places = col_spans + row_spans
-    copies = []
-    for place, (array, index) in enumerate(places):
-        source = arrays[array] if index is None else arrays[array].at[index]
-        copies.append(pltpu.make_async_copy(source, raw.at[place], sems.at[place]))
-        copies[-1].start()
-    for place in range(len(col_spans)):
+    for place in range(col_spans):
         for block in range(CB):
             params = packs[place][RHO : RHO + 8, block * BLK : (block + 1) * BLK]
             col_params[place, block] = params.T
     positions_j = lax.broadcasted_iota(I32, (BLK, BLK), 0)
     positions_i = lax.broadcasted_iota(I32, (BLK, BLK), 1)
-
-    def take(place):
-        copies[place].wait()
-        high[place], low[place] = split(raw[place])
-
-    for place in range(len(col_spans)):
-        take(place)
-    for line in range(len(row_spans)):
-        place = len(col_spans) + line
-        take(place)
+    wanted_seed = lax.broadcasted_iota(I32, (1, SPAN), 1) == col * row_count + row
+
+    for place in range(col_spans):
+        high[place], low[place] = split(arrays[place][...])
+    for line in range(row_spans):
+        place = col_spans + line
+        high[place], low[place] = split(arrays[place][...])
+        group = lax.bitwise_xor(col, line)
         tiles = [(tile, entry) for tile, entry in enumerate(plan) if entry[0] == line]
         picks = {}
         for tile, (_, column, shift) in tiles:
-            group = meta[3 + line]
             other = lax.rem(row + shift, row_count)
             entry = (group * row_count + other) * 2
             start_i = pl.multiple_of(listing[entry] * BLK, BLK)
             start_j = pl.multiple_of(listing[entry + 1] * BLK, BLK)
-            picks[tile] = group, other, start_i, listing[entry + 1]
+            picks[tile] = other, start_i, listing[entry + 1]
             high_j, low_j = high[column, pl.ds(start_j, BLK), :], low[column, pl.ds(start_j, BLK), :]
             high_i, low_i = high[place, pl.ds(start_i, BLK), :], low[place, pl.ds(start_i, BLK), :]
             grams[tile] = nt_dot(high_j, low_i) + nt_dot(low_j, high_i) + nt_dot(high_j, high_i)
         for tile, (_, column, shift) in tiles:
-            group, other, start_i, col_pick = picks[tile]
+            other, start_i, col_pick = picks[tile]
             params_i = packs[place][RHO : RHO + 8, pl.ds(start_i, BLK)]
             rho_i, sigma_i, square_i = params_i[0:1], params_i[1:2], params_i[2:3]
             params_j = col_params[column, col_pick]
@@ -103,7 +93,8 @@
             total = square_j + square_i - 2.0 * grams[tile]
             distance = jnp.sqrt(jnp.maximum(total, 1.0))
             seed = seeds[group * row_count + other]
-            seed_back = seeds_back[shift * col_count + group]
+            plane_seeds = packs[place][SEEDS + shift : SEEDS + shift + 1, :]
+            seed_back = jnp.sum(jnp.where(wanted_seed, plane_seeds, 0.0), axis=1, keepdims=True).astype(I32)
             ahead = hash_bits(seed, positions_i, positions_j) * jnp.exp(
                 jnp.maximum(distance - rho_i, 0.0) * (-1.0 / sigma_i)
             )
@@ -111,28 +102,26 @@
                 jnp.maximum(distance - rho_j, 0.0) * (-1.0 / sigma_j)
             )
             weights = (ahead + behind - ahead * behind).astype(BF16)
-            if shift == 0:
-                weights = (weights.astype(F32) * jnp.where(group == col, 0.5, 1.0)).astype(BF16)
+            if shift == 0 and line == 0:
+                weights = (weights.astype(F32) * 0.5).astype(BF16)
             out[tile] = weights
 
 
-def pair_weights(sizes, plan, row_spans, col_spans, meta, listing, seeds, seeds_back, arrays, packs):
+def pair_weights(sizes, plan, col_spans, meta, listing, seeds, arrays, packs):
     depth = arrays[0].shape[-1]
     smem = pl.BlockSpec(memory_space=pltpu.SMEM)
     vmem = pl.BlockSpec(memory_space=pltpu.VMEM)
-    tiles, count = len(plan), len(row_spans) + len(col_spans)
+    tiles, count = len(plan), len(arrays)
     return pl.pallas_call(
-        functools.partial(weights_kernel, sizes, plan, (row_spans, col_spans)),
-        in_specs=[smem] * 4 + [pl.BlockSpec(memory_space=pl.ANY)] * len(arrays) + [vmem] * count,
+        functools.partial(weights_kernel, sizes, plan, (col_spans, count - col_spans)),
+        in_specs=[smem] * 3 + [vmem] * (2 * count),
         out_specs=vmem,
         out_shape=jax.ShapeDtypeStruct((tiles, BLK, BLK), BF16),
         scratch_shapes=[
-            pltpu.VMEM((count, SPAN, depth), F32),
             pltpu.VMEM((count, SPAN, depth), BF16),
             pltpu.VMEM((count, SPAN, depth), BF16),
-            pltpu.VMEM((len(col_spans), CB, BLK, 8), F32),
+            pltpu.VMEM((col_spans, CB, BLK, 8), F32),
             pltpu.VMEM((tiles, BLK, BLK), F32),
-            pltpu.SemaphoreType.DMA((count,)),
         ],
         compiler_params=pltpu.CompilerParams(vmem_limit_bytes=VMEM_LIMIT),
         cost_estimate=pl.CostEstimate(
@@ -141,11 +130,12 @@
             transcendentals=tiles * 3 * BLK * BLK,
         ),
         name="weights",
-    )(meta, listing, seeds, seeds_back, *arrays, *packs)
-
-
-def force_kernel(row_count, col_count, meta, listing, neg_rows, neg_cols, weights, row_y, *rest):
+    )(meta, listing, seeds, *arrays, *packs)
+
+
+def force_kernel(row_count, col_count, by_bits, meta, listing, neg_rows, neg_cols, weights, *rest):
     shifts = row_count // 2 + 1
+    row_arrays, rest = (rest[:2], rest[2:]) if by_bits else (rest[:1], rest[1:])
     col_y = rest[:row_count]
     row_force, col_force = rest[row_count], rest[row_count + 1 : 2 * row_count + 1]
     left_gram, right_gram, left_pull, right_pull, left_acc, right_acc, held_v, held_h = rest[2 * row_count + 1 :]
@@ -186,10 +176,16 @@
         right_pull[index] = pulls(high, low)
         right_acc[index] = jnp.zeros((PULL, BLK), F32)
 
-    @pl.loop(0, col_count)
-    def _(group):
+    def row_y(line, block):
+        lanes = slice(block * BLK, (block + 1) * BLK)
+        if by_bits:
+            return row_arrays[line % 2][line // 2, :D_EMB, lanes], lax.bitwise_xor(line, col)
+        return row_arrays[0][line, :D_EMB, lanes], line
+
+    for line in range(col_count):
         for block in range(CB):
-            left_block(group * CB + block, row_y[group, :D_EMB, block * BLK : (block + 1) * BLK])
+            value, group = row_y(line, block)
+            left_block(group * CB + block, value)
 
     for shift in range(row_count):
         for block in range(CB):
@@ -227,7 +223,7 @@
             inside = index < last
             shift = jnp.where(inside, shift, 0)
             inside &= (shift > 0) | near_active(group)
-            slot = shift * col_count + group
+            slot = shift * col_count + lax.bitwise_xor(group, col)
             entry = (group * row_count + lax.rem(row + shift, row_count)) * 2
             left = group * CB + listing[entry]
             right = shift * CB + listing[entry + 1]
@@ -258,11 +254,11 @@
     def force_of(acc, value):
         return acc[:D_EMB] + acc[D_EMB + 16 :] - value * acc[D_EMB : D_EMB + 1]
 
-    @pl.loop(0, col_count)
-    def _(group):
+    for line in range(col_count):
         for block in range(CB):
+            value, group = row_y(line, block)
             lanes = slice(block * BLK, (block + 1) * BLK)
-            row_force[group, :, lanes] = force_of(left_acc[group * CB + block], row_y[group, :D_EMB, lanes])
+            row_force[group, :, lanes] = force_of(left_acc[group * CB + block], value)
 
     for shift in range(row_count):
         for block in range(CB):
@@ -270,14 +266,15 @@
             col_force[shift][:, lanes] = force_of(right_acc[shift * CB + block], col_y[shift][:D_EMB, lanes])
 
 
-def pair_forces(row_count, col_count, meta, listing, neg_rows, neg_cols, weights, row_y, col_y):
+def pair_forces(sizes, meta, listing, neg_rows, neg_cols, weights, row_y, col_y):
+    row_count, col_count = sizes
     smem = pl.BlockSpec(memory_space=pltpu.SMEM)
     vmem = pl.BlockSpec(memory_space=pltpu.VMEM)
     lefts, rights = col_count * CB, row_count * CB
     tiles = col_count * 2 + 48
     outs = pl.pallas_call(
-        functools.partial(force_kernel, row_count, col_count),
-        in_specs=[smem] * 4 + [vmem] * (2 + row_count),
+        functools.partial(force_kernel, row_count, col_count, len(row_y) > 1),
+        in_specs=[smem] * 4 + [vmem] * (1 + len(row_y) + row_count),
         out_specs=[vmem] * (1 + row_count),
         out_shape=[jax.ShapeDtypeStruct((col_count, D_EMB, SPAN), F32)]
         + [jax.ShapeDtypeStruct((D_EMB, SPAN), F32)] * row_count,
@@ -298,7 +295,7 @@
             transcendentals=tiles * BLK * BLK,
         ),
         name="forces",
-    )(meta, listing, neg_rows, neg_cols, weights, row_y, *col_y)
+    )(meta, listing, neg_rows, neg_cols, weights, *row_y, *col_y)
     return outs[0], outs[1:]
 
 
@@ -325,52 +322,70 @@
         pairs = [(r, (r + shift) % row_count) for r in range(row_count)]
         return lax.ppermute(value, "row", pairs)
 
-    row_x = lax.all_gather(inputs, "col", axis=0, tiled=False)
-    col_x = [inputs]
-    for shift in range(1, shifts):
-        col_x.append(from_half(inputs) if 2 * shift == row_count else from_shift(inputs, shift))
-
+    def from_bits(value, bits):
+        pairs = [(c ^ bits, c) for c in range(col_count)]
+        return lax.ppermute(value, "col", pairs)
+
+    sizes = row_count, col_count
     squares = jnp.sum(inputs * inputs, axis=1)
     seed_row = jnp.zeros((SPAN,), F32).at[: seeds.shape[0]].set(seeds.astype(F32))
     params = jnp.stack([rho, sigma, squares, seed_row])
     pack = jnp.concatenate([embed, params, jnp.zeros((PACK - D_EMB - 4, SPAN), F32)], axis=0)
-    row_pack = lax.all_gather(pack, "col", axis=0, tiled=False)
-    col_pack = [pack] + [from_shift(pack, shift) for shift in range(1, row_count)]
-
-    plane_seeds = row_pack[:, SEEDS, : seeds.shape[0]].reshape(col_count, col_count, row_count)
-    own_column = lax.dynamic_index_in_dim(plane_seeds, col, 1, keepdims=False)
-    seeds_back = []
-    for shift in range(shifts):
-        wanted = lax.dynamic_index_in_dim(own_column, (row - shift) % row_count, 1, keepdims=False)
-        seeds_back.append(from_shift(wanted, shift) if shift else wanted)
-    seeds_back = jnp.concatenate(seeds_back).astype(I32)
-
-    sizes = row_count, col_count
-    plan = [(group, shift, shift) for shift in range(shifts) for group in range(col_count)]
-    row_spans = [(0, group) for group in range(col_count)]
-    col_spans = [(1 + shift, None) for shift in range(shifts)]
-    row_packs = [row_pack[group] for group in range(col_count)]
+
+    def after(value, *others):
+        return lax.optimization_barrier((value, *others))[0]
+
+    row_x = {0: inputs}
+    bits = 2
+    while bits < col_count:
+        row_x[bits] = from_bits(inputs, bits)
+        bits *= 2
+    col_x = [inputs]
+    for shift in range(1, shifts):
+        if 2 * shift < row_count:
+            col_x.append(from_shift(inputs, shift))
+    row_x[1] = from_bits(after(inputs, pack), 1)
+    col_pack = [pack] + [from_shift(pack, shift) for shift in range(1, shifts)]
+    first = [row_x[2], row_x[4], *col_x[1:], *col_pack[1:]]
+    if row_count % 2 == 0:
+        col_x.append(from_half(after(inputs, *first)))
+    for bits in range(2, col_count, 2):
+        if bits not in row_x:
+            row_x[bits] = from_bits(after(inputs, *first), bits)
+    for bits in range(2, col_count, 2):
+        row_x[bits + 1] = from_bits(row_x[bits], 1)
+    swapped = [row_x[3], row_x[5]]
+    col_pack += [from_shift(after(pack, *swapped), shift) for shift in range(shifts, row_count)]
+
+    own_pack = jnp.concatenate(
+        [pack[: SEEDS + 1]]
+        + [col_pack[shift][SEEDS : SEEDS + 1] for shift in range(1, shifts)]
+        + [pack[SEEDS + shifts :]],
+        axis=0,
+    )
+    own_pack = after(own_pack, *swapped)
+    even_packs = jnp.stack([own_pack] + [from_bits(own_pack, bits) for bits in range(2, col_count, 2)])
+    odd_packs = from_bits(even_packs, 1)
+    row_packs = [(even_packs, odd_packs)[bits % 2][bits // 2] for bits in range(col_count)]
+
+    plan = [(bits, shift, shift) for shift in range(shifts) for bits in range(col_count)]
     weights = pair_weights(
         sizes,
         plan,
-        row_spans,
-        col_spans,
-        jnp.concatenate([meta, jnp.arange(col_count, dtype=I32)]),
+        shifts,
+        meta,
         listing,
         seeds,
-        seeds_back,
-        [row_x] + col_x,
+        col_x + [row_x[bits] for bits in range(col_count)],
         col_pack[:shifts] + row_packs,
     )
 
-    row_y, col_y = row_pack, col_pack
+    row_y, col_y = (even_packs, odd_packs), col_pack
     for step in range(STEPS):
         if step:
-            row_y = lax.all_gather(embed, "col", axis=0, tiled=False)
+            row_y = (lax.all_gather(embed, "col", axis=0, tiled=False),)
             col_y = [embed] + [from_shift(embed, shift) for shift in range(1, row_count)]
-        row_force, col_force = pair_forces(
-            row_count, col_count, meta, listing, row_list, col_list, weights, row_y, col_y
-        )
+        row_force, col_force = pair_forces(sizes, meta, listing, row_list, col_list, weights, row_y, col_y)
         row_parts = lax.all_to_all(row_force, "col", split_axis=0, concat_axis=0, tiled=True)
         force = jnp.sum(row_parts, axis=0) + col_force[0]
         for shift in range(1, row_count):

time: 143 us -> 126 us (0.88)
  blocking collectives: 23.6 us -> 9.08 us
  waiting for transfers between devices: 27.7 us -> 42 us
  between operations: 14.9 us -> 1.56 us
  starting transfers between devices: 36.3 us -> 42.5 us
  Pallas kernels: 25.2 us -> 20.4 us
  other arithmetic: 7.59 us -> 4.18 us
  local copies, waits for them, and re-layouts: 6.77 us -> 5.27 us
    ppermute x0 -> x11, waiting for transfers between devices: none -> 27.9 us  [from_bits(): return lax.ppermute(value, 'col', pairs)]
    all_gather x2 -> x1, blocking collectives: 23.6 us -> 9.08 us  [shards(): row_y = (lax.all_gather(embed, 'col', axis=0, tiled=False),)]
    ppermute x0 -> x11, starting transfers between devices: none -> 7.68 us  [from_bits(): return lax.ppermute(value, 'col', pairs)]
    ppermute x9 -> x7, waiting for transfers between devices: 12.7 us -> 7 us  [from_shift(): return lax.ppermute(value, 'row', pairs)]
    pallas_call x3, Pallas kernels: 25.2 us -> 20.4 us  [the longest x2 11.7 us: pair_forces(): pl.pallas_call(functools.partial(force_kernel, row_count, col_count, len(...]
    all_to_all x2, waiting for transfers between devices: 11.1 us -> 7.12 us  [shards(): lax.all_to_all(row_force, 'col', split_axis=0, concat_axis=0, tiled=True)]
    ppermute x6, starting transfers between devices: 8.43 us -> 12.2 us  [to_shift(): return lax.ppermute(value, 'row', pairs)]
    ppermute x9 -> x7, starting transfers between devices: 17.9 us -> 14.4 us  [from_shift(): return lax.ppermute(value, 'row', pairs)]
  transfers between devices with their start and end apart: 19 -> 27, of which waited for: 6 -> 10; matrix products, arithmetic and copies ran while one was open for 7% -> 4% of each run, Pallas kernels for 8% -> 7%
where the time goes in v3:
time: 126 us; the launch traced here: 125 us
  starting transfers between devices  42.5 us (34%)
  waiting for transfers between devices  42 us (33%)
  Pallas kernels  20.4 us (16%)
  blocking collectives  9.08 us (7%)
  local copies, waits for them, and re-layouts  5.27 us (4%)
  other arithmetic  4.18 us (3%)
  between operations  1.56 us (1%)
    ppermute x11, waiting for transfers between devices, from_bits(): return lax.ppermute(value, 'col', pairs)  27.9 us
    ppermute x7, starting transfers between devices, from_shift(): return lax.ppermute(value, 'row', pairs)  14.4 us
    ppermute x6, starting transfers between devices, to_shift(): return lax.ppermute(value, 'row', pairs)  12.2 us
    pallas_call x2, Pallas kernels, pair_forces(): pl.pallas_call(functools.partial(force_kernel, row_count, col_count, len(...  11.7 us
    all_gather x1, blocking collectives, shards(): row_y = (lax.all_gather(embed, 'col', axis=0, tiled=False),)  9.08 us
    pallas_call x1, Pallas kernels, pair_weights(): pl.pallas_call(functools.partial(weights_kernel, sizes, plan, (col_spans,...  8.7 us
    ppermute x11, starting transfers between devices, from_bits(): return lax.ppermute(value, 'col', pairs)  7.68 us
    all_to_all x2, waiting for transfers between devices, shards(): lax.all_to_all(row_force, 'col', split_axis=0, concat_axis=0, tiled=True)  7.12 us
  transfers between devices with their start and end apart: 27, of which 10 were waited for; matrix products, arithmetic and copies ran while one was open for 4% of the time, Pallas kernels for 7%

profile of v3, /device:TPU:0, one launch (start us, length us, event | category | flops | bytes accessed | tf_op | source)
XLA Modules:
  0.0 125.0 jit_solution(18283028224648022645)
XLA Ops:
  0.6 3.0 %collective-permute-start.1 = (f32[256,768]{1,0:T(8,128)}, f32[256,768]{1,0:T(8,128)S(1)}, u32[]{:S(2)}, u32[]{:S(2)}) collective-permute-start(f32[256,768]{1,0:T(8,128)} %rest_3_.1), channel_id=1, source_target_pairs={{2,0},{3,1},{0,2},{1,3},{6,4},{7,5},{4,6},{5,7},{10,8},{11,9},{8,1... | collective-permute-start | bytes 2359304 | tf_op jit(solution)/shard_map/ppermute | solution.py:327
  3.6 1.5 %collective-permute-start.2 = (f32[256,768]{1,0:T(8,128)}, f32[256,768]{1,0:T(8,128)S(1)}, u32[]{:S(2)}, u32[]{:S(2)}) collective-permute-start(f32[256,768]{1,0:T(8,128)} %rest_3_.1), channel_id=1, source_target_pairs={{4,0},{5,1},{6,2},{7,3},{0,4},{1,5},{2,6},{3,7},{12,8},{13,9},{14,... | collective-permute-start | bytes 2359304 | tf_op jit(solution)/shard_map/ppermute | solution.py:327
  5.2 3.6 %collective-permute-start = (f32[256,768]{1,0:T(8,128)}, f32[256,768]{1,0:T(8,128)S(1)}, u32[]{:S(2)}, u32[]{:S(2)}) collective-permute-start(f32[256,768]{1,0:T(8,128)} %rest_3_.1), channel_id=1, source_target_pairs={{8,0},{16,8},{24,16},{0,24},{9,1},{17,9},{25,17},{1,25},{10,2},{18... | collective-permute-start | bytes 2359304 | tf_op jit(solution)/shard_map/ppermute | solution.py:314
  9.6 1.3 %multiply_reduce_fusion = f32[256]{0:T(256)S(1)} fusion(f32[256,768]{1,0:T(8,128)} %rest_3_.1), kind=kLoop, calls=%fused_computation | loop fusion | flops 392960 | bytes 787456 | tf_op jit(solution)/shard_map/reduce_sum | solution.py:330
  11.6 0.9 concatenate.10.rest_11_.rest_2_
  13.0 8.4 %collective-permute-done.1.rest_5_ = f32[256,768]{1,0:T(8,128)S(1)} collective-permute-done((f32[256,768]{1,0:T(8,128)}, f32[256,768]{1,0:T(8,128)S(1)}, u32[]{:S(2)}, u32[]{:S(2)}) %collective-permute-start.1) | collective-permute-done | bytes 786464 | tf_op jit(solution)/shard_map/ppermute | solution.py:327
  21.4 1.5 %collective-permute-done.2.rest_7_ = f32[256,768]{1,0:T(8,128)S(1)} collective-permute-done((f32[256,768]{1,0:T(8,128)}, f32[256,768]{1,0:T(8,128)S(1)}, u32[]{:S(2)}, u32[]{:S(2)}) %collective-permute-start.2) | collective-permute-done | bytes 786464 | tf_op jit(solution)/shard_map/ppermute | solution.py:327
  22.9 4.8 %collective-permute-done.3.rest_12_.rest_3_ = f32[72,256]{1,0:T(8,128)S(1)} collective-permute-done((f32[72,256]{1,0:T(8,128)S(1)}, f32[72,256]{1,0:T(8,128)S(1)}, u32[]{:S(2)}, u32[]{:S(2)}) %collective-permute-start.3) | collective-permute-done | bytes 73760 | tf_op jit(solution)/shard_map/ppermute | solution.py:314
  27.6 2.2 %collective-permute-done.4.rest_13_.rest_4_ = f32[72,256]{1,0:T(8,128)S(1)} collective-permute-done((f32[72,256]{1,0:T(8,128)S(1)}, f32[72,256]{1,0:T(8,128)S(1)}, u32[]{:S(2)}, u32[]{:S(2)}) %collective-permute-start.4) | collective-permute-done | bytes 73760 | tf_op jit(solution)/shard_map/ppermute | solution.py:314
  31.7 1.6 %collective-permute-start.12 = (f32[72,256]{1,0:T(8,128)S(1)}, f32[72,256]{1,0:T(8,128)S(1)}, u32[]{:S(2)}, u32[]{:S(2)}) collective-permute-start(f32[72,256]{1,0:T(8,128)S(1)} %concatenate.11.rest_14_), channel_id=1, source_target_pairs={{4,0},{5,1},{6,2},{7,3},{0,4},{1,5},{2,6},{3,7},{12,8},{13,9},{14,... | collective-permute-start | bytes 221192 | tf_op jit(solution)/shard_map/ppermute | solution.py:327
  33.2 1.3 %collective-permute-start.5 = (f32[256,768]{1,0:T(8,128)S(1)}, f32[256,768]{1,0:T(8,128)}, u32[]{:S(2)}, u32[]{:S(2)}) collective-permute-start(f32[256,768]{1,0:T(8,128)S(1)} %copy-done), channel_id=1, source_target_pairs={{16,0},{8,24},{17,1},{9,25},{18,2},{10,26},{19,3},{11,27},{20,4},{... | collective-permute-start | bytes 2359304 | tf_op jit(solution)/shard_map/ppermute | solution.py:319
  34.5 12.9 %collective-permute-done.9.rest_9_ = f32[256,768]{1,0:T(8,128)} collective-permute-done((f32[256,768]{1,0:T(8,128)S(1)}, f32[256,768]{1,0:T(8,128)}, u32[]{:S(2)}, u32[]{:S(2)}) %collective-permute-start.9) | collective-permute-done | bytes 786464 | tf_op jit(solution)/shard_map/ppermute | solution.py:327
  47.9 0.9 collective-permute-done.12.rest_18_
  49.4 4.0 %collective-permute-done.13.rest_20_ = f32[72,256]{1,0:T(8,128)S(1)} collective-permute-done((f32[72,256]{1,0:T(8,128)S(1)}, f32[72,256]{1,0:T(8,128)S(1)}, u32[]{:S(2)}, u32[]{:S(2)}) %collective-permute-start.13) | collective-permute-done | bytes 73760 | tf_op jit(solution)/shard_map/ppermute | solution.py:327
  53.7 0.8 pad_maximum_fusion.rest_0_
  55.6 4.6 %collective-permute-start.15 = (f32[72,256]{1,0:T(8,128)S(1)}, f32[72,256]{1,0:T(8,128)S(1)}, u32[]{:S(2)}, u32[]{:S(2)}) collective-permute-start(f32[72,256]{1,0:T(8,128)S(1)} %concatenate.10.rest_11_.rest_2_), channel_id=1, source_target_pairs={{24,0},{0,8},{8,16},{16,24},{25,1},{1,9},{9,17},{17,25},{26,2},{2,... | collective-permute-start | bytes 221192 | tf_op jit(solution)/shard_map/ppermute | solution.py:314
  60.1 1.0 slice_bitcast_fusion
  61.2 8.7 %weights.1 = bf16[24,128,128]{2,1,0:T(8,128)(2,1)S(1)} custom-call(s32[3]{0:T(128)S(1)} %pad_add_fusion.meta, s32[64]{0:T(128)S(1)} %reshape.49.listing, s32[32]{0:T(128)S(1)} %reshape.52.seeds, f32[256,768]{1,0:T(8,128)S(1)} %copy-done, f32[256,768]{1,0:T(8,128)S(1)} %collective-permute-done.rest_1_, f32[256,768]{1,0:T(8,128)} %collective-permute-done.5.rest_2_, ...), custom_call_target="tpu_custom_call" | custom-call | flops 1811939328 | bytes 8650752 | tf_op jit(solution)/shard_map/weights/pallas_call | solution.py:115
  70.7 6.2 %forces.2 = (f32[8,64,256]{2,1,0:T(8,128)}, f32[64,256]{1,0:T(8,128)S(1)}, f32[64,256]{1,0:T(8,128)S(1)}, f32[64,256]{1,0:T(8,128)S(1)}, f32[64,256]{1,0:T(8,128)S(1)}) custom-call(s32[3]{0:T(128)S(1)} %pad_add_fusion.meta, s32[64]{0:T(128)S(1)} %reshape.49.listing, s32[48]{0:T(128)S(1)} %bitcast.31, s32[48]{0:T(128)S(1)} %bitcast.33, ...), custom_call_target="tpu_custom_call" | custom-call | flops 1744830464 | bytes 1572864 | tf_op jit(solution)/shard_map/forces/pallas_call | solution.py:275
  76.9 3.5 %all-to-all-start = ((f32[8,64,256]{2,1,0:T(8,128)}), f32[8,64,256]{2,1,0:T(8,128)S(1)}, u32[]{:S(2)}, u32[]{:S(2)}) async-start(f32[8,64,256]{2,1,0:T(8,128)} %get-tuple-element.32), calls=%async_computation | async-start | bytes 1048576 | tf_op jit(solution)/shard_map/all_to_all | solution.py:389
  80.4 1.8 %collective-permute-start.16 = (f32[64,256]{1,0:T(8,128)S(1)}, f32[64,256]{1,0:T(8,128)S(1)}, u32[]{:S(2)}, u32[]{:S(2)}) collective-permute-start(f32[64,256]{1,0:T(8,128)S(1)} %get-tuple-element.34), channel_id=1, source_target_pairs={{0,8},{8,16},{16,24},{24,0},{1,9},{9,17},{17,25},{25,1},{2,10},{10... | collective-permute-start | bytes 196616 | tf_op jit(solution)/shard_map/ppermute | solution.py:323
  82.1 2.6 %collective-permute-start.17 = (f32[64,256]{1,0:T(8,128)S(1)}, f32[64,256]{1,0:T(8,128)S(1)}, u32[]{:S(2)}, u32[]{:S(2)}) collective-permute-start(f32[64,256]{1,0:T(8,128)S(1)} %get-tuple-element.35), channel_id=1, source_target_pairs={{0,16},{8,24},{16,0},{24,8},{1,17},{9,25},{17,1},{25,9},{2,18},{10... | collective-permute-start | bytes 196616 | tf_op jit(solution)/shard_map/ppermute | solution.py:323
  84.7 2.1 %collective-permute-start.18 = (f32[64,256]{1,0:T(8,128)S(1)}, f32[64,256]{1,0:T(8,128)S(1)}, u32[]{:S(2)}, u32[]{:S(2)}) collective-permute-start(f32[64,256]{1,0:T(8,128)S(1)} %get-tuple-element.36), channel_id=1, source_target_pairs={{0,24},{8,0},{16,8},{24,16},{1,25},{9,1},{17,9},{25,17},{2,26},{10... | collective-permute-start | bytes 196616 | tf_op jit(solution)/shard_map/ppermute | solution.py:323
  86.8 3.2 %all-to-all-done = f32[8,64,256]{2,1,0:T(8,128)S(1)} async-done(((f32[8,64,256]{2,1,0:T(8,128)}), f32[8,64,256]{2,1,0:T(8,128)S(1)}, u32[]{:S(2)}, u32[]{:S(2)}) %all-to-all-start) | async-done | bytes 524320 | tf_op jit(solution)/shard_map/all_to_all | solution.py:389
  90.1 3.9 %collective-permute-start.19 = (f32[64,256]{1,0:T(8,128)S(1)}, f32[64,256]{1,0:T(8,128)S(1)}, u32[]{:S(2)}, u32[]{:S(2)}) collective-permute-start(f32[64,256]{1,0:T(8,128)S(1)} %multiply_add_fusion.1.rest_1_), channel_id=1, source_target_pairs={{8,0},{16,8},{24,16},{0,24},{9,1},{17,9},{25,17},{1,25},{10,2},{18... | collective-permute-start | bytes 196616 | tf_op jit(solution)/shard_map/ppermute | solution.py:314
  94.1 1.8 %collective-permute-start.21 = (f32[64,256]{1,0:T(8,128)S(1)}, f32[64,256]{1,0:T(8,128)S(1)}, u32[]{:S(2)}, u32[]{:S(2)}) collective-permute-start(f32[64,256]{1,0:T(8,128)S(1)} %multiply_add_fusion.1.rest_1_), channel_id=1, source_target_pairs={{24,0},{0,8},{8,16},{16,24},{25,1},{1,9},{9,17},{17,25},{26,2},{2,... | collective-permute-start | bytes 196616 | tf_op jit(solution)/shard_map/ppermute | solution.py:314
  95.8 9.1 %all-gather = f32[512,256]{1,0:T(8,128)S(1)} all-gather(f32[64,256]{1,0:T(8,128)S(1)} %multiply_add_fusion.1.rest_1_), channel_id=2, replica_groups=mesh['row'=4,'col'=8] {'col'}, dimensions={0}, use_global_device_ids=true | all-gather | bytes 589824 | tf_op jit(solution)/shard_map/all_gather | solution.py:386
  104.9 5.6 %forces.3 = (f32[8,64,256]{2,1,0:T(8,128)}, f32[64,256]{1,0:T(8,128)S(1)}, f32[64,256]{1,0:T(8,128)S(1)}, f32[64,256]{1,0:T(8,128)S(1)}, f32[64,256]{1,0:T(8,128)S(1)}) custom-call(s32[3]{0:T(128)S(1)} %pad_add_fusion.meta, s32[64]{0:T(128)S(1)} %reshape.49.listing, s32[48]{0:T(128)S(1)} %bitcast.32, s32[48]{0:T(128)S(1)} %bitcast.34, ...), custom_call_target="tpu_custom_call" | custom-call | flops 1744830464 | bytes 1572864 | tf_op jit(solution)/shard_map/forces/pallas_call | solution.py:275
  110.5 3.5 %all-to-all-start.1 = ((f32[8,64,256]{2,1,0:T(8,128)}), f32[8,64,256]{2,1,0:T(8,128)S(1)}, u32[]{:S(2)}, u32[]{:S(2)}) async-start(f32[8,64,256]{2,1,0:T(8,128)} %get-tuple-element.37), calls=%async_computation.1 | async-start | bytes 1048576 | tf_op jit(solution)/shard_map/all_to_all | solution.py:389
  114.0 3.3 %collective-permute-start.22 = (f32[64,256]{1,0:T(8,128)S(1)}, f32[64,256]{1,0:T(8,128)S(1)}, u32[]{:S(2)}, u32[]{:S(2)}) collective-permute-start(f32[64,256]{1,0:T(8,128)S(1)} %get-tuple-element.39), channel_id=1, source_target_pairs={{0,8},{8,16},{16,24},{24,0},{1,9},{9,17},{17,25},{25,1},{2,10},{10... | collective-permute-start | bytes 196616 | tf_op jit(solution)/shard_map/ppermute | solution.py:323
  117.4 2.4 %collective-permute-start.24 = (f32[64,256]{1,0:T(8,128)S(1)}, f32[64,256]{1,0:T(8,128)S(1)}, u32[]{:S(2)}, u32[]{:S(2)}) collective-permute-start(f32[64,256]{1,0:T(8,128)S(1)} %get-tuple-element.41), channel_id=1, source_target_pairs={{0,24},{8,0},{16,8},{24,16},{1,25},{9,1},{17,9},{25,17},{2,26},{10... | collective-permute-start | bytes 196616 | tf_op jit(solution)/shard_map/ppermute | solution.py:323
  119.8 3.9 %all-to-all-done.1 = f32[8,64,256]{2,1,0:T(8,128)S(1)} async-done(((f32[8,64,256]{2,1,0:T(8,128)}), f32[8,64,256]{2,1,0:T(8,128)S(1)}, u32[]{:S(2)}, u32[]{:S(2)}) %all-to-all-start.1) | async-done | bytes 524320 | tf_op jit(solution)/shard_map/all_to_all | solution.py:389
  (79 shorter events, 7.9 us)
Async XLA Ops:
  0.6 29.2 %copy-start = (f32[256,768]{1,0:T(8,128)S(1)}, f32[256,768]{1,0:T(8,128)}, u32[]{:S(2)}) copy-start(f32[256,768]{1,0:T(8,128)} %rest_3_.1) | copy-start | bytes 2359300
  0.6 20.8 %collective-permute-start.1 = (f32[256,768]{1,0:T(8,128)}, f32[256,768]{1,0:T(8,128)S(1)}, u32[]{:S(2)}, u32[]{:S(2)}) collective-permute-start(f32[256,768]{1,0:T(8,128)} %rest_3_.1), channel_id=1, source_target_pairs={{2,0},{3,1},{0,2},{1,3},{6,4},{7,5},{4,6},{5,7},{10,8},{11,9},{8,1... | collective-permute-start | bytes 2359304 | tf_op jit(solution)/shard_map/ppermute | solution.py:327
  3.6 19.2 %collective-permute-start.2 = (f32[256,768]{1,0:T(8,128)}, f32[256,768]{1,0:T(8,128)S(1)}, u32[]{:S(2)}, u32[]{:S(2)}) collective-permute-start(f32[256,768]{1,0:T(8,128)} %rest_3_.1), channel_id=1, source_target_pairs={{4,0},{5,1},{6,2},{7,3},{0,4},{1,5},{2,6},{3,7},{12,8},{13,9},{14,... | collective-permute-start | bytes 2359304 | tf_op jit(solution)/shard_map/ppermute | solution.py:327
  5.2 24.7 %collective-permute-start = (f32[256,768]{1,0:T(8,128)}, f32[256,768]{1,0:T(8,128)S(1)}, u32[]{:S(2)}, u32[]{:S(2)}) collective-permute-start(f32[256,768]{1,0:T(8,128)} %rest_3_.1), channel_id=1, source_target_pairs={{8,0},{16,8},{24,16},{0,24},{9,1},{17,9},{25,17},{1,25},{10,2},{18... | collective-permute-start | bytes 2359304 | tf_op jit(solution)/shard_map/ppermute | solution.py:314
  11.6 20.0 %copy-start.9 = (f32[64,256]{1,0:T(8,128)S(1)}, f32[64,256]{1,0:T(8,128)}, u32[]{:S(2)}) copy-start(f32[64,256]{1,0:T(8,128)} %param.14) | copy-start | bytes 196612
  12.5 15.1 %collective-permute-start.3 = (f32[72,256]{1,0:T(8,128)S(1)}, f32[72,256]{1,0:T(8,128)S(1)}, u32[]{:S(2)}, u32[]{:S(2)}) collective-permute-start(f32[72,256]{1,0:T(8,128)S(1)} %concatenate.10.rest_11_.rest_2_), channel_id=1, source_target_pairs={{8,0},{16,8},{24,16},{0,24},{9,1},{17,9},{25,17},{1,25},{10,2},{18... | collective-permute-start | bytes 221192 | tf_op jit(solution)/shard_map/ppermute | solution.py:314
  13.0 16.8 %collective-permute-start.4 = (f32[72,256]{1,0:T(8,128)S(1)}, f32[72,256]{1,0:T(8,128)S(1)}, u32[]{:S(2)}, u32[]{:S(2)}) collective-permute-start(f32[72,256]{1,0:T(8,128)S(1)} %concatenate.10.rest_11_.rest_2_), channel_id=1, source_target_pairs={{16,0},{24,8},{0,16},{8,24},{17,1},{25,9},{1,17},{9,25},{18,2},{26... | collective-permute-start | bytes 221192 | tf_op jit(solution)/shard_map/ppermute | solution.py:314
  21.4 10.2 %collective-permute-start.7 = (f32[256,768]{1,0:T(8,128)S(1)}, f32[256,768]{1,0:T(8,128)}, u32[]{:S(2)}, u32[]{:S(2)}) collective-permute-start(f32[256,768]{1,0:T(8,128)S(1)} %collective-permute-done.1.rest_5_), channel_id=1, source_target_pairs={{1,0},{0,1},{3,2},{2,3},{5,4},{4,5},{7,6},{6,7},{9,8},{8,9},{11,10... | collective-permute-start | bytes 2359304 | tf_op jit(solution)/shard_map/ppermute | solution.py:327
  22.9 8.8 %collective-permute-start.8 = (f32[256,768]{1,0:T(8,128)S(1)}, f32[256,768]{1,0:T(8,128)}, u32[]{:S(2)}, u32[]{:S(2)}) collective-permute-start(f32[256,768]{1,0:T(8,128)S(1)} %collective-permute-done.2.rest_7_), channel_id=1, source_target_pairs={{1,0},{0,1},{3,2},{2,3},{5,4},{4,5},{7,6},{6,7},{9,8},{8,9},{11,10... | collective-permute-start | bytes 2359304 | tf_op jit(solution)/shard_map/ppermute | solution.py:327
  29.9 17.6 %collective-permute-start.9 = (f32[256,768]{1,0:T(8,128)S(1)}, f32[256,768]{1,0:T(8,128)}, u32[]{:S(2)}, u32[]{:S(2)}) collective-permute-start(f32[256,768]{1,0:T(8,128)S(1)} %copy-done), channel_id=1, source_target_pairs={{6,0},{7,1},{4,2},{5,3},{2,4},{3,5},{0,6},{1,7},{14,8},{15,9},{12,... | collective-permute-start | bytes 2359304 | tf_op jit(solution)/shard_map/ppermute | solution.py:327
  31.7 17.2 %collective-permute-start.12 = (f32[72,256]{1,0:T(8,128)S(1)}, f32[72,256]{1,0:T(8,128)S(1)}, u32[]{:S(2)}, u32[]{:S(2)}) collective-permute-start(f32[72,256]{1,0:T(8,128)S(1)} %concatenate.11.rest_14_), channel_id=1, source_target_pairs={{4,0},{5,1},{6,2},{7,3},{0,4},{1,5},{2,6},{3,7},{12,8},{13,9},{14,... | collective-permute-start | bytes 221192 | tf_op jit(solution)/shard_map/ppermute | solution.py:327
  33.2 27.9 %collective-permute-start.6 = (f32[256,768]{1,0:T(8,128)S(1)}, f32[256,768]{1,0:T(8,128)}, u32[]{:S(2)}, u32[]{:S(2)}) collective-permute-start(f32[256,768]{1,0:T(8,128)S(1)} %copy-done), channel_id=1, source_target_pairs={{1,0},{0,1},{3,2},{2,3},{5,4},{4,5},{7,6},{6,7},{9,8},{8,9},{11,10... | collective-permute-start | bytes 2359304 | tf_op jit(solution)/shard_map/ppermute | solution.py:327
  33.2 27.9 %collective-permute-start.5 = (f32[256,768]{1,0:T(8,128)S(1)}, f32[256,768]{1,0:T(8,128)}, u32[]{:S(2)}, u32[]{:S(2)}) collective-permute-start(f32[256,768]{1,0:T(8,128)S(1)} %copy-done), channel_id=1, source_target_pairs={{16,0},{8,24},{17,1},{9,25},{18,2},{10,26},{19,3},{11,27},{20,4},{... | collective-permute-start | bytes 2359304 | tf_op jit(solution)/shard_map/ppermute | solution.py:319
  47.4 13.7 %collective-permute-start.10 = (f32[256,768]{1,0:T(8,128)}, f32[256,768]{1,0:T(8,128)}, u32[]{:S(2)}, u32[]{:S(2)}) collective-permute-start(f32[256,768]{1,0:T(8,128)} %collective-permute-done.9.rest_9_), channel_id=1, source_target_pairs={{1,0},{0,1},{3,2},{2,3},{5,4},{4,5},{7,6},{6,7},{9,8},{8,9},{11,10... | collective-permute-start | bytes 2359304 | tf_op jit(solution)/shard_map/ppermute | solution.py:327
  47.4 6.0 %collective-permute-start.13 = (f32[72,256]{1,0:T(8,128)S(1)}, f32[72,256]{1,0:T(8,128)S(1)}, u32[]{:S(2)}, u32[]{:S(2)}) collective-permute-start(f32[72,256]{1,0:T(8,128)S(1)} %concatenate.11.rest_14_), channel_id=1, source_target_pairs={{6,0},{7,1},{4,2},{5,3},{2,4},{3,5},{0,6},{1,7},{14,8},{15,9},{12,... | collective-permute-start | bytes 221192 | tf_op jit(solution)/shard_map/ppermute | solution.py:327
  48.8 4.8 %collective-permute-start.11 = (f32[72,256]{1,0:T(8,128)S(1)}, f32[72,256]{1,0:T(8,128)S(1)}, u32[]{:S(2)}, u32[]{:S(2)}) collective-permute-start(f32[72,256]{1,0:T(8,128)S(1)} %concatenate.11.rest_14_), channel_id=1, source_target_pairs={{2,0},{3,1},{0,2},{1,3},{6,4},{7,5},{4,6},{5,7},{10,8},{11,9},{8,1... | collective-permute-start | bytes 221192 | tf_op jit(solution)/shard_map/ppermute | solution.py:327
  54.4 5.7 %collective-permute-start.14 = (f32[4,72,256]{2,1,0:T(8,128)}, f32[4,72,256]{2,1,0:T(8,128)}, u32[]{:S(2)}, u32[]{:S(2)}) collective-permute-start(f32[4,72,256]{2,1,0:T(8,128)} %pad_maximum_fusion.rest_0_), channel_id=1, source_target_pairs={{1,0},{0,1},{3,2},{2,3},{5,4},{4,5},{7,6},{6,7},{9,8},{8,9},{11,10... | collective-permute-start | bytes 884744 | tf_op jit(solution)/shard_map/ppermute | solution.py:327
  55.6 5.6 %copy-start.6 = (f32[72,256]{1,0:T(8,128)S(1)}, f32[72,256]{1,0:T(8,128)}, u32[]{:S(2)}) copy-start(f32[72,256]{1,0:T(8,128)} %copy-done.5) | copy-start | bytes 221188
  55.6 14.4 %collective-permute-start.15 = (f32[72,256]{1,0:T(8,128)S(1)}, f32[72,256]{1,0:T(8,128)S(1)}, u32[]{:S(2)}, u32[]{:S(2)}) collective-permute-start(f32[72,256]{1,0:T(8,128)S(1)} %concatenate.10.rest_11_.rest_2_), channel_id=1, source_target_pairs={{24,0},{0,8},{8,16},{16,24},{25,1},{1,9},{9,17},{17,25},{26,2},{2,... | collective-permute-start | bytes 221192 | tf_op jit(solution)/shard_map/ppermute | solution.py:314
  69.9 6.9 %copy-start.1 = (bf16[24,128,128]{2,1,0:T(8,128)(2,1)}, bf16[24,128,128]{2,1,0:T(8,128)(2,1)S(1)}, u32[]{:S(2)}) copy-start(bf16[24,128,128]{2,1,0:T(8,128)(2,1)S(1)} %weights.1) | copy-start | bytes 2359300
  76.9 13.2 %all-to-all-start = ((f32[8,64,256]{2,1,0:T(8,128)}), f32[8,64,256]{2,1,0:T(8,128)S(1)}, u32[]{:S(2)}, u32[]{:S(2)}) async-start(f32[8,64,256]{2,1,0:T(8,128)} %get-tuple-element.32), calls=%async_computation | async-start | bytes 1048576 | tf_op jit(solution)/shard_map/all_to_all | solution.py:389
  80.4 9.7 %collective-permute-start.16 = (f32[64,256]{1,0:T(8,128)S(1)}, f32[64,256]{1,0:T(8,128)S(1)}, u32[]{:S(2)}, u32[]{:S(2)}) collective-permute-start(f32[64,256]{1,0:T(8,128)S(1)} %get-tuple-element.34), channel_id=1, source_target_pairs={{0,8},{8,16},{16,24},{24,0},{1,9},{9,17},{17,25},{25,1},{2,10},{10... | collective-permute-start | bytes 196616 | tf_op jit(solution)/shard_map/ppermute | solution.py:323
  82.1 8.0 %collective-permute-start.17 = (f32[64,256]{1,0:T(8,128)S(1)}, f32[64,256]{1,0:T(8,128)S(1)}, u32[]{:S(2)}, u32[]{:S(2)}) collective-permute-start(f32[64,256]{1,0:T(8,128)S(1)} %get-tuple-element.35), channel_id=1, source_target_pairs={{0,16},{8,24},{16,0},{24,8},{1,17},{9,25},{17,1},{25,9},{2,18},{10... | collective-permute-start | bytes 196616 | tf_op jit(solution)/shard_map/ppermute | solution.py:323
  84.7 20.2 %copy-start.2 = (bf16[24,128,128]{2,1,0:T(8,128)(2,1)S(1)}, bf16[24,128,128]{2,1,0:T(8,128)(2,1)}, u32[]{:S(2)}) copy-start(bf16[24,128,128]{2,1,0:T(8,128)(2,1)} %copy-done.1) | copy-start | bytes 2359300
  84.7 5.4 %collective-permute-start.18 = (f32[64,256]{1,0:T(8,128)S(1)}, f32[64,256]{1,0:T(8,128)S(1)}, u32[]{:S(2)}, u32[]{:S(2)}) collective-permute-start(f32[64,256]{1,0:T(8,128)S(1)} %get-tuple-element.36), channel_id=1, source_target_pairs={{0,24},{8,0},{16,8},{24,16},{1,25},{9,1},{17,9},{25,17},{2,26},{10... | collective-permute-start | bytes 196616 | tf_op jit(solution)/shard_map/ppermute | solution.py:323
  90.1 14.8 %collective-permute-start.19 = (f32[64,256]{1,0:T(8,128)S(1)}, f32[64,256]{1,0:T(8,128)S(1)}, u32[]{:S(2)}, u32[]{:S(2)}) collective-permute-start(f32[64,256]{1,0:T(8,128)S(1)} %multiply_add_fusion.1.rest_1_), channel_id=1, source_target_pairs={{8,0},{16,8},{24,16},{0,24},{9,1},{17,9},{25,17},{1,25},{10,2},{18... | collective-permute-start | bytes 196616 | tf_op jit(solution)/shard_map/ppermute | solution.py:314
  94.0 10.9 %collective-permute-start.20 = (f32[64,256]{1,0:T(8,128)S(1)}, f32[64,256]{1,0:T(8,128)S(1)}, u32[]{:S(2)}, u32[]{:S(2)}) collective-permute-start(f32[64,256]{1,0:T(8,128)S(1)} %multiply_add_fusion.1.rest_1_), channel_id=1, source_target_pairs={{16,0},{24,8},{0,16},{8,24},{17,1},{25,9},{1,17},{9,25},{18,2},{26... | collective-permute-start | bytes 196616 | tf_op jit(solution)/shard_map/ppermute | solution.py:314
  94.1 10.9 %collective-permute-start.21 = (f32[64,256]{1,0:T(8,128)S(1)}, f32[64,256]{1,0:T(8,128)S(1)}, u32[]{:S(2)}, u32[]{:S(2)}) collective-permute-start(f32[64,256]{1,0:T(8,128)S(1)} %multiply_add_fusion.1.rest_1_), channel_id=1, source_target_pairs={{24,0},{0,8},{8,16},{16,24},{25,1},{1,9},{9,17},{17,25},{26,2},{2,... | collective-permute-start | bytes 196616 | tf_op jit(solution)/shard_map/ppermute | solution.py:314
  110.5 13.2 %all-to-all-start.1 = ((f32[8,64,256]{2,1,0:T(8,128)}), f32[8,64,256]{2,1,0:T(8,128)S(1)}, u32[]{:S(2)}, u32[]{:S(2)}) async-start(f32[8,64,256]{2,1,0:T(8,128)} %get-tuple-element.37), calls=%async_computation.1 | async-start | bytes 1048576 | tf_op jit(solution)/shard_map/all_to_all | solution.py:389
  114.0 9.7 %collective-permute-start.22 = (f32[64,256]{1,0:T(8,128)S(1)}, f32[64,256]{1,0:T(8,128)S(1)}, u32[]{:S(2)}, u32[]{:S(2)}) collective-permute-start(f32[64,256]{1,0:T(8,128)S(1)} %get-tuple-element.39), channel_id=1, source_target_pairs={{0,8},{8,16},{16,24},{24,0},{1,9},{9,17},{17,25},{25,1},{2,10},{10... | collective-permute-start | bytes 196616 | tf_op jit(solution)/shard_map/ppermute | solution.py:323
  117.3 6.4 %collective-permute-start.23 = (f32[64,256]{1,0:T(8,128)S(1)}, f32[64,256]{1,0:T(8,128)S(1)}, u32[]{:S(2)}, u32[]{:S(2)}) collective-permute-start(f32[64,256]{1,0:T(8,128)S(1)} %get-tuple-element.40), channel_id=1, source_target_pairs={{0,16},{8,24},{16,0},{24,8},{1,17},{9,25},{17,1},{25,9},{2,18},{10... | collective-permute-start | bytes 196616 | tf_op jit(solution)/shard_map/ppermute | solution.py:323
  117.4 6.3 %collective-permute-start.24 = (f32[64,256]{1,0:T(8,128)S(1)}, f32[64,256]{1,0:T(8,128)S(1)}, u32[]{:S(2)}, u32[]{:S(2)}) collective-permute-start(f32[64,256]{1,0:T(8,128)S(1)} %get-tuple-element.41), channel_id=1, source_target_pairs={{0,24},{8,0},{16,8},{24,16},{1,25},{9,1},{17,9},{25,17},{2,26},{10... | collective-permute-start | bytes 196616 | tf_op jit(solution)/shard_map/ppermute | solution.py:323
  (10 other events, 16.6 us)

commit v4 on v3

--- a/solution.py
+++ b/solution.py
@@ -52,85 +52,191 @@
     return jnp.where(row < half, row % 2 == 0, (row - half) % 2 == 1)
 
 
-def weights_kernel(sizes, plan, spans, meta, listing, seeds, *rest):
+def each(count, body):
+    if count <= 8:
+        for index in range(count):
+            body(index)
+    else:
+        pl.loop(0, count)(body)
+
+
+def pick_of(sizes, meta, listing, bits, shift):
+    row_count, _ = sizes
+    place = lax.bitwise_xor(meta[1], bits) * row_count + lax.rem(meta[0] + shift, row_count)
+    start_i = pl.multiple_of(listing[2 * place] * BLK, BLK)
+    start_j = pl.multiple_of(listing[2 * place + 1] * BLK, BLK)
+    return start_i, start_j, place
+
+
+def gram_of(high_j, low_j, high_i, low_i):
+    return nt_dot(high_j, low_i) + nt_dot(low_j, high_i) + nt_dot(high_j, high_i)
+
+
+def grams_kernel(sizes, counts, meta, listing, *rest):
+    shifts_early, rows_early = counts
+    row_count, _ = sizes
+    columns, rows = rest[:shifts_early], rest[shifts_early : shifts_early + rows_early - 1]
+    grams, high_c, low_c, high_last, low_last, high_r, low_r = rest[shifts_early + rows_early - 1 :]
+    for shift in range(shifts_early):
+        high_c[shift], low_c[shift] = split(columns[shift][:SPAN])
+    high_r[0], low_r[0] = high_c[0], low_c[0]
+    for line in range(1, rows_early):
+        high_r[line], low_r[line] = split(rows[line - 1][...])
+
+    def row_span(line):
+        bits = meta[3 + line]
+        for shift in range(shifts_early):
+            start_i, start_j, _ = pick_of(sizes, meta, listing, bits, shift)
+            span_i, span_j = pl.ds(start_i, BLK), pl.ds(start_j, BLK)
+            grams[line, shift] = gram_of(
+                high_c[shift, span_j, :], low_c[shift, span_j, :], high_r[line, span_i, :], low_r[line, span_i, :]
+            )
+        start_i, _, _ = pick_of(sizes, meta, listing, bits, shifts_early)
+        high_last[line] = high_r[line, pl.ds(start_i, BLK), :]
+        low_last[line] = low_r[line, pl.ds(start_i, BLK), :]
+
+    each(rows_early, row_span)
+
+
+def early_grams(sizes, meta, listing, columns, rows):
+    shifts_early, rows_early, depth = len(columns), len(rows) + 1, rows[0].shape[-1]
+    smem = pl.BlockSpec(memory_space=pltpu.SMEM)
+    vmem = pl.BlockSpec(memory_space=pltpu.VMEM)
+    tiles = shifts_early * rows_early
+    return pl.pallas_call(
+        functools.partial(grams_kernel, sizes, (shifts_early, rows_early)),
+        in_specs=[smem] * 2 + [vmem] * (len(columns) + len(rows)),
+        out_specs=[vmem] * 5,
+        out_shape=[
+            jax.ShapeDtypeStruct((rows_early, shifts_early, BLK, BLK), F32),
+            jax.ShapeDtypeStruct((shifts_early, SPAN, depth), BF16),
+            jax.ShapeDtypeStruct((shifts_early, SPAN, depth), BF16),
+            jax.ShapeDtypeStruct((rows_early, BLK, depth), BF16),
+            jax.ShapeDtypeStruct((rows_early, BLK, depth), BF16),
+        ],
+        scratch_shapes=[pltpu.VMEM((rows_early, SPAN, depth), BF16)] * 2,
+        compiler_params=pltpu.CompilerParams(vmem_limit_bytes=VMEM_LIMIT),
+        cost_estimate=pl.CostEstimate(
+            flops=tiles * 6 * BLK * BLK * depth,
+            bytes_accessed=(shifts_early + rows_early) * SPAN * depth * 4,
+            transcendentals=0,
+        ),
+        name="grams",
+    )(meta, listing, *columns, *rows)
+
+
+def weights_kernel(sizes, counts, meta, listing, seeds, grams, high_c, low_c, high_last, low_last, *rest):
     row_count, col_count = sizes
-    col_spans, row_spans = spans
-    count = row_spans + col_spans
-    arrays, packs = rest[:count], rest[count : 2 * count]
-    out, high, low, col_params, grams = rest[2 * count :]
+    shifts_early, rows_early = counts
+    shifts, rows_late = shifts_early + 1, col_count - rows_early
+    columns, late, packs = rest[:shifts], rest[shifts : shifts + rows_late], rest[shifts + rows_late :][:3]
+    out, high_l, low_l, high_r, low_r, late_grams, col_params, row_params = rest[shifts + rows_late + 3 :]
+    own_pack, even_packs, odd_packs = packs
     row, col = meta[0], meta[1]
-    for place in range(col_spans):
+
+    high_l[...], low_l[...] = split(columns[shifts_early][:SPAN])
+    for shift in range(shifts):
         for block in range(CB):
-            params = packs[place][RHO : RHO + 8, block * BLK : (block + 1) * BLK]
-            col_params[place, block] = params.T
+            lanes = slice(block * BLK, (block + 1) * BLK)
+            if shift == 0:
+                params = own_pack[RHO : RHO + 8, lanes]
+            else:
+                params = columns[shift][SPAN + 16 : SPAN + 24, 2 * SPAN :][:, lanes]
+            col_params[shift, block] = params.T
+    for bits in range(col_count):
+        row_params[bits] = (even_packs, odd_packs)[bits % 2][bits // 2, RHO : RHO + 8, :]
+    for line in range(rows_late):
+        high_r[line], low_r[line] = split(late[line][...])
+
+    def early_last(line):
+        _, start_j, _ = pick_of(sizes, meta, listing, meta[3 + line], shifts_early)
+        span_j = pl.ds(start_j, BLK)
+        late_grams[shifts_early, meta[3 + line]] = gram_of(
+            high_l[span_j, :], low_l[span_j, :], high_last[line], low_last[line]
+        )
+
+    each(rows_early, early_last)
+
+    def late_row(line):
+        bits = meta[3 + rows_early + line]
+        for shift in range(shifts):
+            start_i, start_j, _ = pick_of(sizes, meta, listing, bits, shift)
+            span_i, span_j = pl.ds(start_i, BLK), pl.ds(start_j, BLK)
+            if shift == shifts_early:
+                high_j, low_j = high_l[span_j, :], low_l[span_j, :]
+            else:
+                high_j, low_j = high_c[shift, span_j, :], low_c[shift, span_j, :]
+            late_grams[shift, bits] = gram_of(high_j, low_j, high_r[line, span_i, :], low_r[line, span_i, :])
+
+    each(rows_late, late_row)
+
     positions_j = lax.broadcasted_iota(I32, (BLK, BLK), 0)
     positions_i = lax.broadcasted_iota(I32, (BLK, BLK), 1)
     wanted_seed = lax.broadcasted_iota(I32, (1, SPAN), 1) == col * row_count + row
 
-    for place in range(col_spans):
-        high[place], low[place] = split(arrays[place][...])
-    for line in range(row_spans):
-        place = col_spans + line
-        high[place], low[place] = split(arrays[place][...])
-        group = lax.bitwise_xor(col, line)
-        tiles = [(tile, entry) for tile, entry in enumerate(plan) if entry[0] == line]
-        picks = {}
-        for tile, (_, column, shift) in tiles:
-            other = lax.rem(row + shift, row_count)
-            entry = (group * row_count + other) * 2
-            start_i = pl.multiple_of(listing[entry] * BLK, BLK)
-            start_j = pl.multiple_of(listing[entry + 1] * BLK, BLK)
-            picks[tile] = other, start_i, listing[entry + 1]
-            high_j, low_j = high[column, pl.ds(start_j, BLK), :], low[column, pl.ds(start_j, BLK), :]
-            high_i, low_i = high[place, pl.ds(start_i, BLK), :], low[place, pl.ds(start_i, BLK), :]
-            grams[tile] = nt_dot(high_j, low_i) + nt_dot(low_j, high_i) + nt_dot(high_j, high_i)
-        for tile, (_, column, shift) in tiles:
-            other, start_i, col_pick = picks[tile]
-            params_i = packs[place][RHO : RHO + 8, pl.ds(start_i, BLK)]
-            rho_i, sigma_i, square_i = params_i[0:1], params_i[1:2], params_i[2:3]
-            params_j = col_params[column, col_pick]
-            rho_j, sigma_j, square_j = params_j[:, 0:1], params_j[:, 1:2], params_j[:, 2:3]
-            total = square_j + square_i - 2.0 * grams[tile]
-            distance = jnp.sqrt(jnp.maximum(total, 1.0))
-            seed = seeds[group * row_count + other]
-            plane_seeds = packs[place][SEEDS + shift : SEEDS + shift + 1, :]
-            seed_back = jnp.sum(jnp.where(wanted_seed, plane_seeds, 0.0), axis=1, keepdims=True).astype(I32)
-            ahead = hash_bits(seed, positions_i, positions_j) * jnp.exp(
-                jnp.maximum(distance - rho_i, 0.0) * (-1.0 / sigma_i)
-            )
-            behind = hash_bits(seed_back, positions_j, positions_i) * jnp.exp(
-                jnp.maximum(distance - rho_j, 0.0) * (-1.0 / sigma_j)
-            )
-            weights = (ahead + behind - ahead * behind).astype(BF16)
-            if shift == 0 and line == 0:
-                weights = (weights.astype(F32) * 0.5).astype(BF16)
-            out[tile] = weights
-
-
-def pair_weights(sizes, plan, col_spans, meta, listing, seeds, arrays, packs):
-    depth = arrays[0].shape[-1]
+    def finish(bits, shift, gram):
+        start_i, start_j, place = pick_of(sizes, meta, listing, bits, shift)
+        params_i = row_params[bits, :, pl.ds(start_i, BLK)]
+        rho_i, sigma_i, square_i = params_i[0:1], params_i[1:2], params_i[2:3]
+        params_j = col_params[shift, lax.div(start_j, BLK)]
+        rho_j, sigma_j, square_j = params_j[:, 0:1], params_j[:, 1:2], params_j[:, 2:3]
+        distance = jnp.sqrt(jnp.maximum(square_j + square_i - 2.0 * gram, 1.0))
+        plane_seeds = row_params[bits, SEEDS - RHO + shift : SEEDS - RHO + shift + 1, :]
+        seed_back = jnp.sum(jnp.where(wanted_seed, plane_seeds, 0.0), axis=1, keepdims=True).astype(I32)
+        ahead = hash_bits(seeds[place], positions_i, positions_j) * jnp.exp(
+            jnp.maximum(distance - rho_i, 0.0) * (-1.0 / sigma_i)
+        )
+        behind = hash_bits(seed_back, positions_j, positions_i) * jnp.exp(
+            jnp.maximum(distance - rho_j, 0.0) * (-1.0 / sigma_j)
+        )
+        weights = (ahead + behind - ahead * behind).astype(BF16)
+        if shift == 0:
+            weights = (weights.astype(F32) * jnp.where(bits == 0, 0.5, 1.0)).astype(BF16)
+        out[shift * col_count + bits] = weights
+
+    def early_rows(line):
+        bits = meta[3 + line]
+        for shift in range(shifts):
+            finish(bits, shift, grams[line, shift] if shift < shifts_early else late_grams[shift, bits])
+
+    def late_rows(line):
+        bits = meta[3 + rows_early + line]
+        for shift in range(shifts):
+            finish(bits, shift, late_grams[shift, bits])
+
+    each(rows_early, early_rows)
+    each(rows_late, late_rows)
+
+
+def pair_weights(sizes, meta, listing, seeds, early, columns, late, packs):
+    _, col_count = sizes
+    shifts, depth = len(columns), late[0].shape[-1]
+    rows_late = len(late)
     smem = pl.BlockSpec(memory_space=pltpu.SMEM)
     vmem = pl.BlockSpec(memory_space=pltpu.VMEM)
-    tiles, count = len(plan), len(arrays)
+    tiles = shifts * col_count
     return pl.pallas_call(
-        functools.partial(weights_kernel, sizes, plan, (col_spans, count - col_spans)),
-        in_specs=[smem] * 3 + [vmem] * (2 * count),
+        functools.partial(weights_kernel, sizes, (shifts - 1, col_count - rows_late)),
+        in_specs=[smem] * 3 + [vmem] * (5 + shifts + rows_late + 3),
         out_specs=vmem,
         out_shape=jax.ShapeDtypeStruct((tiles, BLK, BLK), BF16),
         scratch_shapes=[
-            pltpu.VMEM((count, SPAN, depth), BF16),
-            pltpu.VMEM((count, SPAN, depth), BF16),
-            pltpu.VMEM((col_spans, CB, BLK, 8), F32),
-            pltpu.VMEM((tiles, BLK, BLK), F32),
+            pltpu.VMEM((SPAN, depth), BF16),
+            pltpu.VMEM((SPAN, depth), BF16),
+            pltpu.VMEM((rows_late, SPAN, depth), BF16),
+            pltpu.VMEM((rows_late, SPAN, depth), BF16),
+            pltpu.VMEM((shifts, col_count, BLK, BLK), F32),
+            pltpu.VMEM((shifts, CB, BLK, 8), F32),
+            pltpu.VMEM((col_count, 8, SPAN), F32),
         ],
         compiler_params=pltpu.CompilerParams(vmem_limit_bytes=VMEM_LIMIT),
         cost_estimate=pl.CostEstimate(
-            flops=tiles * 6 * BLK * BLK * depth,
-            bytes_accessed=count * SPAN * depth * 4,
+            flops=tiles * 3 * BLK * BLK * depth,
+            bytes_accessed=(shifts + rows_late) * SPAN * depth * 4,
             transcendentals=tiles * 3 * BLK * BLK,
         ),
         name="weights",
-    )(meta, listing, seeds, *arrays, *packs)
+    )(meta, listing, seeds, *early, *columns, *late, *packs)
 
 
 def force_kernel(row_count, col_count, by_bits, meta, listing, neg_rows, neg_cols, weights, *rest):
@@ -176,16 +282,19 @@
         right_pull[index] = pulls(high, low)
         right_acc[index] = jnp.zeros((PULL, BLK), F32)
 
-    def row_y(line, block):
+    def row_y(pair, side, block):
         lanes = slice(block * BLK, (block + 1) * BLK)
+        line = pair * 2 + side
         if by_bits:
-            return row_arrays[line % 2][line // 2, :D_EMB, lanes], lax.bitwise_xor(line, col)
+            return row_arrays[side][pair, :D_EMB, lanes], lax.bitwise_xor(line, col)
         return row_arrays[0][line, :D_EMB, lanes], line
 
-    for line in range(col_count):
-        for block in range(CB):
-            value, group = row_y(line, block)
-            left_block(group * CB + block, value)
+    @pl.loop(0, col_count // 2)
+    def _(pair):
+        for side in range(2):
+            for block in range(CB):
+                value, group = row_y(pair, side, block)
+                left_block(group * CB + block, value)
 
     for shift in range(row_count):
         for block in range(CB):
@@ -254,11 +363,13 @@
     def force_of(acc, value):
         return acc[:D_EMB] + acc[D_EMB + 16 :] - value * acc[D_EMB : D_EMB + 1]
 
-    for line in range(col_count):
-        for block in range(CB):
-            value, group = row_y(line, block)
-            lanes = slice(block * BLK, (block + 1) * BLK)
-            row_force[group, :, lanes] = force_of(left_acc[group * CB + block], value)
+    @pl.loop(0, col_count // 2)
+    def _(pair):
+        for side in range(2):
+            for block in range(CB):
+                value, group = row_y(pair, side, block)
+                lanes = slice(block * BLK, (block + 1) * BLK)
+                row_force[group, :, lanes] = force_of(left_acc[group * CB + block], value)
 
     for shift in range(row_count):
         for block in range(CB):
@@ -327,60 +438,71 @@
         return lax.ppermute(value, "col", pairs)
 
     sizes = row_count, col_count
-    squares = jnp.sum(inputs * inputs, axis=1)
-    seed_row = jnp.zeros((SPAN,), F32).at[: seeds.shape[0]].set(seeds.astype(F32))
-    params = jnp.stack([rho, sigma, squares, seed_row])
-    pack = jnp.concatenate([embed, params, jnp.zeros((PACK - D_EMB - 4, SPAN), F32)], axis=0)
+    single = [1 << place for place in range(1, (col_count - 1).bit_length())]
+    early_bits = [0, 1] + [bits + core for bits in single for core in range(2)]
+    late_bits = [bits for bits in range(col_count) if bits not in early_bits]
+    meta = jnp.concatenate([meta, jnp.array(early_bits + late_bits, I32)])
 
     def after(value, *others):
         return lax.optimization_barrier((value, *others))[0]
 
     row_x = {0: inputs}
-    bits = 2
-    while bits < col_count:
+    for bits in single:
         row_x[bits] = from_bits(inputs, bits)
-        bits *= 2
-    col_x = [inputs]
-    for shift in range(1, shifts):
-        if 2 * shift < row_count:
-            col_x.append(from_shift(inputs, shift))
-    row_x[1] = from_bits(after(inputs, pack), 1)
-    col_pack = [pack] + [from_shift(pack, shift) for shift in range(1, shifts)]
-    first = [row_x[2], row_x[4], *col_x[1:], *col_pack[1:]]
-    if row_count % 2 == 0:
-        col_x.append(from_half(after(inputs, *first)))
-    for bits in range(2, col_count, 2):
-        if bits not in row_x:
-            row_x[bits] = from_bits(after(inputs, *first), bits)
-    for bits in range(2, col_count, 2):
-        row_x[bits + 1] = from_bits(row_x[bits], 1)
-    swapped = [row_x[3], row_x[5]]
-    col_pack += [from_shift(after(pack, *swapped), shift) for shift in range(shifts, row_count)]
-
-    own_pack = jnp.concatenate(
-        [pack[: SEEDS + 1]]
-        + [col_pack[shift][SEEDS : SEEDS + 1] for shift in range(1, shifts)]
-        + [pack[SEEDS + shifts :]],
-        axis=0,
+    far_seeds = [from_shift(seeds, shift) for shift in range(1, shifts)]
+
+    squares = jnp.sum(inputs * inputs, axis=1)
+    params = jnp.stack([rho, sigma, squares])
+    pack = jnp.concatenate([embed, params, jnp.zeros((PACK - SEEDS, SPAN), F32)], axis=0)
+    third = PACK // 3
+    below = jnp.concatenate([pack[:third], pack[third : 2 * third], pack[2 * third :]], axis=1)
+    with_pack = jnp.concatenate([inputs, after(below, *far_seeds)], axis=0)
+    col_x = [inputs] + [from_shift(with_pack, shift) for shift in range(1, shifts - 1)]
+    for bits in late_bits:
+        if bits % 2 == 0:
+            row_x[bits] = from_bits(after(inputs, with_pack), bits)
+    row_x[1] = from_bits(after(inputs, with_pack), 1)
+    near = [row_x[bits] for bits in single] + col_x[1:]
+    for bits in single:
+        row_x[bits + 1] = from_bits(after(row_x[bits], *near), 1)
+    col_x.append(from_half(after(with_pack, row_x[1])))
+
+    seed_rows = jnp.pad(
+        jnp.stack([seeds, *far_seeds]).astype(F32), ((0, PACK - SEEDS - shifts), (0, SPAN - seeds.shape[0]))
     )
-    own_pack = after(own_pack, *swapped)
+    own_pack = jnp.concatenate([embed, params, seed_rows], axis=0)
+    early = early_grams(sizes, meta, listing, col_x[:-1], [row_x[bits] for bits in early_bits[1:]])
+    own_pack = after(own_pack, *[row_x[bits + 1] for bits in single])
     even_packs = jnp.stack([own_pack] + [from_bits(own_pack, bits) for bits in range(2, col_count, 2)])
+    even_packs = after(even_packs, early[0])
     odd_packs = from_bits(even_packs, 1)
-    row_packs = [(even_packs, odd_packs)[bits % 2][bits // 2] for bits in range(col_count)]
-
-    plan = [(bits, shift, shift) for shift in range(shifts) for bits in range(col_count)]
+    for bits in late_bits:
+        if bits % 2 == 0:
+            row_x[bits + 1] = from_bits(after(row_x[bits], even_packs), 1)
+
+    col_y = [embed]
+    for shift in range(1, shifts - 1):
+        packed = col_x[shift][SPAN:]
+        col_y.append(
+            jnp.concatenate(
+                [packed[:, :SPAN], packed[:, SPAN : 2 * SPAN], packed[: D_EMB - 2 * third, 2 * SPAN :]], axis=0
+            )
+        )
+    held = after(embed, *[row_x[bits] for bits in late_bits if bits % 2 == 0])
+    col_y += [from_shift(held, shift) for shift in range(shifts - 1, row_count)]
+
     weights = pair_weights(
         sizes,
-        plan,
-        shifts,
         meta,
         listing,
         seeds,
-        col_x + [row_x[bits] for bits in range(col_count)],
-        col_pack[:shifts] + row_packs,
+        early,
+        col_x,
+        [row_x[bits] for bits in late_bits],
+        [own_pack, even_packs, odd_packs],
     )
 
-    row_y, col_y = (even_packs, odd_packs), col_pack
+    row_y = (even_packs, odd_packs)
     for step in range(STEPS):
         if step:
             row_y = (lax.all_gather(embed, "col", axis=0, tiled=False),)

time: 126 us -> 120 us (0.952)
  starting transfers between devices: 42.5 us -> 37.6 us
  local copies, waits for them, and re-layouts: 5.27 us -> 1.94 us
  waiting for transfers between devices: 42 us -> 43.6 us
    all_to_all x2, waiting for transfers between devices: 7.12 us -> 11.9 us  [shards(): lax.all_to_all(row_force, 'col', split_axis=0, concat_axis=0, tiled=True)]
    ppermute x6, starting transfers between devices: 12.2 us -> 7.45 us  [to_shift(): return lax.ppermute(value, 'row', pairs)]
    ppermute x7 -> x8, waiting for transfers between devices: 7 us -> 2.27 us  [from_shift(): return lax.ppermute(value, 'row', pairs)]
    unnamed x32 -> x16, local copies, waits for them, and re-layouts: 2.92 us -> 0.96 us
    ppermute x7 -> x8, starting transfers between devices: 14.4 us -> 12.7 us  [from_shift(): return lax.ppermute(value, 'row', pairs)]
    ppermute x11, starting transfers between devices: 7.68 us -> 9.16 us  [from_bits(): return lax.ppermute(value, 'col', pairs)]
    ppermute x6, waiting for transfers between devices: 0.02 us -> 1.38 us  [to_shift(): return lax.ppermute(value, 'row', pairs)]
    pallas_call x1 -> x2, Pallas kernels: 8.7 us -> 9.72 us  [the longest x1 5.27 us: early_grams(): pl.pallas_call(functools.partial(grams_kernel, sizes, (shifts_early, rows...]
  transfers between devices with their start and end apart: 27 -> 28, of which waited for: 10 -> 11; matrix products, arithmetic and copies ran while one was open for 4% -> 2% of each run, Pallas kernels for 7% -> 8%
where the time goes in v4:
time: 120 us
  waiting for transfers between devices  43.6 us (36%)
  starting transfers between devices  37.6 us (31%)
  Pallas kernels  21.1 us (18%)
  blocking collectives  10.3 us (9%)
  other arithmetic  3.61 us (3%)
  local copies, waits for them, and re-layouts  1.94 us (2%)
  between operations  1.58 us (1%)
    ppermute x11, waiting for transfers between devices, from_bits(): return lax.ppermute(value, 'col', pairs)  28 us
    ppermute x8, starting transfers between devices, from_shift(): return lax.ppermute(value, 'row', pairs)  12.7 us
    all_to_all x2, waiting for transfers between devices, shards(): lax.all_to_all(row_force, 'col', split_axis=0, concat_axis=0, tiled=True)  11.9 us
    pallas_call x2, Pallas kernels, pair_forces(): pl.pallas_call(functools.partial(force_kernel, row_count, col_count, len(...  11.4 us
    all_gather x1, blocking collectives, shards(): row_y = (lax.all_gather(embed, 'col', axis=0, tiled=False),)  10.3 us
    ppermute x11, starting transfers between devices, from_bits(): return lax.ppermute(value, 'col', pairs)  9.16 us
    ppermute x6, starting transfers between devices, to_shift(): return lax.ppermute(value, 'row', pairs)  7.45 us
    all_to_all x2, starting transfers between devices, shards(): lax.all_to_all(row_force, 'col', split_axis=0, concat_axis=0, tiled=True)  6.98 us
  transfers between devices with their start and end apart: 28, of which 11 were waited for; matrix products, arithmetic and copies ran while one was open for 2% of the time, Pallas kernels for 8%

profile of v4, /device:TPU:0, one launch (start us, length us, event | category | flops | bytes accessed | tf_op | source)
XLA Modules:
  0.0 119.8 jit_solution(9366082908538879481)
XLA Ops:
  1.6 5.1 %collective-permute-start = (s32[32]{0:T(128)S(1)}, s32[32]{0:T(128)S(1)}, u32[]{:S(2)}, u32[]{:S(2)}) collective-permute-start(s32[32]{0:T(128)S(1)} %reshape.19.seeds), channel_id=1, source_target_pairs={{8,0},{16,8},{24,16},{0,24},{9,1},{17,9},{25,17},{1,25},{10,2},{18... | collective-permute-start | bytes 392 | tf_op jit(solution)/shard_map/ppermute | solution.py:425
  6.6 2.1 %multiply_reduce_fusion = (f32[256]{0:T(256)S(1)}, f32[280,768]{1,0:T(8,128)}) fusion(f32[256,768]{1,0:T(8,128)} %rest_0_.3), kind=kLoop, calls=%fused_computation | loop fusion | flops 392959 | bytes 1573888 | tf_op jit(solution)/shard_map/reduce_sum | solution.py:454
  8.8 2.3 %collective-permute-done.1 = s32[32]{0:T(128)S(1)} collective-permute-done((s32[32]{0:T(128)S(1)}, s32[32]{0:T(128)S(1)}, u32[]{:S(2)}, u32[]{:S(2)}) %collective-permute-start.1) | collective-permute-done | bytes 160 | tf_op jit(solution)/shard_map/ppermute | solution.py:425
  11.7 0.9 collective-permute-start.2
  12.6 1.5 %collective-permute-start.4 = (f32[256,768]{1,0:T(8,128)S(1)}, f32[256,768]{1,0:T(8,128)S(1)}, u32[]{:S(2)}, u32[]{:S(2)}) collective-permute-start(f32[256,768]{1,0:T(8,128)S(1)} %copy-done), channel_id=1, source_target_pairs={{2,0},{3,1},{0,2},{1,3},{6,4},{7,5},{4,6},{5,7},{10,8},{11,9},{8,1... | collective-permute-start | bytes 2359304 | tf_op jit(solution)/shard_map/ppermute | solution.py:438
  14.1 1.5 %collective-permute-start.5 = (f32[256,768]{1,0:T(8,128)S(1)}, f32[256,768]{1,0:T(8,128)}, u32[]{:S(2)}, u32[]{:S(2)}) collective-permute-start(f32[256,768]{1,0:T(8,128)S(1)} %copy-done), channel_id=1, source_target_pairs={{4,0},{5,1},{6,2},{7,3},{0,4},{1,5},{2,6},{3,7},{12,8},{13,9},{14,... | collective-permute-start | bytes 2359304 | tf_op jit(solution)/shard_map/ppermute | solution.py:438
  15.6 14.8 %collective-permute-done.4.rest_3_ = f32[256,768]{1,0:T(8,128)S(1)} collective-permute-done((f32[256,768]{1,0:T(8,128)S(1)}, f32[256,768]{1,0:T(8,128)S(1)}, u32[]{:S(2)}, u32[]{:S(2)}) %collective-permute-start.4) | collective-permute-done | bytes 786464 | tf_op jit(solution)/shard_map/ppermute | solution.py:438
  30.5 1.3 %collective-permute-done.5.rest_5_ = f32[256,768]{1,0:T(8,128)} collective-permute-done((f32[256,768]{1,0:T(8,128)S(1)}, f32[256,768]{1,0:T(8,128)}, u32[]{:S(2)}, u32[]{:S(2)}) %collective-permute-start.5) | collective-permute-done | bytes 786464 | tf_op jit(solution)/shard_map/ppermute | solution.py:438
  32.3 2.0 %collective-permute-start.9 = (f32[256,768]{1,0:T(8,128)S(1)}, f32[256,768]{1,0:T(8,128)S(1)}, u32[]{:S(2)}, u32[]{:S(2)}) collective-permute-start(f32[256,768]{1,0:T(8,128)S(1)} %copy-done), channel_id=1, source_target_pairs={{6,0},{7,1},{4,2},{5,3},{2,4},{3,5},{0,6},{1,7},{14,8},{15,9},{12,... | collective-permute-start | bytes 2359304 | tf_op jit(solution)/shard_map/ppermute | solution.py:438
  35.4 1.3 %collective-permute-start.8 = (f32[280,768]{1,0:T(8,128)}, f32[280,768]{1,0:T(8,128)S(1)}, u32[]{:S(2)}, u32[]{:S(2)}) collective-permute-start(f32[280,768]{1,0:T(8,128)} %constant_dynamic-update-slice_fusion), channel_id=1, source_target_pairs={{16,0},{8,24},{17,1},{9,25},{18,2},{10,26},{19,3},{11,27},{20,4},{... | collective-permute-start | bytes 2580488 | tf_op jit(solution)/shard_map/ppermute | solution.py:430
  36.8 1.0 collective-permute-start.12
  37.7 1.5 %collective-permute-start.11 = (f32[72,256]{1,0:T(8,128)S(1)}, f32[72,256]{1,0:T(8,128)S(1)}, u32[]{:S(2)}, u32[]{:S(2)}) collective-permute-start(f32[72,256]{1,0:T(8,128)S(1)} %concatenate.24.rest_5_), channel_id=1, source_target_pairs={{4,0},{5,1},{6,2},{7,3},{0,4},{1,5},{2,6},{3,7},{12,8},{13,9},{14,... | collective-permute-start | bytes 221192 | tf_op jit(solution)/shard_map/ppermute | solution.py:438
  39.3 1.1 collective-permute-start.10
  40.3 5.3 %grams.1 = (f32[6,2,128,128]{3,2,1,0:T(8,128)S(1)}, bf16[2,256,768]{2,1,0:T(8,128)(2,1)S(1)}, bf16[2,256,768]{2,1,0:T(8,128)(2,1)S(1)}, bf16[6,128,768]{2,1,0:T(8,128)(2,1)S(1)}, bf16[6,128,768]{2,1,0:T(8,128)(2,1)S(1)}) custom-call(s32[11]{0:T(128)S(1)} %pad_add_fusion.meta, s32[64]{0:T(128)S(1)} %reshape.16.listing, f32[256,768]{1,0:T(8,128)S(1)} %copy-done, ...), custom_call_target="tpu_custom_call" | custom-call | flops 905969664 | bytes 6291456 | tf_op jit(solution)/shard_map/grams/pallas_call | solution.py:106
  45.6 9.5 %collective-permute-done.12 = f32[72,256]{1,0:T(8,128)S(1)} collective-permute-done((f32[72,256]{1,0:T(8,128)S(1)}, f32[72,256]{1,0:T(8,128)S(1)}, u32[]{:S(2)}, u32[]{:S(2)}) %collective-permute-start.12) | collective-permute-done | bytes 73760 | tf_op jit(solution)/shard_map/ppermute | solution.py:438
  56.0 1.2 collective-permute-start.15
  57.2 2.0 %collective-permute-start.16 = (f32[64,256]{1,0:T(8,128)S(1)}, f32[64,256]{1,0:T(8,128)S(1)}, u32[]{:S(2)}, u32[]{:S(2)}) collective-permute-start(f32[64,256]{1,0:T(8,128)S(1)} %copy-done.1), channel_id=1, source_target_pairs={{24,0},{0,8},{8,16},{16,24},{25,1},{1,9},{9,17},{17,25},{26,2},{2,... | collective-permute-start | bytes 196616 | tf_op jit(solution)/shard_map/ppermute | solution.py:425
  59.2 1.5 %collective-permute-done.14.rest_7_.rest_1_ = f32[4,72,256]{2,1,0:T(8,128)S(1)} collective-permute-done((f32[4,72,256]{2,1,0:T(8,128)S(1)}, f32[4,72,256]{2,1,0:T(8,128)S(1)}, u32[]{:S(2)}, u32[]{:S(2)}) %collective-permute-start.14) | collective-permute-done | bytes 294944 | tf_op jit(solution)/shard_map/ppermute | solution.py:438
  60.8 4.5 %weights.1 = bf16[24,128,128]{2,1,0:T(8,128)(2,1)S(1)} custom-call(s32[11]{0:T(128)S(1)} %pad_add_fusion.meta, s32[64]{0:T(128)S(1)} %reshape.16.listing, s32[32]{0:T(128)S(1)} %reshape.19.seeds, f32[6,2,128,128]{3,2,1,0:T(8,128)S(1)} %get-tuple-element.30.grams, bf16[2,256,768]{2,1,0:T(8,128)(2,1)S(1)} %get-tuple-element.31.high_c, ...), custom_call_target="tpu_custom_call" | custom-call | flops 905969664 | bytes 3932160 | tf_op jit(solution)/shard_map/weights/pallas_call | solution.py:218
  65.3 5.7 %forces.2 = (f32[8,64,256]{2,1,0:T(8,128)}, f32[64,256]{1,0:T(8,128)S(1)}, f32[64,256]{1,0:T(8,128)S(1)}, f32[64,256]{1,0:T(8,128)S(1)}, f32[64,256]{1,0:T(8,128)S(1)}) custom-call(s32[11]{0:T(128)S(1)} %pad_add_fusion.meta, s32[64]{0:T(128)S(1)} %reshape.16.listing, s32[48]{0:T(128)S(1)} %bitcast.22, s32[48]{0:T(128)S(1)} %bitcast.24, ...), custom_call_target="tpu_custom_call" | custom-call | flops 1744830464 | bytes 1572864 | tf_op jit(solution)/shard_map/forces/pallas_call | solution.py:386
  71.0 3.5 %all-to-all-start = ((f32[8,64,256]{2,1,0:T(8,128)}), f32[8,64,256]{2,1,0:T(8,128)S(1)}, u32[]{:S(2)}, u32[]{:S(2)}) async-start(f32[8,64,256]{2,1,0:T(8,128)} %get-tuple-element.40), calls=%async_computation | async-start | bytes 1048576 | tf_op jit(solution)/shard_map/all_to_all | solution.py:511
  74.5 2.9 %collective-permute-start.19 = (f32[64,256]{1,0:T(8,128)S(1)}, f32[64,256]{1,0:T(8,128)S(1)}, u32[]{:S(2)}, u32[]{:S(2)}) collective-permute-start(f32[64,256]{1,0:T(8,128)S(1)} %get-tuple-element.44), channel_id=1, source_target_pairs={{0,24},{8,0},{16,8},{24,16},{1,25},{9,1},{17,9},{25,17},{2,26},{10... | collective-permute-start | bytes 196616 | tf_op jit(solution)/shard_map/ppermute | solution.py:434
  78.0 6.2 %all-to-all-done = f32[8,64,256]{2,1,0:T(8,128)S(1)} async-done(((f32[8,64,256]{2,1,0:T(8,128)}), f32[8,64,256]{2,1,0:T(8,128)S(1)}, u32[]{:S(2)}, u32[]{:S(2)}) %all-to-all-start) | async-done | bytes 524320 | tf_op jit(solution)/shard_map/all_to_all | solution.py:511
  84.5 2.7 %collective-permute-start.20 = (f32[64,256]{1,0:T(8,128)S(1)}, f32[64,256]{1,0:T(8,128)S(1)}, u32[]{:S(2)}, u32[]{:S(2)}) collective-permute-start(f32[64,256]{1,0:T(8,128)S(1)} %multiply_add_fusion.1.rest_1_), channel_id=1, source_target_pairs={{8,0},{16,8},{24,16},{0,24},{9,1},{17,9},{25,17},{1,25},{10,2},{18... | collective-permute-start | bytes 196616 | tf_op jit(solution)/shard_map/ppermute | solution.py:425
  87.2 0.9 collective-permute-start.22
  88.1 10.3 %all-gather = f32[512,256]{1,0:T(8,128)S(1)} all-gather(f32[64,256]{1,0:T(8,128)S(1)} %multiply_add_fusion.1.rest_1_), channel_id=2, replica_groups=mesh['row'=4,'col'=8] {'col'}, dimensions={0}, use_global_device_ids=true | all-gather | bytes 589824 | tf_op jit(solution)/shard_map/all_gather | solution.py:508
  98.4 5.6 %forces.3 = (f32[8,64,256]{2,1,0:T(8,128)}, f32[64,256]{1,0:T(8,128)S(1)}, f32[64,256]{1,0:T(8,128)S(1)}, f32[64,256]{1,0:T(8,128)S(1)}, f32[64,256]{1,0:T(8,128)S(1)}) custom-call(s32[11]{0:T(128)S(1)} %pad_add_fusion.meta, s32[64]{0:T(128)S(1)} %reshape.16.listing, s32[48]{0:T(128)S(1)} %bitcast.23, s32[48]{0:T(128)S(1)} %bitcast.25, ...), custom_call_target="tpu_custom_call" | custom-call | flops 1744830464 | bytes 1572864 | tf_op jit(solution)/shard_map/forces/pallas_call | solution.py:386
  104.1 3.5 %all-to-all-start.1 = ((f32[8,64,256]{2,1,0:T(8,128)}), f32[8,64,256]{2,1,0:T(8,128)S(1)}, u32[]{:S(2)}, u32[]{:S(2)}) async-start(f32[8,64,256]{2,1,0:T(8,128)} %get-tuple-element.45), calls=%async_computation.1 | async-start | bytes 1048576 | tf_op jit(solution)/shard_map/all_to_all | solution.py:511
  107.6 1.9 %collective-permute-start.25 = (f32[64,256]{1,0:T(8,128)S(1)}, f32[64,256]{1,0:T(8,128)S(1)}, u32[]{:S(2)}, u32[]{:S(2)}) collective-permute-start(f32[64,256]{1,0:T(8,128)S(1)} %get-tuple-element.49), channel_id=1, source_target_pairs={{0,24},{8,0},{16,8},{24,16},{1,25},{9,1},{17,9},{25,17},{2,26},{10... | collective-permute-start | bytes 196616 | tf_op jit(solution)/shard_map/ppermute | solution.py:434
  109.5 2.0 %collective-permute-start.24 = (f32[64,256]{1,0:T(8,128)S(1)}, f32[64,256]{1,0:T(8,128)S(1)}, u32[]{:S(2)}, u32[]{:S(2)}) collective-permute-start(f32[64,256]{1,0:T(8,128)S(1)} %get-tuple-element.48), channel_id=1, source_target_pairs={{0,16},{8,24},{16,0},{24,8},{1,17},{9,25},{17,1},{25,9},{2,18},{10... | collective-permute-start | bytes 196616 | tf_op jit(solution)/shard_map/ppermute | solution.py:434
  111.5 5.7 %all-to-all-done.1 = f32[8,64,256]{2,1,0:T(8,128)S(1)} async-done(((f32[8,64,256]{2,1,0:T(8,128)}), f32[8,64,256]{2,1,0:T(8,128)S(1)}, u32[]{:S(2)}, u32[]{:S(2)}) %all-to-all-start.1) | async-done | bytes 524320 | tf_op jit(solution)/shard_map/all_to_all | solution.py:511
  117.3 1.2 collective-permute-done.24
  (69 shorter events, 5.8 us)
Async XLA Ops:
  0.6 12.0 %copy-start = (f32[256,768]{1,0:T(8,128)S(1)}, f32[256,768]{1,0:T(8,128)}, u32[]{:S(2)}) copy-start(f32[256,768]{1,0:T(8,128)} %rest_0_.3) | copy-start | bytes 2359300
  0.7 8.1 %copy-start.4 = (f32[256]{0:T(256)S(1)}, f32[256]{0:T(256)}, u32[]{:S(2)}) copy-start(f32[256]{0:T(256)} %param.11) | copy-start | bytes 3076
  0.7 8.1 %copy-start.5 = (f32[256]{0:T(256)S(1)}, f32[256]{0:T(256)}, u32[]{:S(2)}) copy-start(f32[256]{0:T(256)} %param.12) | copy-start | bytes 3076
  0.7 34.4 %copy-start.6 = (s32[1,1,8,4,2]{2,4,3,1,0:T(2,128)S(1)}, s32[1,1,8,4,2]{2,4,3,1,0:T(2,128)}, u32[]{:S(2)}) copy-start(s32[1,1,8,4,2]{2,4,3,1,0:T(2,128)} %param.14) | copy-start | bytes 772
  1.6 7.2 %collective-permute-start = (s32[32]{0:T(128)S(1)}, s32[32]{0:T(128)S(1)}, u32[]{:S(2)}, u32[]{:S(2)}) collective-permute-start(s32[32]{0:T(128)S(1)} %reshape.19.seeds), channel_id=1, source_target_pairs={{8,0},{16,8},{24,16},{0,24},{9,1},{17,9},{25,17},{1,25},{10,2},{18... | collective-permute-start | bytes 392 | tf_op jit(solution)/shard_map/ppermute | solution.py:425
  6.6 4.4 %collective-permute-start.1 = (s32[32]{0:T(128)S(1)}, s32[32]{0:T(128)S(1)}, u32[]{:S(2)}, u32[]{:S(2)}) collective-permute-start(s32[32]{0:T(128)S(1)} %reshape.19.seeds), channel_id=1, source_target_pairs={{16,0},{24,8},{0,16},{8,24},{17,1},{25,9},{1,17},{9,25},{18,2},{26... | collective-permute-start | bytes 392 | tf_op jit(solution)/shard_map/ppermute | solution.py:425
  11.7 20.1 %collective-permute-start.2 = (f32[280,768]{1,0:T(8,128)}, f32[280,768]{1,0:T(8,128)S(1)}, u32[]{:S(2)}, u32[]{:S(2)}) collective-permute-start(f32[280,768]{1,0:T(8,128)} %constant_dynamic-update-slice_fusion), channel_id=1, source_target_pairs={{8,0},{16,8},{24,16},{0,24},{9,1},{17,9},{25,17},{1,25},{10,2},{18... | collective-permute-start | bytes 2580488 | tf_op jit(solution)/shard_map/ppermute | solution.py:425
  12.6 17.9 %collective-permute-start.4 = (f32[256,768]{1,0:T(8,128)S(1)}, f32[256,768]{1,0:T(8,128)S(1)}, u32[]{:S(2)}, u32[]{:S(2)}) collective-permute-start(f32[256,768]{1,0:T(8,128)S(1)} %copy-done), channel_id=1, source_target_pairs={{2,0},{3,1},{0,2},{1,3},{6,4},{7,5},{4,6},{5,7},{10,8},{11,9},{8,1... | collective-permute-start | bytes 2359304 | tf_op jit(solution)/shard_map/ppermute | solution.py:438
  14.1 17.7 %collective-permute-start.5 = (f32[256,768]{1,0:T(8,128)S(1)}, f32[256,768]{1,0:T(8,128)}, u32[]{:S(2)}, u32[]{:S(2)}) collective-permute-start(f32[256,768]{1,0:T(8,128)S(1)} %copy-done), channel_id=1, source_target_pairs={{4,0},{5,1},{6,2},{7,3},{0,4},{1,5},{2,6},{3,7},{12,8},{13,9},{14,... | collective-permute-start | bytes 2359304 | tf_op jit(solution)/shard_map/ppermute | solution.py:438
  15.6 19.8 %collective-permute-start.3 = (f32[256,768]{1,0:T(8,128)S(1)}, f32[256,768]{1,0:T(8,128)}, u32[]{:S(2)}, u32[]{:S(2)}) collective-permute-start(f32[256,768]{1,0:T(8,128)S(1)} %copy-done), channel_id=1, source_target_pairs={{1,0},{0,1},{3,2},{2,3},{5,4},{4,5},{7,6},{6,7},{9,8},{8,9},{11,10... | collective-permute-start | bytes 2359304 | tf_op jit(solution)/shard_map/ppermute | solution.py:438
  31.8 4.9 %collective-permute-start.6 = (f32[256,768]{1,0:T(8,128)S(1)}, f32[256,768]{1,0:T(8,128)}, u32[]{:S(2)}, u32[]{:S(2)}) collective-permute-start(f32[256,768]{1,0:T(8,128)S(1)} %collective-permute-done.4.rest_3_), channel_id=1, source_target_pairs={{1,0},{0,1},{3,2},{2,3},{5,4},{4,5},{7,6},{6,7},{9,8},{8,9},{11,10... | collective-permute-start | bytes 2359304 | tf_op jit(solution)/shard_map/ppermute | solution.py:438
  31.8 5.0 %collective-permute-start.7 = (f32[256,768]{1,0:T(8,128)}, f32[256,768]{1,0:T(8,128)}, u32[]{:S(2)}, u32[]{:S(2)}) collective-permute-start(f32[256,768]{1,0:T(8,128)} %collective-permute-done.5.rest_5_), channel_id=1, source_target_pairs={{1,0},{0,1},{3,2},{2,3},{5,4},{4,5},{7,6},{6,7},{9,8},{8,9},{11,10... | collective-permute-start | bytes 2359304 | tf_op jit(solution)/shard_map/ppermute | solution.py:438
  32.3 23.6 %collective-permute-start.9 = (f32[256,768]{1,0:T(8,128)S(1)}, f32[256,768]{1,0:T(8,128)S(1)}, u32[]{:S(2)}, u32[]{:S(2)}) collective-permute-start(f32[256,768]{1,0:T(8,128)S(1)} %copy-done), channel_id=1, source_target_pairs={{6,0},{7,1},{4,2},{5,3},{2,4},{3,5},{0,6},{1,7},{14,8},{15,9},{12,... | collective-permute-start | bytes 2359304 | tf_op jit(solution)/shard_map/ppermute | solution.py:438
  35.4 23.8 %collective-permute-start.8 = (f32[280,768]{1,0:T(8,128)}, f32[280,768]{1,0:T(8,128)S(1)}, u32[]{:S(2)}, u32[]{:S(2)}) collective-permute-start(f32[280,768]{1,0:T(8,128)} %constant_dynamic-update-slice_fusion), channel_id=1, source_target_pairs={{16,0},{8,24},{17,1},{9,25},{18,2},{10,26},{19,3},{11,27},{20,4},{... | collective-permute-start | bytes 2580488 | tf_op jit(solution)/shard_map/ppermute | solution.py:430
  36.8 18.3 %collective-permute-start.12 = (f32[72,256]{1,0:T(8,128)S(1)}, f32[72,256]{1,0:T(8,128)S(1)}, u32[]{:S(2)}, u32[]{:S(2)}) collective-permute-start(f32[72,256]{1,0:T(8,128)S(1)} %concatenate.24.rest_5_), channel_id=1, source_target_pairs={{6,0},{7,1},{4,2},{5,3},{2,4},{3,5},{0,6},{1,7},{14,8},{15,9},{12,... | collective-permute-start | bytes 221192 | tf_op jit(solution)/shard_map/ppermute | solution.py:438
  37.7 18.1 %collective-permute-start.11 = (f32[72,256]{1,0:T(8,128)S(1)}, f32[72,256]{1,0:T(8,128)S(1)}, u32[]{:S(2)}, u32[]{:S(2)}) collective-permute-start(f32[72,256]{1,0:T(8,128)S(1)} %concatenate.24.rest_5_), channel_id=1, source_target_pairs={{4,0},{5,1},{6,2},{7,3},{0,4},{1,5},{2,6},{3,7},{12,8},{13,9},{14,... | collective-permute-start | bytes 221192 | tf_op jit(solution)/shard_map/ppermute | solution.py:438
  39.3 16.7 %collective-permute-start.10 = (f32[72,256]{1,0:T(8,128)S(1)}, f32[72,256]{1,0:T(8,128)S(1)}, u32[]{:S(2)}, u32[]{:S(2)}) collective-permute-start(f32[72,256]{1,0:T(8,128)S(1)} %concatenate.24.rest_5_), channel_id=1, source_target_pairs={{2,0},{3,1},{0,2},{1,3},{6,4},{7,5},{4,6},{5,7},{10,8},{11,9},{8,1... | collective-permute-start | bytes 221192 | tf_op jit(solution)/shard_map/ppermute | solution.py:438
  55.9 4.8 %collective-permute-start.13 = (f32[256,768]{1,0:T(8,128)S(1)}, f32[256,768]{1,0:T(8,128)S(1)}, u32[]{:S(2)}, u32[]{:S(2)}) collective-permute-start(f32[256,768]{1,0:T(8,128)S(1)} %collective-permute-done.9.rest_3_), channel_id=1, source_target_pairs={{1,0},{0,1},{3,2},{2,3},{5,4},{4,5},{7,6},{6,7},{9,8},{8,9},{11,10... | collective-permute-start | bytes 2359304 | tf_op jit(solution)/shard_map/ppermute | solution.py:438
  56.0 9.2 %collective-permute-start.15 = (f32[64,256]{1,0:T(8,128)S(1)}, f32[64,256]{1,0:T(8,128)S(1)}, u32[]{:S(2)}, u32[]{:S(2)}) collective-permute-start(f32[64,256]{1,0:T(8,128)S(1)} %copy-done.1), channel_id=1, source_target_pairs={{16,0},{24,8},{0,16},{8,24},{17,1},{25,9},{1,17},{9,25},{18,2},{26... | collective-permute-start | bytes 196616 | tf_op jit(solution)/shard_map/ppermute | solution.py:425
  57.2 8.1 %collective-permute-start.16 = (f32[64,256]{1,0:T(8,128)S(1)}, f32[64,256]{1,0:T(8,128)S(1)}, u32[]{:S(2)}, u32[]{:S(2)}) collective-permute-start(f32[64,256]{1,0:T(8,128)S(1)} %copy-done.1), channel_id=1, source_target_pairs={{24,0},{0,8},{8,16},{16,24},{25,1},{1,9},{9,17},{17,25},{26,2},{2,... | collective-permute-start | bytes 196616 | tf_op jit(solution)/shard_map/ppermute | solution.py:425
  59.2 1.6 %collective-permute-start.14 = (f32[4,72,256]{2,1,0:T(8,128)S(1)}, f32[4,72,256]{2,1,0:T(8,128)S(1)}, u32[]{:S(2)}, u32[]{:S(2)}) collective-permute-start(f32[4,72,256]{2,1,0:T(8,128)S(1)} %pad_maximum_fusion.rest_6_.rest_0_), channel_id=1, source_target_pairs={{1,0},{0,1},{3,2},{2,3},{5,4},{4,5},{7,6},{6,7},{9,8},{8,9},{11,10... | collective-permute-start | bytes 884744 | tf_op jit(solution)/shard_map/ppermute | solution.py:438
  71.0 13.2 %all-to-all-start = ((f32[8,64,256]{2,1,0:T(8,128)}), f32[8,64,256]{2,1,0:T(8,128)S(1)}, u32[]{:S(2)}, u32[]{:S(2)}) async-start(f32[8,64,256]{2,1,0:T(8,128)} %get-tuple-element.40), calls=%async_computation | async-start | bytes 1048576 | tf_op jit(solution)/shard_map/all_to_all | solution.py:511
  74.5 9.7 %collective-permute-start.19 = (f32[64,256]{1,0:T(8,128)S(1)}, f32[64,256]{1,0:T(8,128)S(1)}, u32[]{:S(2)}, u32[]{:S(2)}) collective-permute-start(f32[64,256]{1,0:T(8,128)S(1)} %get-tuple-element.44), channel_id=1, source_target_pairs={{0,24},{8,0},{16,8},{24,16},{1,25},{9,1},{17,9},{25,17},{2,26},{10... | collective-permute-start | bytes 196616 | tf_op jit(solution)/shard_map/ppermute | solution.py:434
  77.4 7.0 %collective-permute-start.18 = (f32[64,256]{1,0:T(8,128)S(1)}, f32[64,256]{1,0:T(8,128)S(1)}, u32[]{:S(2)}, u32[]{:S(2)}) collective-permute-start(f32[64,256]{1,0:T(8,128)S(1)} %get-tuple-element.43), channel_id=1, source_target_pairs={{0,16},{8,24},{16,0},{24,8},{1,17},{9,25},{17,1},{25,9},{2,18},{10... | collective-permute-start | bytes 196616 | tf_op jit(solution)/shard_map/ppermute | solution.py:434
  77.4 7.0 %collective-permute-start.17 = (f32[64,256]{1,0:T(8,128)S(1)}, f32[64,256]{1,0:T(8,128)S(1)}, u32[]{:S(2)}, u32[]{:S(2)}) collective-permute-start(f32[64,256]{1,0:T(8,128)S(1)} %get-tuple-element.42), channel_id=1, source_target_pairs={{0,8},{8,16},{16,24},{24,0},{1,9},{9,17},{17,25},{25,1},{2,10},{10... | collective-permute-start | bytes 196616 | tf_op jit(solution)/shard_map/ppermute | solution.py:434
  84.5 13.9 %collective-permute-start.20 = (f32[64,256]{1,0:T(8,128)S(1)}, f32[64,256]{1,0:T(8,128)S(1)}, u32[]{:S(2)}, u32[]{:S(2)}) collective-permute-start(f32[64,256]{1,0:T(8,128)S(1)} %multiply_add_fusion.1.rest_1_), channel_id=1, source_target_pairs={{8,0},{16,8},{24,16},{0,24},{9,1},{17,9},{25,17},{1,25},{10,2},{18... | collective-permute-start | bytes 196616 | tf_op jit(solution)/shard_map/ppermute | solution.py:425
  87.2 11.2 %collective-permute-start.21 = (f32[64,256]{1,0:T(8,128)S(1)}, f32[64,256]{1,0:T(8,128)S(1)}, u32[]{:S(2)}, u32[]{:S(2)}) collective-permute-start(f32[64,256]{1,0:T(8,128)S(1)} %multiply_add_fusion.1.rest_1_), channel_id=1, source_target_pairs={{16,0},{24,8},{0,16},{8,24},{17,1},{25,9},{1,17},{9,25},{18,2},{26... | collective-permute-start | bytes 196616 | tf_op jit(solution)/shard_map/ppermute | solution.py:425
  87.2 11.2 %collective-permute-start.22 = (f32[64,256]{1,0:T(8,128)S(1)}, f32[64,256]{1,0:T(8,128)S(1)}, u32[]{:S(2)}, u32[]{:S(2)}) collective-permute-start(f32[64,256]{1,0:T(8,128)S(1)} %multiply_add_fusion.1.rest_1_), channel_id=1, source_target_pairs={{24,0},{0,8},{8,16},{16,24},{25,1},{1,9},{9,17},{17,25},{26,2},{2,... | collective-permute-start | bytes 196616 | tf_op jit(solution)/shard_map/ppermute | solution.py:425
  104.1 13.2 %all-to-all-start.1 = ((f32[8,64,256]{2,1,0:T(8,128)}), f32[8,64,256]{2,1,0:T(8,128)S(1)}, u32[]{:S(2)}, u32[]{:S(2)}) async-start(f32[8,64,256]{2,1,0:T(8,128)} %get-tuple-element.45), calls=%async_computation.1 | async-start | bytes 1048576 | tf_op jit(solution)/shard_map/all_to_all | solution.py:511
  107.6 9.7 %collective-permute-start.25 = (f32[64,256]{1,0:T(8,128)S(1)}, f32[64,256]{1,0:T(8,128)S(1)}, u32[]{:S(2)}, u32[]{:S(2)}) collective-permute-start(f32[64,256]{1,0:T(8,128)S(1)} %get-tuple-element.49), channel_id=1, source_target_pairs={{0,24},{8,0},{16,8},{24,16},{1,25},{9,1},{17,9},{25,17},{2,26},{10... | collective-permute-start | bytes 196616 | tf_op jit(solution)/shard_map/ppermute | solution.py:434
  109.5 9.0 %collective-permute-start.24 = (f32[64,256]{1,0:T(8,128)S(1)}, f32[64,256]{1,0:T(8,128)S(1)}, u32[]{:S(2)}, u32[]{:S(2)}) collective-permute-start(f32[64,256]{1,0:T(8,128)S(1)} %get-tuple-element.48), channel_id=1, source_target_pairs={{0,16},{8,24},{16,0},{24,8},{1,17},{9,25},{17,1},{25,9},{2,18},{10... | collective-permute-start | bytes 196616 | tf_op jit(solution)/shard_map/ppermute | solution.py:434
  111.5 7.0 %collective-permute-start.23 = (f32[64,256]{1,0:T(8,128)S(1)}, f32[64,256]{1,0:T(8,128)S(1)}, u32[]{:S(2)}, u32[]{:S(2)}) collective-permute-start(f32[64,256]{1,0:T(8,128)S(1)} %get-tuple-element.47), channel_id=1, source_target_pairs={{0,8},{8,16},{16,24},{24,0},{1,9},{9,17},{17,25},{25,1},{2,10},{10... | collective-permute-start | bytes 196616 | tf_op jit(solution)/shard_map/ppermute | solution.py:434
  (3 other events, 17.1 us)

commit v5 on v4

--- a/solution.py
+++ b/solution.py
@@ -78,7 +78,7 @@
     columns, rows = rest[:shifts_early], rest[shifts_early : shifts_early + rows_early - 1]
     grams, high_c, low_c, high_last, low_last, high_r, low_r = rest[shifts_early + rows_early - 1 :]
     for shift in range(shifts_early):
-        high_c[shift], low_c[shift] = split(columns[shift][:SPAN])
+        high_c[shift], low_c[shift] = split(columns[shift][...])
     high_r[0], low_r[0] = high_c[0], low_c[0]
     for line in range(1, rows_early):
         high_r[line], low_r[line] = split(rows[line - 1][...])
@@ -129,20 +129,16 @@
     row_count, col_count = sizes
     shifts_early, rows_early = counts
     shifts, rows_late = shifts_early + 1, col_count - rows_early
-    columns, late, packs = rest[:shifts], rest[shifts : shifts + rows_late], rest[shifts + rows_late :][:3]
-    out, high_l, low_l, high_r, low_r, late_grams, col_params, row_params = rest[shifts + rows_late + 3 :]
-    own_pack, even_packs, odd_packs = packs
+    last, late, col_packs = rest[0], rest[1 : 1 + rows_late], rest[1 + rows_late :][:shifts]
+    even_packs, odd_packs = rest[1 + rows_late + shifts :][:2]
+    out, high_l, low_l, high_r, low_r, late_grams, col_params, row_params = rest[3 + rows_late + shifts :]
     row, col = meta[0], meta[1]
 
-    high_l[...], low_l[...] = split(columns[shifts_early][:SPAN])
+    high_l[...], low_l[...] = split(last[...])
     for shift in range(shifts):
         for block in range(CB):
             lanes = slice(block * BLK, (block + 1) * BLK)
-            if shift == 0:
-                params = own_pack[RHO : RHO + 8, lanes]
-            else:
-                params = columns[shift][SPAN + 16 : SPAN + 24, 2 * SPAN :][:, lanes]
-            col_params[shift, block] = params.T
+            col_params[shift, block] = col_packs[shift][RHO : RHO + 8, lanes].T
     for bits in range(col_count):
         row_params[bits] = (even_packs, odd_packs)[bits % 2][bits // 2, RHO : RHO + 8, :]
     for line in range(rows_late):
@@ -208,16 +204,16 @@
     each(rows_late, late_rows)
 
 
-def pair_weights(sizes, meta, listing, seeds, early, columns, late, packs):
+def pair_weights(sizes, meta, listing, seeds, early, last, late, packs):
     _, col_count = sizes
-    shifts, depth = len(columns), late[0].shape[-1]
+    shifts, depth = len(packs) - 2, late[0].shape[-1]
     rows_late = len(late)
     smem = pl.BlockSpec(memory_space=pltpu.SMEM)
     vmem = pl.BlockSpec(memory_space=pltpu.VMEM)
     tiles = shifts * col_count
     return pl.pallas_call(
         functools.partial(weights_kernel, sizes, (shifts - 1, col_count - rows_late)),
-        in_specs=[smem] * 3 + [vmem] * (5 + shifts + rows_late + 3),
+        in_specs=[smem] * 3 + [vmem] * (5 + 1 + rows_late + len(packs)),
         out_specs=vmem,
         out_shape=jax.ShapeDtypeStruct((tiles, BLK, BLK), BF16),
         scratch_shapes=[
@@ -232,11 +228,11 @@
         compiler_params=pltpu.CompilerParams(vmem_limit_bytes=VMEM_LIMIT),
         cost_estimate=pl.CostEstimate(
             flops=tiles * 3 * BLK * BLK * depth,
-            bytes_accessed=(shifts + rows_late) * SPAN * depth * 4,
+            bytes_accessed=(1 + rows_late) * SPAN * depth * 4,
             transcendentals=tiles * 3 * BLK * BLK,
         ),
         name="weights",
-    )(meta, listing, seeds, *early, *columns, *late, *packs)
+    )(meta, listing, seeds, *early, last, *late, *packs)
 
 
 def force_kernel(row_count, col_count, by_bits, meta, listing, neg_rows, neg_cols, weights, *rest):
@@ -449,47 +445,33 @@
     row_x = {0: inputs}
     for bits in single:
         row_x[bits] = from_bits(inputs, bits)
-    far_seeds = [from_shift(seeds, shift) for shift in range(1, shifts)]
-
-    squares = jnp.sum(inputs * inputs, axis=1)
-    params = jnp.stack([rho, sigma, squares])
-    pack = jnp.concatenate([embed, params, jnp.zeros((PACK - SEEDS, SPAN), F32)], axis=0)
-    third = PACK // 3
-    below = jnp.concatenate([pack[:third], pack[third : 2 * third], pack[2 * third :]], axis=1)
-    with_pack = jnp.concatenate([inputs, after(below, *far_seeds)], axis=0)
-    col_x = [inputs] + [from_shift(with_pack, shift) for shift in range(1, shifts - 1)]
+    col_x = [inputs] + [from_shift(inputs, shift) for shift in range(1, shifts - 1)]
+    near = [row_x[bits] for bits in single] + col_x[1:]
     for bits in late_bits:
         if bits % 2 == 0:
-            row_x[bits] = from_bits(after(inputs, with_pack), bits)
-    row_x[1] = from_bits(after(inputs, with_pack), 1)
-    near = [row_x[bits] for bits in single] + col_x[1:]
+            row_x[bits] = from_bits(inputs, bits)
+    far_seeds = [from_shift(seeds, shift) for shift in range(1, shifts)]
+    row_x[1] = from_bits(after(inputs, *far_seeds), 1)
     for bits in single:
         row_x[bits + 1] = from_bits(after(row_x[bits], *near), 1)
-    col_x.append(from_half(after(with_pack, row_x[1])))
-
+    col_x.append(from_half(after(inputs, row_x[1])))
+
+    squares = jnp.sum(inputs * inputs, axis=1)
     seed_rows = jnp.pad(
         jnp.stack([seeds, *far_seeds]).astype(F32), ((0, PACK - SEEDS - shifts), (0, SPAN - seeds.shape[0]))
     )
-    own_pack = jnp.concatenate([embed, params, seed_rows], axis=0)
+    own_pack = jnp.concatenate([embed, jnp.stack([rho, sigma, squares]), seed_rows], axis=0)
+    own_pack = after(own_pack, *[row_x[bits + 1] for bits in single])
     early = early_grams(sizes, meta, listing, col_x[:-1], [row_x[bits] for bits in early_bits[1:]])
-    own_pack = after(own_pack, *[row_x[bits + 1] for bits in single])
     even_packs = jnp.stack([own_pack] + [from_bits(own_pack, bits) for bits in range(2, col_count, 2)])
     even_packs = after(even_packs, early[0])
     odd_packs = from_bits(even_packs, 1)
     for bits in late_bits:
         if bits % 2 == 0:
             row_x[bits + 1] = from_bits(after(row_x[bits], even_packs), 1)
-
-    col_y = [embed]
-    for shift in range(1, shifts - 1):
-        packed = col_x[shift][SPAN:]
-        col_y.append(
-            jnp.concatenate(
-                [packed[:, :SPAN], packed[:, SPAN : 2 * SPAN], packed[: D_EMB - 2 * third, 2 * SPAN :]], axis=0
-            )
-        )
-    held = after(embed, *[row_x[bits] for bits in late_bits if bits % 2 == 0])
-    col_y += [from_shift(held, shift) for shift in range(shifts - 1, row_count)]
+    held = after(own_pack, *[row_x[bits] for bits in late_bits if bits % 2 == 0])
+    col_packs = [own_pack] + [from_shift(held, shift) for shift in range(1, row_count)]
+    col_y = col_packs
 
     weights = pair_weights(
         sizes,
@@ -497,9 +479,9 @@
         listing,
         seeds,
         early,
-        col_x,
+        col_x[-1],
         [row_x[bits] for bits in late_bits],
-        [own_pack, even_packs, odd_packs],
+        col_packs[:shifts] + [even_packs, odd_packs],
     )
 
     row_y = (even_packs, odd_packs)

time: 120 us -> 121 us (level)
  local copies, waits for them, and re-layouts: 1.94 us -> 3.4 us
    ppermute x11, waiting for transfers between devices: 28 us -> 11.1 us  [from_bits(): return lax.ppermute(value, 'col', pairs)]
    ppermute x8 -> x9, waiting for transfers between devices: 2.27 us -> 15 us  [from_shift(): return lax.ppermute(value, 'row', pairs)]
    ppermute x1, waiting for transfers between devices: 0.01 us -> 3.16 us  [from_half(): return lax.ppermute(value, 'row', pairs)]
    all_to_all x2, waiting for transfers between devices: 11.9 us -> 13.8 us  [shards(): lax.all_to_all(row_force, 'col', split_axis=0, concat_axis=0, tiled=True)]
    ppermute x6, starting transfers between devices: 7.45 us -> 5.65 us  [to_shift(): return lax.ppermute(value, 'row', pairs)]
    all_to_all x2, starting transfers between devices: 6.98 us -> 8.63 us  [shards(): lax.all_to_all(row_force, 'col', split_axis=0, concat_axis=0, tiled=True)]
    ppermute x6, waiting for transfers between devices: 1.38 us -> 0.02 us  [to_shift(): return lax.ppermute(value, 'row', pairs)]
    ppermute x8 -> x9, starting transfers between devices: 12.7 us -> 12.7 us  [from_shift(): return lax.ppermute(value, 'row', pairs)]
  transfers between devices with their start and end apart: 28 -> 29, of which waited for: 11 -> 10; matrix products, arithmetic and copies ran while one was open for 2% -> 4% of each run, Pallas kernels for 8% -> 9%
where the time goes in v5:
time: 121 us; the launch traced here: 120 us
  waiting for transfers between devices  43.1 us (36%)
  starting transfers between devices  37.4 us (31%)
  Pallas kernels  21.6 us (18%)
  blocking collectives  10.2 us (8%)
  local copies, waits for them, and re-layouts  3.4 us (3%)
  other arithmetic  2.78 us (2%)
  between operations  1.5 us (1%)
    ppermute x9, waiting for transfers between devices, from_shift(): return lax.ppermute(value, 'row', pairs)  15 us
    all_to_all x2, waiting for transfers between devices, shards(): lax.all_to_all(row_force, 'col', split_axis=0, concat_axis=0, tiled=True)  13.8 us
    ppermute x9, starting transfers between devices, from_shift(): return lax.ppermute(value, 'row', pairs)  12.7 us
    pallas_call x2, Pallas kernels, pair_forces(): pl.pallas_call(functools.partial(force_kernel, row_count, col_count, len(...  11.4 us
    ppermute x11, waiting for transfers between devices, from_bits(): return lax.ppermute(value, 'col', pairs)  11.1 us
    all_gather x1, blocking collectives, shards(): row_y = (lax.all_gather(embed, 'col', axis=0, tiled=False),)  10.2 us
    ppermute x11, starting transfers between devices, from_bits(): return lax.ppermute(value, 'col', pairs)  9.14 us
    all_to_all x2, starting transfers between devices, shards(): lax.all_to_all(row_force, 'col', split_axis=0, concat_axis=0, tiled=True)  8.63 us
  transfers between devices with their start and end apart: 29, of which 10 were waited for; matrix products, arithmetic and copies ran while one was open for 4% of the time, Pallas kernels for 9%

profile of v5, /device:TPU:0, one launch (start us, length us, event | category | flops | bytes accessed | tf_op | source)
XLA Modules:
  0.0 120.0 jit_solution(11982458072850366682)
XLA Ops:
  0.6 5.1 %collective-permute-start = (f32[256,768]{1,0:T(8,128)}, f32[256,768]{1,0:T(8,128)S(1)}, u32[]{:S(2)}, u32[]{:S(2)}) collective-permute-start(f32[256,768]{1,0:T(8,128)} %rest_0_.1), channel_id=1, source_target_pairs={{8,0},{16,8},{24,16},{0,24},{9,1},{17,9},{25,17},{1,25},{10,2},{18... | collective-permute-start | bytes 2359304 | tf_op jit(solution)/shard_map/ppermute | solution.py:421
  5.7 1.5 %collective-permute-start.4 = (f32[256,768]{1,0:T(8,128)}, f32[256,768]{1,0:T(8,128)S(1)}, u32[]{:S(2)}, u32[]{:S(2)}) collective-permute-start(f32[256,768]{1,0:T(8,128)} %rest_0_.1), channel_id=1, source_target_pairs={{2,0},{3,1},{0,2},{1,3},{6,4},{7,5},{4,6},{5,7},{10,8},{11,9},{8,1... | collective-permute-start | bytes 2359304 | tf_op jit(solution)/shard_map/ppermute | solution.py:434
  7.2 1.5 %collective-permute-start.5 = (f32[256,768]{1,0:T(8,128)}, f32[256,768]{1,0:T(8,128)S(1)}, u32[]{:S(2)}, u32[]{:S(2)}) collective-permute-start(f32[256,768]{1,0:T(8,128)} %rest_0_.1), channel_id=1, source_target_pairs={{4,0},{5,1},{6,2},{7,3},{0,4},{1,5},{2,6},{3,7},{12,8},{13,9},{14,... | collective-permute-start | bytes 2359304 | tf_op jit(solution)/shard_map/ppermute | solution.py:434
  10.0 12.8 %collective-permute-done.1 = s32[32]{0:T(128)S(1)} collective-permute-done((s32[32]{0:T(128)S(1)}, s32[32]{0:T(128)S(1)}, u32[]{:S(2)}, u32[]{:S(2)}) %collective-permute-start.1) | collective-permute-done | bytes 160 | tf_op jit(solution)/shard_map/ppermute | solution.py:421
  22.9 2.1 %collective-permute-done.4.rest_3_ = f32[256,768]{1,0:T(8,128)S(1)} collective-permute-done((f32[256,768]{1,0:T(8,128)}, f32[256,768]{1,0:T(8,128)S(1)}, u32[]{:S(2)}, u32[]{:S(2)}) %collective-permute-start.4) | collective-permute-done | bytes 786464 | tf_op jit(solution)/shard_map/ppermute | solution.py:434
  25.0 1.2 %collective-permute-done.5.rest_5_ = f32[256,768]{1,0:T(8,128)S(1)} collective-permute-done((f32[256,768]{1,0:T(8,128)}, f32[256,768]{1,0:T(8,128)S(1)}, u32[]{:S(2)}, u32[]{:S(2)}) %collective-permute-start.5) | collective-permute-done | bytes 786464 | tf_op jit(solution)/shard_map/ppermute | solution.py:434
  26.7 1.5 %collective-permute-start.9 = (f32[256,768]{1,0:T(8,128)}, f32[256,768]{1,0:T(8,128)}, u32[]{:S(2)}, u32[]{:S(2)}) collective-permute-start(f32[256,768]{1,0:T(8,128)} %rest_0_.1), channel_id=1, source_target_pairs={{6,0},{7,1},{4,2},{5,3},{2,4},{3,5},{0,6},{1,7},{14,8},{15,9},{12,... | collective-permute-start | bytes 2359304 | tf_op jit(solution)/shard_map/ppermute | solution.py:434
  28.9 0.8 copy.15
  29.9 1.3 %multiply_reduce_fusion = f32[256]{0:T(256)S(1)} fusion(f32[256,768]{1,0:T(8,128)} %rest_0_.1), kind=kLoop, calls=%fused_computation | loop fusion | flops 392960 | bytes 787456 | tf_op jit(solution)/shard_map/reduce_sum | solution.py:459
  31.2 1.6 %concatenate.7.rest_3_.rest_2_ = f32[72,256]{1,0:T(8,128)S(1)} concatenate(f32[64,256]{1,0:T(8,128)} %param.13, f32[1,256]{1,0:T(1,128)} %bitcast.30, f32[1,256]{1,0:T(1,128)} %bitcast.31, f32[1,256]{1,0:T(1,128)S(1)} %bitcast.29, f32[5,256]{1,0:T(8,128)S(1)} %pad.4), dimensions={0} | concatenate | bytes 147456 | tf_op jit(solution)/shard_map/concatenate | solution.py:463
  32.8 1.3 %collective-permute-start.8 = (f32[256,768]{1,0:T(8,128)}, f32[256,768]{1,0:T(8,128)S(1)}, u32[]{:S(2)}, u32[]{:S(2)}) collective-permute-start(f32[256,768]{1,0:T(8,128)} %rest_0_.1), channel_id=1, source_target_pairs={{16,0},{8,24},{17,1},{9,25},{18,2},{10,26},{19,3},{11,27},{20,4},{... | collective-permute-start | bytes 2359304 | tf_op jit(solution)/shard_map/ppermute | solution.py:426
  34.1 1.5 %collective-permute-start.12 = (f32[72,256]{1,0:T(8,128)S(1)}, f32[72,256]{1,0:T(8,128)S(1)}, u32[]{:S(2)}, u32[]{:S(2)}) collective-permute-start(f32[72,256]{1,0:T(8,128)S(1)} %concatenate.7.rest_3_.rest_2_), channel_id=1, source_target_pairs={{6,0},{7,1},{4,2},{5,3},{2,4},{3,5},{0,6},{1,7},{14,8},{15,9},{12,... | collective-permute-start | bytes 221192 | tf_op jit(solution)/shard_map/ppermute | solution.py:434
  35.6 1.5 %collective-permute-start.11 = (f32[72,256]{1,0:T(8,128)S(1)}, f32[72,256]{1,0:T(8,128)S(1)}, u32[]{:S(2)}, u32[]{:S(2)}) collective-permute-start(f32[72,256]{1,0:T(8,128)S(1)} %concatenate.7.rest_3_.rest_2_), channel_id=1, source_target_pairs={{4,0},{5,1},{6,2},{7,3},{0,4},{1,5},{2,6},{3,7},{12,8},{13,9},{14,... | collective-permute-start | bytes 221192 | tf_op jit(solution)/shard_map/ppermute | solution.py:434
  37.6 5.1 %grams.1 = (f32[6,2,128,128]{3,2,1,0:T(8,128)S(1)}, bf16[2,256,768]{2,1,0:T(8,128)(2,1)S(1)}, bf16[2,256,768]{2,1,0:T(8,128)(2,1)S(1)}, bf16[6,128,768]{2,1,0:T(8,128)(2,1)S(1)}, bf16[6,128,768]{2,1,0:T(8,128)(2,1)S(1)}) custom-call(s32[11]{0:T(128)S(1)} %pad_add_fusion.meta, s32[64]{0:T(128)S(1)} %reshape.16.listing, f32[256,768]{1,0:T(8,128)S(1)} %copy-done, ...), custom_call_target="tpu_custom_call" | custom-call | flops 905969664 | bytes 6291456 | tf_op jit(solution)/shard_map/grams/pallas_call | solution.py:106
  42.7 7.0 %collective-permute-done.12 = f32[72,256]{1,0:T(8,128)S(1)} collective-permute-done((f32[72,256]{1,0:T(8,128)S(1)}, f32[72,256]{1,0:T(8,128)S(1)}, u32[]{:S(2)}, u32[]{:S(2)}) %collective-permute-start.12) | collective-permute-done | bytes 73760 | tf_op jit(solution)/shard_map/ppermute | solution.py:434
  51.1 1.6 %collective-permute-start.14 = (f32[72,256]{1,0:T(8,128)S(1)}, f32[72,256]{1,0:T(8,128)S(1)}, u32[]{:S(2)}, u32[]{:S(2)}) collective-permute-start(f32[72,256]{1,0:T(8,128)S(1)} %concatenate.7.rest_3_.rest_2_), channel_id=1, source_target_pairs={{8,0},{16,8},{24,16},{0,24},{9,1},{17,9},{25,17},{1,25},{10,2},{18... | collective-permute-start | bytes 221192 | tf_op jit(solution)/shard_map/ppermute | solution.py:421
  52.7 3.2 %collective-permute-done.8.rest_0_ = f32[256,768]{1,0:T(8,128)S(1)} collective-permute-done((f32[256,768]{1,0:T(8,128)}, f32[256,768]{1,0:T(8,128)S(1)}, u32[]{:S(2)}, u32[]{:S(2)}) %collective-permute-start.8) | collective-permute-done | bytes 786464 | tf_op jit(solution)/shard_map/ppermute | solution.py:426
  55.8 2.5 %collective-permute-start.17 = (f32[72,256]{1,0:T(8,128)S(1)}, f32[72,256]{1,0:T(8,128)S(1)}, u32[]{:S(2)}, u32[]{:S(2)}) collective-permute-start(f32[72,256]{1,0:T(8,128)S(1)} %concatenate.7.rest_3_.rest_2_), channel_id=1, source_target_pairs={{24,0},{0,8},{8,16},{16,24},{25,1},{1,9},{9,17},{17,25},{26,2},{2,... | collective-permute-start | bytes 221192 | tf_op jit(solution)/shard_map/ppermute | solution.py:421
  58.3 2.1 %collective-permute-done.15.rest_5_.rest_4_ = f32[72,256]{1,0:T(8,128)S(1)} collective-permute-done((f32[72,256]{1,0:T(8,128)S(1)}, f32[72,256]{1,0:T(8,128)S(1)}, u32[]{:S(2)}, u32[]{:S(2)}) %collective-permute-start.15) | collective-permute-done | bytes 73760 | tf_op jit(solution)/shard_map/ppermute | solution.py:421
  60.5 5.2 %weights.1 = bf16[24,128,128]{2,1,0:T(8,128)(2,1)S(1)} custom-call(s32[11]{0:T(128)S(1)} %pad_add_fusion.meta, s32[64]{0:T(128)S(1)} %reshape.16.listing, s32[32]{0:T(128)S(1)} %reshape.19.seeds, f32[6,2,128,128]{3,2,1,0:T(8,128)S(1)} %get-tuple-element.28.grams, bf16[2,256,768]{2,1,0:T(8,128)(2,1)S(1)} %get-tuple-element.29.high_c, ...), custom_call_target="tpu_custom_call" | custom-call | flops 905969664 | bytes 2359296 | tf_op jit(solution)/shard_map/weights/pallas_call | solution.py:214
  65.7 5.7 %forces.2 = (f32[8,64,256]{2,1,0:T(8,128)}, f32[64,256]{1,0:T(8,128)S(1)}, f32[64,256]{1,0:T(8,128)S(1)}, f32[64,256]{1,0:T(8,128)S(1)}, f32[64,256]{1,0:T(8,128)S(1)}) custom-call(s32[11]{0:T(128)S(1)} %pad_add_fusion.meta, s32[64]{0:T(128)S(1)} %reshape.16.listing, s32[48]{0:T(128)S(1)} %bitcast.22, s32[48]{0:T(128)S(1)} %bitcast.24, ...), custom_call_target="tpu_custom_call" | custom-call | flops 1744830464 | bytes 1572864 | tf_op jit(solution)/shard_map/forces/pallas_call | solution.py:382
  71.4 4.2 %all-to-all-start = ((f32[8,64,256]{2,1,0:T(8,128)}), f32[8,64,256]{2,1,0:T(8,128)S(1)}, u32[]{:S(2)}, u32[]{:S(2)}) async-start(f32[8,64,256]{2,1,0:T(8,128)} %get-tuple-element.38), calls=%async_computation | async-start | bytes 1048576 | tf_op jit(solution)/shard_map/all_to_all | solution.py:493
  75.6 1.9 %collective-permute-start.20 = (f32[64,256]{1,0:T(8,128)S(1)}, f32[64,256]{1,0:T(8,128)S(1)}, u32[]{:S(2)}, u32[]{:S(2)}) collective-permute-start(f32[64,256]{1,0:T(8,128)S(1)} %get-tuple-element.42), channel_id=1, source_target_pairs={{0,24},{8,0},{16,8},{24,16},{1,25},{9,1},{17,9},{25,17},{2,26},{10... | collective-permute-start | bytes 196616 | tf_op jit(solution)/shard_map/ppermute | solution.py:430
  77.6 1.1 collective-permute-start.18
  78.6 6.7 %all-to-all-done = f32[8,64,256]{2,1,0:T(8,128)S(1)} async-done(((f32[8,64,256]{2,1,0:T(8,128)}), f32[8,64,256]{2,1,0:T(8,128)S(1)}, u32[]{:S(2)}, u32[]{:S(2)}) %all-to-all-start) | async-done | bytes 524320 | tf_op jit(solution)/shard_map/all_to_all | solution.py:493
  85.5 2.0 %collective-permute-start.21 = (f32[64,256]{1,0:T(8,128)S(1)}, f32[64,256]{1,0:T(8,128)S(1)}, u32[]{:S(2)}, u32[]{:S(2)}) collective-permute-start(f32[64,256]{1,0:T(8,128)S(1)} %multiply_add_fusion.1.rest_1_), channel_id=1, source_target_pairs={{8,0},{16,8},{24,16},{0,24},{9,1},{17,9},{25,17},{1,25},{10,2},{18... | collective-permute-start | bytes 196616 | tf_op jit(solution)/shard_map/ppermute | solution.py:421
  87.5 1.1 collective-permute-start.23
  88.6 10.2 %all-gather = f32[512,256]{1,0:T(8,128)S(1)} all-gather(f32[64,256]{1,0:T(8,128)S(1)} %multiply_add_fusion.1.rest_1_), channel_id=2, replica_groups=mesh['row'=4,'col'=8] {'col'}, dimensions={0}, use_global_device_ids=true | all-gather | bytes 589824 | tf_op jit(solution)/shard_map/all_gather | solution.py:490
  98.8 5.7 %forces.3 = (f32[8,64,256]{2,1,0:T(8,128)}, f32[64,256]{1,0:T(8,128)S(1)}, f32[64,256]{1,0:T(8,128)S(1)}, f32[64,256]{1,0:T(8,128)S(1)}, f32[64,256]{1,0:T(8,128)S(1)}) custom-call(s32[11]{0:T(128)S(1)} %pad_add_fusion.meta, s32[64]{0:T(128)S(1)} %reshape.16.listing, s32[48]{0:T(128)S(1)} %bitcast.23, s32[48]{0:T(128)S(1)} %bitcast.25, ...), custom_call_target="tpu_custom_call" | custom-call | flops 1744830464 | bytes 1572864 | tf_op jit(solution)/shard_map/forces/pallas_call | solution.py:382
  104.5 4.4 %all-to-all-start.1 = ((f32[8,64,256]{2,1,0:T(8,128)}), f32[8,64,256]{2,1,0:T(8,128)S(1)}, u32[]{:S(2)}, u32[]{:S(2)}) async-start(f32[8,64,256]{2,1,0:T(8,128)} %get-tuple-element.43), calls=%async_computation.1 | async-start | bytes 1048576 | tf_op jit(solution)/shard_map/all_to_all | solution.py:493
  108.9 2.0 %collective-permute-start.26 = (f32[64,256]{1,0:T(8,128)S(1)}, f32[64,256]{1,0:T(8,128)S(1)}, u32[]{:S(2)}, u32[]{:S(2)}) collective-permute-start(f32[64,256]{1,0:T(8,128)S(1)} %get-tuple-element.47), channel_id=1, source_target_pairs={{0,24},{8,0},{16,8},{24,16},{1,25},{9,1},{17,9},{25,17},{2,26},{10... | collective-permute-start | bytes 196616 | tf_op jit(solution)/shard_map/ppermute | solution.py:430
  111.5 7.1 %all-to-all-done.1 = f32[8,64,256]{2,1,0:T(8,128)S(1)} async-done(((f32[8,64,256]{2,1,0:T(8,128)}), f32[8,64,256]{2,1,0:T(8,128)S(1)}, u32[]{:S(2)}, u32[]{:S(2)}) %all-to-all-start.1) | async-done | bytes 524320 | tf_op jit(solution)/shard_map/all_to_all | solution.py:493
  (56 shorter events, 6.2 us)
Async XLA Ops:
  0.6 37.0 %copy-start = (f32[256,768]{1,0:T(8,128)S(1)}, f32[256,768]{1,0:T(8,128)}, u32[]{:S(2)}) copy-start(f32[256,768]{1,0:T(8,128)} %rest_0_.1) | copy-start | bytes 2359300
  0.6 22.2 %collective-permute-start = (f32[256,768]{1,0:T(8,128)}, f32[256,768]{1,0:T(8,128)S(1)}, u32[]{:S(2)}, u32[]{:S(2)}) collective-permute-start(f32[256,768]{1,0:T(8,128)} %rest_0_.1), channel_id=1, source_target_pairs={{8,0},{16,8},{24,16},{0,24},{9,1},{17,9},{25,17},{1,25},{10,2},{18... | collective-permute-start | bytes 2359304 | tf_op jit(solution)/shard_map/ppermute | solution.py:421
  5.7 19.2 %collective-permute-start.4 = (f32[256,768]{1,0:T(8,128)}, f32[256,768]{1,0:T(8,128)S(1)}, u32[]{:S(2)}, u32[]{:S(2)}) collective-permute-start(f32[256,768]{1,0:T(8,128)} %rest_0_.1), channel_id=1, source_target_pairs={{2,0},{3,1},{0,2},{1,3},{6,4},{7,5},{4,6},{5,7},{10,8},{11,9},{8,1... | collective-permute-start | bytes 2359304 | tf_op jit(solution)/shard_map/ppermute | solution.py:434
  7.2 18.9 %collective-permute-start.5 = (f32[256,768]{1,0:T(8,128)}, f32[256,768]{1,0:T(8,128)S(1)}, u32[]{:S(2)}, u32[]{:S(2)}) collective-permute-start(f32[256,768]{1,0:T(8,128)} %rest_0_.1), channel_id=1, source_target_pairs={{4,0},{5,1},{6,2},{7,3},{0,4},{1,5},{2,6},{3,7},{12,8},{13,9},{14,... | collective-permute-start | bytes 2359304 | tf_op jit(solution)/shard_map/ppermute | solution.py:434
  9.6 13.3 %collective-permute-start.1 = (s32[32]{0:T(128)S(1)}, s32[32]{0:T(128)S(1)}, u32[]{:S(2)}, u32[]{:S(2)}) collective-permute-start(s32[32]{0:T(128)S(1)} %reshape.19.seeds), channel_id=1, source_target_pairs={{8,0},{16,8},{24,16},{0,24},{9,1},{17,9},{25,17},{1,25},{10,2},{18... | collective-permute-start | bytes 392 | tf_op jit(solution)/shard_map/ppermute | solution.py:421
  10.0 12.8 %collective-permute-start.2 = (s32[32]{0:T(128)S(1)}, s32[32]{0:T(128)S(1)}, u32[]{:S(2)}, u32[]{:S(2)}) collective-permute-start(s32[32]{0:T(128)S(1)} %reshape.19.seeds), channel_id=1, source_target_pairs={{16,0},{24,8},{0,16},{8,24},{17,1},{25,9},{1,17},{9,25},{18,2},{26... | collective-permute-start | bytes 392 | tf_op jit(solution)/shard_map/ppermute | solution.py:421
  22.9 9.9 %collective-permute-start.3 = (f32[256,768]{1,0:T(8,128)}, f32[256,768]{1,0:T(8,128)}, u32[]{:S(2)}, u32[]{:S(2)}) collective-permute-start(f32[256,768]{1,0:T(8,128)} %rest_0_.1), channel_id=1, source_target_pairs={{1,0},{0,1},{3,2},{2,3},{5,4},{4,5},{7,6},{6,7},{9,8},{8,9},{11,10... | collective-permute-start | bytes 2359304 | tf_op jit(solution)/shard_map/ppermute | solution.py:434
  26.2 7.9 %collective-permute-start.6 = (f32[256,768]{1,0:T(8,128)S(1)}, f32[256,768]{1,0:T(8,128)}, u32[]{:S(2)}, u32[]{:S(2)}) collective-permute-start(f32[256,768]{1,0:T(8,128)S(1)} %collective-permute-done.4.rest_3_), channel_id=1, source_target_pairs={{1,0},{0,1},{3,2},{2,3},{5,4},{4,5},{7,6},{6,7},{9,8},{8,9},{11,10... | collective-permute-start | bytes 2359304 | tf_op jit(solution)/shard_map/ppermute | solution.py:434
  26.2 7.9 %collective-permute-start.7 = (f32[256,768]{1,0:T(8,128)S(1)}, f32[256,768]{1,0:T(8,128)}, u32[]{:S(2)}, u32[]{:S(2)}) collective-permute-start(f32[256,768]{1,0:T(8,128)S(1)} %collective-permute-done.5.rest_5_), channel_id=1, source_target_pairs={{1,0},{0,1},{3,2},{2,3},{5,4},{4,5},{7,6},{6,7},{9,8},{8,9},{11,10... | collective-permute-start | bytes 2359304 | tf_op jit(solution)/shard_map/ppermute | solution.py:434
  26.7 23.9 %collective-permute-start.9 = (f32[256,768]{1,0:T(8,128)}, f32[256,768]{1,0:T(8,128)}, u32[]{:S(2)}, u32[]{:S(2)}) collective-permute-start(f32[256,768]{1,0:T(8,128)} %rest_0_.1), channel_id=1, source_target_pairs={{6,0},{7,1},{4,2},{5,3},{2,4},{3,5},{0,6},{1,7},{14,8},{15,9},{12,... | collective-permute-start | bytes 2359304 | tf_op jit(solution)/shard_map/ppermute | solution.py:434
  32.8 23.1 %collective-permute-start.8 = (f32[256,768]{1,0:T(8,128)}, f32[256,768]{1,0:T(8,128)S(1)}, u32[]{:S(2)}, u32[]{:S(2)}) collective-permute-start(f32[256,768]{1,0:T(8,128)} %rest_0_.1), channel_id=1, source_target_pairs={{16,0},{8,24},{17,1},{9,25},{18,2},{10,26},{19,3},{11,27},{20,4},{... | collective-permute-start | bytes 2359304 | tf_op jit(solution)/shard_map/ppermute | solution.py:426
  34.1 15.6 %collective-permute-start.12 = (f32[72,256]{1,0:T(8,128)S(1)}, f32[72,256]{1,0:T(8,128)S(1)}, u32[]{:S(2)}, u32[]{:S(2)}) collective-permute-start(f32[72,256]{1,0:T(8,128)S(1)} %concatenate.7.rest_3_.rest_2_), channel_id=1, source_target_pairs={{6,0},{7,1},{4,2},{5,3},{2,4},{3,5},{0,6},{1,7},{14,8},{15,9},{12,... | collective-permute-start | bytes 221192 | tf_op jit(solution)/shard_map/ppermute | solution.py:434
  35.6 14.8 %collective-permute-start.11 = (f32[72,256]{1,0:T(8,128)S(1)}, f32[72,256]{1,0:T(8,128)S(1)}, u32[]{:S(2)}, u32[]{:S(2)}) collective-permute-start(f32[72,256]{1,0:T(8,128)S(1)} %concatenate.7.rest_3_.rest_2_), channel_id=1, source_target_pairs={{4,0},{5,1},{6,2},{7,3},{0,4},{1,5},{2,6},{3,7},{12,8},{13,9},{14,... | collective-permute-start | bytes 221192 | tf_op jit(solution)/shard_map/ppermute | solution.py:434
  37.1 13.4 %collective-permute-start.10 = (f32[72,256]{1,0:T(8,128)S(1)}, f32[72,256]{1,0:T(8,128)S(1)}, u32[]{:S(2)}, u32[]{:S(2)}) collective-permute-start(f32[72,256]{1,0:T(8,128)S(1)} %concatenate.7.rest_3_.rest_2_), channel_id=1, source_target_pairs={{2,0},{3,1},{0,2},{1,3},{6,4},{7,5},{4,6},{5,7},{10,8},{11,9},{8,1... | collective-permute-start | bytes 221192 | tf_op jit(solution)/shard_map/ppermute | solution.py:434
  50.5 9.9 %collective-permute-start.13 = (f32[256,768]{1,0:T(8,128)}, f32[256,768]{1,0:T(8,128)S(1)}, u32[]{:S(2)}, u32[]{:S(2)}) collective-permute-start(f32[256,768]{1,0:T(8,128)} %collective-permute-done.9.rest_1_), channel_id=1, source_target_pairs={{1,0},{0,1},{3,2},{2,3},{5,4},{4,5},{7,6},{6,7},{9,8},{8,9},{11,10... | collective-permute-start | bytes 2359304 | tf_op jit(solution)/shard_map/ppermute | solution.py:434
  50.6 9.8 %collective-permute-start.16 = (f32[4,72,256]{2,1,0:T(8,128)S(1)}, f32[4,72,256]{2,1,0:T(8,128)S(1)}, u32[]{:S(2)}, u32[]{:S(2)}) collective-permute-start(f32[4,72,256]{2,1,0:T(8,128)S(1)} %pad_maximum_fusion.rest_6_.rest_0_), channel_id=1, source_target_pairs={{1,0},{0,1},{3,2},{2,3},{5,4},{4,5},{7,6},{6,7},{9,8},{8,9},{11,10... | collective-permute-start | bytes 884744 | tf_op jit(solution)/shard_map/ppermute | solution.py:434
  51.1 7.2 %collective-permute-start.14 = (f32[72,256]{1,0:T(8,128)S(1)}, f32[72,256]{1,0:T(8,128)S(1)}, u32[]{:S(2)}, u32[]{:S(2)}) collective-permute-start(f32[72,256]{1,0:T(8,128)S(1)} %concatenate.7.rest_3_.rest_2_), channel_id=1, source_target_pairs={{8,0},{16,8},{24,16},{0,24},{9,1},{17,9},{25,17},{1,25},{10,2},{18... | collective-permute-start | bytes 221192 | tf_op jit(solution)/shard_map/ppermute | solution.py:421
  52.7 7.8 %collective-permute-start.15 = (f32[72,256]{1,0:T(8,128)S(1)}, f32[72,256]{1,0:T(8,128)S(1)}, u32[]{:S(2)}, u32[]{:S(2)}) collective-permute-start(f32[72,256]{1,0:T(8,128)S(1)} %concatenate.7.rest_3_.rest_2_), channel_id=1, source_target_pairs={{16,0},{24,8},{0,16},{8,24},{17,1},{25,9},{1,17},{9,25},{18,2},{26... | collective-permute-start | bytes 221192 | tf_op jit(solution)/shard_map/ppermute | solution.py:421
  55.8 9.8 %collective-permute-start.17 = (f32[72,256]{1,0:T(8,128)S(1)}, f32[72,256]{1,0:T(8,128)S(1)}, u32[]{:S(2)}, u32[]{:S(2)}) collective-permute-start(f32[72,256]{1,0:T(8,128)S(1)} %concatenate.7.rest_3_.rest_2_), channel_id=1, source_target_pairs={{24,0},{0,8},{8,16},{16,24},{25,1},{1,9},{9,17},{17,25},{26,2},{2,... | collective-permute-start | bytes 221192 | tf_op jit(solution)/shard_map/ppermute | solution.py:421
  60.5 5.2 %copy-start.2 = (s32[1,1,48]{2,1,0:T(1,128)S(1)}, s32[1,1,48]{2,1,0:T(1,128)}, u32[]{:S(2)}) copy-start(s32[1,1,48]{2,1,0:T(1,128)} %param.17) | copy-start | bytes 580
  71.4 14.0 %copy-start.3 = (f32[64,256]{1,0:T(8,128)S(1)}, f32[64,256]{1,0:T(8,128)}, u32[]{:S(2)}) copy-start(f32[64,256]{1,0:T(8,128)} %param.13) | copy-start | bytes 196612
  71.4 13.9 %all-to-all-start = ((f32[8,64,256]{2,1,0:T(8,128)}), f32[8,64,256]{2,1,0:T(8,128)S(1)}, u32[]{:S(2)}, u32[]{:S(2)}) async-start(f32[8,64,256]{2,1,0:T(8,128)} %get-tuple-element.38), calls=%async_computation | async-start | bytes 1048576 | tf_op jit(solution)/shard_map/all_to_all | solution.py:493
  75.6 9.8 %collective-permute-start.20 = (f32[64,256]{1,0:T(8,128)S(1)}, f32[64,256]{1,0:T(8,128)S(1)}, u32[]{:S(2)}, u32[]{:S(2)}) collective-permute-start(f32[64,256]{1,0:T(8,128)S(1)} %get-tuple-element.42), channel_id=1, source_target_pairs={{0,24},{8,0},{16,8},{24,16},{1,25},{9,1},{17,9},{25,17},{2,26},{10... | collective-permute-start | bytes 196616 | tf_op jit(solution)/shard_map/ppermute | solution.py:430
  77.6 7.8 %collective-permute-start.19 = (f32[64,256]{1,0:T(8,128)S(1)}, f32[64,256]{1,0:T(8,128)S(1)}, u32[]{:S(2)}, u32[]{:S(2)}) collective-permute-start(f32[64,256]{1,0:T(8,128)S(1)} %get-tuple-element.41), channel_id=1, source_target_pairs={{0,16},{8,24},{16,0},{24,8},{1,17},{9,25},{17,1},{25,9},{2,18},{10... | collective-permute-start | bytes 196616 | tf_op jit(solution)/shard_map/ppermute | solution.py:430
  77.6 7.9 %collective-permute-start.18 = (f32[64,256]{1,0:T(8,128)S(1)}, f32[64,256]{1,0:T(8,128)S(1)}, u32[]{:S(2)}, u32[]{:S(2)}) collective-permute-start(f32[64,256]{1,0:T(8,128)S(1)} %get-tuple-element.40), channel_id=1, source_target_pairs={{0,8},{8,16},{16,24},{24,0},{1,9},{9,17},{17,25},{25,1},{2,10},{10... | collective-permute-start | bytes 196616 | tf_op jit(solution)/shard_map/ppermute | solution.py:430
  85.5 13.3 %collective-permute-start.21 = (f32[64,256]{1,0:T(8,128)S(1)}, f32[64,256]{1,0:T(8,128)S(1)}, u32[]{:S(2)}, u32[]{:S(2)}) collective-permute-start(f32[64,256]{1,0:T(8,128)S(1)} %multiply_add_fusion.1.rest_1_), channel_id=1, source_target_pairs={{8,0},{16,8},{24,16},{0,24},{9,1},{17,9},{25,17},{1,25},{10,2},{18... | collective-permute-start | bytes 196616 | tf_op jit(solution)/shard_map/ppermute | solution.py:421
  87.5 11.3 %collective-permute-start.22 = (f32[64,256]{1,0:T(8,128)S(1)}, f32[64,256]{1,0:T(8,128)S(1)}, u32[]{:S(2)}, u32[]{:S(2)}) collective-permute-start(f32[64,256]{1,0:T(8,128)S(1)} %multiply_add_fusion.1.rest_1_), channel_id=1, source_target_pairs={{16,0},{24,8},{0,16},{8,24},{17,1},{25,9},{1,17},{9,25},{18,2},{26... | collective-permute-start | bytes 196616 | tf_op jit(solution)/shard_map/ppermute | solution.py:421
  87.5 11.3 %collective-permute-start.23 = (f32[64,256]{1,0:T(8,128)S(1)}, f32[64,256]{1,0:T(8,128)S(1)}, u32[]{:S(2)}, u32[]{:S(2)}) collective-permute-start(f32[64,256]{1,0:T(8,128)S(1)} %multiply_add_fusion.1.rest_1_), channel_id=1, source_target_pairs={{24,0},{0,8},{8,16},{16,24},{25,1},{1,9},{9,17},{17,25},{26,2},{2,... | collective-permute-start | bytes 196616 | tf_op jit(solution)/shard_map/ppermute | solution.py:421
  104.5 14.2 %all-to-all-start.1 = ((f32[8,64,256]{2,1,0:T(8,128)}), f32[8,64,256]{2,1,0:T(8,128)S(1)}, u32[]{:S(2)}, u32[]{:S(2)}) async-start(f32[8,64,256]{2,1,0:T(8,128)} %get-tuple-element.43), calls=%async_computation.1 | async-start | bytes 1048576 | tf_op jit(solution)/shard_map/all_to_all | solution.py:493
  108.9 9.8 %collective-permute-start.26 = (f32[64,256]{1,0:T(8,128)S(1)}, f32[64,256]{1,0:T(8,128)S(1)}, u32[]{:S(2)}, u32[]{:S(2)}) collective-permute-start(f32[64,256]{1,0:T(8,128)S(1)} %get-tuple-element.47), channel_id=1, source_target_pairs={{0,24},{8,0},{16,8},{24,16},{1,25},{9,1},{17,9},{25,17},{2,26},{10... | collective-permute-start | bytes 196616 | tf_op jit(solution)/shard_map/ppermute | solution.py:430
  110.9 7.8 %collective-permute-start.25 = (f32[64,256]{1,0:T(8,128)S(1)}, f32[64,256]{1,0:T(8,128)S(1)}, u32[]{:S(2)}, u32[]{:S(2)}) collective-permute-start(f32[64,256]{1,0:T(8,128)S(1)} %get-tuple-element.46), channel_id=1, source_target_pairs={{0,16},{8,24},{16,0},{24,8},{1,17},{9,25},{17,1},{25,9},{2,18},{10... | collective-permute-start | bytes 196616 | tf_op jit(solution)/shard_map/ppermute | solution.py:430
  110.9 7.8 %collective-permute-start.24 = (f32[64,256]{1,0:T(8,128)S(1)}, f32[64,256]{1,0:T(8,128)S(1)}, u32[]{:S(2)}, u32[]{:S(2)}) collective-permute-start(f32[64,256]{1,0:T(8,128)S(1)} %get-tuple-element.45), channel_id=1, source_target_pairs={{0,8},{8,16},{16,24},{24,0},{1,9},{9,17},{17,25},{25,1},{2,10},{10... | collective-permute-start | bytes 196616 | tf_op jit(solution)/shard_map/ppermute | solution.py:430
  (1 other events, 5.2 us)

commit v6 on v5

--- a/solution.py
+++ b/solution.py
@@ -76,9 +76,11 @@
     shifts_early, rows_early = counts
     row_count, _ = sizes
     columns, rows = rest[:shifts_early], rest[shifts_early : shifts_early + rows_early - 1]
-    grams, high_c, low_c, high_last, low_last, high_r, low_r = rest[shifts_early + rows_early - 1 :]
+    grams, high_c, low_c, high_last, low_last, squares, high_r, low_r = rest[shifts_early + rows_early - 1 :]
     for shift in range(shifts_early):
-        high_c[shift], low_c[shift] = split(columns[shift][...])
+        value = columns[shift][...]
+        high_c[shift], low_c[shift] = split(value)
+        squares[shift] = jnp.sum(value * value, axis=1, keepdims=True)
     high_r[0], low_r[0] = high_c[0], low_c[0]
     for line in range(1, rows_early):
         high_r[line], low_r[line] = split(rows[line - 1][...])
@@ -106,13 +108,14 @@
     return pl.pallas_call(
         functools.partial(grams_kernel, sizes, (shifts_early, rows_early)),
         in_specs=[smem] * 2 + [vmem] * (len(columns) + len(rows)),
-        out_specs=[vmem] * 5,
+        out_specs=[vmem] * 6,
         out_shape=[
             jax.ShapeDtypeStruct((rows_early, shifts_early, BLK, BLK), F32),
             jax.ShapeDtypeStruct((shifts_early, SPAN, depth), BF16),
             jax.ShapeDtypeStruct((shifts_early, SPAN, depth), BF16),
             jax.ShapeDtypeStruct((rows_early, BLK, depth), BF16),
             jax.ShapeDtypeStruct((rows_early, BLK, depth), BF16),
+            jax.ShapeDtypeStruct((shifts_early, SPAN, 1), F32),
         ],
         scratch_shapes=[pltpu.VMEM((rows_early, SPAN, depth), BF16)] * 2,
         compiler_params=pltpu.CompilerParams(vmem_limit_bytes=VMEM_LIMIT),
@@ -125,16 +128,17 @@
     )(meta, listing, *columns, *rows)
 
 
-def weights_kernel(sizes, counts, meta, listing, seeds, grams, high_c, low_c, high_last, low_last, *rest):
+def weights_kernel(sizes, counts, meta, listing, seeds, grams, high_c, low_c, high_last, low_last, squares, *rest):
     row_count, col_count = sizes
     shifts_early, rows_early = counts
     shifts, rows_late = shifts_early + 1, col_count - rows_early
     last, late, col_packs = rest[0], rest[1 : 1 + rows_late], rest[1 + rows_late :][:shifts]
     even_packs, odd_packs = rest[1 + rows_late + shifts :][:2]
-    out, high_l, low_l, high_r, low_r, late_grams, col_params, row_params = rest[3 + rows_late + shifts :]
+    out, high_l, low_l, high_r, low_r, late_grams, col_params, row_params, last_squares = rest[3 + rows_late + shifts :]
     row, col = meta[0], meta[1]
 
     high_l[...], low_l[...] = split(last[...])
+    last_squares[...] = jnp.sum(last[...] * last[...], axis=1, keepdims=True)
     for shift in range(shifts):
         for block in range(CB):
             lanes = slice(block * BLK, (block + 1) * BLK)
@@ -175,7 +179,9 @@
         params_i = row_params[bits, :, pl.ds(start_i, BLK)]
         rho_i, sigma_i, square_i = params_i[0:1], params_i[1:2], params_i[2:3]
         params_j = col_params[shift, lax.div(start_j, BLK)]
-        rho_j, sigma_j, square_j = params_j[:, 0:1], params_j[:, 1:2], params_j[:, 2:3]
+        rho_j, sigma_j = params_j[:, 0:1], params_j[:, 1:2]
+        span_j = pl.ds(start_j, BLK)
+        square_j = squares[shift, span_j, :] if shift < shifts_early else last_squares[span_j, :]
         distance = jnp.sqrt(jnp.maximum(square_j + square_i - 2.0 * gram, 1.0))
         plane_seeds = row_params[bits, SEEDS - RHO + shift : SEEDS - RHO + shift + 1, :]
         seed_back = jnp.sum(jnp.where(wanted_seed, plane_seeds, 0.0), axis=1, keepdims=True).astype(I32)
@@ -213,7 +219,7 @@
     tiles = shifts * col_count
     return pl.pallas_call(
         functools.partial(weights_kernel, sizes, (shifts - 1, col_count - rows_late)),
-        in_specs=[smem] * 3 + [vmem] * (5 + 1 + rows_late + len(packs)),
+        in_specs=[smem] * 3 + [vmem] * (6 + 1 + rows_late + len(packs)),
         out_specs=vmem,
         out_shape=jax.ShapeDtypeStruct((tiles, BLK, BLK), BF16),
         scratch_shapes=[
@@ -224,6 +230,7 @@
             pltpu.VMEM((shifts, col_count, BLK, BLK), F32),
             pltpu.VMEM((shifts, CB, BLK, 8), F32),
             pltpu.VMEM((col_count, 8, SPAN), F32),
+            pltpu.VMEM((SPAN, 1), F32),
         ],
         compiler_params=pltpu.CompilerParams(vmem_limit_bytes=VMEM_LIMIT),
         cost_estimate=pl.CostEstimate(
@@ -450,17 +457,19 @@
     for bits in late_bits:
         if bits % 2 == 0:
             row_x[bits] = from_bits(inputs, bits)
-    far_seeds = [from_shift(seeds, shift) for shift in range(1, shifts)]
-    row_x[1] = from_bits(after(inputs, *far_seeds), 1)
+    seed_row = jnp.pad(seeds.astype(F32)[None], ((0, 0), (0, SPAN - seeds.shape[0])))
+    params = jnp.stack([rho, sigma])
+    blank = jnp.zeros((PACK - SEEDS - 1, SPAN), F32)
+    pack = jnp.concatenate([embed, params, jnp.zeros((1, SPAN), F32), seed_row, blank], axis=0)
+    col_packs = [pack] + [from_shift(pack, shift) for shift in range(1, shifts)]
+    row_x[1] = from_bits(after(inputs, *col_packs[1:]), 1)
     for bits in single:
         row_x[bits + 1] = from_bits(after(row_x[bits], *near), 1)
     col_x.append(from_half(after(inputs, row_x[1])))
 
-    squares = jnp.sum(inputs * inputs, axis=1)
-    seed_rows = jnp.pad(
-        jnp.stack([seeds, *far_seeds]).astype(F32), ((0, PACK - SEEDS - shifts), (0, SPAN - seeds.shape[0]))
-    )
-    own_pack = jnp.concatenate([embed, jnp.stack([rho, sigma, squares]), seed_rows], axis=0)
+    squares = jnp.sum(inputs * inputs, axis=1)[None]
+    far_seeds = [far[SEEDS : SEEDS + 1] for far in col_packs[1:]]
+    own_pack = jnp.concatenate([embed, params, squares, seed_row, *far_seeds, blank[shifts - 1 :]], axis=0)
     own_pack = after(own_pack, *[row_x[bits + 1] for bits in single])
     early = early_grams(sizes, meta, listing, col_x[:-1], [row_x[bits] for bits in early_bits[1:]])
     even_packs = jnp.stack([own_pack] + [from_bits(own_pack, bits) for bits in range(2, col_count, 2)])
@@ -469,9 +478,8 @@
     for bits in late_bits:
         if bits % 2 == 0:
             row_x[bits + 1] = from_bits(after(row_x[bits], even_packs), 1)
-    held = after(own_pack, *[row_x[bits] for bits in late_bits if bits % 2 == 0])
-    col_packs = [own_pack] + [from_shift(held, shift) for shift in range(1, row_count)]
-    col_y = col_packs
+    held = after(embed, *[row_x[bits] for bits in late_bits if bits % 2 == 0])
+    col_y = col_packs + [from_shift(held, shift) for shift in range(shifts, row_count)]
 
     weights = pair_weights(
         sizes,
@@ -481,7 +489,7 @@
         early,
         col_x[-1],
         [row_x[bits] for bits in late_bits],
-        col_packs[:shifts] + [even_packs, odd_packs],
+        col_packs + [even_packs, odd_packs],
     )
 
     row_y = (even_packs, odd_packs)

time: 121 us -> 131 us (1.083)
  local copies, waits for them, and re-layouts: 3.4 us -> 18.3 us
  waiting for transfers between devices: 43.1 us -> 29.9 us
  starting transfers between devices: 37.4 us -> 41.1 us
  Pallas kernels: 21.6 us -> 24.9 us
  other arithmetic: 2.78 us -> 4.32 us
    unnamed x10 -> x46, local copies, waits for them, and re-layouts: 1.56 us -> 13.6 us
    ppermute x11, waiting for transfers between devices: 11.1 us -> 0.72 us  [from_bits(): return lax.ppermute(value, 'col', pairs)]
    ppermute x1, waiting for transfers between devices: 3.16 us -> 0.01 us  [from_half(): return lax.ppermute(value, 'row', pairs)]
    concatenate x1 -> x2, local copies, waits for them, and re-layouts: 1.56 us -> 4.35 us  [the longest x1 2.78 us: shards(): jnp.concatenate([embed, params, squares, seed_row, *far_seeds, blank[shif...]
    ppermute x9 -> x7, starting transfers between devices: 12.7 us -> 15.4 us  [from_shift(): return lax.ppermute(value, 'row', pairs)]
    pallas_call x2, Pallas kernels: 11.4 us -> 13.2 us  [pair_forces(): pl.pallas_call(functools.partial(force_kernel, row_count, col_count, len(...]
    all_to_all x2, starting transfers between devices: 8.63 us -> 7.11 us  [shards(): lax.all_to_all(row_force, 'col', split_axis=0, concat_axis=0, tiled=True)]
    all_to_all x2, waiting for transfers between devices: 13.8 us -> 12.4 us  [shards(): lax.all_to_all(row_force, 'col', split_axis=0, concat_axis=0, tiled=True)]
  transfers between devices with their start and end apart: 29 -> 27, of which waited for: 10 -> 7; matrix products, arithmetic and copies ran while one was open for 4% -> 7% of each run, Pallas kernels for 9% -> 9%
where the time goes in v6:
time: 131 us; the launch traced here: 130 us
  starting transfers between devices  41.1 us (31%)
  waiting for transfers between devices  29.9 us (23%)
  Pallas kernels  24.9 us (19%)
  local copies, waits for them, and re-layouts  18.3 us (14%)
  blocking collectives  10.2 us (8%)
  other arithmetic  4.32 us (3%)
  between operations  1.55 us (1%)
    ppermute x7, waiting for transfers between devices, from_shift(): return lax.ppermute(value, 'row', pairs)  15.7 us
    ppermute x7, starting transfers between devices, from_shift(): return lax.ppermute(value, 'row', pairs)  15.4 us
    unnamed x46, local copies, waits for them, and re-layouts  13.6 us
    pallas_call x2, Pallas kernels, pair_forces(): pl.pallas_call(functools.partial(force_kernel, row_count, col_count, len(...  13.2 us
    all_to_all x2, waiting for transfers between devices, shards(): lax.all_to_all(row_force, 'col', split_axis=0, concat_axis=0, tiled=True)  12.4 us
    ppermute x11, starting transfers between devices, from_bits(): return lax.ppermute(value, 'col', pairs)  10.3 us
    all_gather x1, blocking collectives, shards(): row_y = (lax.all_gather(embed, 'col', axis=0, tiled=False),)  10.2 us
    all_to_all x2, starting transfers between devices, shards(): lax.all_to_all(row_force, 'col', split_axis=0, concat_axis=0, tiled=True)  7.11 us
  transfers between devices with their start and end apart: 27, of which 7 were waited for; matrix products, arithmetic and copies ran while one was open for 7% of the time, Pallas kernels for 9%

profile of v6, /device:TPU:0, one launch (start us, length us, event | category | flops | bytes accessed | tf_op | source)
XLA Modules:
  0.0 130.2 jit_solution(6018806178682732921)
XLA Ops:
  0.6 5.1 %collective-permute-start = (f32[256,768]{1,0:T(8,128)}, f32[256,768]{1,0:T(8,128)S(1)}, u32[]{:S(2)}, u32[]{:S(2)}) collective-permute-start(f32[256,768]{1,0:T(8,128)} %rest_0_.1), channel_id=1, source_target_pairs={{8,0},{16,8},{24,16},{0,24},{9,1},{17,9},{25,17},{1,25},{10,2},{18... | collective-permute-start | bytes 2359304 | tf_op jit(solution)/shard_map/ppermute | solution.py:428
  5.7 1.5 %collective-permute-start.4 = (f32[256,768]{1,0:T(8,128)}, f32[256,768]{1,0:T(8,128)S(1)}, u32[]{:S(2)}, u32[]{:S(2)}) collective-permute-start(f32[256,768]{1,0:T(8,128)} %rest_0_.1), channel_id=1, source_target_pairs={{2,0},{3,1},{0,2},{1,3},{6,4},{7,5},{4,6},{5,7},{10,8},{11,9},{8,1... | collective-permute-start | bytes 2359304 | tf_op jit(solution)/shard_map/ppermute | solution.py:441
  7.2 1.5 %collective-permute-start.5 = (f32[256,768]{1,0:T(8,128)}, f32[256,768]{1,0:T(8,128)S(1)}, u32[]{:S(2)}, u32[]{:S(2)}) collective-permute-start(f32[256,768]{1,0:T(8,128)} %rest_0_.1), channel_id=1, source_target_pairs={{4,0},{5,1},{6,2},{7,3},{0,4},{1,5},{2,6},{3,7},{12,8},{13,9},{14,... | collective-permute-start | bytes 2359304 | tf_op jit(solution)/shard_map/ppermute | solution.py:441
  9.6 1.6 %concatenate.12.rest_3_.rest_2_ = f32[72,256]{1,0:T(8,128)S(1)} concatenate(f32[64,256]{1,0:T(8,128)} %param.13, f32[1,256]{1,0:T(1,128)} %bitcast.26, f32[1,256]{1,0:T(1,128)} %bitcast.28, f32[1,256]{1,0:T(1,128)S(1)} %broadcast_in_dim.10, f32[1,256]{1,0:T(1,128)S(1)} %pad.4, f32[4,256]{1,0:T(4,128)S(1)} %broadcast_in_dim.11), dimensions={0} | concatenate | bytes 147456 | tf_op jit(solution)/shard_map/concatenate | solution.py:463
  11.7 13.5 %collective-permute-done.1.rest_4_.rest_3_ = f32[72,256]{1,0:T(8,128)S(1)} collective-permute-done((f32[72,256]{1,0:T(8,128)S(1)}, f32[72,256]{1,0:T(8,128)S(1)}, u32[]{:S(2)}, u32[]{:S(2)}) %collective-permute-start.1) | collective-permute-done | bytes 73760 | tf_op jit(solution)/shard_map/ppermute | solution.py:428
  25.2 2.2 %collective-permute-done.2.rest_5_.rest_4_ = f32[72,256]{1,0:T(8,128)S(1)} collective-permute-done((f32[72,256]{1,0:T(8,128)S(1)}, f32[72,256]{1,0:T(8,128)S(1)}, u32[]{:S(2)}, u32[]{:S(2)}) %collective-permute-start.2) | collective-permute-done | bytes 73760 | tf_op jit(solution)/shard_map/ppermute | solution.py:428
  28.1 2.4 %collective-permute-start.9 = (f32[256,768]{1,0:T(8,128)}, f32[256,768]{1,0:T(8,128)}, u32[]{:S(2)}, u32[]{:S(2)}) collective-permute-start(f32[256,768]{1,0:T(8,128)} %rest_0_.1), channel_id=1, source_target_pairs={{6,0},{7,1},{4,2},{5,3},{2,4},{3,5},{0,6},{1,7},{14,8},{15,9},{12,... | collective-permute-start | bytes 2359304 | tf_op jit(solution)/shard_map/ppermute | solution.py:441
  32.2 1.3 multiply_reduce_fusion
  34.1 2.8 %concatenate.13 = f32[72,256]{1,0:T(8,128)} concatenate(f32[64,256]{1,0:T(8,128)} %param.13, f32[1,256]{1,0:T(1,128)} %bitcast.27, f32[1,256]{1,0:T(1,128)} %bitcast.29, f32[1,256]{1,0:T(1,128)S(1)} %bitcast.30, f32[1,256]{1,0:T(1,128)S(1)} %pad.4, f32[1,256]{1,0:T(1,128)S(1)} %slice.12, f32[1,256]{1,0:T(1,128)S(1)} %slice.13, f32[2,256]{1,0:T(2,128)S(1)} %slice.11), dimensions={0} | concatenate | bytes 147456 | tf_op jit(solution)/shard_map/concatenate | solution.py:472
  36.9 1.3 collective-permute-start.8
  38.7 1.5 %collective-permute-start.11 = (f32[72,256]{1,0:T(8,128)}, f32[72,256]{1,0:T(8,128)S(1)}, u32[]{:S(2)}, u32[]{:S(2)}) collective-permute-start(f32[72,256]{1,0:T(8,128)} %concatenate.13), channel_id=1, source_target_pairs={{4,0},{5,1},{6,2},{7,3},{0,4},{1,5},{2,6},{3,7},{12,8},{13,9},{14,... | collective-permute-start | bytes 221192 | tf_op jit(solution)/shard_map/ppermute | solution.py:441
  40.2 1.6 %collective-permute-start.10 = (f32[72,256]{1,0:T(8,128)}, f32[72,256]{1,0:T(8,128)S(1)}, u32[]{:S(2)}, u32[]{:S(2)}) collective-permute-start(f32[72,256]{1,0:T(8,128)} %concatenate.13), channel_id=1, source_target_pairs={{2,0},{3,1},{0,2},{1,3},{6,4},{7,5},{4,6},{5,7},{10,8},{11,9},{8,1... | collective-permute-start | bytes 221192 | tf_op jit(solution)/shard_map/ppermute | solution.py:441
  41.8 1.1 copy-done.3
  42.9 6.0 %grams.1 = (f32[6,2,128,128]{3,2,1,0:T(8,128)S(1)}, bf16[2,256,768]{2,1,0:T(8,128)(2,1)S(1)}, bf16[2,256,768]{2,1,0:T(8,128)(2,1)S(1)}, bf16[6,128,768]{2,1,0:T(...) custom-call(s32[11]{0:T(128)S(1)} %pad_add_fusion.meta, s32[64]{0:T(128)S(1)} %reshape.27.listing, ...), custom_call_target="tpu_custom_call" | custom-call | flops 905969664 | bytes 6291456 | tf_op jit(solution)/shard_map/grams/pallas_call | solution.py:108
  54.0 5.8 %collective-permute-start.15 = (f32[64,256]{1,0:T(8,128)}, f32[64,256]{1,0:T(8,128)S(1)}, u32[]{:S(2)}, u32[]{:S(2)}) collective-permute-start(f32[64,256]{1,0:T(8,128)} %param.13), channel_id=1, source_target_pairs={{24,0},{0,8},{8,16},{16,24},{25,1},{1,9},{9,17},{17,25},{26,2},{2,... | collective-permute-start | bytes 196616 | tf_op jit(solution)/shard_map/ppermute | solution.py:428
  59.8 1.3 copy-done.1
  61.1 1.1 copy-done.5
  62.2 1.1 copy-done.7
  63.3 1.1 copy-done.9
  65.4 0.9 copy-done.13
  68.1 5.6 %weights.1 = bf16[24,128,128]{2,1,0:T(8,128)(2,1)S(1)} custom-call(s32[11]{0:T(128)S(1)} %pad_add_fusion.meta, s32[64]{0:T(128)S(1)} %reshape.27.listing, s32[32]{0:T(128)S(1)} %reshape.30.seeds, f32[6,2,128,128]{3,2,1,0:T(8,128)S(1)} %copy-done.5, bf16[2,256,768]{2,1,0:T(8,128)(2,1)S(1)} %copy-done.7, bf16[2,256,768]{2,1,0:T(8,128)(2,1)S(1)} %copy-done.9, ...), custom_call_target="tpu_custom_call" | custom-call | flops 905969664 | bytes 2359296 | tf_op jit(solution)/shard_map/weights/pallas_call | solution.py:220
  73.8 6.6 %forces.2 = (f32[8,64,256]{2,1,0:T(8,128)}, f32[64,256]{1,0:T(8,128)S(1)}, f32[64,256]{1,0:T(8,128)S(1)}, f32[64,256]{1,0:T(8,128)S(1)}, f32[64,256]{1,0:T(8,128)S(1)}) custom-call(s32[11]{0:T(128)S(1)} %pad_add_fusion.meta, s32[64]{0:T(128)S(1)} %reshape.27.listing, s32[48]{0:T(128)S(1)} %bitcast.19, s32[48]{0:T(128)S(1)} %bitcast.21, ...), custom_call_target="tpu_custom_call" | custom-call | flops 1744830464 | bytes 1572864 | tf_op jit(solution)/shard_map/forces/pallas_call | solution.py:389
  80.4 3.6 %all-to-all-start = ((f32[8,64,256]{2,1,0:T(8,128)}), f32[8,64,256]{2,1,0:T(8,128)S(1)}, u32[]{:S(2)}, u32[]{:S(2)}) async-start(f32[8,64,256]{2,1,0:T(8,128)} %get-tuple-element.40), calls=%async_computation | async-start | bytes 1048576 | tf_op jit(solution)/shard_map/all_to_all | solution.py:501
  84.1 3.8 %collective-permute-start.18 = (f32[64,256]{1,0:T(8,128)S(1)}, f32[64,256]{1,0:T(8,128)S(1)}, u32[]{:S(2)}, u32[]{:S(2)}) collective-permute-start(f32[64,256]{1,0:T(8,128)S(1)} %get-tuple-element.44), channel_id=1, source_target_pairs={{0,24},{8,0},{16,8},{24,16},{1,25},{9,1},{17,9},{25,17},{2,26},{10... | collective-permute-start | bytes 196616 | tf_op jit(solution)/shard_map/ppermute | solution.py:437
  88.5 5.3 %all-to-all-done = f32[8,64,256]{2,1,0:T(8,128)S(1)} async-done(((f32[8,64,256]{2,1,0:T(8,128)}), f32[8,64,256]{2,1,0:T(8,128)S(1)}, u32[]{:S(2)}, u32[]{:S(2)}) %all-to-all-start) | async-done | bytes 524320 | tf_op jit(solution)/shard_map/all_to_all | solution.py:501
  93.8 1.0 collective-permute-done.17
  94.8 3.1 %collective-permute-start.19 = (f32[64,256]{1,0:T(8,128)S(1)}, f32[64,256]{1,0:T(8,128)S(1)}, u32[]{:S(2)}, u32[]{:S(2)}) collective-permute-start(f32[64,256]{1,0:T(8,128)S(1)} %multiply_add_fusion.1.rest_1_), channel_id=1, source_target_pairs={{8,0},{16,8},{24,16},{0,24},{9,1},{17,9},{25,17},{1,25},{10,2},{18... | collective-permute-start | bytes 196616 | tf_op jit(solution)/shard_map/ppermute | solution.py:428
  98.9 10.2 %all-gather = f32[512,256]{1,0:T(8,128)S(1)} all-gather(f32[64,256]{1,0:T(8,128)S(1)} %multiply_add_fusion.1.rest_1_), channel_id=2, replica_groups=mesh['row'=4,'col'=8] {'col'}, dimensions={0}, use_global_device_ids=true | all-gather | bytes 589824 | tf_op jit(solution)/shard_map/all_gather | solution.py:498
  109.0 6.6 %forces.3 = (f32[8,64,256]{2,1,0:T(8,128)}, f32[64,256]{1,0:T(8,128)S(1)}, f32[64,256]{1,0:T(8,128)S(1)}, f32[64,256]{1,0:T(8,128)S(1)}, f32[64,256]{1,0:T(8,128)S(1)}) custom-call(s32[11]{0:T(128)S(1)} %pad_add_fusion.meta, s32[64]{0:T(128)S(1)} %reshape.27.listing, s32[48]{0:T(128)S(1)} %bitcast.20, s32[48]{0:T(128)S(1)} %bitcast.22, ...), custom_call_target="tpu_custom_call" | custom-call | flops 1744830464 | bytes 1572864 | tf_op jit(solution)/shard_map/forces/pallas_call | solution.py:389
  115.6 3.5 %all-to-all-start.1 = ((f32[8,64,256]{2,1,0:T(8,128)}), f32[8,64,256]{2,1,0:T(8,128)S(1)}, u32[]{:S(2)}, u32[]{:S(2)}) async-start(f32[8,64,256]{2,1,0:T(8,128)} %get-tuple-element.45), calls=%async_computation.1 | async-start | bytes 1048576 | tf_op jit(solution)/shard_map/all_to_all | solution.py:501
  119.1 1.9 %collective-permute-start.24 = (f32[64,256]{1,0:T(8,128)S(1)}, f32[64,256]{1,0:T(8,128)S(1)}, u32[]{:S(2)}, u32[]{:S(2)}) collective-permute-start(f32[64,256]{1,0:T(8,128)S(1)} %get-tuple-element.49), channel_id=1, source_target_pairs={{0,24},{8,0},{16,8},{24,16},{1,25},{9,1},{17,9},{25,17},{2,26},{10... | collective-permute-start | bytes 196616 | tf_op jit(solution)/shard_map/ppermute | solution.py:437
  121.7 7.2 %all-to-all-done.1 = f32[8,64,256]{2,1,0:T(8,128)S(1)} async-done(((f32[8,64,256]{2,1,0:T(8,128)}), f32[8,64,256]{2,1,0:T(8,128)S(1)}, u32[]{:S(2)}, u32[]{:S(2)}) %all-to-all-start.1) | async-done | bytes 524320 | tf_op jit(solution)/shard_map/all_to_all | solution.py:501
  (95 shorter events, 15.5 us)
Async XLA Ops:
  0.6 41.2 %copy-start = (f32[256,768]{1,0:T(8,128)S(1)}, f32[256,768]{1,0:T(8,128)}, u32[]{:S(2)}) copy-start(f32[256,768]{1,0:T(8,128)} %rest_0_.1) | copy-start | bytes 2359300
  0.6 26.8 %collective-permute-start = (f32[256,768]{1,0:T(8,128)}, f32[256,768]{1,0:T(8,128)S(1)}, u32[]{:S(2)}, u32[]{:S(2)}) collective-permute-start(f32[256,768]{1,0:T(8,128)} %rest_0_.1), channel_id=1, source_target_pairs={{8,0},{16,8},{24,16},{0,24},{9,1},{17,9},{25,17},{1,25},{10,2},{18... | collective-permute-start | bytes 2359304 | tf_op jit(solution)/shard_map/ppermute | solution.py:428
  5.7 21.7 %collective-permute-start.4 = (f32[256,768]{1,0:T(8,128)}, f32[256,768]{1,0:T(8,128)S(1)}, u32[]{:S(2)}, u32[]{:S(2)}) collective-permute-start(f32[256,768]{1,0:T(8,128)} %rest_0_.1), channel_id=1, source_target_pairs={{2,0},{3,1},{0,2},{1,3},{6,4},{7,5},{4,6},{5,7},{10,8},{11,9},{8,1... | collective-permute-start | bytes 2359304 | tf_op jit(solution)/shard_map/ppermute | solution.py:441
  7.2 20.2 %collective-permute-start.5 = (f32[256,768]{1,0:T(8,128)}, f32[256,768]{1,0:T(8,128)S(1)}, u32[]{:S(2)}, u32[]{:S(2)}) collective-permute-start(f32[256,768]{1,0:T(8,128)} %rest_0_.1), channel_id=1, source_target_pairs={{4,0},{5,1},{6,2},{7,3},{0,4},{1,5},{2,6},{3,7},{12,8},{13,9},{14,... | collective-permute-start | bytes 2359304 | tf_op jit(solution)/shard_map/ppermute | solution.py:441
  11.2 29.0 %copy-start.10 = (f32[72,256]{1,0:T(8,128)}, f32[72,256]{1,0:T(8,128)S(1)}, u32[]{:S(2)}) copy-start(f32[72,256]{1,0:T(8,128)S(1)} %concatenate.12.rest_3_.rest_2_) | copy-start | bytes 221188
  11.2 14.0 %collective-permute-start.1 = (f32[72,256]{1,0:T(8,128)S(1)}, f32[72,256]{1,0:T(8,128)S(1)}, u32[]{:S(2)}, u32[]{:S(2)}) collective-permute-start(f32[72,256]{1,0:T(8,128)S(1)} %concatenate.12.rest_3_.rest_2_), channel_id=1, source_target_pairs={{8,0},{16,8},{24,16},{0,24},{9,1},{17,9},{25,17},{1,25},{10,2},{18... | collective-permute-start | bytes 221192 | tf_op jit(solution)/shard_map/ppermute | solution.py:428
  11.7 15.7 %collective-permute-start.2 = (f32[72,256]{1,0:T(8,128)S(1)}, f32[72,256]{1,0:T(8,128)S(1)}, u32[]{:S(2)}, u32[]{:S(2)}) collective-permute-start(f32[72,256]{1,0:T(8,128)S(1)} %concatenate.12.rest_3_.rest_2_), channel_id=1, source_target_pairs={{16,0},{24,8},{0,16},{8,24},{17,1},{25,9},{1,17},{9,25},{18,2},{26... | collective-permute-start | bytes 221192 | tf_op jit(solution)/shard_map/ppermute | solution.py:428
  25.2 15.1 %copy-start.14 = (f32[72,256]{1,0:T(8,128)}, f32[72,256]{1,0:T(8,128)S(1)}, u32[]{:S(2)}) copy-start(f32[72,256]{1,0:T(8,128)S(1)} %collective-permute-done.1.rest_4_.rest_3_) | copy-start | bytes 221188
  27.4 9.5 %collective-permute-start.3 = (f32[256,768]{1,0:T(8,128)}, f32[256,768]{1,0:T(8,128)}, u32[]{:S(2)}, u32[]{:S(2)}) collective-permute-start(f32[256,768]{1,0:T(8,128)} %rest_0_.1), channel_id=1, source_target_pairs={{1,0},{0,1},{3,2},{2,3},{5,4},{4,5},{7,6},{6,7},{9,8},{8,9},{11,10... | collective-permute-start | bytes 2359304 | tf_op jit(solution)/shard_map/ppermute | solution.py:441
  27.4 10.7 %collective-permute-start.6 = (f32[256,768]{1,0:T(8,128)S(1)}, f32[256,768]{1,0:T(8,128)}, u32[]{:S(2)}, u32[]{:S(2)}) collective-permute-start(f32[256,768]{1,0:T(8,128)S(1)} %collective-permute-done.4.rest_3_), channel_id=1, source_target_pairs={{1,0},{0,1},{3,2},{2,3},{5,4},{4,5},{7,6},{6,7},{9,8},{8,9},{11,10... | collective-permute-start | bytes 2359304 | tf_op jit(solution)/shard_map/ppermute | solution.py:441
  28.0 10.2 %collective-permute-start.7 = (f32[256,768]{1,0:T(8,128)S(1)}, f32[256,768]{1,0:T(8,128)}, u32[]{:S(2)}, u32[]{:S(2)}) collective-permute-start(f32[256,768]{1,0:T(8,128)S(1)} %collective-permute-done.5.rest_5_), channel_id=1, source_target_pairs={{1,0},{0,1},{3,2},{2,3},{5,4},{4,5},{7,6},{6,7},{9,8},{8,9},{11,10... | collective-permute-start | bytes 2359304 | tf_op jit(solution)/shard_map/ppermute | solution.py:441
  28.1 25.2 %collective-permute-start.9 = (f32[256,768]{1,0:T(8,128)}, f32[256,768]{1,0:T(8,128)}, u32[]{:S(2)}, u32[]{:S(2)}) collective-permute-start(f32[256,768]{1,0:T(8,128)} %rest_0_.1), channel_id=1, source_target_pairs={{6,0},{7,1},{4,2},{5,3},{2,4},{3,5},{0,6},{1,7},{14,8},{15,9},{12,... | collective-permute-start | bytes 2359304 | tf_op jit(solution)/shard_map/ppermute | solution.py:441
  34.1 19.8 %copy-start.21 = (s32[1,1,8,4]{2,3,1,0:T(4,128)S(1)}, s32[1,1,8,4]{2,3,1,0:T(4,128)}, u32[]{:S(2)}) copy-start(s32[1,1,8,4]{2,3,1,0:T(4,128)} %param.15) | copy-start | bytes 388
  36.9 22.9 %collective-permute-start.8 = (f32[256,768]{1,0:T(8,128)}, f32[256,768]{1,0:T(8,128)}, u32[]{:S(2)}, u32[]{:S(2)}) collective-permute-start(f32[256,768]{1,0:T(8,128)} %rest_0_.1), channel_id=1, source_target_pairs={{16,0},{8,24},{17,1},{9,25},{18,2},{10,26},{19,3},{11,27},{20,4},{... | collective-permute-start | bytes 2359304 | tf_op jit(solution)/shard_map/ppermute | solution.py:433
  38.2 13.5 %collective-permute-start.12 = (f32[72,256]{1,0:T(8,128)}, f32[72,256]{1,0:T(8,128)S(1)}, u32[]{:S(2)}, u32[]{:S(2)}) collective-permute-start(f32[72,256]{1,0:T(8,128)} %concatenate.13), channel_id=1, source_target_pairs={{6,0},{7,1},{4,2},{5,3},{2,4},{3,5},{0,6},{1,7},{14,8},{15,9},{12,... | collective-permute-start | bytes 221192 | tf_op jit(solution)/shard_map/ppermute | solution.py:441
  38.7 13.5 %collective-permute-start.11 = (f32[72,256]{1,0:T(8,128)}, f32[72,256]{1,0:T(8,128)S(1)}, u32[]{:S(2)}, u32[]{:S(2)}) collective-permute-start(f32[72,256]{1,0:T(8,128)} %concatenate.13), channel_id=1, source_target_pairs={{4,0},{5,1},{6,2},{7,3},{0,4},{1,5},{2,6},{3,7},{12,8},{13,9},{14,... | collective-permute-start | bytes 221192 | tf_op jit(solution)/shard_map/ppermute | solution.py:441
  40.2 12.1 %collective-permute-start.10 = (f32[72,256]{1,0:T(8,128)}, f32[72,256]{1,0:T(8,128)S(1)}, u32[]{:S(2)}, u32[]{:S(2)}) collective-permute-start(f32[72,256]{1,0:T(8,128)} %concatenate.13), channel_id=1, source_target_pairs={{2,0},{3,1},{0,2},{1,3},{6,4},{7,5},{4,6},{5,7},{10,8},{11,9},{8,1... | collective-permute-start | bytes 221192 | tf_op jit(solution)/shard_map/ppermute | solution.py:441
  53.3 6.6 %collective-permute-start.13 = (f32[256,768]{1,0:T(8,128)}, f32[256,768]{1,0:T(8,128)S(1)}, u32[]{:S(2)}, u32[]{:S(2)}) collective-permute-start(f32[256,768]{1,0:T(8,128)} %collective-permute-done.9.rest_1_), channel_id=1, source_target_pairs={{1,0},{0,1},{3,2},{2,3},{5,4},{4,5},{7,6},{6,7},{9,8},{8,9},{11,10... | collective-permute-start | bytes 2359304 | tf_op jit(solution)/shard_map/ppermute | solution.py:441
  53.3 6.5 %collective-permute-start.14 = (f32[4,72,256]{2,1,0:T(8,128)S(1)}, f32[4,72,256]{2,1,0:T(8,128)S(1)}, u32[]{:S(2)}, u32[]{:S(2)}) collective-permute-start(f32[4,72,256]{2,1,0:T(8,128)S(1)} %pad_maximum_fusion.rest_6_.rest_0_), channel_id=1, source_target_pairs={{1,0},{0,1},{3,2},{2,3},{5,4},{4,5},{7,6},{6,7},{9,8},{8,9},{11,10... | collective-permute-start | bytes 884744 | tf_op jit(solution)/shard_map/ppermute | solution.py:441
  54.0 19.8 %collective-permute-start.15 = (f32[64,256]{1,0:T(8,128)}, f32[64,256]{1,0:T(8,128)S(1)}, u32[]{:S(2)}, u32[]{:S(2)}) collective-permute-start(f32[64,256]{1,0:T(8,128)} %param.13), channel_id=1, source_target_pairs={{24,0},{0,8},{8,16},{16,24},{25,1},{1,9},{9,17},{17,25},{26,2},{2,... | collective-permute-start | bytes 196616 | tf_op jit(solution)/shard_map/ppermute | solution.py:428
  80.4 14.4 %copy-start.20 = (f32[64,256]{1,0:T(8,128)S(1)}, f32[64,256]{1,0:T(8,128)}, u32[]{:S(2)}) copy-start(f32[64,256]{1,0:T(8,128)} %param.13) | copy-start | bytes 196612
  80.4 13.3 %all-to-all-start = ((f32[8,64,256]{2,1,0:T(8,128)}), f32[8,64,256]{2,1,0:T(8,128)S(1)}, u32[]{:S(2)}, u32[]{:S(2)}) async-start(f32[8,64,256]{2,1,0:T(8,128)} %get-tuple-element.40), calls=%async_computation | async-start | bytes 1048576 | tf_op jit(solution)/shard_map/all_to_all | solution.py:501
  84.1 9.7 %collective-permute-start.18 = (f32[64,256]{1,0:T(8,128)S(1)}, f32[64,256]{1,0:T(8,128)S(1)}, u32[]{:S(2)}, u32[]{:S(2)}) collective-permute-start(f32[64,256]{1,0:T(8,128)S(1)} %get-tuple-element.44), channel_id=1, source_target_pairs={{0,24},{8,0},{16,8},{24,16},{1,25},{9,1},{17,9},{25,17},{2,26},{10... | collective-permute-start | bytes 196616 | tf_op jit(solution)/shard_map/ppermute | solution.py:437
  87.8 7.0 %collective-permute-start.17 = (f32[64,256]{1,0:T(8,128)S(1)}, f32[64,256]{1,0:T(8,128)S(1)}, u32[]{:S(2)}, u32[]{:S(2)}) collective-permute-start(f32[64,256]{1,0:T(8,128)S(1)} %get-tuple-element.43), channel_id=1, source_target_pairs={{0,16},{8,24},{16,0},{24,8},{1,17},{9,25},{17,1},{25,9},{2,18},{10... | collective-permute-start | bytes 196616 | tf_op jit(solution)/shard_map/ppermute | solution.py:437
  87.8 7.0 %collective-permute-start.16 = (f32[64,256]{1,0:T(8,128)S(1)}, f32[64,256]{1,0:T(8,128)S(1)}, u32[]{:S(2)}, u32[]{:S(2)}) collective-permute-start(f32[64,256]{1,0:T(8,128)S(1)} %get-tuple-element.42), channel_id=1, source_target_pairs={{0,8},{8,16},{16,24},{24,0},{1,9},{9,17},{17,25},{25,1},{2,10},{10... | collective-permute-start | bytes 196616 | tf_op jit(solution)/shard_map/ppermute | solution.py:437
  94.8 14.2 %collective-permute-start.19 = (f32[64,256]{1,0:T(8,128)S(1)}, f32[64,256]{1,0:T(8,128)S(1)}, u32[]{:S(2)}, u32[]{:S(2)}) collective-permute-start(f32[64,256]{1,0:T(8,128)S(1)} %multiply_add_fusion.1.rest_1_), channel_id=1, source_target_pairs={{8,0},{16,8},{24,16},{0,24},{9,1},{17,9},{25,17},{1,25},{10,2},{18... | collective-permute-start | bytes 196616 | tf_op jit(solution)/shard_map/ppermute | solution.py:428
  97.9 11.1 %collective-permute-start.20 = (f32[64,256]{1,0:T(8,128)S(1)}, f32[64,256]{1,0:T(8,128)S(1)}, u32[]{:S(2)}, u32[]{:S(2)}) collective-permute-start(f32[64,256]{1,0:T(8,128)S(1)} %multiply_add_fusion.1.rest_1_), channel_id=1, source_target_pairs={{16,0},{24,8},{0,16},{8,24},{17,1},{25,9},{1,17},{9,25},{18,2},{26... | collective-permute-start | bytes 196616 | tf_op jit(solution)/shard_map/ppermute | solution.py:428
  97.9 11.1 %collective-permute-start.21 = (f32[64,256]{1,0:T(8,128)S(1)}, f32[64,256]{1,0:T(8,128)S(1)}, u32[]{:S(2)}, u32[]{:S(2)}) collective-permute-start(f32[64,256]{1,0:T(8,128)S(1)} %multiply_add_fusion.1.rest_1_), channel_id=1, source_target_pairs={{24,0},{0,8},{8,16},{16,24},{25,1},{1,9},{9,17},{17,25},{26,2},{2,... | collective-permute-start | bytes 196616 | tf_op jit(solution)/shard_map/ppermute | solution.py:428
  115.6 13.2 %all-to-all-start.1 = ((f32[8,64,256]{2,1,0:T(8,128)}), f32[8,64,256]{2,1,0:T(8,128)S(1)}, u32[]{:S(2)}, u32[]{:S(2)}) async-start(f32[8,64,256]{2,1,0:T(8,128)} %get-tuple-element.45), calls=%async_computation.1 | async-start | bytes 1048576 | tf_op jit(solution)/shard_map/all_to_all | solution.py:501
  119.1 9.8 %collective-permute-start.24 = (f32[64,256]{1,0:T(8,128)S(1)}, f32[64,256]{1,0:T(8,128)S(1)}, u32[]{:S(2)}, u32[]{:S(2)}) collective-permute-start(f32[64,256]{1,0:T(8,128)S(1)} %get-tuple-element.49), channel_id=1, source_target_pairs={{0,24},{8,0},{16,8},{24,16},{1,25},{9,1},{17,9},{25,17},{2,26},{10... | collective-permute-start | bytes 196616 | tf_op jit(solution)/shard_map/ppermute | solution.py:437
  121.0 7.9 %collective-permute-start.23 = (f32[64,256]{1,0:T(8,128)S(1)}, f32[64,256]{1,0:T(8,128)S(1)}, u32[]{:S(2)}, u32[]{:S(2)}) collective-permute-start(f32[64,256]{1,0:T(8,128)S(1)} %get-tuple-element.48), channel_id=1, source_target_pairs={{0,16},{8,24},{16,0},{24,8},{1,17},{9,25},{17,1},{25,9},{2,18},{10... | collective-permute-start | bytes 196616 | tf_op jit(solution)/shard_map/ppermute | solution.py:437
  121.3 7.6 %collective-permute-start.22 = (f32[64,256]{1,0:T(8,128)S(1)}, f32[64,256]{1,0:T(8,128)S(1)}, u32[]{:S(2)}, u32[]{:S(2)}) collective-permute-start(f32[64,256]{1,0:T(8,128)S(1)} %get-tuple-element.47), channel_id=1, source_target_pairs={{0,8},{8,16},{16,24},{24,0},{1,9},{9,17},{17,25},{25,1},{2,10},{10... | collective-permute-start | bytes 196616 | tf_op jit(solution)/shard_map/ppermute | solution.py:437
  (17 other events, 38.5 us)

commit v7 on v5

--- a/solution.py
+++ b/solution.py
@@ -23,7 +23,6 @@
 PULL = 2 * D_EMB + 16
 UNROLL = 12
 F32, BF16, I32 = jnp.float32, jnp.bfloat16, jnp.int32
-VMEM_LIMIT = 44 * 2**20
 
 
 def split(value):
@@ -66,6 +65,10 @@
     start_i = pl.multiple_of(listing[2 * place] * BLK, BLK)
     start_j = pl.multiple_of(listing[2 * place + 1] * BLK, BLK)
     return start_i, start_j, place
+
+
+def vmem_limit(sizes):
+    return (8 + 2 * sizes[1]) * 2**20
 
 
 def gram_of(high_j, low_j, high_i, low_i):
@@ -115,7 +118,7 @@
             jax.ShapeDtypeStruct((rows_early, BLK, depth), BF16),
         ],
         scratch_shapes=[pltpu.VMEM((rows_early, SPAN, depth), BF16)] * 2,
-        compiler_params=pltpu.CompilerParams(vmem_limit_bytes=VMEM_LIMIT),
+        compiler_params=pltpu.CompilerParams(vmem_limit_bytes=vmem_limit(sizes)),
         cost_estimate=pl.CostEstimate(
             flops=tiles * 6 * BLK * BLK * depth,
             bytes_accessed=(shifts_early + rows_early) * SPAN * depth * 4,
@@ -225,7 +228,7 @@
             pltpu.VMEM((shifts, CB, BLK, 8), F32),
             pltpu.VMEM((col_count, 8, SPAN), F32),
         ],
-        compiler_params=pltpu.CompilerParams(vmem_limit_bytes=VMEM_LIMIT),
+        compiler_params=pltpu.CompilerParams(vmem_limit_bytes=vmem_limit(sizes)),
         cost_estimate=pl.CostEstimate(
             flops=tiles * 3 * BLK * BLK * depth,
             bytes_accessed=(1 + rows_late) * SPAN * depth * 4,
@@ -395,7 +398,7 @@
             pltpu.VMEM((UNROLL, 2 * BLK, BLK), BF16),
             pltpu.VMEM((UNROLL, BLK, 2 * BLK), BF16),
         ],
-        compiler_params=pltpu.CompilerParams(vmem_limit_bytes=VMEM_LIMIT),
+        compiler_params=pltpu.CompilerParams(vmem_limit_bytes=vmem_limit(sizes)),
         cost_estimate=pl.CostEstimate(
             flops=tiles * 2 * BLK * BLK * (STACK + 4 * PULL),
             bytes_accessed=4 * D_EMB * SPAN * 2 * (col_count + row_count),
@@ -450,17 +453,22 @@
     for bits in late_bits:
         if bits % 2 == 0:
             row_x[bits] = from_bits(inputs, bits)
-    far_seeds = [from_shift(seeds, shift) for shift in range(1, shifts)]
-    row_x[1] = from_bits(after(inputs, *far_seeds), 1)
+    seed_row = jnp.pad(seeds.astype(F32)[None], ((0, 0), (0, SPAN - seeds.shape[0])))
+    params = jnp.stack([rho, sigma, jnp.sum(inputs * inputs, axis=1)])
+    blank = jnp.zeros((PACK - SEEDS - 1, SPAN), F32)
+    pack = jnp.concatenate([embed, params, seed_row, blank], axis=0)
+    col_packs = [pack] + [from_shift(pack, shift) for shift in range(1, shifts)]
+    held, meta, listing, seeds = lax.optimization_barrier((inputs, meta, listing, seeds, *col_packs[1:]))[:4]
+    row_x[1] = from_bits(held, 1)
     for bits in single:
         row_x[bits + 1] = from_bits(after(row_x[bits], *near), 1)
     col_x.append(from_half(after(inputs, row_x[1])))
 
-    squares = jnp.sum(inputs * inputs, axis=1)
-    seed_rows = jnp.pad(
-        jnp.stack([seeds, *far_seeds]).astype(F32), ((0, PACK - SEEDS - shifts), (0, SPAN - seeds.shape[0]))
-    )
-    own_pack = jnp.concatenate([embed, jnp.stack([rho, sigma, squares]), seed_rows], axis=0)
+    own_pack = pack
+    for shift in range(1, shifts):
+        place = SEEDS + shift
+        far_seed = col_packs[shift][SEEDS : SEEDS + 1]
+        own_pack = own_pack + jnp.pad(far_seed, ((place, PACK - place - 1), (0, 0)))
     own_pack = after(own_pack, *[row_x[bits + 1] for bits in single])
     early = early_grams(sizes, meta, listing, col_x[:-1], [row_x[bits] for bits in early_bits[1:]])
     even_packs = jnp.stack([own_pack] + [from_bits(own_pack, bits) for bits in range(2, col_count, 2)])
@@ -469,9 +477,8 @@
     for bits in late_bits:
         if bits % 2 == 0:
             row_x[bits + 1] = from_bits(after(row_x[bits], even_packs), 1)
-    held = after(own_pack, *[row_x[bits] for bits in late_bits if bits % 2 == 0])
-    col_packs = [own_pack] + [from_shift(held, shift) for shift in range(1, row_count)]
-    col_y = col_packs
+    held = after(embed, *[row_x[bits] for bits in late_bits if bits % 2 == 0])
+    col_y = col_packs + [from_shift(held, shift) for shift in range(shifts, row_count)]
 
     weights = pair_weights(
         sizes,
@@ -481,14 +488,15 @@
         early,
         col_x[-1],
         [row_x[bits] for bits in late_bits],
-        col_packs[:shifts] + [even_packs, odd_packs],
+        col_packs + [even_packs, odd_packs],
     )
 
     row_y = (even_packs, odd_packs)
     for step in range(STEPS):
         if step:
-            row_y = (lax.all_gather(embed, "col", axis=0, tiled=False),)
             col_y = [embed] + [from_shift(embed, shift) for shift in range(1, row_count)]
+            even = jnp.stack([embed] + [from_bits(embed, bits) for bits in range(2, col_count, 2)])
+            row_y = (even, from_bits(even, 1))
         row_force, col_force = pair_forces(sizes, meta, listing, row_list, col_list, weights, row_y, col_y)
         row_parts = lax.all_to_all(row_force, "col", split_axis=0, concat_axis=0, tiled=True)
         force = jnp.sum(row_parts, axis=0) + col_force[0]

time: 121 us -> 119 us (0.983); the launches traced: 120 us -> 120 us
  starting transfers between devices: 37.4 us -> 47.6 us
  blocking collectives: 10.2 us -> 0 us
  Pallas kernels: 21.6 us -> 18.3 us
  waiting for transfers between devices: 43.1 us -> 45.3 us
    all_gather x1 -> x0, blocking collectives: 10.2 us -> none  [shards(): row_y = (lax.all_gather(embed, 'col', axis=0, tiled=False),)]
    all_to_all x2, waiting for transfers between devices: 13.8 us -> 6.66 us  [shards(): lax.all_to_all(row_force, 'col', split_axis=0, concat_axis=0, tiled=True)]
    ppermute x6, starting transfers between devices: 5.65 us -> 12.8 us  [to_shift(): return lax.ppermute(value, 'row', pairs)]
    ppermute x11 -> x15, waiting for transfers between devices: 11.1 us -> 17.3 us  [from_bits(): return lax.ppermute(value, 'col', pairs)]
    ppermute x11 -> x15, starting transfers between devices: 9.14 us -> 13.8 us  [from_bits(): return lax.ppermute(value, 'col', pairs)]
    ppermute x6, waiting for transfers between devices: 0.02 us -> 4.09 us  [to_shift(): return lax.ppermute(value, 'row', pairs)]
    ppermute x1, waiting for transfers between devices: 3.16 us -> 0.01 us  [from_half(): return lax.ppermute(value, 'row', pairs)]
    ppermute x9 -> x7, waiting for transfers between devices: 15 us -> 17.3 us  [from_shift(): return lax.ppermute(value, 'row', pairs)]
  transfers between devices with their start and end apart: 29 -> 31, of which waited for: 10 -> 16; matrix products, arithmetic and copies ran while one was open for 4% -> 5% of each run, Pallas kernels for 9% -> 7%
where the time goes in v7:
time: 119 us; the launch traced here: 120 us
  starting transfers between devices  47.6 us (40%)
  waiting for transfers between devices  45.3 us (38%)
  Pallas kernels  18.3 us (15%)
  local copies, waits for them, and re-layouts  3.5 us (3%)
  other arithmetic  3.48 us (3%)
  between operations  1.47 us (1%)
    ppermute x7, waiting for transfers between devices, from_shift(): return lax.ppermute(value, 'row', pairs)  17.3 us
    ppermute x15, waiting for transfers between devices, from_bits(): return lax.ppermute(value, 'col', pairs)  17.3 us
    ppermute x15, starting transfers between devices, from_bits(): return lax.ppermute(value, 'col', pairs)  13.8 us
    ppermute x6, starting transfers between devices, to_shift(): return lax.ppermute(value, 'row', pairs)  12.8 us
    ppermute x7, starting transfers between devices, from_shift(): return lax.ppermute(value, 'row', pairs)  11.5 us
    pallas_call x2, Pallas kernels, pair_forces(): pl.pallas_call(functools.partial(force_kernel, row_count, col_count, len(...  9.71 us
    all_to_all x2, starting transfers between devices, shards(): lax.all_to_all(row_force, 'col', split_axis=0, concat_axis=0, tiled=True)  8.27 us
    all_to_all x2, waiting for transfers between devices, shards(): lax.all_to_all(row_force, 'col', split_axis=0, concat_axis=0, tiled=True)  6.66 us
  transfers between devices with their start and end apart: 31, of which 16 were waited for; matrix products, arithmetic and copies ran while one was open for 5% of the time, Pallas kernels for 7%

profile of v7, /device:TPU:0, one launch (start us, length us, event | category | flops | bytes accessed | tf_op | source)
XLA Modules:
  0.0 119.7 jit_solution(2737819337484060847)
XLA Ops:
  0.6 5.1 %collective-permute-start.2 = (f32[256,768]{1,0:T(8,128)}, f32[256,768]{1,0:T(8,128)S(1)}, u32[]{:S(2)}, u32[]{:S(2)}) collective-permute-start(f32[256,768]{1,0:T(8,128)} %rest_0_.1), channel_id=1, source_target_pairs={{8,0},{16,8},{24,16},{0,24},{9,1},{17,9},{25,17},{1,25},{10,2},{18... | collective-permute-start | bytes 2359304 | tf_op jit(solution)/shard_map/ppermute | solution.py:424
  5.7 1.5 %collective-permute-start.4 = (f32[256,768]{1,0:T(8,128)}, f32[256,768]{1,0:T(8,128)S(1)}, u32[]{:S(2)}, u32[]{:S(2)}) collective-permute-start(f32[256,768]{1,0:T(8,128)} %rest_0_.1), channel_id=1, source_target_pairs={{2,0},{3,1},{0,2},{1,3},{6,4},{7,5},{4,6},{5,7},{10,8},{11,9},{8,1... | collective-permute-start | bytes 2359304 | tf_op jit(solution)/shard_map/ppermute | solution.py:437
  7.2 1.5 %collective-permute-start.5 = (f32[256,768]{1,0:T(8,128)}, f32[256,768]{1,0:T(8,128)S(1)}, u32[]{:S(2)}, u32[]{:S(2)}) collective-permute-start(f32[256,768]{1,0:T(8,128)} %rest_0_.1), channel_id=1, source_target_pairs={{4,0},{5,1},{6,2},{7,3},{0,4},{1,5},{2,6},{3,7},{12,8},{13,9},{14,... | collective-permute-start | bytes 2359304 | tf_op jit(solution)/shard_map/ppermute | solution.py:437
  9.6 1.3 %multiply_reduce_fusion = f32[256]{0:T(256)S(1)} fusion(f32[256,768]{1,0:T(8,128)} %rest_0_.1), kind=kLoop, calls=%fused_computation | loop fusion | flops 392960 | bytes 787456 | tf_op jit(solution)/shard_map/reduce_sum | solution.py:457
  10.9 1.6 %concatenate.7.rest_3_.rest_2_ = f32[72,256]{1,0:T(8,128)S(1)} concatenate(f32[64,256]{1,0:T(8,128)} %param.13, f32[1,256]{1,0:T(1,128)} %bitcast.34, f32[1,256]{1,0:T(1,128)} %bitcast.35, f32[1,256]{1,0:T(1,128)S(1)} %bitcast.33, f32[1,256]{1,0:T(1,128)S(1)} %pad.12, f32[4,256]{1,0:T(4,128)S(1)} %broadcast_in_dim.4), dimensions={0} | concatenate | bytes 147456 | tf_op jit(solution)/shard_map/concatenate | solution.py:459
  15.4 9.7 %collective-permute-done.rest_4_.rest_3_ = f32[72,256]{1,0:T(8,128)S(1)} collective-permute-done((f32[72,256]{1,0:T(8,128)S(1)}, f32[72,256]{1,0:T(8,128)S(1)}, u32[]{:S(2)}, u32[]{:S(2)}) %collective-permute-start) | collective-permute-done | bytes 73760 | tf_op jit(solution)/shard_map/ppermute | solution.py:424
  25.2 2.2 %collective-permute-done.1.rest_5_.rest_4_ = f32[72,256]{1,0:T(8,128)S(1)} collective-permute-done((f32[72,256]{1,0:T(8,128)S(1)}, f32[72,256]{1,0:T(8,128)S(1)}, u32[]{:S(2)}, u32[]{:S(2)}) %collective-permute-start.1) | collective-permute-done | bytes 73760 | tf_op jit(solution)/shard_map/ppermute | solution.py:424
  28.1 2.4 %collective-permute-start.9 = (f32[256,768]{1,0:T(8,128)}, f32[256,768]{1,0:T(8,128)S(1)}, u32[]{:S(2)}, u32[]{:S(2)}) collective-permute-start(f32[256,768]{1,0:T(8,128)} %rest_0_.1), channel_id=1, source_target_pairs={{6,0},{7,1},{4,2},{5,3},{2,4},{3,5},{0,6},{1,7},{14,8},{15,9},{12,... | collective-permute-start | bytes 2359304 | tf_op jit(solution)/shard_map/ppermute | solution.py:437
  30.6 1.3 %collective-permute-start.8 = (f32[256,768]{1,0:T(8,128)S(1)}, f32[256,768]{1,0:T(8,128)S(1)}, u32[]{:S(2)}, u32[]{:S(2)}) collective-permute-start(f32[256,768]{1,0:T(8,128)S(1)} %copy-done), channel_id=1, source_target_pairs={{16,0},{8,24},{17,1},{9,25},{18,2},{10,26},{19,3},{11,27},{20,4},{... | collective-permute-start | bytes 2359304 | tf_op jit(solution)/shard_map/ppermute | solution.py:429
  31.9 2.4 %collective-permute-start.12 = (f32[72,256]{1,0:T(8,128)S(1)}, f32[72,256]{1,0:T(8,128)S(1)}, u32[]{:S(2)}, u32[]{:S(2)}) collective-permute-start(f32[72,256]{1,0:T(8,128)S(1)} %pad_add_fusion), channel_id=1, source_target_pairs={{6,0},{7,1},{4,2},{5,3},{2,4},{3,5},{0,6},{1,7},{14,8},{15,9},{12,... | collective-permute-start | bytes 221192 | tf_op jit(solution)/shard_map/ppermute | solution.py:437
  35.4 4.0 %grams.1 = (f32[6,2,128,128]{3,2,1,0:T(8,128)S(1)}, bf16[2,256,768]{2,1,0:T(8,128)(2,1)S(1)}, bf16[2,256,768]{2,1,0:T(8,128)(2,1)S(1)}, bf16[6,128,768]{2,1,0:T(8,128)(2,1)S(1)}, bf16[6,128,768]{2,1,0:T(8,128)(2,1)S(1)}) custom-call(s32[11]{0:T(128)S(1)} %pad_add_fusion.1.meta, s32[64]{0:T(128)S(1)} %reshape.27.listing, f32[256,768]{1,0:T(8,128)S(1)} %copy-done, ...), custom_call_target="tpu_custom_call" | custom-call | flops 905969664 | bytes 6291456 | tf_op jit(solution)/shard_map/grams/pallas_call | solution.py:109
  39.4 11.7 %collective-permute-done.12 = f32[72,256]{1,0:T(8,128)S(1)} collective-permute-done((f32[72,256]{1,0:T(8,128)S(1)}, f32[72,256]{1,0:T(8,128)S(1)}, u32[]{:S(2)}, u32[]{:S(2)}) %collective-permute-start.12) | collective-permute-done | bytes 73760 | tf_op jit(solution)/shard_map/ppermute | solution.py:437
  52.9 1.6 %collective-permute-start.15 = (f32[64,256]{1,0:T(8,128)S(1)}, f32[64,256]{1,0:T(8,128)S(1)}, u32[]{:S(2)}, u32[]{:S(2)}) collective-permute-start(f32[64,256]{1,0:T(8,128)S(1)} %copy-done.3), channel_id=1, source_target_pairs={{24,0},{0,8},{8,16},{16,24},{25,1},{1,9},{9,17},{17,25},{26,2},{2,... | collective-permute-start | bytes 196616 | tf_op jit(solution)/shard_map/ppermute | solution.py:424
  55.1 4.6 %weights.1 = bf16[24,128,128]{2,1,0:T(8,128)(2,1)S(1)} custom-call(s32[11]{0:T(128)S(1)} %pad_add_fusion.1.meta, s32[64]{0:T(128)S(1)} %reshape.27.listing, s32[32]{0:T(128)S(1)} %reshape.28.seeds, f32[6,2,128,128]{3,2,1,0:T(8,128)S(1)} %get-tuple-element.34.grams, bf16[2,256,768]{2,1,0:T(8,128)(2,1)S(1)} %get-tuple-element.35.high_c, ...), custom_call_target="tpu_custom_call" | custom-call | flops 905969664 | bytes 2359296 | tf_op jit(solution)/shard_map/weights/pallas_call | solution.py:217
  59.8 4.9 %forces.2 = (f32[8,64,256]{2,1,0:T(8,128)}, f32[64,256]{1,0:T(8,128)S(1)}, f32[64,256]{1,0:T(8,128)S(1)}, f32[64,256]{1,0:T(8,128)S(1)}, f32[64,256]{1,0:T(8,128)S(1)}) custom-call(s32[11]{0:T(128)S(1)} %pad_add_fusion.1.meta, s32[64]{0:T(128)S(1)} %reshape.27.listing, s32[48]{0:T(128)S(1)} %bitcast.22, s32[48]{0:T(128)S(1)} %bitcast.24, ...), custom_call_target="tpu_custom_call" | custom-call | flops 1744830464 | bytes 1572864 | tf_op jit(solution)/shard_map/forces/pallas_call | solution.py:385
  64.6 4.5 %all-to-all-start = ((f32[8,64,256]{2,1,0:T(8,128)}), f32[8,64,256]{2,1,0:T(8,128)S(1)}, u32[]{:S(2)}, u32[]{:S(2)}) async-start(f32[8,64,256]{2,1,0:T(8,128)} %get-tuple-element.44), calls=%async_computation | async-start | bytes 1048576 | tf_op jit(solution)/shard_map/all_to_all | solution.py:501
  69.1 5.1 %collective-permute-start.18 = (f32[64,256]{1,0:T(8,128)S(1)}, f32[64,256]{1,0:T(8,128)S(1)}, u32[]{:S(2)}, u32[]{:S(2)}) collective-permute-start(f32[64,256]{1,0:T(8,128)S(1)} %get-tuple-element.48), channel_id=1, source_target_pairs={{0,24},{8,0},{16,8},{24,16},{1,25},{9,1},{17,9},{25,17},{2,26},{10... | collective-permute-start | bytes 196616 | tf_op jit(solution)/shard_map/ppermute | solution.py:433
  74.3 1.4 %collective-permute-start.16 = (f32[64,256]{1,0:T(8,128)S(1)}, f32[64,256]{1,0:T(8,128)S(1)}, u32[]{:S(2)}, u32[]{:S(2)}) collective-permute-start(f32[64,256]{1,0:T(8,128)S(1)} %get-tuple-element.46), channel_id=1, source_target_pairs={{0,8},{8,16},{16,24},{24,0},{1,9},{9,17},{17,25},{25,1},{2,10},{10... | collective-permute-start | bytes 196616 | tf_op jit(solution)/shard_map/ppermute | solution.py:433
  75.7 3.2 %all-to-all-done = f32[8,64,256]{2,1,0:T(8,128)S(1)} async-done(((f32[8,64,256]{2,1,0:T(8,128)}), f32[8,64,256]{2,1,0:T(8,128)S(1)}, u32[]{:S(2)}, u32[]{:S(2)}) %all-to-all-start) | async-done | bytes 524320 | tf_op jit(solution)/shard_map/all_to_all | solution.py:501
  78.9 2.8 %collective-permute-done.17 = f32[64,256]{1,0:T(8,128)S(1)} collective-permute-done((f32[64,256]{1,0:T(8,128)S(1)}, f32[64,256]{1,0:T(8,128)S(1)}, u32[]{:S(2)}, u32[]{:S(2)}) %collective-permute-start.17) | collective-permute-done | bytes 65568 | tf_op jit(solution)/shard_map/ppermute | solution.py:433
  81.8 2.4 %collective-permute-start.21 = (f32[64,256]{1,0:T(8,128)S(1)}, f32[64,256]{1,0:T(8,128)S(1)}, u32[]{:S(2)}, u32[]{:S(2)}) collective-permute-start(f32[64,256]{1,0:T(8,128)S(1)} %multiply_add_fusion.1.rest_2_), channel_id=1, source_target_pairs={{6,0},{7,1},{4,2},{5,3},{2,4},{3,5},{0,6},{1,7},{14,8},{15,9},{12,... | collective-permute-start | bytes 196616 | tf_op jit(solution)/shard_map/ppermute | solution.py:437
  85.4 1.8 %collective-permute-done.21 = f32[64,256]{1,0:T(8,128)S(1)} collective-permute-done((f32[64,256]{1,0:T(8,128)S(1)}, f32[64,256]{1,0:T(8,128)S(1)}, u32[]{:S(2)}, u32[]{:S(2)}) %collective-permute-start.21) | collective-permute-done | bytes 65568 | tf_op jit(solution)/shard_map/ppermute | solution.py:437
  87.1 1.4 %collective-permute-done.20 = f32[64,256]{1,0:T(8,128)S(1)} collective-permute-done((f32[64,256]{1,0:T(8,128)S(1)}, f32[64,256]{1,0:T(8,128)S(1)}, u32[]{:S(2)}, u32[]{:S(2)}) %collective-permute-start.20) | collective-permute-done | bytes 65568 | tf_op jit(solution)/shard_map/ppermute | solution.py:437
  89.2 2.0 %collective-permute-start.23 = (f32[64,256]{1,0:T(8,128)S(1)}, f32[64,256]{1,0:T(8,128)S(1)}, u32[]{:S(2)}, u32[]{:S(2)}) collective-permute-start(f32[64,256]{1,0:T(8,128)S(1)} %multiply_add_fusion.1.rest_2_), channel_id=1, source_target_pairs={{8,0},{16,8},{24,16},{0,24},{9,1},{17,9},{25,17},{1,25},{10,2},{18... | collective-permute-start | bytes 196616 | tf_op jit(solution)/shard_map/ppermute | solution.py:424
  91.5 1.9 %collective-permute-start.25 = (f32[64,256]{1,0:T(8,128)S(1)}, f32[64,256]{1,0:T(8,128)S(1)}, u32[]{:S(2)}, u32[]{:S(2)}) collective-permute-start(f32[64,256]{1,0:T(8,128)S(1)} %multiply_add_fusion.1.rest_2_), channel_id=1, source_target_pairs={{24,0},{0,8},{8,16},{16,24},{25,1},{1,9},{9,17},{17,25},{26,2},{2,... | collective-permute-start | bytes 196616 | tf_op jit(solution)/shard_map/ppermute | solution.py:424
  93.7 5.1 %collective-permute-done.24.rest_4_ = f32[64,256]{1,0:T(8,128)S(1)} collective-permute-done((f32[64,256]{1,0:T(8,128)S(1)}, f32[64,256]{1,0:T(8,128)S(1)}, u32[]{:S(2)}, u32[]{:S(2)}) %collective-permute-start.24) | collective-permute-done | bytes 65568 | tf_op jit(solution)/shard_map/ppermute | solution.py:424
  98.8 4.8 %forces.3 = (f32[8,64,256]{2,1,0:T(8,128)}, f32[64,256]{1,0:T(8,128)S(1)}, f32[64,256]{1,0:T(8,128)S(1)}, f32[64,256]{1,0:T(8,128)S(1)}, f32[64,256]{1,0:T(8,128)S(1)}) custom-call(s32[11]{0:T(128)S(1)} %pad_add_fusion.1.meta, s32[64]{0:T(128)S(1)} %reshape.27.listing, s32[48]{0:T(128)S(1)} %bitcast.23, s32[48]{0:T(128)S(1)} %bitcast.25, ...), custom_call_target="tpu_custom_call" | custom-call | flops 1744830464 | bytes 1572864 | tf_op jit(solution)/shard_map/forces/pallas_call | solution.py:385
  103.6 3.7 %all-to-all-start.1 = ((f32[8,64,256]{2,1,0:T(8,128)}), f32[8,64,256]{2,1,0:T(8,128)S(1)}, u32[]{:S(2)}, u32[]{:S(2)}) async-start(f32[8,64,256]{2,1,0:T(8,128)} %get-tuple-element.49), calls=%async_computation.1 | async-start | bytes 1048576 | tf_op jit(solution)/shard_map/all_to_all | solution.py:501
  107.4 2.9 %collective-permute-start.28 = (f32[64,256]{1,0:T(8,128)S(1)}, f32[64,256]{1,0:T(8,128)S(1)}, u32[]{:S(2)}, u32[]{:S(2)}) collective-permute-start(f32[64,256]{1,0:T(8,128)S(1)} %get-tuple-element.53), channel_id=1, source_target_pairs={{0,24},{8,0},{16,8},{24,16},{1,25},{9,1},{17,9},{25,17},{2,26},{10... | collective-permute-start | bytes 196616 | tf_op jit(solution)/shard_map/ppermute | solution.py:433
  110.3 1.4 %collective-permute-start.27 = (f32[64,256]{1,0:T(8,128)S(1)}, f32[64,256]{1,0:T(8,128)S(1)}, u32[]{:S(2)}, u32[]{:S(2)}) collective-permute-start(f32[64,256]{1,0:T(8,128)S(1)} %get-tuple-element.52), channel_id=1, source_target_pairs={{0,16},{8,24},{16,0},{24,8},{1,17},{9,25},{17,1},{25,9},{2,18},{10... | collective-permute-start | bytes 196616 | tf_op jit(solution)/shard_map/ppermute | solution.py:433
  111.7 1.9 %collective-permute-start.26 = (f32[64,256]{1,0:T(8,128)S(1)}, f32[64,256]{1,0:T(8,128)S(1)}, u32[]{:S(2)}, u32[]{:S(2)}) collective-permute-start(f32[64,256]{1,0:T(8,128)S(1)} %get-tuple-element.51), channel_id=1, source_target_pairs={{0,8},{8,16},{16,24},{24,0},{1,9},{9,17},{17,25},{25,1},{2,10},{10... | collective-permute-start | bytes 196616 | tf_op jit(solution)/shard_map/ppermute | solution.py:433
  113.6 3.5 %all-to-all-done.1 = f32[8,64,256]{2,1,0:T(8,128)S(1)} async-done(((f32[8,64,256]{2,1,0:T(8,128)}), f32[8,64,256]{2,1,0:T(8,128)S(1)}, u32[]{:S(2)}, u32[]{:S(2)}) %all-to-all-start.1) | async-done | bytes 524320 | tf_op jit(solution)/shard_map/all_to_all | solution.py:501
  (65 shorter events, 12.3 us)
Async XLA Ops:
  0.6 29.9 %copy-start = (f32[256,768]{1,0:T(8,128)S(1)}, f32[256,768]{1,0:T(8,128)}, u32[]{:S(2)}) copy-start(f32[256,768]{1,0:T(8,128)} %rest_0_.1) | copy-start | bytes 2359300
  0.6 26.8 %collective-permute-start.2 = (f32[256,768]{1,0:T(8,128)}, f32[256,768]{1,0:T(8,128)S(1)}, u32[]{:S(2)}, u32[]{:S(2)}) collective-permute-start(f32[256,768]{1,0:T(8,128)} %rest_0_.1), channel_id=1, source_target_pairs={{8,0},{16,8},{24,16},{0,24},{9,1},{17,9},{25,17},{1,25},{10,2},{18... | collective-permute-start | bytes 2359304 | tf_op jit(solution)/shard_map/ppermute | solution.py:424
  5.7 21.7 %collective-permute-start.4 = (f32[256,768]{1,0:T(8,128)}, f32[256,768]{1,0:T(8,128)S(1)}, u32[]{:S(2)}, u32[]{:S(2)}) collective-permute-start(f32[256,768]{1,0:T(8,128)} %rest_0_.1), channel_id=1, source_target_pairs={{2,0},{3,1},{0,2},{1,3},{6,4},{7,5},{4,6},{5,7},{10,8},{11,9},{8,1... | collective-permute-start | bytes 2359304 | tf_op jit(solution)/shard_map/ppermute | solution.py:437
  7.2 20.2 %collective-permute-start.5 = (f32[256,768]{1,0:T(8,128)}, f32[256,768]{1,0:T(8,128)S(1)}, u32[]{:S(2)}, u32[]{:S(2)}) collective-permute-start(f32[256,768]{1,0:T(8,128)} %rest_0_.1), channel_id=1, source_target_pairs={{4,0},{5,1},{6,2},{7,3},{0,4},{1,5},{2,6},{3,7},{12,8},{13,9},{14,... | collective-permute-start | bytes 2359304 | tf_op jit(solution)/shard_map/ppermute | solution.py:437
  12.4 12.7 %collective-permute-start = (f32[72,256]{1,0:T(8,128)S(1)}, f32[72,256]{1,0:T(8,128)S(1)}, u32[]{:S(2)}, u32[]{:S(2)}) collective-permute-start(f32[72,256]{1,0:T(8,128)S(1)} %concatenate.7.rest_3_.rest_2_), channel_id=1, source_target_pairs={{8,0},{16,8},{24,16},{0,24},{9,1},{17,9},{25,17},{1,25},{10,2},{18... | collective-permute-start | bytes 221192 | tf_op jit(solution)/shard_map/ppermute | solution.py:424
  12.9 14.4 %collective-permute-start.1 = (f32[72,256]{1,0:T(8,128)S(1)}, f32[72,256]{1,0:T(8,128)S(1)}, u32[]{:S(2)}, u32[]{:S(2)}) collective-permute-start(f32[72,256]{1,0:T(8,128)S(1)} %concatenate.7.rest_3_.rest_2_), channel_id=1, source_target_pairs={{16,0},{24,8},{0,16},{8,24},{17,1},{25,9},{1,17},{9,25},{18,2},{26... | collective-permute-start | bytes 221192 | tf_op jit(solution)/shard_map/ppermute | solution.py:424
  27.4 3.2 %collective-permute-start.3 = (f32[256,768]{1,0:T(8,128)}, f32[256,768]{1,0:T(8,128)S(1)}, u32[]{:S(2)}, u32[]{:S(2)}) collective-permute-start(f32[256,768]{1,0:T(8,128)} %rest_0_.1), channel_id=1, source_target_pairs={{1,0},{0,1},{3,2},{2,3},{5,4},{4,5},{7,6},{6,7},{9,8},{8,9},{11,10... | collective-permute-start | bytes 2359304 | tf_op jit(solution)/shard_map/ppermute | solution.py:437
  27.4 4.4 %collective-permute-start.6 = (f32[256,768]{1,0:T(8,128)S(1)}, f32[256,768]{1,0:T(8,128)S(1)}, u32[]{:S(2)}, u32[]{:S(2)}) collective-permute-start(f32[256,768]{1,0:T(8,128)S(1)} %collective-permute-done.4.rest_3_), channel_id=1, source_target_pairs={{1,0},{0,1},{3,2},{2,3},{5,4},{4,5},{7,6},{6,7},{9,8},{8,9},{11,10... | collective-permute-start | bytes 2359304 | tf_op jit(solution)/shard_map/ppermute | solution.py:437
  28.0 3.9 %collective-permute-start.7 = (f32[256,768]{1,0:T(8,128)S(1)}, f32[256,768]{1,0:T(8,128)S(1)}, u32[]{:S(2)}, u32[]{:S(2)}) collective-permute-start(f32[256,768]{1,0:T(8,128)S(1)} %collective-permute-done.5.rest_5_), channel_id=1, source_target_pairs={{1,0},{0,1},{3,2},{2,3},{5,4},{4,5},{7,6},{6,7},{9,8},{8,9},{11,10... | collective-permute-start | bytes 2359304 | tf_op jit(solution)/shard_map/ppermute | solution.py:437
  28.1 24.3 %collective-permute-start.9 = (f32[256,768]{1,0:T(8,128)}, f32[256,768]{1,0:T(8,128)S(1)}, u32[]{:S(2)}, u32[]{:S(2)}) collective-permute-start(f32[256,768]{1,0:T(8,128)} %rest_0_.1), channel_id=1, source_target_pairs={{6,0},{7,1},{4,2},{5,3},{2,4},{3,5},{0,6},{1,7},{14,8},{15,9},{12,... | collective-permute-start | bytes 2359304 | tf_op jit(solution)/shard_map/ppermute | solution.py:437
  30.6 23.9 %collective-permute-start.8 = (f32[256,768]{1,0:T(8,128)S(1)}, f32[256,768]{1,0:T(8,128)S(1)}, u32[]{:S(2)}, u32[]{:S(2)}) collective-permute-start(f32[256,768]{1,0:T(8,128)S(1)} %copy-done), channel_id=1, source_target_pairs={{16,0},{8,24},{17,1},{9,25},{18,2},{10,26},{19,3},{11,27},{20,4},{... | collective-permute-start | bytes 2359304 | tf_op jit(solution)/shard_map/ppermute | solution.py:429
  31.9 19.2 %collective-permute-start.12 = (f32[72,256]{1,0:T(8,128)S(1)}, f32[72,256]{1,0:T(8,128)S(1)}, u32[]{:S(2)}, u32[]{:S(2)}) collective-permute-start(f32[72,256]{1,0:T(8,128)S(1)} %pad_add_fusion), channel_id=1, source_target_pairs={{6,0},{7,1},{4,2},{5,3},{2,4},{3,5},{0,6},{1,7},{14,8},{15,9},{12,... | collective-permute-start | bytes 221192 | tf_op jit(solution)/shard_map/ppermute | solution.py:437
  34.4 17.8 %collective-permute-start.11 = (f32[72,256]{1,0:T(8,128)S(1)}, f32[72,256]{1,0:T(8,128)S(1)}, u32[]{:S(2)}, u32[]{:S(2)}) collective-permute-start(f32[72,256]{1,0:T(8,128)S(1)} %pad_add_fusion), channel_id=1, source_target_pairs={{4,0},{5,1},{6,2},{7,3},{0,4},{1,5},{2,6},{3,7},{12,8},{13,9},{14,... | collective-permute-start | bytes 221192 | tf_op jit(solution)/shard_map/ppermute | solution.py:437
  34.9 17.4 %collective-permute-start.10 = (f32[72,256]{1,0:T(8,128)S(1)}, f32[72,256]{1,0:T(8,128)S(1)}, u32[]{:S(2)}, u32[]{:S(2)}) collective-permute-start(f32[72,256]{1,0:T(8,128)S(1)} %pad_add_fusion), channel_id=1, source_target_pairs={{2,0},{3,1},{0,2},{1,3},{6,4},{7,5},{4,6},{5,7},{10,8},{11,9},{8,1... | collective-permute-start | bytes 221192 | tf_op jit(solution)/shard_map/ppermute | solution.py:437
  52.3 2.8 %collective-permute-start.13 = (f32[256,768]{1,0:T(8,128)S(1)}, f32[256,768]{1,0:T(8,128)S(1)}, u32[]{:S(2)}, u32[]{:S(2)}) collective-permute-start(f32[256,768]{1,0:T(8,128)S(1)} %collective-permute-done.9.rest_1_), channel_id=1, source_target_pairs={{1,0},{0,1},{3,2},{2,3},{5,4},{4,5},{7,6},{6,7},{9,8},{8,9},{11,10... | collective-permute-start | bytes 2359304 | tf_op jit(solution)/shard_map/ppermute | solution.py:437
  52.4 2.7 %collective-permute-start.14 = (f32[4,72,256]{2,1,0:T(8,128)S(1)}, f32[4,72,256]{2,1,0:T(8,128)S(1)}, u32[]{:S(2)}, u32[]{:S(2)}) collective-permute-start(f32[4,72,256]{2,1,0:T(8,128)S(1)} %pad_maximum_fusion.rest_6_.rest_0_), channel_id=1, source_target_pairs={{1,0},{0,1},{3,2},{2,3},{5,4},{4,5},{7,6},{6,7},{9,8},{8,9},{11,10... | collective-permute-start | bytes 884744 | tf_op jit(solution)/shard_map/ppermute | solution.py:437
  52.9 6.8 %collective-permute-start.15 = (f32[64,256]{1,0:T(8,128)S(1)}, f32[64,256]{1,0:T(8,128)S(1)}, u32[]{:S(2)}, u32[]{:S(2)}) collective-permute-start(f32[64,256]{1,0:T(8,128)S(1)} %copy-done.3), channel_id=1, source_target_pairs={{24,0},{0,8},{8,16},{16,24},{25,1},{1,9},{9,17},{17,25},{26,2},{2,... | collective-permute-start | bytes 196616 | tf_op jit(solution)/shard_map/ppermute | solution.py:424
  64.6 14.3 %all-to-all-start = ((f32[8,64,256]{2,1,0:T(8,128)}), f32[8,64,256]{2,1,0:T(8,128)S(1)}, u32[]{:S(2)}, u32[]{:S(2)}) async-start(f32[8,64,256]{2,1,0:T(8,128)} %get-tuple-element.44), calls=%async_computation | async-start | bytes 1048576 | tf_op jit(solution)/shard_map/all_to_all | solution.py:501
  69.1 9.8 %collective-permute-start.18 = (f32[64,256]{1,0:T(8,128)S(1)}, f32[64,256]{1,0:T(8,128)S(1)}, u32[]{:S(2)}, u32[]{:S(2)}) collective-permute-start(f32[64,256]{1,0:T(8,128)S(1)} %get-tuple-element.48), channel_id=1, source_target_pairs={{0,24},{8,0},{16,8},{24,16},{1,25},{9,1},{17,9},{25,17},{2,26},{10... | collective-permute-start | bytes 196616 | tf_op jit(solution)/shard_map/ppermute | solution.py:433
  74.3 7.5 %collective-permute-start.17 = (f32[64,256]{1,0:T(8,128)S(1)}, f32[64,256]{1,0:T(8,128)S(1)}, u32[]{:S(2)}, u32[]{:S(2)}) collective-permute-start(f32[64,256]{1,0:T(8,128)S(1)} %get-tuple-element.47), channel_id=1, source_target_pairs={{0,16},{8,24},{16,0},{24,8},{1,17},{9,25},{17,1},{25,9},{2,18},{10... | collective-permute-start | bytes 196616 | tf_op jit(solution)/shard_map/ppermute | solution.py:433
  74.3 7.5 %collective-permute-start.16 = (f32[64,256]{1,0:T(8,128)S(1)}, f32[64,256]{1,0:T(8,128)S(1)}, u32[]{:S(2)}, u32[]{:S(2)}) collective-permute-start(f32[64,256]{1,0:T(8,128)S(1)} %get-tuple-element.46), channel_id=1, source_target_pairs={{0,8},{8,16},{16,24},{24,0},{1,9},{9,17},{17,25},{25,1},{2,10},{10... | collective-permute-start | bytes 196616 | tf_op jit(solution)/shard_map/ppermute | solution.py:433
  81.8 5.3 %collective-permute-start.21 = (f32[64,256]{1,0:T(8,128)S(1)}, f32[64,256]{1,0:T(8,128)S(1)}, u32[]{:S(2)}, u32[]{:S(2)}) collective-permute-start(f32[64,256]{1,0:T(8,128)S(1)} %multiply_add_fusion.1.rest_2_), channel_id=1, source_target_pairs={{6,0},{7,1},{4,2},{5,3},{2,4},{3,5},{0,6},{1,7},{14,8},{15,9},{12,... | collective-permute-start | bytes 196616 | tf_op jit(solution)/shard_map/ppermute | solution.py:437
  84.3 4.3 %collective-permute-start.20 = (f32[64,256]{1,0:T(8,128)S(1)}, f32[64,256]{1,0:T(8,128)S(1)}, u32[]{:S(2)}, u32[]{:S(2)}) collective-permute-start(f32[64,256]{1,0:T(8,128)S(1)} %multiply_add_fusion.1.rest_2_), channel_id=1, source_target_pairs={{4,0},{5,1},{6,2},{7,3},{0,4},{1,5},{2,6},{3,7},{12,8},{13,9},{14,... | collective-permute-start | bytes 196616 | tf_op jit(solution)/shard_map/ppermute | solution.py:437
  84.8 4.3 %collective-permute-start.19 = (f32[64,256]{1,0:T(8,128)S(1)}, f32[64,256]{1,0:T(8,128)S(1)}, u32[]{:S(2)}, u32[]{:S(2)}) collective-permute-start(f32[64,256]{1,0:T(8,128)S(1)} %multiply_add_fusion.1.rest_2_), channel_id=1, source_target_pairs={{2,0},{3,1},{0,2},{1,3},{6,4},{7,5},{4,6},{5,7},{10,8},{11,9},{8,1... | collective-permute-start | bytes 196616 | tf_op jit(solution)/shard_map/ppermute | solution.py:437
  89.1 9.7 %collective-permute-start.22 = (f32[4,64,256]{2,1,0:T(8,128)S(1)}, f32[4,64,256]{2,1,0:T(8,128)S(1)}, u32[]{:S(2)}, u32[]{:S(2)}) collective-permute-start(f32[4,64,256]{2,1,0:T(8,128)S(1)} %pad_maximum_fusion.1.rest_0_), channel_id=1, source_target_pairs={{1,0},{0,1},{3,2},{2,3},{5,4},{4,5},{7,6},{6,7},{9,8},{8,9},{11,10... | collective-permute-start | bytes 786440 | tf_op jit(solution)/shard_map/ppermute | solution.py:437
  89.2 4.5 %collective-permute-start.23 = (f32[64,256]{1,0:T(8,128)S(1)}, f32[64,256]{1,0:T(8,128)S(1)}, u32[]{:S(2)}, u32[]{:S(2)}) collective-permute-start(f32[64,256]{1,0:T(8,128)S(1)} %multiply_add_fusion.1.rest_2_), channel_id=1, source_target_pairs={{8,0},{16,8},{24,16},{0,24},{9,1},{17,9},{25,17},{1,25},{10,2},{18... | collective-permute-start | bytes 196616 | tf_op jit(solution)/shard_map/ppermute | solution.py:424
  91.2 7.6 %collective-permute-start.24 = (f32[64,256]{1,0:T(8,128)S(1)}, f32[64,256]{1,0:T(8,128)S(1)}, u32[]{:S(2)}, u32[]{:S(2)}) collective-permute-start(f32[64,256]{1,0:T(8,128)S(1)} %multiply_add_fusion.1.rest_2_), channel_id=1, source_target_pairs={{16,0},{24,8},{0,16},{8,24},{17,1},{25,9},{1,17},{9,25},{18,2},{26... | collective-permute-start | bytes 196616 | tf_op jit(solution)/shard_map/ppermute | solution.py:424
  91.5 7.3 %collective-permute-start.25 = (f32[64,256]{1,0:T(8,128)S(1)}, f32[64,256]{1,0:T(8,128)S(1)}, u32[]{:S(2)}, u32[]{:S(2)}) collective-permute-start(f32[64,256]{1,0:T(8,128)S(1)} %multiply_add_fusion.1.rest_2_), channel_id=1, source_target_pairs={{24,0},{0,8},{8,16},{16,24},{25,1},{1,9},{9,17},{17,25},{26,2},{2,... | collective-permute-start | bytes 196616 | tf_op jit(solution)/shard_map/ppermute | solution.py:424
  103.6 13.5 %all-to-all-start.1 = ((f32[8,64,256]{2,1,0:T(8,128)}), f32[8,64,256]{2,1,0:T(8,128)S(1)}, u32[]{:S(2)}, u32[]{:S(2)}) async-start(f32[8,64,256]{2,1,0:T(8,128)} %get-tuple-element.49), calls=%async_computation.1 | async-start | bytes 1048576 | tf_op jit(solution)/shard_map/all_to_all | solution.py:501
  107.4 9.8 %collective-permute-start.28 = (f32[64,256]{1,0:T(8,128)S(1)}, f32[64,256]{1,0:T(8,128)S(1)}, u32[]{:S(2)}, u32[]{:S(2)}) collective-permute-start(f32[64,256]{1,0:T(8,128)S(1)} %get-tuple-element.53), channel_id=1, source_target_pairs={{0,24},{8,0},{16,8},{24,16},{1,25},{9,1},{17,9},{25,17},{2,26},{10... | collective-permute-start | bytes 196616 | tf_op jit(solution)/shard_map/ppermute | solution.py:433
  110.3 8.1 %collective-permute-start.27 = (f32[64,256]{1,0:T(8,128)S(1)}, f32[64,256]{1,0:T(8,128)S(1)}, u32[]{:S(2)}, u32[]{:S(2)}) collective-permute-start(f32[64,256]{1,0:T(8,128)S(1)} %get-tuple-element.52), channel_id=1, source_target_pairs={{0,16},{8,24},{16,0},{24,8},{1,17},{9,25},{17,1},{25,9},{2,18},{10... | collective-permute-start | bytes 196616 | tf_op jit(solution)/shard_map/ppermute | solution.py:433
  111.7 6.7 %collective-permute-start.26 = (f32[64,256]{1,0:T(8,128)S(1)}, f32[64,256]{1,0:T(8,128)S(1)}, u32[]{:S(2)}, u32[]{:S(2)}) collective-permute-start(f32[64,256]{1,0:T(8,128)S(1)} %get-tuple-element.51), channel_id=1, source_target_pairs={{0,8},{8,16},{16,24},{24,0},{1,9},{9,17},{17,25},{25,1},{2,10},{10... | collective-permute-start | bytes 196616 | tf_op jit(solution)/shard_map/ppermute | solution.py:433
  (3 other events, 31.6 us)

commit v8 on v7

--- a/solution.py
+++ b/solution.py
@@ -132,12 +132,14 @@
     row_count, col_count = sizes
     shifts_early, rows_early = counts
     shifts, rows_late = shifts_early + 1, col_count - rows_early
-    last, late, col_packs = rest[0], rest[1 : 1 + rows_late], rest[1 + rows_late :][:shifts]
-    even_packs, odd_packs = rest[1 + rows_late + shifts :][:2]
-    out, high_l, low_l, high_r, low_r, late_grams, col_params, row_params = rest[3 + rows_late + shifts :]
+    spans = CB * (1 + rows_late)
+    last, late, col_packs = rest[:CB], rest[CB:spans], rest[spans : spans + shifts]
+    even_packs, odd_packs = rest[spans + shifts :][:2]
+    out, high_l, low_l, high_r, low_r, late_grams, col_params, row_params = rest[spans + shifts + 2 :]
     row, col = meta[0], meta[1]
 
-    high_l[...], low_l[...] = split(last[...])
+    for block in range(CB):
+        high_l[block * BLK : (block + 1) * BLK], low_l[block * BLK : (block + 1) * BLK] = split(last[block][...])
     for shift in range(shifts):
         for block in range(CB):
             lanes = slice(block * BLK, (block + 1) * BLK)
@@ -145,7 +147,9 @@
     for bits in range(col_count):
         row_params[bits] = (even_packs, odd_packs)[bits % 2][bits // 2, RHO : RHO + 8, :]
     for line in range(rows_late):
-        high_r[line], low_r[line] = split(late[line][...])
+        for block in range(CB):
+            part = slice(block * BLK, (block + 1) * BLK)
+            high_r[line, part], low_r[line, part] = split(late[CB * line + block][...])
 
     def early_last(line):
         _, start_j, _ = pick_of(sizes, meta, listing, meta[3 + line], shifts_early)
@@ -210,13 +214,13 @@
 def pair_weights(sizes, meta, listing, seeds, early, last, late, packs):
     _, col_count = sizes
     shifts, depth = len(packs) - 2, late[0].shape[-1]
-    rows_late = len(late)
+    rows_late = len(late) // CB
     smem = pl.BlockSpec(memory_space=pltpu.SMEM)
     vmem = pl.BlockSpec(memory_space=pltpu.VMEM)
     tiles = shifts * col_count
     return pl.pallas_call(
         functools.partial(weights_kernel, sizes, (shifts - 1, col_count - rows_late)),
-        in_specs=[smem] * 3 + [vmem] * (5 + 1 + rows_late + len(packs)),
+        in_specs=[smem] * 3 + [vmem] * (5 + CB * (1 + rows_late) + len(packs)),
         out_specs=vmem,
         out_shape=jax.ShapeDtypeStruct((tiles, BLK, BLK), BF16),
         scratch_shapes=[
@@ -235,7 +239,7 @@
             transcendentals=tiles * 3 * BLK * BLK,
         ),
         name="weights",
-    )(meta, listing, seeds, *early, last, *late, *packs)
+    )(meta, listing, seeds, *early, *last, *late, *packs)
 
 
 def force_kernel(row_count, col_count, by_bits, meta, listing, neg_rows, neg_cols, weights, *rest):
@@ -449,10 +453,8 @@
     for bits in single:
         row_x[bits] = from_bits(inputs, bits)
     col_x = [inputs] + [from_shift(inputs, shift) for shift in range(1, shifts - 1)]
-    near = [row_x[bits] for bits in single] + col_x[1:]
-    for bits in late_bits:
-        if bits % 2 == 0:
-            row_x[bits] = from_bits(inputs, bits)
+    blocks = [inputs[block * BLK : (block + 1) * BLK] for block in range(CB)]
+    first = {bits: from_bits(blocks[0], bits) for bits in late_bits if bits % 2 == 0}
     seed_row = jnp.pad(seeds.astype(F32)[None], ((0, 0), (0, SPAN - seeds.shape[0])))
     params = jnp.stack([rho, sigma, jnp.sum(inputs * inputs, axis=1)])
     blank = jnp.zeros((PACK - SEEDS - 1, SPAN), F32)
@@ -460,9 +462,13 @@
     col_packs = [pack] + [from_shift(pack, shift) for shift in range(1, shifts)]
     held, meta, listing, seeds = lax.optimization_barrier((inputs, meta, listing, seeds, *col_packs[1:]))[:4]
     row_x[1] = from_bits(held, 1)
+    last = [from_half(after(blocks[0], *col_packs[1:]))]
+    near = [row_x[bits] for bits in single] + col_x[1:] + list(first.values()) + last
     for bits in single:
         row_x[bits + 1] = from_bits(after(row_x[bits], *near), 1)
-    col_x.append(from_half(after(inputs, row_x[1])))
+    last.append(from_half(after(blocks[1], *near)))
+    late_x = {bits: [first[bits], from_bits(after(blocks[1], *near), bits)] for bits in first}
+    late_x |= {bits + 1: [from_bits(after(first[bits], *near), 1)] for bits in first}
 
     own_pack = pack
     for shift in range(1, shifts):
@@ -470,14 +476,14 @@
         far_seed = col_packs[shift][SEEDS : SEEDS + 1]
         own_pack = own_pack + jnp.pad(far_seed, ((place, PACK - place - 1), (0, 0)))
     own_pack = after(own_pack, *[row_x[bits + 1] for bits in single])
-    early = early_grams(sizes, meta, listing, col_x[:-1], [row_x[bits] for bits in early_bits[1:]])
+    early = early_grams(sizes, meta, listing, col_x, [row_x[bits] for bits in early_bits[1:]])
     even_packs = jnp.stack([own_pack] + [from_bits(own_pack, bits) for bits in range(2, col_count, 2)])
     even_packs = after(even_packs, early[0])
     odd_packs = from_bits(even_packs, 1)
     for bits in late_bits:
         if bits % 2 == 0:
-            row_x[bits + 1] = from_bits(after(row_x[bits], even_packs), 1)
-    held = after(embed, *[row_x[bits] for bits in late_bits if bits % 2 == 0])
+            late_x[bits + 1].append(from_bits(after(late_x[bits][1], even_packs), 1))
+    held = after(embed, *[late_x[bits][1] for bits in first])
     col_y = col_packs + [from_shift(held, shift) for shift in range(shifts, row_count)]
 
     weights = pair_weights(
@@ -486,17 +492,16 @@
         listing,
         seeds,
         early,
-        col_x[-1],
-        [row_x[bits] for bits in late_bits],
+        last,
+        [part for bits in late_bits for part in late_x[bits]],
         col_packs + [even_packs, odd_packs],
     )
 
     row_y = (even_packs, odd_packs)
     for step in range(STEPS):
         if step:
+            row_y = (lax.all_gather(embed, "col", axis=0, tiled=False),)
             col_y = [embed] + [from_shift(embed, shift) for shift in range(1, row_count)]
-            even = jnp.stack([embed] + [from_bits(embed, bits) for bits in range(2, col_count, 2)])
-            row_y = (even, from_bits(even, 1))
         row_force, col_force = pair_forces(sizes, meta, listing, row_list, col_list, weights, row_y, col_y)
         row_parts = lax.all_to_all(row_force, "col", split_axis=0, concat_axis=0, tiled=True)
         force = jnp.sum(row_parts, axis=0) + col_force[0]

time: 119 us -> 123 us (1.034)
  blocking collectives: 0 us -> 10.2 us
  waiting for transfers between devices: 45.3 us -> 37.7 us
  Pallas kernels: 18.3 us -> 21.4 us
  starting transfers between devices: 47.6 us -> 45.3 us
    all_gather x0 -> x1, blocking collectives: none -> 10.2 us  [shards(): row_y = (lax.all_gather(embed, 'col', axis=0, tiled=False),)]
    ppermute x15 -> x13, waiting for transfers between devices: 17.3 us -> 9.64 us  [from_bits(): return lax.ppermute(value, 'col', pairs)]
    ppermute x7, waiting for transfers between devices: 17.3 us -> 11.3 us  [from_shift(): return lax.ppermute(value, 'row', pairs)]
    ppermute x1 -> x2, waiting for transfers between devices: 0.01 us -> 4.06 us  [from_half(): return lax.ppermute(value, 'row', pairs)]
    ppermute x6, starting transfers between devices: 12.8 us -> 9.29 us  [to_shift(): return lax.ppermute(value, 'row', pairs)]
    all_to_all x2, waiting for transfers between devices: 6.66 us -> 10.2 us  [shards(): lax.all_to_all(row_force, 'col', split_axis=0, concat_axis=0, tiled=True)]
    ppermute x7, starting transfers between devices: 11.5 us -> 13.7 us  [from_shift(): return lax.ppermute(value, 'row', pairs)]
    pallas_call x2, Pallas kernels: 9.71 us -> 11.4 us  [pair_forces(): pl.pallas_call(functools.partial(force_kernel, row_count, col_count, len(...]
  transfers between devices with their start and end apart: 31 -> 30, of which waited for: 16 -> 10; matrix products, arithmetic and copies ran while one was open for 5% -> 4% of each run, Pallas kernels for 7% -> 8%
where the time goes in v8:
time: 123 us
  starting transfers between devices  45.3 us (37%)
  waiting for transfers between devices  37.7 us (31%)
  Pallas kernels  21.4 us (17%)
  blocking collectives  10.2 us (8%)
  other arithmetic  3.48 us (3%)
  local copies, waits for them, and re-layouts  3.09 us (3%)
  between operations  1.52 us (1%)
    ppermute x7, starting transfers between devices, from_shift(): return lax.ppermute(value, 'row', pairs)  13.7 us
    ppermute x13, starting transfers between devices, from_bits(): return lax.ppermute(value, 'col', pairs)  12.2 us
    pallas_call x2, Pallas kernels, pair_forces(): pl.pallas_call(functools.partial(force_kernel, row_count, col_count, len(...  11.4 us
    ppermute x7, waiting for transfers between devices, from_shift(): return lax.ppermute(value, 'row', pairs)  11.3 us
    all_gather x1, blocking collectives, shards(): row_y = (lax.all_gather(embed, 'col', axis=0, tiled=False),)  10.2 us
    all_to_all x2, waiting for transfers between devices, shards(): lax.all_to_all(row_force, 'col', split_axis=0, concat_axis=0, tiled=True)  10.2 us
    ppermute x13, waiting for transfers between devices, from_bits(): return lax.ppermute(value, 'col', pairs)  9.64 us
    ppermute x6, starting transfers between devices, to_shift(): return lax.ppermute(value, 'row', pairs)  9.29 us
  transfers between devices with their start and end apart: 30, of which 10 were waited for; matrix products, arithmetic and copies ran while one was open for 4% of the time, Pallas kernels for 8%

profile of v8, /device:TPU:0, one launch (start us, length us, event | category | flops | bytes accessed | tf_op | source)
XLA Modules:
  0.0 122.7 jit_solution(2751248822027548787)
XLA Ops:
  0.6 5.1 %collective-permute-start.2 = (f32[256,768]{1,0:T(8,128)}, f32[256,768]{1,0:T(8,128)S(1)}, u32[]{:S(2)}, u32[]{:S(2)}) collective-permute-start(f32[256,768]{1,0:T(8,128)} %rest_0_.1), channel_id=1, source_target_pairs={{8,0},{16,8},{24,16},{0,24},{9,1},{17,9},{25,17},{1,25},{10,2},{18... | collective-permute-start | bytes 2359304 | tf_op jit(solution)/shard_map/ppermute | solution.py:428
  5.7 1.5 %collective-permute-start.4 = (f32[256,768]{1,0:T(8,128)}, f32[256,768]{1,0:T(8,128)S(1)}, u32[]{:S(2)}, u32[]{:S(2)}) collective-permute-start(f32[256,768]{1,0:T(8,128)} %rest_0_.1), channel_id=1, source_target_pairs={{2,0},{3,1},{0,2},{1,3},{6,4},{7,5},{4,6},{5,7},{10,8},{11,9},{8,1... | collective-permute-start | bytes 2359304 | tf_op jit(solution)/shard_map/ppermute | solution.py:441
  7.2 1.5 %collective-permute-start.5 = (f32[256,768]{1,0:T(8,128)}, f32[256,768]{1,0:T(8,128)S(1)}, u32[]{:S(2)}, u32[]{:S(2)}) collective-permute-start(f32[256,768]{1,0:T(8,128)} %rest_0_.1), channel_id=1, source_target_pairs={{4,0},{5,1},{6,2},{7,3},{0,4},{1,5},{2,6},{3,7},{12,8},{13,9},{14,... | collective-permute-start | bytes 2359304 | tf_op jit(solution)/shard_map/ppermute | solution.py:441
  9.6 1.3 %multiply_reduce_fusion = f32[256]{0:T(256)S(1)} fusion(f32[256,768]{1,0:T(8,128)} %rest_0_.1), kind=kLoop, calls=%fused_computation | loop fusion | flops 392960 | bytes 787456 | tf_op jit(solution)/shard_map/reduce_sum | solution.py:459
  10.9 1.6 %concatenate.7.rest_6_.rest_2_ = f32[72,256]{1,0:T(8,128)S(1)} concatenate(f32[64,256]{1,0:T(8,128)} %param.13, f32[1,256]{1,0:T(1,128)} %bitcast.28, f32[1,256]{1,0:T(1,128)} %bitcast.29, f32[1,256]{1,0:T(1,128)S(1)} %bitcast.27, f32[1,256]{1,0:T(1,128)S(1)} %pad.12, f32[4,256]{1,0:T(4,128)S(1)} %broadcast_in_dim.4), dimensions={0} | concatenate | bytes 147456 | tf_op jit(solution)/shard_map/concatenate | solution.py:461
  13.9 11.2 %collective-permute-done.rest_7_.rest_3_ = f32[72,256]{1,0:T(8,128)S(1)} collective-permute-done((f32[72,256]{1,0:T(8,128)S(1)}, f32[72,256]{1,0:T(8,128)S(1)}, u32[]{:S(2)}, u32[]{:S(2)}) %collective-permute-start) | collective-permute-done | bytes 73760 | tf_op jit(solution)/shard_map/ppermute | solution.py:428
  25.2 2.4 %collective-permute-start.6 = (f32[128,768]{1,0:T(8,128)}, f32[128,768]{1,0:T(8,128)}, u32[]{:S(2)}, u32[]{:S(2)}) collective-permute-start(f32[128,768]{1,0:T(8,128)} %get-tuple-element.34), channel_id=1, source_target_pairs={{6,0},{7,1},{4,2},{5,3},{2,4},{3,5},{0,6},{1,7},{14,8},{15,9},{12,... | collective-permute-start | bytes 1179656 | tf_op jit(solution)/shard_map/ppermute | solution.py:441
  27.6 1.3 %collective-permute-start.7 = (f32[128,768]{1,0:T(8,128)}, f32[128,768]{1,0:T(8,128)}, u32[]{:S(2)}, u32[]{:S(2)}) collective-permute-start(f32[128,768]{1,0:T(8,128)} %get-tuple-element.34), channel_id=1, source_target_pairs={{16,0},{8,24},{17,1},{9,25},{18,2},{10,26},{19,3},{11,27},{20,4},{... | collective-permute-start | bytes 1179656 | tf_op jit(solution)/shard_map/ppermute | solution.py:433
  29.9 5.7 %collective-permute-done.6.rest_2_ = f32[128,768]{1,0:T(8,128)} collective-permute-done((f32[128,768]{1,0:T(8,128)}, f32[128,768]{1,0:T(8,128)}, u32[]{:S(2)}, u32[]{:S(2)}) %collective-permute-start.6) | collective-permute-done | bytes 393248 | tf_op jit(solution)/shard_map/ppermute | solution.py:441
  35.6 4.1 %collective-permute-done.7.rest_0_ = f32[128,768]{1,0:T(8,128)} collective-permute-done((f32[128,768]{1,0:T(8,128)}, f32[128,768]{1,0:T(8,128)}, u32[]{:S(2)}, u32[]{:S(2)}) %collective-permute-start.7) | collective-permute-done | bytes 393248 | tf_op jit(solution)/shard_map/ppermute | solution.py:433
  40.5 2.0 %collective-permute-start.11 = (f32[128,768]{1,0:T(8,128)}, f32[128,768]{1,0:T(8,128)S(1)}, u32[]{:S(2)}, u32[]{:S(2)}) collective-permute-start(f32[128,768]{1,0:T(8,128)} %get-tuple-element.42), channel_id=1, source_target_pairs={{6,0},{7,1},{4,2},{5,3},{2,4},{3,5},{0,6},{1,7},{14,8},{15,9},{12,... | collective-permute-start | bytes 1179656 | tf_op jit(solution)/shard_map/ppermute | solution.py:441
  42.6 1.4 %collective-permute-start.10 = (f32[128,768]{1,0:T(8,128)}, f32[128,768]{1,0:T(8,128)S(1)}, u32[]{:S(2)}, u32[]{:S(2)}) collective-permute-start(f32[128,768]{1,0:T(8,128)} %get-tuple-element.42), channel_id=1, source_target_pairs={{16,0},{8,24},{17,1},{9,25},{18,2},{10,26},{19,3},{11,27},{20,4},{... | collective-permute-start | bytes 1179656 | tf_op jit(solution)/shard_map/ppermute | solution.py:433
  44.4 2.0 %collective-permute-start.15 = (f32[72,256]{1,0:T(8,128)S(1)}, f32[72,256]{1,0:T(8,128)S(1)}, u32[]{:S(2)}, u32[]{:S(2)}) collective-permute-start(f32[72,256]{1,0:T(8,128)S(1)} %pad_add_fusion), channel_id=1, source_target_pairs={{6,0},{7,1},{4,2},{5,3},{2,4},{3,5},{0,6},{1,7},{14,8},{15,9},{12,... | collective-permute-start | bytes 221192 | tf_op jit(solution)/shard_map/ppermute | solution.py:441
  46.9 1.0 collective-permute-start.13
  47.9 4.8 %grams.1 = (f32[6,2,128,128]{3,2,1,0:T(8,128)S(1)}, bf16[2,256,768]{2,1,0:T(8,128)(2,1)S(1)}, bf16[2,256,768]{2,1,0:T(8,128)(2,1)S(1)}, bf16[6,128,768]{2,1,0:T(8,128)(2,1)S(1)}, bf16[6,128,768]{2,1,0:T(8,128)(2,1)S(1)}) custom-call(s32[11]{0:T(128)S(1)} %pad_add_fusion.1.meta, s32[64]{0:T(128)S(1)} %reshape.27.listing, f32[256,768]{1,0:T(8,128)S(1)} %copy-done, ...), custom_call_target="tpu_custom_call" | custom-call | flops 905969664 | bytes 6291456 | tf_op jit(solution)/shard_map/grams/pallas_call | solution.py:109
  52.7 2.6 %collective-permute-done.15 = f32[72,256]{1,0:T(8,128)S(1)} collective-permute-done((f32[72,256]{1,0:T(8,128)S(1)}, f32[72,256]{1,0:T(8,128)S(1)}, u32[]{:S(2)}, u32[]{:S(2)}) %collective-permute-start.15) | collective-permute-done | bytes 73760 | tf_op jit(solution)/shard_map/ppermute | solution.py:441
  56.8 4.3 %collective-permute-start.18 = (f32[64,256]{1,0:T(8,128)S(1)}, f32[64,256]{1,0:T(8,128)S(1)}, u32[]{:S(2)}, u32[]{:S(2)}) collective-permute-start(f32[64,256]{1,0:T(8,128)S(1)} %copy-done.3), channel_id=1, source_target_pairs={{24,0},{0,8},{8,16},{16,24},{25,1},{1,9},{9,17},{17,25},{26,2},{2,... | collective-permute-start | bytes 196616 | tf_op jit(solution)/shard_map/ppermute | solution.py:428
  61.2 5.2 %weights.1 = bf16[24,128,128]{2,1,0:T(8,128)(2,1)S(1)} custom-call(s32[11]{0:T(128)S(1)} %pad_add_fusion.1.meta, s32[64]{0:T(128)S(1)} %reshape.27.listing, s32[32]{0:T(128)S(1)} %reshape.28.seeds, f32[6,2,128,128]{3,2,1,0:T(8,128)S(1)} %get-tuple-element.37.grams, bf16[2,256,768]{2,1,0:T(8,128)(2,1)S(1)} %get-tuple-element.38.high_c, ...), custom_call_target="tpu_custom_call" | custom-call | flops 905969664 | bytes 2359296 | tf_op jit(solution)/shard_map/weights/pallas_call | solution.py:221
  66.4 5.8 %forces.2 = (f32[8,64,256]{2,1,0:T(8,128)}, f32[64,256]{1,0:T(8,128)S(1)}, f32[64,256]{1,0:T(8,128)S(1)}, f32[64,256]{1,0:T(8,128)S(1)}, f32[64,256]{1,0:T(8,128)S(1)}) custom-call(s32[11]{0:T(128)S(1)} %pad_add_fusion.1.meta, s32[64]{0:T(128)S(1)} %reshape.27.listing, s32[48]{0:T(128)S(1)} %bitcast.19, s32[48]{0:T(128)S(1)} %bitcast.21, ...), custom_call_target="tpu_custom_call" | custom-call | flops 1744830464 | bytes 1572864 | tf_op jit(solution)/shard_map/forces/pallas_call | solution.py:389
  72.1 3.8 %all-to-all-start = ((f32[8,64,256]{2,1,0:T(8,128)}), f32[8,64,256]{2,1,0:T(8,128)S(1)}, u32[]{:S(2)}, u32[]{:S(2)}) async-start(f32[8,64,256]{2,1,0:T(8,128)} %get-tuple-element.48), calls=%async_computation | async-start | bytes 1048576 | tf_op jit(solution)/shard_map/all_to_all | solution.py:506
  75.9 4.4 %collective-permute-start.21 = (f32[64,256]{1,0:T(8,128)S(1)}, f32[64,256]{1,0:T(8,128)S(1)}, u32[]{:S(2)}, u32[]{:S(2)}) collective-permute-start(f32[64,256]{1,0:T(8,128)S(1)} %get-tuple-element.52), channel_id=1, source_target_pairs={{0,24},{8,0},{16,8},{24,16},{1,25},{9,1},{17,9},{25,17},{2,26},{10... | collective-permute-start | bytes 196616 | tf_op jit(solution)/shard_map/ppermute | solution.py:437
  80.3 1.0 collective-permute-start.19
  81.3 4.3 %all-to-all-done = f32[8,64,256]{2,1,0:T(8,128)S(1)} async-done(((f32[8,64,256]{2,1,0:T(8,128)}), f32[8,64,256]{2,1,0:T(8,128)S(1)}, u32[]{:S(2)}, u32[]{:S(2)}) %all-to-all-start) | async-done | bytes 524320 | tf_op jit(solution)/shard_map/all_to_all | solution.py:506
  85.7 1.8 %collective-permute-done.20 = f32[64,256]{1,0:T(8,128)S(1)} collective-permute-done((f32[64,256]{1,0:T(8,128)S(1)}, f32[64,256]{1,0:T(8,128)S(1)}, u32[]{:S(2)}, u32[]{:S(2)}) %collective-permute-start.20) | collective-permute-done | bytes 65568 | tf_op jit(solution)/shard_map/ppermute | solution.py:437
  87.5 2.7 %collective-permute-start.22 = (f32[64,256]{1,0:T(8,128)S(1)}, f32[64,256]{1,0:T(8,128)S(1)}, u32[]{:S(2)}, u32[]{:S(2)}) collective-permute-start(f32[64,256]{1,0:T(8,128)S(1)} %multiply_add_fusion.1.rest_1_), channel_id=1, source_target_pairs={{8,0},{16,8},{24,16},{0,24},{9,1},{17,9},{25,17},{1,25},{10,2},{18... | collective-permute-start | bytes 196616 | tf_op jit(solution)/shard_map/ppermute | solution.py:428
  90.2 1.1 collective-permute-start.24
  91.3 10.2 %all-gather = f32[512,256]{1,0:T(8,128)S(1)} all-gather(f32[64,256]{1,0:T(8,128)S(1)} %multiply_add_fusion.1.rest_1_), channel_id=2, replica_groups=mesh['row'=4,'col'=8] {'col'}, dimensions={0}, use_global_device_ids=true | all-gather | bytes 589824 | tf_op jit(solution)/shard_map/all_gather | solution.py:503
  101.5 5.7 %forces.3 = (f32[8,64,256]{2,1,0:T(8,128)}, f32[64,256]{1,0:T(8,128)S(1)}, f32[64,256]{1,0:T(8,128)S(1)}, f32[64,256]{1,0:T(8,128)S(1)}, f32[64,256]{1,0:T(8,128)S(1)}) custom-call(s32[11]{0:T(128)S(1)} %pad_add_fusion.1.meta, s32[64]{0:T(128)S(1)} %reshape.27.listing, s32[48]{0:T(128)S(1)} %bitcast.20, s32[48]{0:T(128)S(1)} %bitcast.22, ...), custom_call_target="tpu_custom_call" | custom-call | flops 1744830464 | bytes 1572864 | tf_op jit(solution)/shard_map/forces/pallas_call | solution.py:389
  107.2 3.6 %all-to-all-start.1 = ((f32[8,64,256]{2,1,0:T(8,128)}), f32[8,64,256]{2,1,0:T(8,128)S(1)}, u32[]{:S(2)}, u32[]{:S(2)}) async-start(f32[8,64,256]{2,1,0:T(8,128)} %get-tuple-element.53), calls=%async_computation.1 | async-start | bytes 1048576 | tf_op jit(solution)/shard_map/all_to_all | solution.py:506
  110.8 2.6 %collective-permute-start.27 = (f32[64,256]{1,0:T(8,128)S(1)}, f32[64,256]{1,0:T(8,128)S(1)}, u32[]{:S(2)}, u32[]{:S(2)}) collective-permute-start(f32[64,256]{1,0:T(8,128)S(1)} %get-tuple-element.57), channel_id=1, source_target_pairs={{0,24},{8,0},{16,8},{24,16},{1,25},{9,1},{17,9},{25,17},{2,26},{10... | collective-permute-start | bytes 196616 | tf_op jit(solution)/shard_map/ppermute | solution.py:437
  113.4 1.3 %collective-permute-start.26 = (f32[64,256]{1,0:T(8,128)S(1)}, f32[64,256]{1,0:T(8,128)S(1)}, u32[]{:S(2)}, u32[]{:S(2)}) collective-permute-start(f32[64,256]{1,0:T(8,128)S(1)} %get-tuple-element.56), channel_id=1, source_target_pairs={{0,16},{8,24},{16,0},{24,8},{1,17},{9,25},{17,1},{25,9},{2,18},{10... | collective-permute-start | bytes 196616 | tf_op jit(solution)/shard_map/ppermute | solution.py:437
  114.7 5.9 %all-to-all-done.1 = f32[8,64,256]{2,1,0:T(8,128)S(1)} async-done(((f32[8,64,256]{2,1,0:T(8,128)}), f32[8,64,256]{2,1,0:T(8,128)S(1)}, u32[]{:S(2)}, u32[]{:S(2)}) %all-to-all-start.1) | async-done | bytes 524320 | tf_op jit(solution)/shard_map/all_to_all | solution.py:506
  (68 shorter events, 8.1 us)
Async XLA Ops:
  0.6 39.0 %collective-permute-start.2 = (f32[256,768]{1,0:T(8,128)}, f32[256,768]{1,0:T(8,128)S(1)}, u32[]{:S(2)}, u32[]{:S(2)}) collective-permute-start(f32[256,768]{1,0:T(8,128)} %rest_0_.1), channel_id=1, source_target_pairs={{8,0},{16,8},{24,16},{0,24},{9,1},{17,9},{25,17},{1,25},{10,2},{18... | collective-permute-start | bytes 2359304 | tf_op jit(solution)/shard_map/ppermute | solution.py:428
  5.7 33.9 %collective-permute-start.4 = (f32[256,768]{1,0:T(8,128)}, f32[256,768]{1,0:T(8,128)S(1)}, u32[]{:S(2)}, u32[]{:S(2)}) collective-permute-start(f32[256,768]{1,0:T(8,128)} %rest_0_.1), channel_id=1, source_target_pairs={{2,0},{3,1},{0,2},{1,3},{6,4},{7,5},{4,6},{5,7},{10,8},{11,9},{8,1... | collective-permute-start | bytes 2359304 | tf_op jit(solution)/shard_map/ppermute | solution.py:441
  7.2 32.4 %collective-permute-start.5 = (f32[256,768]{1,0:T(8,128)}, f32[256,768]{1,0:T(8,128)S(1)}, u32[]{:S(2)}, u32[]{:S(2)}) collective-permute-start(f32[256,768]{1,0:T(8,128)} %rest_0_.1), channel_id=1, source_target_pairs={{4,0},{5,1},{6,2},{7,3},{0,4},{1,5},{2,6},{3,7},{12,8},{13,9},{14,... | collective-permute-start | bytes 2359304 | tf_op jit(solution)/shard_map/ppermute | solution.py:441
  9.6 19.3 %copy-start.4 = (s32[1,1,8,4]{2,3,1,0:T(4,128)S(1)}, s32[1,1,8,4]{2,3,1,0:T(4,128)}, u32[]{:S(2)}) copy-start(s32[1,1,8,4]{2,3,1,0:T(4,128)} %param.15) | copy-start | bytes 388
  9.6 20.0 %copy-start.5 = (s32[1,1,8,4,2]{2,4,3,1,0:T(2,128)S(1)}, s32[1,1,8,4,2]{2,4,3,1,0:T(2,128)}, u32[]{:S(2)}) copy-start(s32[1,1,8,4,2]{2,4,3,1,0:T(2,128)} %param.14) | copy-start | bytes 772
  12.5 12.7 %collective-permute-start = (f32[72,256]{1,0:T(8,128)S(1)}, f32[72,256]{1,0:T(8,128)S(1)}, u32[]{:S(2)}, u32[]{:S(2)}) collective-permute-start(f32[72,256]{1,0:T(8,128)S(1)} %concatenate.7.rest_6_.rest_2_), channel_id=1, source_target_pairs={{8,0},{16,8},{24,16},{0,24},{9,1},{17,9},{25,17},{1,25},{10,2},{18... | collective-permute-start | bytes 221192 | tf_op jit(solution)/shard_map/ppermute | solution.py:428
  13.0 14.6 %collective-permute-start.1 = (f32[72,256]{1,0:T(8,128)S(1)}, f32[72,256]{1,0:T(8,128)S(1)}, u32[]{:S(2)}, u32[]{:S(2)}) collective-permute-start(f32[72,256]{1,0:T(8,128)S(1)} %concatenate.7.rest_6_.rest_2_), channel_id=1, source_target_pairs={{16,0},{24,8},{0,16},{8,24},{17,1},{25,9},{1,17},{9,25},{18,2},{26... | collective-permute-start | bytes 221192 | tf_op jit(solution)/shard_map/ppermute | solution.py:428
  25.2 10.4 %collective-permute-start.6 = (f32[128,768]{1,0:T(8,128)}, f32[128,768]{1,0:T(8,128)}, u32[]{:S(2)}, u32[]{:S(2)}) collective-permute-start(f32[128,768]{1,0:T(8,128)} %get-tuple-element.34), channel_id=1, source_target_pairs={{6,0},{7,1},{4,2},{5,3},{2,4},{3,5},{0,6},{1,7},{14,8},{15,9},{12,... | collective-permute-start | bytes 1179656 | tf_op jit(solution)/shard_map/ppermute | solution.py:441
  27.6 12.0 %collective-permute-start.7 = (f32[128,768]{1,0:T(8,128)}, f32[128,768]{1,0:T(8,128)}, u32[]{:S(2)}, u32[]{:S(2)}) collective-permute-start(f32[128,768]{1,0:T(8,128)} %get-tuple-element.34), channel_id=1, source_target_pairs={{16,0},{8,24},{17,1},{9,25},{18,2},{10,26},{19,3},{11,27},{20,4},{... | collective-permute-start | bytes 1179656 | tf_op jit(solution)/shard_map/ppermute | solution.py:433
  39.6 4.4 %collective-permute-start.8 = (f32[256,768]{1,0:T(8,128)S(1)}, f32[256,768]{1,0:T(8,128)}, u32[]{:S(2)}, u32[]{:S(2)}) collective-permute-start(f32[256,768]{1,0:T(8,128)S(1)} %collective-permute-done.4.rest_3_), channel_id=1, source_target_pairs={{1,0},{0,1},{3,2},{2,3},{5,4},{4,5},{7,6},{6,7},{9,8},{8,9},{11,10... | collective-permute-start | bytes 2359304 | tf_op jit(solution)/shard_map/ppermute | solution.py:441
  39.7 4.7 %collective-permute-start.9 = (f32[256,768]{1,0:T(8,128)S(1)}, f32[256,768]{1,0:T(8,128)}, u32[]{:S(2)}, u32[]{:S(2)}) collective-permute-start(f32[256,768]{1,0:T(8,128)S(1)} %collective-permute-done.5.rest_5_), channel_id=1, source_target_pairs={{1,0},{0,1},{3,2},{2,3},{5,4},{4,5},{7,6},{6,7},{9,8},{8,9},{11,10... | collective-permute-start | bytes 2359304 | tf_op jit(solution)/shard_map/ppermute | solution.py:441
  40.4 6.4 %collective-permute-start.3 = (f32[256,768]{1,0:T(8,128)S(1)}, f32[256,768]{1,0:T(8,128)S(1)}, u32[]{:S(2)}, u32[]{:S(2)}) collective-permute-start(f32[256,768]{1,0:T(8,128)S(1)} %copy-done), channel_id=1, source_target_pairs={{1,0},{0,1},{3,2},{2,3},{5,4},{4,5},{7,6},{6,7},{9,8},{8,9},{11,10... | collective-permute-start | bytes 2359304 | tf_op jit(solution)/shard_map/ppermute | solution.py:441
  40.5 15.8 %collective-permute-start.11 = (f32[128,768]{1,0:T(8,128)}, f32[128,768]{1,0:T(8,128)S(1)}, u32[]{:S(2)}, u32[]{:S(2)}) collective-permute-start(f32[128,768]{1,0:T(8,128)} %get-tuple-element.42), channel_id=1, source_target_pairs={{6,0},{7,1},{4,2},{5,3},{2,4},{3,5},{0,6},{1,7},{14,8},{15,9},{12,... | collective-permute-start | bytes 1179656 | tf_op jit(solution)/shard_map/ppermute | solution.py:441
  42.6 18.6 %collective-permute-start.10 = (f32[128,768]{1,0:T(8,128)}, f32[128,768]{1,0:T(8,128)S(1)}, u32[]{:S(2)}, u32[]{:S(2)}) collective-permute-start(f32[128,768]{1,0:T(8,128)} %get-tuple-element.42), channel_id=1, source_target_pairs={{16,0},{8,24},{17,1},{9,25},{18,2},{10,26},{19,3},{11,27},{20,4},{... | collective-permute-start | bytes 1179656 | tf_op jit(solution)/shard_map/ppermute | solution.py:433
  44.4 10.9 %collective-permute-start.15 = (f32[72,256]{1,0:T(8,128)S(1)}, f32[72,256]{1,0:T(8,128)S(1)}, u32[]{:S(2)}, u32[]{:S(2)}) collective-permute-start(f32[72,256]{1,0:T(8,128)S(1)} %pad_add_fusion), channel_id=1, source_target_pairs={{6,0},{7,1},{4,2},{5,3},{2,4},{3,5},{0,6},{1,7},{14,8},{15,9},{12,... | collective-permute-start | bytes 221192 | tf_op jit(solution)/shard_map/ppermute | solution.py:441
  46.3 9.9 %collective-permute-start.14 = (f32[72,256]{1,0:T(8,128)S(1)}, f32[72,256]{1,0:T(8,128)S(1)}, u32[]{:S(2)}, u32[]{:S(2)}) collective-permute-start(f32[72,256]{1,0:T(8,128)S(1)} %pad_add_fusion), channel_id=1, source_target_pairs={{4,0},{5,1},{6,2},{7,3},{0,4},{1,5},{2,6},{3,7},{12,8},{13,9},{14,... | collective-permute-start | bytes 221192 | tf_op jit(solution)/shard_map/ppermute | solution.py:441
  46.9 9.4 %collective-permute-start.13 = (f32[72,256]{1,0:T(8,128)S(1)}, f32[72,256]{1,0:T(8,128)S(1)}, u32[]{:S(2)}, u32[]{:S(2)}) collective-permute-start(f32[72,256]{1,0:T(8,128)S(1)} %pad_add_fusion), channel_id=1, source_target_pairs={{2,0},{3,1},{0,2},{1,3},{6,4},{7,5},{4,6},{5,7},{10,8},{11,9},{8,1... | collective-permute-start | bytes 221192 | tf_op jit(solution)/shard_map/ppermute | solution.py:441
  55.2 5.9 %collective-permute-start.12 = (f32[128,768]{1,0:T(8,128)}, f32[128,768]{1,0:T(8,128)S(1)}, u32[]{:S(2)}, u32[]{:S(2)}) collective-permute-start(f32[128,768]{1,0:T(8,128)} %collective-permute-done.6.rest_2_), channel_id=1, source_target_pairs={{1,0},{0,1},{3,2},{2,3},{5,4},{4,5},{7,6},{6,7},{9,8},{8,9},{11,10... | collective-permute-start | bytes 1179656 | tf_op jit(solution)/shard_map/ppermute | solution.py:441
  56.3 4.9 %collective-permute-start.16 = (f32[128,768]{1,0:T(8,128)S(1)}, f32[128,768]{1,0:T(8,128)S(1)}, u32[]{:S(2)}, u32[]{:S(2)}) collective-permute-start(f32[128,768]{1,0:T(8,128)S(1)} %collective-permute-done.11.rest_3_), channel_id=1, source_target_pairs={{1,0},{0,1},{3,2},{2,3},{5,4},{4,5},{7,6},{6,7},{9,8},{8,9},{11,10... | collective-permute-start | bytes 1179656 | tf_op jit(solution)/shard_map/ppermute | solution.py:441
  56.3 4.8 %collective-permute-start.17 = (f32[4,72,256]{2,1,0:T(8,128)S(1)}, f32[4,72,256]{2,1,0:T(8,128)S(1)}, u32[]{:S(2)}, u32[]{:S(2)}) collective-permute-start(f32[4,72,256]{2,1,0:T(8,128)S(1)} %pad_maximum_fusion.rest_9_.rest_0_), channel_id=1, source_target_pairs={{1,0},{0,1},{3,2},{2,3},{5,4},{4,5},{7,6},{6,7},{9,8},{8,9},{11,10... | collective-permute-start | bytes 884744 | tf_op jit(solution)/shard_map/ppermute | solution.py:441
  56.8 9.5 %collective-permute-start.18 = (f32[64,256]{1,0:T(8,128)S(1)}, f32[64,256]{1,0:T(8,128)S(1)}, u32[]{:S(2)}, u32[]{:S(2)}) collective-permute-start(f32[64,256]{1,0:T(8,128)S(1)} %copy-done.3), channel_id=1, source_target_pairs={{24,0},{0,8},{8,16},{16,24},{25,1},{1,9},{9,17},{17,25},{26,2},{2,... | collective-permute-start | bytes 196616 | tf_op jit(solution)/shard_map/ppermute | solution.py:428
  72.1 13.5 %all-to-all-start = ((f32[8,64,256]{2,1,0:T(8,128)}), f32[8,64,256]{2,1,0:T(8,128)S(1)}, u32[]{:S(2)}, u32[]{:S(2)}) async-start(f32[8,64,256]{2,1,0:T(8,128)} %get-tuple-element.48), calls=%async_computation | async-start | bytes 1048576 | tf_op jit(solution)/shard_map/all_to_all | solution.py:506
  75.9 9.8 %collective-permute-start.21 = (f32[64,256]{1,0:T(8,128)S(1)}, f32[64,256]{1,0:T(8,128)S(1)}, u32[]{:S(2)}, u32[]{:S(2)}) collective-permute-start(f32[64,256]{1,0:T(8,128)S(1)} %get-tuple-element.52), channel_id=1, source_target_pairs={{0,24},{8,0},{16,8},{24,16},{1,25},{9,1},{17,9},{25,17},{2,26},{10... | collective-permute-start | bytes 196616 | tf_op jit(solution)/shard_map/ppermute | solution.py:437
  80.3 7.1 %collective-permute-start.20 = (f32[64,256]{1,0:T(8,128)S(1)}, f32[64,256]{1,0:T(8,128)S(1)}, u32[]{:S(2)}, u32[]{:S(2)}) collective-permute-start(f32[64,256]{1,0:T(8,128)S(1)} %get-tuple-element.51), channel_id=1, source_target_pairs={{0,16},{8,24},{16,0},{24,8},{1,17},{9,25},{17,1},{25,9},{2,18},{10... | collective-permute-start | bytes 196616 | tf_op jit(solution)/shard_map/ppermute | solution.py:437
  80.3 7.1 %collective-permute-start.19 = (f32[64,256]{1,0:T(8,128)S(1)}, f32[64,256]{1,0:T(8,128)S(1)}, u32[]{:S(2)}, u32[]{:S(2)}) collective-permute-start(f32[64,256]{1,0:T(8,128)S(1)} %get-tuple-element.50), channel_id=1, source_target_pairs={{0,8},{8,16},{16,24},{24,0},{1,9},{9,17},{17,25},{25,1},{2,10},{10... | collective-permute-start | bytes 196616 | tf_op jit(solution)/shard_map/ppermute | solution.py:437
  87.5 14.1 %collective-permute-start.22 = (f32[64,256]{1,0:T(8,128)S(1)}, f32[64,256]{1,0:T(8,128)S(1)}, u32[]{:S(2)}, u32[]{:S(2)}) collective-permute-start(f32[64,256]{1,0:T(8,128)S(1)} %multiply_add_fusion.1.rest_1_), channel_id=1, source_target_pairs={{8,0},{16,8},{24,16},{0,24},{9,1},{17,9},{25,17},{1,25},{10,2},{18... | collective-permute-start | bytes 196616 | tf_op jit(solution)/shard_map/ppermute | solution.py:428
  90.2 11.3 %collective-permute-start.23 = (f32[64,256]{1,0:T(8,128)S(1)}, f32[64,256]{1,0:T(8,128)S(1)}, u32[]{:S(2)}, u32[]{:S(2)}) collective-permute-start(f32[64,256]{1,0:T(8,128)S(1)} %multiply_add_fusion.1.rest_1_), channel_id=1, source_target_pairs={{16,0},{24,8},{0,16},{8,24},{17,1},{25,9},{1,17},{9,25},{18,2},{26... | collective-permute-start | bytes 196616 | tf_op jit(solution)/shard_map/ppermute | solution.py:428
  90.2 11.3 %collective-permute-start.24 = (f32[64,256]{1,0:T(8,128)S(1)}, f32[64,256]{1,0:T(8,128)S(1)}, u32[]{:S(2)}, u32[]{:S(2)}) collective-permute-start(f32[64,256]{1,0:T(8,128)S(1)} %multiply_add_fusion.1.rest_1_), channel_id=1, source_target_pairs={{24,0},{0,8},{8,16},{16,24},{25,1},{1,9},{9,17},{17,25},{26,2},{2,... | collective-permute-start | bytes 196616 | tf_op jit(solution)/shard_map/ppermute | solution.py:428
  107.2 13.4 %all-to-all-start.1 = ((f32[8,64,256]{2,1,0:T(8,128)}), f32[8,64,256]{2,1,0:T(8,128)S(1)}, u32[]{:S(2)}, u32[]{:S(2)}) async-start(f32[8,64,256]{2,1,0:T(8,128)} %get-tuple-element.53), calls=%async_computation.1 | async-start | bytes 1048576 | tf_op jit(solution)/shard_map/all_to_all | solution.py:506
  110.8 9.8 %collective-permute-start.27 = (f32[64,256]{1,0:T(8,128)S(1)}, f32[64,256]{1,0:T(8,128)S(1)}, u32[]{:S(2)}, u32[]{:S(2)}) collective-permute-start(f32[64,256]{1,0:T(8,128)S(1)} %get-tuple-element.57), channel_id=1, source_target_pairs={{0,24},{8,0},{16,8},{24,16},{1,25},{9,1},{17,9},{25,17},{2,26},{10... | collective-permute-start | bytes 196616 | tf_op jit(solution)/shard_map/ppermute | solution.py:437
  113.4 8.0 %collective-permute-start.26 = (f32[64,256]{1,0:T(8,128)S(1)}, f32[64,256]{1,0:T(8,128)S(1)}, u32[]{:S(2)}, u32[]{:S(2)}) collective-permute-start(f32[64,256]{1,0:T(8,128)S(1)} %get-tuple-element.56), channel_id=1, source_target_pairs={{0,16},{8,24},{16,0},{24,8},{1,17},{9,25},{17,1},{25,9},{2,18},{10... | collective-permute-start | bytes 196616 | tf_op jit(solution)/shard_map/ppermute | solution.py:437
  114.7 6.7 %collective-permute-start.25 = (f32[64,256]{1,0:T(8,128)S(1)}, f32[64,256]{1,0:T(8,128)S(1)}, u32[]{:S(2)}, u32[]{:S(2)}) collective-permute-start(f32[64,256]{1,0:T(8,128)S(1)} %get-tuple-element.55), channel_id=1, source_target_pairs={{0,8},{8,16},{16,24},{24,0},{1,9},{9,17},{17,25},{25,1},{2,10},{10... | collective-permute-start | bytes 196616 | tf_op jit(solution)/shard_map/ppermute | solution.py:437
  (4 other events, 37.0 us)

commit v9 on v7

--- a/solution.py
+++ b/solution.py
@@ -458,11 +458,12 @@
     blank = jnp.zeros((PACK - SEEDS - 1, SPAN), F32)
     pack = jnp.concatenate([embed, params, seed_row, blank], axis=0)
     col_packs = [pack] + [from_shift(pack, shift) for shift in range(1, shifts)]
-    held, meta, listing, seeds = lax.optimization_barrier((inputs, meta, listing, seeds, *col_packs[1:]))[:4]
+    far_y = [from_shift(embed, shift) for shift in range(shifts, row_count)]
+    held, meta, listing, seeds = lax.optimization_barrier((inputs, meta, listing, seeds, *col_packs[1:], *far_y))[:4]
     row_x[1] = from_bits(held, 1)
     for bits in single:
         row_x[bits + 1] = from_bits(after(row_x[bits], *near), 1)
-    col_x.append(from_half(after(inputs, row_x[1])))
+    col_x.append(from_half(after(inputs, *col_packs[1:], *far_y)))
 
     own_pack = pack
     for shift in range(1, shifts):
@@ -477,8 +478,7 @@
     for bits in late_bits:
         if bits % 2 == 0:
             row_x[bits + 1] = from_bits(after(row_x[bits], even_packs), 1)
-    held = after(embed, *[row_x[bits] for bits in late_bits if bits % 2 == 0])
-    col_y = col_packs + [from_shift(held, shift) for shift in range(shifts, row_count)]
+    col_y = col_packs + far_y
 
     weights = pair_weights(
         sizes,
@@ -494,9 +494,8 @@
     row_y = (even_packs, odd_packs)
     for step in range(STEPS):
         if step:
+            row_y = (lax.all_gather(embed, "col", axis=0, tiled=False),)
             col_y = [embed] + [from_shift(embed, shift) for shift in range(1, row_count)]
-            even = jnp.stack([embed] + [from_bits(embed, bits) for bits in range(2, col_count, 2)])
-            row_y = (even, from_bits(even, 1))
         row_force, col_force = pair_forces(sizes, meta, listing, row_list, col_list, weights, row_y, col_y)
         row_parts = lax.all_to_all(row_force, "col", split_axis=0, concat_axis=0, tiled=True)
         force = jnp.sum(row_parts, axis=0) + col_force[0]

time: 119 us -> 118 us (level)
  starting transfers between devices: 47.6 us -> 33.9 us
  blocking collectives: 0 us -> 10 us
  Pallas kernels: 18.3 us -> 23.5 us
  waiting for transfers between devices: 45.3 us -> 43.1 us
    all_gather x0 -> x1, blocking collectives: none -> 10 us  [shards(): row_y = (lax.all_gather(embed, 'col', axis=0, tiled=False),)]
    ppermute x6, starting transfers between devices: 12.8 us -> 5.87 us  [to_shift(): return lax.ppermute(value, 'row', pairs)]
    all_to_all x2, waiting for transfers between devices: 6.66 us -> 13.5 us  [shards(): lax.all_to_all(row_force, 'col', split_axis=0, concat_axis=0, tiled=True)]
    pallas_call x2, Pallas kernels: 9.71 us -> 14.9 us  [pair_forces(): pl.pallas_call(functools.partial(force_kernel, row_count, col_count, len(...]
    ppermute x7, waiting for transfers between devices: 17.3 us -> 12.8 us  [from_shift(): return lax.ppermute(value, 'row', pairs)]
    ppermute x6, waiting for transfers between devices: 4.09 us -> 0.02 us  [to_shift(): return lax.ppermute(value, 'row', pairs)]
    ppermute x15 -> x11, starting transfers between devices: 13.8 us -> 10.2 us  [from_bits(): return lax.ppermute(value, 'col', pairs)]
    ppermute x7, starting transfers between devices: 11.5 us -> 9.48 us  [from_shift(): return lax.ppermute(value, 'row', pairs)]
  transfers between devices with their start and end apart: 31 -> 27, of which waited for: 16 -> 11; matrix products, arithmetic and copies ran while one was open for 5% -> 5% of each run, Pallas kernels for 7% -> 3%
where the time goes in v9:
time: 118 us; the launch traced here: 119 us
  waiting for transfers between devices  43.1 us (37%)
  starting transfers between devices  33.9 us (29%)
  Pallas kernels  23.5 us (20%)
  blocking collectives  10 us (8%)
  local copies, waits for them, and re-layouts  3.49 us (3%)
  other arithmetic  3.47 us (3%)
  between operations  1.51 us (1%)
    ppermute x11, waiting for transfers between devices, from_bits(): return lax.ppermute(value, 'col', pairs)  16.6 us
    pallas_call x2, Pallas kernels, pair_forces(): pl.pallas_call(functools.partial(force_kernel, row_count, col_count, len(...  14.9 us
    all_to_all x2, waiting for transfers between devices, shards(): lax.all_to_all(row_force, 'col', split_axis=0, concat_axis=0, tiled=True)  13.5 us
    ppermute x7, waiting for transfers between devices, from_shift(): return lax.ppermute(value, 'row', pairs)  12.8 us
    ppermute x11, starting transfers between devices, from_bits(): return lax.ppermute(value, 'col', pairs)  10.2 us
    all_gather x1, blocking collectives, shards(): row_y = (lax.all_gather(embed, 'col', axis=0, tiled=False),)  10 us
    ppermute x7, starting transfers between devices, from_shift(): return lax.ppermute(value, 'row', pairs)  9.48 us
    all_to_all x2, starting transfers between devices, shards(): lax.all_to_all(row_force, 'col', split_axis=0, concat_axis=0, tiled=True)  7.11 us
  transfers between devices with their start and end apart: 27, of which 11 were waited for; matrix products, arithmetic and copies ran while one was open for 5% of the time, Pallas kernels for 3%

profile of v9, /device:TPU:0, one launch (start us, length us, event | category | flops | bytes accessed | tf_op | source)
XLA Modules:
  0.0 119.0 jit_solution(11930403106891911406)
XLA Ops:
  0.6 5.1 %collective-permute-start.3 = (f32[256,768]{1,0:T(8,128)}, f32[256,768]{1,0:T(8,128)S(1)}, u32[]{:S(2)}, u32[]{:S(2)}) collective-permute-start(f32[256,768]{1,0:T(8,128)} %rest_0_.1), channel_id=1, source_target_pairs={{8,0},{16,8},{24,16},{0,24},{9,1},{17,9},{25,17},{1,25},{10,2},{18... | collective-permute-start | bytes 2359304 | tf_op jit(solution)/shard_map/ppermute | solution.py:424
  5.7 1.5 %collective-permute-start.5 = (f32[256,768]{1,0:T(8,128)}, f32[256,768]{1,0:T(8,128)S(1)}, u32[]{:S(2)}, u32[]{:S(2)}) collective-permute-start(f32[256,768]{1,0:T(8,128)} %rest_0_.1), channel_id=1, source_target_pairs={{2,0},{3,1},{0,2},{1,3},{6,4},{7,5},{4,6},{5,7},{10,8},{11,9},{8,1... | collective-permute-start | bytes 2359304 | tf_op jit(solution)/shard_map/ppermute | solution.py:437
  7.2 1.5 %collective-permute-start.6 = (f32[256,768]{1,0:T(8,128)}, f32[256,768]{1,0:T(8,128)S(1)}, u32[]{:S(2)}, u32[]{:S(2)}) collective-permute-start(f32[256,768]{1,0:T(8,128)} %rest_0_.1), channel_id=1, source_target_pairs={{4,0},{5,1},{6,2},{7,3},{0,4},{1,5},{2,6},{3,7},{12,8},{13,9},{14,... | collective-permute-start | bytes 2359304 | tf_op jit(solution)/shard_map/ppermute | solution.py:437
  9.6 1.3 %multiply_reduce_fusion = f32[256]{0:T(256)S(1)} fusion(f32[256,768]{1,0:T(8,128)} %rest_0_.1), kind=kLoop, calls=%fused_computation | loop fusion | flops 392960 | bytes 787456 | tf_op jit(solution)/shard_map/reduce_sum | solution.py:457
  10.9 1.6 %concatenate.7.rest_3_.rest_2_ = f32[72,256]{1,0:T(8,128)S(1)} concatenate(f32[64,256]{1,0:T(8,128)} %param.13, f32[1,256]{1,0:T(1,128)} %bitcast.28, f32[1,256]{1,0:T(1,128)} %bitcast.29, f32[1,256]{1,0:T(1,128)S(1)} %bitcast.27, f32[1,256]{1,0:T(1,128)S(1)} %pad.12, f32[4,256]{1,0:T(4,128)S(1)} %broadcast_in_dim.4), dimensions={0} | concatenate | bytes 147456 | tf_op jit(solution)/shard_map/concatenate | solution.py:459
  13.0 0.8 copy.16
  14.4 0.8 copy.15
  15.3 8.7 %collective-permute-done.3.rest_1_ = f32[256,768]{1,0:T(8,128)S(1)} collective-permute-done((f32[256,768]{1,0:T(8,128)}, f32[256,768]{1,0:T(8,128)S(1)}, u32[]{:S(2)}, u32[]{:S(2)}) %collective-permute-start.3) | collective-permute-done | bytes 786464 | tf_op jit(solution)/shard_map/ppermute | solution.py:424
  25.0 1.2 %collective-permute-done.6.rest_5_ = f32[256,768]{1,0:T(8,128)S(1)} collective-permute-done((f32[256,768]{1,0:T(8,128)}, f32[256,768]{1,0:T(8,128)S(1)}, u32[]{:S(2)}, u32[]{:S(2)}) %collective-permute-start.6) | collective-permute-done | bytes 786464 | tf_op jit(solution)/shard_map/ppermute | solution.py:437
  26.7 4.1 %collective-permute-done.2.rest_5_ = f32[64,256]{1,0:T(8,128)S(1)} collective-permute-done((f32[64,256]{1,0:T(8,128)}, f32[64,256]{1,0:T(8,128)S(1)}, u32[]{:S(2)}, u32[]{:S(2)}) %collective-permute-start.2) | collective-permute-done | bytes 65568 | tf_op jit(solution)/shard_map/ppermute | solution.py:424
  30.7 2.5 %collective-permute-start.10 = (f32[256,768]{1,0:T(8,128)}, f32[256,768]{1,0:T(8,128)S(1)}, u32[]{:S(2)}, u32[]{:S(2)}) collective-permute-start(f32[256,768]{1,0:T(8,128)} %rest_0_.1), channel_id=1, source_target_pairs={{6,0},{7,1},{4,2},{5,3},{2,4},{3,5},{0,6},{1,7},{14,8},{15,9},{12,... | collective-permute-start | bytes 2359304 | tf_op jit(solution)/shard_map/ppermute | solution.py:437
  33.3 1.3 %collective-permute-start.9 = (f32[256,768]{1,0:T(8,128)}, f32[256,768]{1,0:T(8,128)S(1)}, u32[]{:S(2)}, u32[]{:S(2)}) collective-permute-start(f32[256,768]{1,0:T(8,128)} %rest_0_.1), channel_id=1, source_target_pairs={{16,0},{8,24},{17,1},{9,25},{18,2},{10,26},{19,3},{11,27},{20,4},{... | collective-permute-start | bytes 2359304 | tf_op jit(solution)/shard_map/ppermute | solution.py:429
  35.2 1.5 %collective-permute-start.12 = (f32[72,256]{1,0:T(8,128)S(1)}, f32[72,256]{1,0:T(8,128)S(1)}, u32[]{:S(2)}, u32[]{:S(2)}) collective-permute-start(f32[72,256]{1,0:T(8,128)S(1)} %pad_add_fusion), channel_id=1, source_target_pairs={{4,0},{5,1},{6,2},{7,3},{0,4},{1,5},{2,6},{3,7},{12,8},{13,9},{14,... | collective-permute-start | bytes 221192 | tf_op jit(solution)/shard_map/ppermute | solution.py:437
  36.7 1.5 %collective-permute-start.11 = (f32[72,256]{1,0:T(8,128)S(1)}, f32[72,256]{1,0:T(8,128)S(1)}, u32[]{:S(2)}, u32[]{:S(2)}) collective-permute-start(f32[72,256]{1,0:T(8,128)S(1)} %pad_add_fusion), channel_id=1, source_target_pairs={{2,0},{3,1},{0,2},{1,3},{6,4},{7,5},{4,6},{5,7},{10,8},{11,9},{8,1... | collective-permute-start | bytes 221192 | tf_op jit(solution)/shard_map/ppermute | solution.py:437
  38.2 4.0 %grams.1 = (f32[6,2,128,128]{3,2,1,0:T(8,128)S(1)}, bf16[2,256,768]{2,1,0:T(8,128)(2,1)S(1)}, bf16[2,256,768]{2,1,0:T(8,128)(2,1)S(1)}, bf16[6,128,768]{2,1,0:T(8,128)(2,1)S(1)}, bf16[6,128,768]{2,1,0:T(8,128)(2,1)S(1)}) custom-call(s32[11]{0:T(128)S(1)} %pad_add_fusion.1.meta, s32[64]{0:T(128)S(1)} %reshape.27.listing, f32[256,768]{1,0:T(8,128)S(1)} %copy-done, ...), custom_call_target="tpu_custom_call" | custom-call | flops 905969664 | bytes 6291456 | tf_op jit(solution)/shard_map/grams/pallas_call | solution.py:109
  42.2 11.7 %collective-permute-done.13 = f32[72,256]{1,0:T(8,128)S(1)} collective-permute-done((f32[72,256]{1,0:T(8,128)S(1)}, f32[72,256]{1,0:T(8,128)S(1)}, u32[]{:S(2)}, u32[]{:S(2)}) %collective-permute-start.13) | collective-permute-done | bytes 73760 | tf_op jit(solution)/shard_map/ppermute | solution.py:437
  53.9 1.1 collective-permute-done.12
  55.9 2.0 %collective-permute-done.15.rest_7_.rest_1_ = f32[4,72,256]{2,1,0:T(8,128)S(1)} collective-permute-done((f32[4,72,256]{2,1,0:T(8,128)S(1)}, f32[4,72,256]{2,1,0:T(8,128)S(1)}, u32[]{:S(2)}, u32[]{:S(2)}) %collective-permute-start.15) | collective-permute-done | bytes 294944 | tf_op jit(solution)/shard_map/ppermute | solution.py:437
  57.9 4.6 %weights.1 = bf16[24,128,128]{2,1,0:T(8,128)(2,1)S(1)} custom-call(s32[11]{0:T(128)S(1)} %pad_add_fusion.1.meta, s32[64]{0:T(128)S(1)} %reshape.27.listing, s32[32]{0:T(128)S(1)} %reshape.28.seeds, f32[6,2,128,128]{3,2,1,0:T(8,128)S(1)} %get-tuple-element.33.grams, bf16[2,256,768]{2,1,0:T(8,128)(2,1)S(1)} %get-tuple-element.34.high_c, ...), custom_call_target="tpu_custom_call" | custom-call | flops 905969664 | bytes 2359296 | tf_op jit(solution)/shard_map/weights/pallas_call | solution.py:217
  62.5 7.5 %forces.2 = (f32[8,64,256]{2,1,0:T(8,128)}, f32[64,256]{1,0:T(8,128)S(1)}, f32[64,256]{1,0:T(8,128)S(1)}, f32[64,256]{1,0:T(8,128)S(1)}, f32[64,256]{1,0:T(8,128)S(1)}) custom-call(s32[11]{0:T(128)S(1)} %pad_add_fusion.1.meta, s32[64]{0:T(128)S(1)} %reshape.27.listing, s32[48]{0:T(128)S(1)} %bitcast.19, s32[48]{0:T(128)S(1)} %bitcast.21, ...), custom_call_target="tpu_custom_call" | custom-call | flops 1744830464 | bytes 1572864 | tf_op jit(solution)/shard_map/forces/pallas_call | solution.py:385
  70.0 3.6 %all-to-all-start = ((f32[8,64,256]{2,1,0:T(8,128)}), f32[8,64,256]{2,1,0:T(8,128)S(1)}, u32[]{:S(2)}, u32[]{:S(2)}) async-start(f32[8,64,256]{2,1,0:T(8,128)} %get-tuple-element.42), calls=%async_computation | async-start | bytes 1048576 | tf_op jit(solution)/shard_map/all_to_all | solution.py:500
  73.6 1.3 %collective-permute-start.18 = (f32[64,256]{1,0:T(8,128)S(1)}, f32[64,256]{1,0:T(8,128)S(1)}, u32[]{:S(2)}, u32[]{:S(2)}) collective-permute-start(f32[64,256]{1,0:T(8,128)S(1)} %get-tuple-element.46), channel_id=1, source_target_pairs={{0,24},{8,0},{16,8},{24,16},{1,25},{9,1},{17,9},{25,17},{2,26},{10... | collective-permute-start | bytes 196616 | tf_op jit(solution)/shard_map/ppermute | solution.py:433
  75.1 2.0 %collective-permute-start.16 = (f32[64,256]{1,0:T(8,128)S(1)}, f32[64,256]{1,0:T(8,128)S(1)}, u32[]{:S(2)}, u32[]{:S(2)}) collective-permute-start(f32[64,256]{1,0:T(8,128)S(1)} %get-tuple-element.44), channel_id=1, source_target_pairs={{0,8},{8,16},{16,24},{24,0},{1,9},{9,17},{17,25},{25,1},{2,10},{10... | collective-permute-start | bytes 196616 | tf_op jit(solution)/shard_map/ppermute | solution.py:433
  77.0 6.2 %all-to-all-done = f32[8,64,256]{2,1,0:T(8,128)S(1)} async-done(((f32[8,64,256]{2,1,0:T(8,128)}), f32[8,64,256]{2,1,0:T(8,128)S(1)}, u32[]{:S(2)}, u32[]{:S(2)}) %all-to-all-start) | async-done | bytes 524320 | tf_op jit(solution)/shard_map/all_to_all | solution.py:500
  83.4 1.4 %collective-permute-start.19 = (f32[64,256]{1,0:T(8,128)S(1)}, f32[64,256]{1,0:T(8,128)S(1)}, u32[]{:S(2)}, u32[]{:S(2)}) collective-permute-start(f32[64,256]{1,0:T(8,128)S(1)} %multiply_add_fusion.1.rest_1_), channel_id=1, source_target_pairs={{8,0},{16,8},{24,16},{0,24},{9,1},{17,9},{25,17},{1,25},{10,2},{18... | collective-permute-start | bytes 196616 | tf_op jit(solution)/shard_map/ppermute | solution.py:424
  85.0 1.9 %collective-permute-start.21 = (f32[64,256]{1,0:T(8,128)S(1)}, f32[64,256]{1,0:T(8,128)S(1)}, u32[]{:S(2)}, u32[]{:S(2)}) collective-permute-start(f32[64,256]{1,0:T(8,128)S(1)} %multiply_add_fusion.1.rest_1_), channel_id=1, source_target_pairs={{24,0},{0,8},{8,16},{16,24},{25,1},{1,9},{9,17},{17,25},{26,2},{2,... | collective-permute-start | bytes 196616 | tf_op jit(solution)/shard_map/ppermute | solution.py:424
  87.0 10.0 %all-gather = f32[512,256]{1,0:T(8,128)S(1)} all-gather(f32[64,256]{1,0:T(8,128)S(1)} %multiply_add_fusion.1.rest_1_), channel_id=2, replica_groups=mesh['row'=4,'col'=8] {'col'}, dimensions={0}, use_global_device_ids=true | all-gather | bytes 589824 | tf_op jit(solution)/shard_map/all_gather | solution.py:497
  97.0 7.4 %forces.3 = (f32[8,64,256]{2,1,0:T(8,128)}, f32[64,256]{1,0:T(8,128)S(1)}, f32[64,256]{1,0:T(8,128)S(1)}, f32[64,256]{1,0:T(8,128)S(1)}, f32[64,256]{1,0:T(8,128)S(1)}) custom-call(s32[11]{0:T(128)S(1)} %pad_add_fusion.1.meta, s32[64]{0:T(128)S(1)} %reshape.27.listing, s32[48]{0:T(128)S(1)} %bitcast.20, s32[48]{0:T(128)S(1)} %bitcast.22, ...), custom_call_target="tpu_custom_call" | custom-call | flops 1744830464 | bytes 1572864 | tf_op jit(solution)/shard_map/forces/pallas_call | solution.py:385
  104.4 3.5 %all-to-all-start.1 = ((f32[8,64,256]{2,1,0:T(8,128)}), f32[8,64,256]{2,1,0:T(8,128)S(1)}, u32[]{:S(2)}, u32[]{:S(2)}) async-start(f32[8,64,256]{2,1,0:T(8,128)} %get-tuple-element.47), calls=%async_computation.1 | async-start | bytes 1048576 | tf_op jit(solution)/shard_map/all_to_all | solution.py:500
  107.9 0.9 collective-permute-start.24
  108.8 0.8 collective-permute-start.23
  110.3 7.2 %all-to-all-done.1 = f32[8,64,256]{2,1,0:T(8,128)S(1)} async-done(((f32[8,64,256]{2,1,0:T(8,128)}), f32[8,64,256]{2,1,0:T(8,128)S(1)}, u32[]{:S(2)}, u32[]{:S(2)}) %all-to-all-start.1) | async-done | bytes 524320 | tf_op jit(solution)/shard_map/all_to_all | solution.py:500
  (57 shorter events, 6.9 us)
Async XLA Ops:
  0.6 37.5 %copy-start = (f32[256,768]{1,0:T(8,128)S(1)}, f32[256,768]{1,0:T(8,128)}, u32[]{:S(2)}) copy-start(f32[256,768]{1,0:T(8,128)} %rest_0_.1) | copy-start | bytes 2359300
  0.6 23.4 %collective-permute-start.3 = (f32[256,768]{1,0:T(8,128)}, f32[256,768]{1,0:T(8,128)S(1)}, u32[]{:S(2)}, u32[]{:S(2)}) collective-permute-start(f32[256,768]{1,0:T(8,128)} %rest_0_.1), channel_id=1, source_target_pairs={{8,0},{16,8},{24,16},{0,24},{9,1},{17,9},{25,17},{1,25},{10,2},{18... | collective-permute-start | bytes 2359304 | tf_op jit(solution)/shard_map/ppermute | solution.py:424
  5.7 19.2 %collective-permute-start.5 = (f32[256,768]{1,0:T(8,128)}, f32[256,768]{1,0:T(8,128)S(1)}, u32[]{:S(2)}, u32[]{:S(2)}) collective-permute-start(f32[256,768]{1,0:T(8,128)} %rest_0_.1), channel_id=1, source_target_pairs={{2,0},{3,1},{0,2},{1,3},{6,4},{7,5},{4,6},{5,7},{10,8},{11,9},{8,1... | collective-permute-start | bytes 2359304 | tf_op jit(solution)/shard_map/ppermute | solution.py:437
  7.2 18.9 %collective-permute-start.6 = (f32[256,768]{1,0:T(8,128)}, f32[256,768]{1,0:T(8,128)S(1)}, u32[]{:S(2)}, u32[]{:S(2)}) collective-permute-start(f32[256,768]{1,0:T(8,128)} %rest_0_.1), channel_id=1, source_target_pairs={{4,0},{5,1},{6,2},{7,3},{0,4},{1,5},{2,6},{3,7},{12,8},{13,9},{14,... | collective-permute-start | bytes 2359304 | tf_op jit(solution)/shard_map/ppermute | solution.py:437
  12.4 18.3 %collective-permute-start = (f32[72,256]{1,0:T(8,128)S(1)}, f32[72,256]{1,0:T(8,128)S(1)}, u32[]{:S(2)}, u32[]{:S(2)}) collective-permute-start(f32[72,256]{1,0:T(8,128)S(1)} %concatenate.7.rest_3_.rest_2_), channel_id=1, source_target_pairs={{8,0},{16,8},{24,16},{0,24},{9,1},{17,9},{25,17},{1,25},{10,2},{18... | collective-permute-start | bytes 221192 | tf_op jit(solution)/shard_map/ppermute | solution.py:424
  12.9 17.8 %collective-permute-start.1 = (f32[72,256]{1,0:T(8,128)S(1)}, f32[72,256]{1,0:T(8,128)S(1)}, u32[]{:S(2)}, u32[]{:S(2)}) collective-permute-start(f32[72,256]{1,0:T(8,128)S(1)} %concatenate.7.rest_3_.rest_2_), channel_id=1, source_target_pairs={{16,0},{24,8},{0,16},{8,24},{17,1},{25,9},{1,17},{9,25},{18,2},{26... | collective-permute-start | bytes 221192 | tf_op jit(solution)/shard_map/ppermute | solution.py:424
  24.0 6.7 %collective-permute-start.2 = (f32[64,256]{1,0:T(8,128)}, f32[64,256]{1,0:T(8,128)S(1)}, u32[]{:S(2)}, u32[]{:S(2)}) collective-permute-start(f32[64,256]{1,0:T(8,128)} %param.13), channel_id=1, source_target_pairs={{24,0},{0,8},{8,16},{16,24},{25,1},{1,9},{9,17},{17,25},{26,2},{2,... | collective-permute-start | bytes 196616 | tf_op jit(solution)/shard_map/ppermute | solution.py:424
  26.2 8.4 %collective-permute-start.7 = (f32[256,768]{1,0:T(8,128)S(1)}, f32[256,768]{1,0:T(8,128)S(1)}, u32[]{:S(2)}, u32[]{:S(2)}) collective-permute-start(f32[256,768]{1,0:T(8,128)S(1)} %collective-permute-done.5.rest_3_), channel_id=1, source_target_pairs={{1,0},{0,1},{3,2},{2,3},{5,4},{4,5},{7,6},{6,7},{9,8},{8,9},{11,10... | collective-permute-start | bytes 2359304 | tf_op jit(solution)/shard_map/ppermute | solution.py:437
  26.2 8.4 %collective-permute-start.8 = (f32[256,768]{1,0:T(8,128)S(1)}, f32[256,768]{1,0:T(8,128)S(1)}, u32[]{:S(2)}, u32[]{:S(2)}) collective-permute-start(f32[256,768]{1,0:T(8,128)S(1)} %collective-permute-done.6.rest_5_), channel_id=1, source_target_pairs={{1,0},{0,1},{3,2},{2,3},{5,4},{4,5},{7,6},{6,7},{9,8},{8,9},{11,10... | collective-permute-start | bytes 2359304 | tf_op jit(solution)/shard_map/ppermute | solution.py:437
  30.7 5.9 %collective-permute-start.4 = (f32[256,768]{1,0:T(8,128)}, f32[256,768]{1,0:T(8,128)S(1)}, u32[]{:S(2)}, u32[]{:S(2)}) collective-permute-start(f32[256,768]{1,0:T(8,128)} %rest_0_.1), channel_id=1, source_target_pairs={{1,0},{0,1},{3,2},{2,3},{5,4},{4,5},{7,6},{6,7},{9,8},{8,9},{11,10... | collective-permute-start | bytes 2359304 | tf_op jit(solution)/shard_map/ppermute | solution.py:437
  30.7 24.3 %collective-permute-start.10 = (f32[256,768]{1,0:T(8,128)}, f32[256,768]{1,0:T(8,128)S(1)}, u32[]{:S(2)}, u32[]{:S(2)}) collective-permute-start(f32[256,768]{1,0:T(8,128)} %rest_0_.1), channel_id=1, source_target_pairs={{6,0},{7,1},{4,2},{5,3},{2,4},{3,5},{0,6},{1,7},{14,8},{15,9},{12,... | collective-permute-start | bytes 2359304 | tf_op jit(solution)/shard_map/ppermute | solution.py:437
  33.3 22.6 %collective-permute-start.9 = (f32[256,768]{1,0:T(8,128)}, f32[256,768]{1,0:T(8,128)S(1)}, u32[]{:S(2)}, u32[]{:S(2)}) collective-permute-start(f32[256,768]{1,0:T(8,128)} %rest_0_.1), channel_id=1, source_target_pairs={{16,0},{8,24},{17,1},{9,25},{18,2},{10,26},{19,3},{11,27},{20,4},{... | collective-permute-start | bytes 2359304 | tf_op jit(solution)/shard_map/ppermute | solution.py:429
  34.6 19.3 %collective-permute-start.13 = (f32[72,256]{1,0:T(8,128)S(1)}, f32[72,256]{1,0:T(8,128)S(1)}, u32[]{:S(2)}, u32[]{:S(2)}) collective-permute-start(f32[72,256]{1,0:T(8,128)S(1)} %pad_add_fusion), channel_id=1, source_target_pairs={{6,0},{7,1},{4,2},{5,3},{2,4},{3,5},{0,6},{1,7},{14,8},{15,9},{12,... | collective-permute-start | bytes 221192 | tf_op jit(solution)/shard_map/ppermute | solution.py:437
  35.2 19.8 %collective-permute-start.12 = (f32[72,256]{1,0:T(8,128)S(1)}, f32[72,256]{1,0:T(8,128)S(1)}, u32[]{:S(2)}, u32[]{:S(2)}) collective-permute-start(f32[72,256]{1,0:T(8,128)S(1)} %pad_add_fusion), channel_id=1, source_target_pairs={{4,0},{5,1},{6,2},{7,3},{0,4},{1,5},{2,6},{3,7},{12,8},{13,9},{14,... | collective-permute-start | bytes 221192 | tf_op jit(solution)/shard_map/ppermute | solution.py:437
  36.7 18.4 %collective-permute-start.11 = (f32[72,256]{1,0:T(8,128)S(1)}, f32[72,256]{1,0:T(8,128)S(1)}, u32[]{:S(2)}, u32[]{:S(2)}) collective-permute-start(f32[72,256]{1,0:T(8,128)S(1)} %pad_add_fusion), channel_id=1, source_target_pairs={{2,0},{3,1},{0,2},{1,3},{6,4},{7,5},{4,6},{5,7},{10,8},{11,9},{8,1... | collective-permute-start | bytes 221192 | tf_op jit(solution)/shard_map/ppermute | solution.py:437
  55.1 2.8 %collective-permute-start.14 = (f32[256,768]{1,0:T(8,128)S(1)}, f32[256,768]{1,0:T(8,128)S(1)}, u32[]{:S(2)}, u32[]{:S(2)}) collective-permute-start(f32[256,768]{1,0:T(8,128)S(1)} %collective-permute-done.10.rest_1_), channel_id=1, source_target_pairs={{1,0},{0,1},{3,2},{2,3},{5,4},{4,5},{7,6},{6,7},{9,8},{8,9},{11,10... | collective-permute-start | bytes 2359304 | tf_op jit(solution)/shard_map/ppermute | solution.py:437
  55.2 2.7 %collective-permute-start.15 = (f32[4,72,256]{2,1,0:T(8,128)S(1)}, f32[4,72,256]{2,1,0:T(8,128)S(1)}, u32[]{:S(2)}, u32[]{:S(2)}) collective-permute-start(f32[4,72,256]{2,1,0:T(8,128)S(1)} %pad_maximum_fusion.rest_6_.rest_0_), channel_id=1, source_target_pairs={{1,0},{0,1},{3,2},{2,3},{5,4},{4,5},{7,6},{6,7},{9,8},{8,9},{11,10... | collective-permute-start | bytes 884744 | tf_op jit(solution)/shard_map/ppermute | solution.py:437
  57.9 4.6 %copy-start.1 = (s32[1,1,48]{2,1,0:T(1,128)S(1)}, s32[1,1,48]{2,1,0:T(1,128)}, u32[]{:S(2)}) copy-start(s32[1,1,48]{2,1,0:T(1,128)} %param.16) | copy-start | bytes 580
  57.9 4.6 %copy-start.2 = (s32[1,1,48]{2,1,0:T(1,128)S(1)}, s32[1,1,48]{2,1,0:T(1,128)}, u32[]{:S(2)}) copy-start(s32[1,1,48]{2,1,0:T(1,128)} %param.17) | copy-start | bytes 580
  70.0 13.4 %copy-start.3 = (f32[64,256]{1,0:T(8,128)S(1)}, f32[64,256]{1,0:T(8,128)}, u32[]{:S(2)}) copy-start(f32[64,256]{1,0:T(8,128)} %param.13) | copy-start | bytes 196612
  70.0 13.3 %all-to-all-start = ((f32[8,64,256]{2,1,0:T(8,128)}), f32[8,64,256]{2,1,0:T(8,128)S(1)}, u32[]{:S(2)}, u32[]{:S(2)}) async-start(f32[8,64,256]{2,1,0:T(8,128)} %get-tuple-element.42), calls=%async_computation | async-start | bytes 1048576 | tf_op jit(solution)/shard_map/all_to_all | solution.py:500
  73.6 9.7 %collective-permute-start.18 = (f32[64,256]{1,0:T(8,128)S(1)}, f32[64,256]{1,0:T(8,128)S(1)}, u32[]{:S(2)}, u32[]{:S(2)}) collective-permute-start(f32[64,256]{1,0:T(8,128)S(1)} %get-tuple-element.46), channel_id=1, source_target_pairs={{0,24},{8,0},{16,8},{24,16},{1,25},{9,1},{17,9},{25,17},{2,26},{10... | collective-permute-start | bytes 196616 | tf_op jit(solution)/shard_map/ppermute | solution.py:433
  74.9 8.4 %collective-permute-start.17 = (f32[64,256]{1,0:T(8,128)S(1)}, f32[64,256]{1,0:T(8,128)S(1)}, u32[]{:S(2)}, u32[]{:S(2)}) collective-permute-start(f32[64,256]{1,0:T(8,128)S(1)} %get-tuple-element.45), channel_id=1, source_target_pairs={{0,16},{8,24},{16,0},{24,8},{1,17},{9,25},{17,1},{25,9},{2,18},{10... | collective-permute-start | bytes 196616 | tf_op jit(solution)/shard_map/ppermute | solution.py:433
  75.1 8.2 %collective-permute-start.16 = (f32[64,256]{1,0:T(8,128)S(1)}, f32[64,256]{1,0:T(8,128)S(1)}, u32[]{:S(2)}, u32[]{:S(2)}) collective-permute-start(f32[64,256]{1,0:T(8,128)S(1)} %get-tuple-element.44), channel_id=1, source_target_pairs={{0,8},{8,16},{16,24},{24,0},{1,9},{9,17},{17,25},{25,1},{2,10},{10... | collective-permute-start | bytes 196616 | tf_op jit(solution)/shard_map/ppermute | solution.py:433
  83.4 13.6 %collective-permute-start.19 = (f32[64,256]{1,0:T(8,128)S(1)}, f32[64,256]{1,0:T(8,128)S(1)}, u32[]{:S(2)}, u32[]{:S(2)}) collective-permute-start(f32[64,256]{1,0:T(8,128)S(1)} %multiply_add_fusion.1.rest_1_), channel_id=1, source_target_pairs={{8,0},{16,8},{24,16},{0,24},{9,1},{17,9},{25,17},{1,25},{10,2},{18... | collective-permute-start | bytes 196616 | tf_op jit(solution)/shard_map/ppermute | solution.py:424
  84.8 12.2 %collective-permute-start.20 = (f32[64,256]{1,0:T(8,128)S(1)}, f32[64,256]{1,0:T(8,128)S(1)}, u32[]{:S(2)}, u32[]{:S(2)}) collective-permute-start(f32[64,256]{1,0:T(8,128)S(1)} %multiply_add_fusion.1.rest_1_), channel_id=1, source_target_pairs={{16,0},{24,8},{0,16},{8,24},{17,1},{25,9},{1,17},{9,25},{18,2},{26... | collective-permute-start | bytes 196616 | tf_op jit(solution)/shard_map/ppermute | solution.py:424
  85.0 12.0 %collective-permute-start.21 = (f32[64,256]{1,0:T(8,128)S(1)}, f32[64,256]{1,0:T(8,128)S(1)}, u32[]{:S(2)}, u32[]{:S(2)}) collective-permute-start(f32[64,256]{1,0:T(8,128)S(1)} %multiply_add_fusion.1.rest_1_), channel_id=1, source_target_pairs={{24,0},{0,8},{8,16},{16,24},{25,1},{1,9},{9,17},{17,25},{26,2},{2,... | collective-permute-start | bytes 196616 | tf_op jit(solution)/shard_map/ppermute | solution.py:424
  104.4 13.2 %all-to-all-start.1 = ((f32[8,64,256]{2,1,0:T(8,128)}), f32[8,64,256]{2,1,0:T(8,128)S(1)}, u32[]{:S(2)}, u32[]{:S(2)}) async-start(f32[8,64,256]{2,1,0:T(8,128)} %get-tuple-element.47), calls=%async_computation.1 | async-start | bytes 1048576 | tf_op jit(solution)/shard_map/all_to_all | solution.py:500
  107.9 9.7 %collective-permute-start.24 = (f32[64,256]{1,0:T(8,128)S(1)}, f32[64,256]{1,0:T(8,128)S(1)}, u32[]{:S(2)}, u32[]{:S(2)}) collective-permute-start(f32[64,256]{1,0:T(8,128)S(1)} %get-tuple-element.51), channel_id=1, source_target_pairs={{0,24},{8,0},{16,8},{24,16},{1,25},{9,1},{17,9},{25,17},{2,26},{10... | collective-permute-start | bytes 196616 | tf_op jit(solution)/shard_map/ppermute | solution.py:433
  108.8 8.8 %collective-permute-start.23 = (f32[64,256]{1,0:T(8,128)S(1)}, f32[64,256]{1,0:T(8,128)S(1)}, u32[]{:S(2)}, u32[]{:S(2)}) collective-permute-start(f32[64,256]{1,0:T(8,128)S(1)} %get-tuple-element.50), channel_id=1, source_target_pairs={{0,16},{8,24},{16,0},{24,8},{1,17},{9,25},{17,1},{25,9},{2,18},{10... | collective-permute-start | bytes 196616 | tf_op jit(solution)/shard_map/ppermute | solution.py:433
  109.6 8.0 %collective-permute-start.22 = (f32[64,256]{1,0:T(8,128)S(1)}, f32[64,256]{1,0:T(8,128)S(1)}, u32[]{:S(2)}, u32[]{:S(2)}) collective-permute-start(f32[64,256]{1,0:T(8,128)S(1)} %get-tuple-element.49), channel_id=1, source_target_pairs={{0,8},{8,16},{16,24},{24,0},{1,9},{9,17},{17,25},{25,1},{2,10},{10... | collective-permute-start | bytes 196616 | tf_op jit(solution)/shard_map/ppermute | solution.py:433

commit v10 on v8

--- a/solution.py
+++ b/solution.py
@@ -220,7 +220,7 @@
     tiles = shifts * col_count
     return pl.pallas_call(
         functools.partial(weights_kernel, sizes, (shifts - 1, col_count - rows_late)),
-        in_specs=[smem] * 3 + [vmem] * (5 + CB * (1 + rows_late) + len(packs)),
+        in_specs=[smem] * 3 + [vmem] * (5 + len(last) + len(late) + len(packs)),
         out_specs=vmem,
         out_shape=jax.ShapeDtypeStruct((tiles, BLK, BLK), BF16),
         scratch_shapes=[
@@ -453,21 +453,24 @@
     for bits in single:
         row_x[bits] = from_bits(inputs, bits)
     col_x = [inputs] + [from_shift(inputs, shift) for shift in range(1, shifts - 1)]
+    row_x[1] = from_bits(inputs, 1)
     blocks = [inputs[block * BLK : (block + 1) * BLK] for block in range(CB)]
     first = {bits: from_bits(blocks[0], bits) for bits in late_bits if bits % 2 == 0}
     seed_row = jnp.pad(seeds.astype(F32)[None], ((0, 0), (0, SPAN - seeds.shape[0])))
     params = jnp.stack([rho, sigma, jnp.sum(inputs * inputs, axis=1)])
     blank = jnp.zeros((PACK - SEEDS - 1, SPAN), F32)
     pack = jnp.concatenate([embed, params, seed_row, blank], axis=0)
-    col_packs = [pack] + [from_shift(pack, shift) for shift in range(1, shifts)]
-    held, meta, listing, seeds = lax.optimization_barrier((inputs, meta, listing, seeds, *col_packs[1:]))[:4]
-    row_x[1] = from_bits(held, 1)
-    last = [from_half(after(blocks[0], *col_packs[1:]))]
+    held_pack, held_y = lax.optimization_barrier((pack, embed, *[row_x[bits] for bits in single]))[:2]
+    col_packs = [pack] + [from_shift(held_pack, shift) for shift in range(1, shifts)]
+    far_y = [from_shift(held_y, shift) for shift in range(shifts, row_count)]
+    last = [from_half(blocks[0])]
     near = [row_x[bits] for bits in single] + col_x[1:] + list(first.values()) + last
+    near += col_packs[1:] + far_y
+    meta, listing, seeds, *near = lax.optimization_barrier((meta, listing, seeds, *near))
     for bits in single:
         row_x[bits + 1] = from_bits(after(row_x[bits], *near), 1)
-    last.append(from_half(after(blocks[1], *near)))
-    late_x = {bits: [first[bits], from_bits(after(blocks[1], *near), bits)] for bits in first}
+    last.append(from_half(after(blocks[1], last[0])))
+    late_x = {bits: [first[bits], from_bits(after(blocks[1], first[bits]), bits)] for bits in first}
     late_x |= {bits + 1: [from_bits(after(first[bits], *near), 1)] for bits in first}
 
     own_pack = pack
@@ -483,8 +486,7 @@
     for bits in late_bits:
         if bits % 2 == 0:
             late_x[bits + 1].append(from_bits(after(late_x[bits][1], even_packs), 1))
-    held = after(embed, *[late_x[bits][1] for bits in first])
-    col_y = col_packs + [from_shift(held, shift) for shift in range(shifts, row_count)]
+    col_y = col_packs + far_y
 
     weights = pair_weights(
         sizes,

time: 123 us -> 122 us (level); the launches traced: 123 us -> 120 us
  waiting for transfers between devices: 37.7 us -> 41.8 us
  Pallas kernels: 21.4 us -> 19 us
  other arithmetic: 3.48 us -> 1.65 us
    ppermute x13, waiting for transfers between devices: 9.64 us -> 25.6 us  [from_bits(): return lax.ppermute(value, 'col', pairs)]
    ppermute x7, waiting for transfers between devices: 11.3 us -> 4.15 us  [from_shift(): return lax.ppermute(value, 'row', pairs)]
    ppermute x2, waiting for transfers between devices: 4.06 us -> 0.83 us  [from_half(): return lax.ppermute(value, 'row', pairs)]
    pallas_call x2, Pallas kernels: 11.4 us -> 9.77 us  [pair_forces(): pl.pallas_call(functools.partial(force_kernel, row_count, col_count, len(...]
    concatenate x1, local copies, waits for them, and re-layouts: 1.56 us -> 0.03 us  [shards(): pack = jnp.concatenate([embed, params, seed_row, blank], axis=0)]
    ppermute x6, starting transfers between devices: 9.29 us -> 10.6 us  [to_shift(): return lax.ppermute(value, 'row', pairs)]
    all_to_all x2, waiting for transfers between devices: 10.2 us -> 8.86 us  [shards(): lax.all_to_all(row_force, 'col', split_axis=0, concat_axis=0, tiled=True)]
  transfers between devices with their start and end apart: 30 -> 30, of which waited for: 10 -> 13; matrix products, arithmetic and copies ran while one was open for 4% -> 2% of each run, Pallas kernels for 8% -> 3%
where the time goes in v10:
time: 122 us; the launch traced here: 120 us
  starting transfers between devices  44.6 us (37%)
  waiting for transfers between devices  41.8 us (34%)
  Pallas kernels  19 us (16%)
  blocking collectives  9.09 us (7%)
  local copies, waits for them, and re-layouts  2.67 us (2%)
  other arithmetic  1.65 us (1%)
  between operations  1.54 us (1%)
    ppermute x13, waiting for transfers between devices, from_bits(): return lax.ppermute(value, 'col', pairs)  25.6 us
    ppermute x7, starting transfers between devices, from_shift(): return lax.ppermute(value, 'row', pairs)  13 us
    ppermute x13, starting transfers between devices, from_bits(): return lax.ppermute(value, 'col', pairs)  11.3 us
    ppermute x6, starting transfers between devices, to_shift(): return lax.ppermute(value, 'row', pairs)  10.6 us
    pallas_call x2, Pallas kernels, pair_forces(): pl.pallas_call(functools.partial(force_kernel, row_count, col_count, len(...  9.77 us
    all_gather x1, blocking collectives, shards(): row_y = (lax.all_gather(embed, 'col', axis=0, tiled=False),)  9.09 us
    all_to_all x2, waiting for transfers between devices, shards(): lax.all_to_all(row_force, 'col', split_axis=0, concat_axis=0, tiled=True)  8.86 us
    all_to_all x2, starting transfers between devices, shards(): lax.all_to_all(row_force, 'col', split_axis=0, concat_axis=0, tiled=True)  7.13 us
  transfers between devices with their start and end apart: 30, of which 13 were waited for; matrix products, arithmetic and copies ran while one was open for 2% of the time, Pallas kernels for 3%

profile of v10, /device:TPU:0, one launch (start us, length us, event | category | flops | bytes accessed | tf_op | source)
XLA Modules:
  0.0 120.4 jit_solution(8121892845476107322)
XLA Ops:
  0.7 3.0 %collective-permute-start = (f32[256,768]{1,0:T(8,128)}, f32[256,768]{1,0:T(8,128)S(1)}, u32[]{:S(2)}, u32[]{:S(2)}) collective-permute-start(f32[256,768]{1,0:T(8,128)} %rest_0_.1), channel_id=1, source_target_pairs={{2,0},{3,1},{0,2},{1,3},{6,4},{7,5},{4,6},{5,7},{10,8},{11,9},{8,1... | collective-permute-start | bytes 2359304 | tf_op jit(solution)/shard_map/ppermute | solution.py:441
  3.7 1.5 %collective-permute-start.1 = (f32[256,768]{1,0:T(8,128)}, f32[256,768]{1,0:T(8,128)S(1)}, u32[]{:S(2)}, u32[]{:S(2)}) collective-permute-start(f32[256,768]{1,0:T(8,128)} %rest_0_.1), channel_id=1, source_target_pairs={{4,0},{5,1},{6,2},{7,3},{0,4},{1,5},{2,6},{3,7},{12,8},{13,9},{14,... | collective-permute-start | bytes 2359304 | tf_op jit(solution)/shard_map/ppermute | solution.py:441
  5.2 3.6 %collective-permute-start.2 = (f32[256,768]{1,0:T(8,128)}, f32[256,768]{1,0:T(8,128)S(1)}, u32[]{:S(2)}, u32[]{:S(2)}) collective-permute-start(f32[256,768]{1,0:T(8,128)} %rest_0_.1), channel_id=1, source_target_pairs={{8,0},{16,8},{24,16},{0,24},{9,1},{17,9},{25,17},{1,25},{10,2},{18... | collective-permute-start | bytes 2359304 | tf_op jit(solution)/shard_map/ppermute | solution.py:428
  8.8 2.1 %fusion = (f32[128,768]{1,0:T(8,128)}, f32[128,768]{1,0:T(8,128)}) fusion(f32[256,768]{1,0:T(8,128)} %rest_0_.1), kind=kLoop, calls=%fused_computation.8 | loop fusion | bytes 1572864 | tf_op jit(solution)/shard_map/slice | solution.py:457
  11.3 1.3 %collective-permute-start.4 = (f32[128,768]{1,0:T(8,128)}, f32[128,768]{1,0:T(8,128)}, u32[]{:S(2)}, u32[]{:S(2)}) collective-permute-start(f32[128,768]{1,0:T(8,128)} %get-tuple-element.77), channel_id=1, source_target_pairs={{16,0},{8,24},{17,1},{9,25},{18,2},{10,26},{19,3},{11,27},{20,4},{... | collective-permute-start | bytes 1179656 | tf_op jit(solution)/shard_map/ppermute | solution.py:433
  14.1 8.2 %collective-permute-done.rest_3_ = f32[256,768]{1,0:T(8,128)S(1)} collective-permute-done((f32[256,768]{1,0:T(8,128)}, f32[256,768]{1,0:T(8,128)S(1)}, u32[]{:S(2)}, u32[]{:S(2)}) %collective-permute-start) | collective-permute-done | bytes 786464 | tf_op jit(solution)/shard_map/ppermute | solution.py:441
  22.3 9.1 %collective-permute-done.1.rest_5_ = f32[256,768]{1,0:T(8,128)S(1)} collective-permute-done((f32[256,768]{1,0:T(8,128)}, f32[256,768]{1,0:T(8,128)S(1)}, u32[]{:S(2)}, u32[]{:S(2)}) %collective-permute-start.1) | collective-permute-done | bytes 786464 | tf_op jit(solution)/shard_map/ppermute | solution.py:441
  31.3 3.6 %collective-permute-start.5 = (f32[72,256]{1,0:T(8,128)S(1)}, f32[72,256]{1,0:T(8,128)S(1)}, u32[]{:S(2)}, u32[]{:S(2)}) collective-permute-start(f32[72,256]{1,0:T(8,128)S(1)} %concatenate.7.rest_6_.rest_2_), channel_id=1, source_target_pairs={{8,0},{16,8},{24,16},{0,24},{9,1},{17,9},{25,17},{1,25},{10,2},{18... | collective-permute-start | bytes 221192 | tf_op jit(solution)/shard_map/ppermute | solution.py:428
  36.9 4.1 %collective-permute-done.7.rest_5_ = f32[64,256]{1,0:T(8,128)S(1)} collective-permute-done((f32[64,256]{1,0:T(8,128)S(1)}, f32[64,256]{1,0:T(8,128)S(1)}, u32[]{:S(2)}, u32[]{:S(2)}) %collective-permute-start.7) | collective-permute-done | bytes 65568 | tf_op jit(solution)/shard_map/ppermute | solution.py:428
  41.6 1.3 %collective-permute-start.11 = (f32[128,768]{1,0:T(8,128)}, f32[128,768]{1,0:T(8,128)S(1)}, u32[]{:S(2)}, u32[]{:S(2)}) collective-permute-start(f32[128,768]{1,0:T(8,128)} %get-tuple-element.59), channel_id=1, source_target_pairs={{16,0},{8,24},{17,1},{9,25},{18,2},{10,26},{19,3},{11,27},{20,4},{... | collective-permute-start | bytes 1179656 | tf_op jit(solution)/shard_map/ppermute | solution.py:433
  42.9 1.6 %collective-permute-start.12 = (f32[128,768]{1,0:T(8,128)}, f32[128,768]{1,0:T(8,128)S(1)}, u32[]{:S(2)}, u32[]{:S(2)}) collective-permute-start(f32[128,768]{1,0:T(8,128)} %get-tuple-element.59), channel_id=1, source_target_pairs={{6,0},{7,1},{4,2},{5,3},{2,4},{3,5},{0,6},{1,7},{14,8},{15,9},{12,... | collective-permute-start | bytes 1179656 | tf_op jit(solution)/shard_map/ppermute | solution.py:441
  44.5 1.5 %collective-permute-start.16 = (f32[72,256]{1,0:T(8,128)S(1)}, f32[72,256]{1,0:T(8,128)S(1)}, u32[]{:S(2)}, u32[]{:S(2)}) collective-permute-start(f32[72,256]{1,0:T(8,128)S(1)} %pad_add_fusion), channel_id=1, source_target_pairs={{6,0},{7,1},{4,2},{5,3},{2,4},{3,5},{0,6},{1,7},{14,8},{15,9},{12,... | collective-permute-start | bytes 221192 | tf_op jit(solution)/shard_map/ppermute | solution.py:441
  46.0 1.5 %collective-permute-start.15 = (f32[72,256]{1,0:T(8,128)S(1)}, f32[72,256]{1,0:T(8,128)S(1)}, u32[]{:S(2)}, u32[]{:S(2)}) collective-permute-start(f32[72,256]{1,0:T(8,128)S(1)} %pad_add_fusion), channel_id=1, source_target_pairs={{4,0},{5,1},{6,2},{7,3},{0,4},{1,5},{2,6},{3,7},{12,8},{13,9},{14,... | collective-permute-start | bytes 221192 | tf_op jit(solution)/shard_map/ppermute | solution.py:441
  48.0 4.0 %grams.1 = (f32[6,2,128,128]{3,2,1,0:T(8,128)S(1)}, bf16[2,256,768]{2,1,0:T(8,128)(2,1)S(1)}, bf16[2,256,768]{2,1,0:T(8,128)(2,1)S(1)}, bf16[6,128,768]{2,1,0:T(8,128)(2,1)S(1)}, bf16[6,128,768]{2,1,0:T(8,128)(2,1)S(1)}) custom-call(s32[11]{0:T(128)S(1)} %pad_add_fusion.1.meta, s32[64]{0:T(128)S(1)} %reshape.27.listing, f32[256,768]{1,0:T(8,128)S(1)} %copy-done, ...), custom_call_target="tpu_custom_call" | custom-call | flops 905969664 | bytes 6291456 | tf_op jit(solution)/shard_map/grams/pallas_call | solution.py:109
  52.0 5.6 %collective-permute-done.16 = f32[72,256]{1,0:T(8,128)S(1)} collective-permute-done((f32[72,256]{1,0:T(8,128)S(1)}, f32[72,256]{1,0:T(8,128)S(1)}, u32[]{:S(2)}, u32[]{:S(2)}) %collective-permute-start.16) | collective-permute-done | bytes 73760 | tf_op jit(solution)/shard_map/ppermute | solution.py:441
  59.5 1.5 %collective-permute-done.18.rest_10_.rest_1_ = f32[4,72,256]{2,1,0:T(8,128)S(1)} collective-permute-done((f32[4,72,256]{2,1,0:T(8,128)S(1)}, f32[4,72,256]{2,1,0:T(8,128)S(1)}, u32[]{:S(2)}, u32[]{:S(2)}) %collective-permute-start.18) | collective-permute-done | bytes 294944 | tf_op jit(solution)/shard_map/ppermute | solution.py:441
  61.0 5.3 %weights.1 = bf16[24,128,128]{2,1,0:T(8,128)(2,1)S(1)} custom-call(s32[11]{0:T(128)S(1)} %pad_add_fusion.1.meta, s32[64]{0:T(128)S(1)} %reshape.27.listing, s32[32]{0:T(128)S(1)} %reshape.28.seeds, f32[6,2,128,128]{3,2,1,0:T(8,128)S(1)} %get-tuple-element.53.grams, bf16[2,256,768]{2,1,0:T(8,128)(2,1)S(1)} %get-tuple-element.54.high_c, ...), custom_call_target="tpu_custom_call" | custom-call | flops 905969664 | bytes 2359296 | tf_op jit(solution)/shard_map/weights/pallas_call | solution.py:221
  66.3 4.9 %forces.2 = (f32[8,64,256]{2,1,0:T(8,128)}, f32[64,256]{1,0:T(8,128)S(1)}, f32[64,256]{1,0:T(8,128)S(1)}, f32[64,256]{1,0:T(8,128)S(1)}, f32[64,256]{1,0:T(8,128)S(1)}) custom-call(s32[11]{0:T(128)S(1)} %pad_add_fusion.1.meta, s32[64]{0:T(128)S(1)} %reshape.27.listing, s32[48]{0:T(128)S(1)} %bitcast.19, s32[48]{0:T(128)S(1)} %bitcast.21, ...), custom_call_target="tpu_custom_call" | custom-call | flops 1744830464 | bytes 1572864 | tf_op jit(solution)/shard_map/forces/pallas_call | solution.py:389
  71.2 3.5 %all-to-all-start = ((f32[8,64,256]{2,1,0:T(8,128)}), f32[8,64,256]{2,1,0:T(8,128)S(1)}, u32[]{:S(2)}, u32[]{:S(2)}) async-start(f32[8,64,256]{2,1,0:T(8,128)} %get-tuple-element.64), calls=%async_computation | async-start | bytes 1048576 | tf_op jit(solution)/shard_map/all_to_all | solution.py:508
  74.8 2.9 %collective-permute-start.21 = (f32[64,256]{1,0:T(8,128)S(1)}, f32[64,256]{1,0:T(8,128)S(1)}, u32[]{:S(2)}, u32[]{:S(2)}) collective-permute-start(f32[64,256]{1,0:T(8,128)S(1)} %get-tuple-element.68), channel_id=1, source_target_pairs={{0,24},{8,0},{16,8},{24,16},{1,25},{9,1},{17,9},{25,17},{2,26},{10... | collective-permute-start | bytes 196616 | tf_op jit(solution)/shard_map/ppermute | solution.py:437
  77.7 1.7 %collective-permute-start.20 = (f32[64,256]{1,0:T(8,128)S(1)}, f32[64,256]{1,0:T(8,128)S(1)}, u32[]{:S(2)}, u32[]{:S(2)}) collective-permute-start(f32[64,256]{1,0:T(8,128)S(1)} %get-tuple-element.67), channel_id=1, source_target_pairs={{0,16},{8,24},{16,0},{24,8},{1,17},{9,25},{17,1},{25,9},{2,18},{10... | collective-permute-start | bytes 196616 | tf_op jit(solution)/shard_map/ppermute | solution.py:437
  79.4 1.6 %collective-permute-start.19 = (f32[64,256]{1,0:T(8,128)S(1)}, f32[64,256]{1,0:T(8,128)S(1)}, u32[]{:S(2)}, u32[]{:S(2)}) collective-permute-start(f32[64,256]{1,0:T(8,128)S(1)} %get-tuple-element.66), channel_id=1, source_target_pairs={{0,8},{8,16},{16,24},{24,0},{1,9},{9,17},{17,25},{25,1},{2,10},{10... | collective-permute-start | bytes 196616 | tf_op jit(solution)/shard_map/ppermute | solution.py:437
  81.0 3.5 %all-to-all-done = f32[8,64,256]{2,1,0:T(8,128)S(1)} async-done(((f32[8,64,256]{2,1,0:T(8,128)}), f32[8,64,256]{2,1,0:T(8,128)S(1)}, u32[]{:S(2)}, u32[]{:S(2)}) %all-to-all-start) | async-done | bytes 524320 | tf_op jit(solution)/shard_map/all_to_all | solution.py:508
  84.6 1.4 %collective-permute-done.20 = f32[64,256]{1,0:T(8,128)S(1)} collective-permute-done((f32[64,256]{1,0:T(8,128)S(1)}, f32[64,256]{1,0:T(8,128)S(1)}, u32[]{:S(2)}, u32[]{:S(2)}) %collective-permute-start.20) | collective-permute-done | bytes 65568 | tf_op jit(solution)/shard_map/ppermute | solution.py:437
  86.0 1.6 %collective-permute-start.22 = (f32[64,256]{1,0:T(8,128)S(1)}, f32[64,256]{1,0:T(8,128)S(1)}, u32[]{:S(2)}, u32[]{:S(2)}) collective-permute-start(f32[64,256]{1,0:T(8,128)S(1)} %multiply_add_fusion.1.rest_1_), channel_id=1, source_target_pairs={{8,0},{16,8},{24,16},{0,24},{9,1},{17,9},{25,17},{1,25},{10,2},{18... | collective-permute-start | bytes 196616 | tf_op jit(solution)/shard_map/ppermute | solution.py:428
  87.6 1.6 %collective-permute-start.23 = (f32[64,256]{1,0:T(8,128)S(1)}, f32[64,256]{1,0:T(8,128)S(1)}, u32[]{:S(2)}, u32[]{:S(2)}) collective-permute-start(f32[64,256]{1,0:T(8,128)S(1)} %multiply_add_fusion.1.rest_1_), channel_id=1, source_target_pairs={{16,0},{24,8},{0,16},{8,24},{17,1},{25,9},{1,17},{9,25},{18,2},{26... | collective-permute-start | bytes 196616 | tf_op jit(solution)/shard_map/ppermute | solution.py:428
  89.1 1.6 %collective-permute-start.24 = (f32[64,256]{1,0:T(8,128)S(1)}, f32[64,256]{1,0:T(8,128)S(1)}, u32[]{:S(2)}, u32[]{:S(2)}) collective-permute-start(f32[64,256]{1,0:T(8,128)S(1)} %multiply_add_fusion.1.rest_1_), channel_id=1, source_target_pairs={{24,0},{0,8},{8,16},{16,24},{25,1},{1,9},{9,17},{17,25},{26,2},{2,... | collective-permute-start | bytes 196616 | tf_op jit(solution)/shard_map/ppermute | solution.py:428
  90.8 9.1 %all-gather = f32[512,256]{1,0:T(8,128)S(1)} all-gather(f32[64,256]{1,0:T(8,128)S(1)} %multiply_add_fusion.1.rest_1_), channel_id=2, replica_groups=mesh['row'=4,'col'=8] {'col'}, dimensions={0}, use_global_device_ids=true | all-gather | bytes 589824 | tf_op jit(solution)/shard_map/all_gather | solution.py:505
  99.9 4.9 %forces.3 = (f32[8,64,256]{2,1,0:T(8,128)}, f32[64,256]{1,0:T(8,128)S(1)}, f32[64,256]{1,0:T(8,128)S(1)}, f32[64,256]{1,0:T(8,128)S(1)}, f32[64,256]{1,0:T(8,128)S(1)}) custom-call(s32[11]{0:T(128)S(1)} %pad_add_fusion.1.meta, s32[64]{0:T(128)S(1)} %reshape.27.listing, s32[48]{0:T(128)S(1)} %bitcast.20, s32[48]{0:T(128)S(1)} %bitcast.22, ...), custom_call_target="tpu_custom_call" | custom-call | flops 1744830464 | bytes 1572864 | tf_op jit(solution)/shard_map/forces/pallas_call | solution.py:389
  104.7 3.6 %all-to-all-start.1 = ((f32[8,64,256]{2,1,0:T(8,128)}), f32[8,64,256]{2,1,0:T(8,128)S(1)}, u32[]{:S(2)}, u32[]{:S(2)}) async-start(f32[8,64,256]{2,1,0:T(8,128)} %get-tuple-element.69), calls=%async_computation.1 | async-start | bytes 1048576 | tf_op jit(solution)/shard_map/all_to_all | solution.py:508
  108.3 3.8 %collective-permute-start.27 = (f32[64,256]{1,0:T(8,128)S(1)}, f32[64,256]{1,0:T(8,128)S(1)}, u32[]{:S(2)}, u32[]{:S(2)}) collective-permute-start(f32[64,256]{1,0:T(8,128)S(1)} %get-tuple-element.73), channel_id=1, source_target_pairs={{0,24},{8,0},{16,8},{24,16},{1,25},{9,1},{17,9},{25,17},{2,26},{10... | collective-permute-start | bytes 196616 | tf_op jit(solution)/shard_map/ppermute | solution.py:437
  112.8 5.3 %all-to-all-done.1 = f32[8,64,256]{2,1,0:T(8,128)S(1)} async-done(((f32[8,64,256]{2,1,0:T(8,128)}), f32[8,64,256]{2,1,0:T(8,128)S(1)}, u32[]{:S(2)}, u32[]{:S(2)}) %all-to-all-start.1) | async-done | bytes 524320 | tf_op jit(solution)/shard_map/all_to_all | solution.py:508
  (72 shorter events, 9.2 us)
Async XLA Ops:
  0.7 13.4 %copy-start.3 = (f32[64,256]{1,0:T(8,128)S(1)}, f32[64,256]{1,0:T(8,128)}, u32[]{:S(2)}) copy-start(f32[64,256]{1,0:T(8,128)} %param.13) | copy-start | bytes 196612
  0.7 13.4 %copy-start.6 = (f32[256]{0:T(256)S(1)}, f32[256]{0:T(256)}, u32[]{:S(2)}) copy-start(f32[256]{0:T(256)} %param.11) | copy-start | bytes 3076
  0.7 21.6 %collective-permute-start = (f32[256,768]{1,0:T(8,128)}, f32[256,768]{1,0:T(8,128)S(1)}, u32[]{:S(2)}, u32[]{:S(2)}) collective-permute-start(f32[256,768]{1,0:T(8,128)} %rest_0_.1), channel_id=1, source_target_pairs={{2,0},{3,1},{0,2},{1,3},{6,4},{7,5},{4,6},{5,7},{10,8},{11,9},{8,1... | collective-permute-start | bytes 2359304 | tf_op jit(solution)/shard_map/ppermute | solution.py:441
  3.7 27.6 %collective-permute-start.1 = (f32[256,768]{1,0:T(8,128)}, f32[256,768]{1,0:T(8,128)S(1)}, u32[]{:S(2)}, u32[]{:S(2)}) collective-permute-start(f32[256,768]{1,0:T(8,128)} %rest_0_.1), channel_id=1, source_target_pairs={{4,0},{5,1},{6,2},{7,3},{0,4},{1,5},{2,6},{3,7},{12,8},{13,9},{14,... | collective-permute-start | bytes 2359304 | tf_op jit(solution)/shard_map/ppermute | solution.py:441
  5.2 31.7 %collective-permute-start.2 = (f32[256,768]{1,0:T(8,128)}, f32[256,768]{1,0:T(8,128)S(1)}, u32[]{:S(2)}, u32[]{:S(2)}) collective-permute-start(f32[256,768]{1,0:T(8,128)} %rest_0_.1), channel_id=1, source_target_pairs={{8,0},{16,8},{24,16},{0,24},{9,1},{17,9},{25,17},{1,25},{10,2},{18... | collective-permute-start | bytes 2359304 | tf_op jit(solution)/shard_map/ppermute | solution.py:428
  10.9 24.1 %collective-permute-start.3 = (f32[128,768]{1,0:T(8,128)}, f32[128,768]{1,0:T(8,128)}, u32[]{:S(2)}, u32[]{:S(2)}) collective-permute-start(f32[128,768]{1,0:T(8,128)} %get-tuple-element.77), channel_id=1, source_target_pairs={{6,0},{7,1},{4,2},{5,3},{2,4},{3,5},{0,6},{1,7},{14,8},{15,9},{12,... | collective-permute-start | bytes 1179656 | tf_op jit(solution)/shard_map/ppermute | solution.py:441
  11.3 25.5 %collective-permute-start.4 = (f32[128,768]{1,0:T(8,128)}, f32[128,768]{1,0:T(8,128)}, u32[]{:S(2)}, u32[]{:S(2)}) collective-permute-start(f32[128,768]{1,0:T(8,128)} %get-tuple-element.77), channel_id=1, source_target_pairs={{16,0},{8,24},{17,1},{9,25},{18,2},{10,26},{19,3},{11,27},{20,4},{... | collective-permute-start | bytes 1179656 | tf_op jit(solution)/shard_map/ppermute | solution.py:433
  31.3 9.7 %collective-permute-start.5 = (f32[72,256]{1,0:T(8,128)S(1)}, f32[72,256]{1,0:T(8,128)S(1)}, u32[]{:S(2)}, u32[]{:S(2)}) collective-permute-start(f32[72,256]{1,0:T(8,128)S(1)} %concatenate.7.rest_6_.rest_2_), channel_id=1, source_target_pairs={{8,0},{16,8},{24,16},{0,24},{9,1},{17,9},{25,17},{1,25},{10,2},{18... | collective-permute-start | bytes 221192 | tf_op jit(solution)/shard_map/ppermute | solution.py:428
  34.9 6.1 %collective-permute-start.6 = (f32[72,256]{1,0:T(8,128)S(1)}, f32[72,256]{1,0:T(8,128)S(1)}, u32[]{:S(2)}, u32[]{:S(2)}) collective-permute-start(f32[72,256]{1,0:T(8,128)S(1)} %concatenate.7.rest_6_.rest_2_), channel_id=1, source_target_pairs={{16,0},{24,8},{0,16},{8,24},{17,1},{25,9},{1,17},{9,25},{18,2},{26... | collective-permute-start | bytes 221192 | tf_op jit(solution)/shard_map/ppermute | solution.py:428
  34.9 6.1 %collective-permute-start.7 = (f32[64,256]{1,0:T(8,128)S(1)}, f32[64,256]{1,0:T(8,128)S(1)}, u32[]{:S(2)}, u32[]{:S(2)}) collective-permute-start(f32[64,256]{1,0:T(8,128)S(1)} %copy-done.3), channel_id=1, source_target_pairs={{24,0},{0,8},{8,16},{16,24},{25,1},{1,9},{9,17},{17,25},{26,2},{2,... | collective-permute-start | bytes 196616 | tf_op jit(solution)/shard_map/ppermute | solution.py:428
  41.0 3.5 %collective-permute-start.9 = (f32[256,768]{1,0:T(8,128)S(1)}, f32[256,768]{1,0:T(8,128)S(1)}, u32[]{:S(2)}, u32[]{:S(2)}) collective-permute-start(f32[256,768]{1,0:T(8,128)S(1)} %collective-permute-done.rest_3_), channel_id=1, source_target_pairs={{1,0},{0,1},{3,2},{2,3},{5,4},{4,5},{7,6},{6,7},{9,8},{8,9},{11,10... | collective-permute-start | bytes 2359304 | tf_op jit(solution)/shard_map/ppermute | solution.py:441
  41.0 3.5 %collective-permute-start.10 = (f32[256,768]{1,0:T(8,128)S(1)}, f32[256,768]{1,0:T(8,128)S(1)}, u32[]{:S(2)}, u32[]{:S(2)}) collective-permute-start(f32[256,768]{1,0:T(8,128)S(1)} %collective-permute-done.1.rest_5_), channel_id=1, source_target_pairs={{1,0},{0,1},{3,2},{2,3},{5,4},{4,5},{7,6},{6,7},{9,8},{8,9},{11,10... | collective-permute-start | bytes 2359304 | tf_op jit(solution)/shard_map/ppermute | solution.py:441
  41.5 6.0 %collective-permute-start.8 = (f32[256,768]{1,0:T(8,128)S(1)}, f32[256,768]{1,0:T(8,128)S(1)}, u32[]{:S(2)}, u32[]{:S(2)}) collective-permute-start(f32[256,768]{1,0:T(8,128)S(1)} %copy-done), channel_id=1, source_target_pairs={{1,0},{0,1},{3,2},{2,3},{5,4},{4,5},{7,6},{6,7},{9,8},{8,9},{11,10... | collective-permute-start | bytes 2359304 | tf_op jit(solution)/shard_map/ppermute | solution.py:441
  41.6 17.8 %collective-permute-start.11 = (f32[128,768]{1,0:T(8,128)}, f32[128,768]{1,0:T(8,128)S(1)}, u32[]{:S(2)}, u32[]{:S(2)}) collective-permute-start(f32[128,768]{1,0:T(8,128)} %get-tuple-element.59), channel_id=1, source_target_pairs={{16,0},{8,24},{17,1},{9,25},{18,2},{10,26},{19,3},{11,27},{20,4},{... | collective-permute-start | bytes 1179656 | tf_op jit(solution)/shard_map/ppermute | solution.py:433
  42.9 15.9 %collective-permute-start.12 = (f32[128,768]{1,0:T(8,128)}, f32[128,768]{1,0:T(8,128)S(1)}, u32[]{:S(2)}, u32[]{:S(2)}) collective-permute-start(f32[128,768]{1,0:T(8,128)} %get-tuple-element.59), channel_id=1, source_target_pairs={{6,0},{7,1},{4,2},{5,3},{2,4},{3,5},{0,6},{1,7},{14,8},{15,9},{12,... | collective-permute-start | bytes 1179656 | tf_op jit(solution)/shard_map/ppermute | solution.py:441
  44.5 13.1 %collective-permute-start.16 = (f32[72,256]{1,0:T(8,128)S(1)}, f32[72,256]{1,0:T(8,128)S(1)}, u32[]{:S(2)}, u32[]{:S(2)}) collective-permute-start(f32[72,256]{1,0:T(8,128)S(1)} %pad_add_fusion), channel_id=1, source_target_pairs={{6,0},{7,1},{4,2},{5,3},{2,4},{3,5},{0,6},{1,7},{14,8},{15,9},{12,... | collective-permute-start | bytes 221192 | tf_op jit(solution)/shard_map/ppermute | solution.py:441
  46.0 12.7 %collective-permute-start.15 = (f32[72,256]{1,0:T(8,128)S(1)}, f32[72,256]{1,0:T(8,128)S(1)}, u32[]{:S(2)}, u32[]{:S(2)}) collective-permute-start(f32[72,256]{1,0:T(8,128)S(1)} %pad_add_fusion), channel_id=1, source_target_pairs={{4,0},{5,1},{6,2},{7,3},{0,4},{1,5},{2,6},{3,7},{12,8},{13,9},{14,... | collective-permute-start | bytes 221192 | tf_op jit(solution)/shard_map/ppermute | solution.py:441
  47.5 11.3 %collective-permute-start.14 = (f32[72,256]{1,0:T(8,128)S(1)}, f32[72,256]{1,0:T(8,128)S(1)}, u32[]{:S(2)}, u32[]{:S(2)}) collective-permute-start(f32[72,256]{1,0:T(8,128)S(1)} %pad_add_fusion), channel_id=1, source_target_pairs={{2,0},{3,1},{0,2},{1,3},{6,4},{7,5},{4,6},{5,7},{10,8},{11,9},{8,1... | collective-permute-start | bytes 221192 | tf_op jit(solution)/shard_map/ppermute | solution.py:441
  57.6 1.9 %collective-permute-start.13 = (f32[128,768]{1,0:T(8,128)}, f32[128,768]{1,0:T(8,128)S(1)}, u32[]{:S(2)}, u32[]{:S(2)}) collective-permute-start(f32[128,768]{1,0:T(8,128)} %collective-permute-done.3.rest_2_), channel_id=1, source_target_pairs={{1,0},{0,1},{3,2},{2,3},{5,4},{4,5},{7,6},{6,7},{9,8},{8,9},{11,10... | collective-permute-start | bytes 1179656 | tf_op jit(solution)/shard_map/ppermute | solution.py:441
  58.8 2.2 %collective-permute-start.17 = (f32[128,768]{1,0:T(8,128)S(1)}, f32[128,768]{1,0:T(8,128)S(1)}, u32[]{:S(2)}, u32[]{:S(2)}) collective-permute-start(f32[128,768]{1,0:T(8,128)S(1)} %collective-permute-done.12.rest_3_), channel_id=1, source_target_pairs={{1,0},{0,1},{3,2},{2,3},{5,4},{4,5},{7,6},{6,7},{9,8},{8,9},{11,10... | collective-permute-start | bytes 1179656 | tf_op jit(solution)/shard_map/ppermute | solution.py:441
  58.9 2.1 %collective-permute-start.18 = (f32[4,72,256]{2,1,0:T(8,128)S(1)}, f32[4,72,256]{2,1,0:T(8,128)S(1)}, u32[]{:S(2)}, u32[]{:S(2)}) collective-permute-start(f32[4,72,256]{2,1,0:T(8,128)S(1)} %pad_maximum_fusion.rest_9_.rest_0_), channel_id=1, source_target_pairs={{1,0},{0,1},{3,2},{2,3},{5,4},{4,5},{7,6},{6,7},{9,8},{8,9},{11,10... | collective-permute-start | bytes 884744 | tf_op jit(solution)/shard_map/ppermute | solution.py:441
  71.2 13.3 %all-to-all-start = ((f32[8,64,256]{2,1,0:T(8,128)}), f32[8,64,256]{2,1,0:T(8,128)S(1)}, u32[]{:S(2)}, u32[]{:S(2)}) async-start(f32[8,64,256]{2,1,0:T(8,128)} %get-tuple-element.64), calls=%async_computation | async-start | bytes 1048576 | tf_op jit(solution)/shard_map/all_to_all | solution.py:508
  74.8 9.8 %collective-permute-start.21 = (f32[64,256]{1,0:T(8,128)S(1)}, f32[64,256]{1,0:T(8,128)S(1)}, u32[]{:S(2)}, u32[]{:S(2)}) collective-permute-start(f32[64,256]{1,0:T(8,128)S(1)} %get-tuple-element.68), channel_id=1, source_target_pairs={{0,24},{8,0},{16,8},{24,16},{1,25},{9,1},{17,9},{25,17},{2,26},{10... | collective-permute-start | bytes 196616 | tf_op jit(solution)/shard_map/ppermute | solution.py:437
  77.7 8.3 %collective-permute-start.20 = (f32[64,256]{1,0:T(8,128)S(1)}, f32[64,256]{1,0:T(8,128)S(1)}, u32[]{:S(2)}, u32[]{:S(2)}) collective-permute-start(f32[64,256]{1,0:T(8,128)S(1)} %get-tuple-element.67), channel_id=1, source_target_pairs={{0,16},{8,24},{16,0},{24,8},{1,17},{9,25},{17,1},{25,9},{2,18},{10... | collective-permute-start | bytes 196616 | tf_op jit(solution)/shard_map/ppermute | solution.py:437
  79.4 6.5 %collective-permute-start.19 = (f32[64,256]{1,0:T(8,128)S(1)}, f32[64,256]{1,0:T(8,128)S(1)}, u32[]{:S(2)}, u32[]{:S(2)}) collective-permute-start(f32[64,256]{1,0:T(8,128)S(1)} %get-tuple-element.66), channel_id=1, source_target_pairs={{0,8},{8,16},{16,24},{24,0},{1,9},{9,17},{17,25},{25,1},{2,10},{10... | collective-permute-start | bytes 196616 | tf_op jit(solution)/shard_map/ppermute | solution.py:437
  86.0 13.9 %collective-permute-start.22 = (f32[64,256]{1,0:T(8,128)S(1)}, f32[64,256]{1,0:T(8,128)S(1)}, u32[]{:S(2)}, u32[]{:S(2)}) collective-permute-start(f32[64,256]{1,0:T(8,128)S(1)} %multiply_add_fusion.1.rest_1_), channel_id=1, source_target_pairs={{8,0},{16,8},{24,16},{0,24},{9,1},{17,9},{25,17},{1,25},{10,2},{18... | collective-permute-start | bytes 196616 | tf_op jit(solution)/shard_map/ppermute | solution.py:428
  87.6 12.3 %collective-permute-start.23 = (f32[64,256]{1,0:T(8,128)S(1)}, f32[64,256]{1,0:T(8,128)S(1)}, u32[]{:S(2)}, u32[]{:S(2)}) collective-permute-start(f32[64,256]{1,0:T(8,128)S(1)} %multiply_add_fusion.1.rest_1_), channel_id=1, source_target_pairs={{16,0},{24,8},{0,16},{8,24},{17,1},{25,9},{1,17},{9,25},{18,2},{26... | collective-permute-start | bytes 196616 | tf_op jit(solution)/shard_map/ppermute | solution.py:428
  89.1 10.7 %collective-permute-start.24 = (f32[64,256]{1,0:T(8,128)S(1)}, f32[64,256]{1,0:T(8,128)S(1)}, u32[]{:S(2)}, u32[]{:S(2)}) collective-permute-start(f32[64,256]{1,0:T(8,128)S(1)} %multiply_add_fusion.1.rest_1_), channel_id=1, source_target_pairs={{24,0},{0,8},{8,16},{16,24},{25,1},{1,9},{9,17},{17,25},{26,2},{2,... | collective-permute-start | bytes 196616 | tf_op jit(solution)/shard_map/ppermute | solution.py:428
  104.7 13.4 %all-to-all-start.1 = ((f32[8,64,256]{2,1,0:T(8,128)}), f32[8,64,256]{2,1,0:T(8,128)S(1)}, u32[]{:S(2)}, u32[]{:S(2)}) async-start(f32[8,64,256]{2,1,0:T(8,128)} %get-tuple-element.69), calls=%async_computation.1 | async-start | bytes 1048576 | tf_op jit(solution)/shard_map/all_to_all | solution.py:508
  108.3 9.8 %collective-permute-start.27 = (f32[64,256]{1,0:T(8,128)S(1)}, f32[64,256]{1,0:T(8,128)S(1)}, u32[]{:S(2)}, u32[]{:S(2)}) collective-permute-start(f32[64,256]{1,0:T(8,128)S(1)} %get-tuple-element.73), channel_id=1, source_target_pairs={{0,24},{8,0},{16,8},{24,16},{1,25},{9,1},{17,9},{25,17},{2,26},{10... | collective-permute-start | bytes 196616 | tf_op jit(solution)/shard_map/ppermute | solution.py:437
  112.1 7.0 %collective-permute-start.26 = (f32[64,256]{1,0:T(8,128)S(1)}, f32[64,256]{1,0:T(8,128)S(1)}, u32[]{:S(2)}, u32[]{:S(2)}) collective-permute-start(f32[64,256]{1,0:T(8,128)S(1)} %get-tuple-element.72), channel_id=1, source_target_pairs={{0,16},{8,24},{16,0},{24,8},{1,17},{9,25},{17,1},{25,9},{2,18},{10... | collective-permute-start | bytes 196616 | tf_op jit(solution)/shard_map/ppermute | solution.py:437
  112.1 7.0 %collective-permute-start.25 = (f32[64,256]{1,0:T(8,128)S(1)}, f32[64,256]{1,0:T(8,128)S(1)}, u32[]{:S(2)}, u32[]{:S(2)}) collective-permute-start(f32[64,256]{1,0:T(8,128)S(1)} %get-tuple-element.71), channel_id=1, source_target_pairs={{0,8},{8,16},{16,24},{24,0},{1,9},{9,17},{17,25},{25,1},{2,10},{10... | collective-permute-start | bytes 196616 | tf_op jit(solution)/shard_map/ppermute | solution.py:437
  (6 other events, 61.9 us)

commit v11 on v7

--- a/solution.py
+++ b/solution.py
@@ -494,9 +494,8 @@
     row_y = (even_packs, odd_packs)
     for step in range(STEPS):
         if step:
+            row_y = (lax.all_gather(embed, "col", axis=0, tiled=False),)
             col_y = [embed] + [from_shift(embed, shift) for shift in range(1, row_count)]
-            even = jnp.stack([embed] + [from_bits(embed, bits) for bits in range(2, col_count, 2)])
-            row_y = (even, from_bits(even, 1))
         row_force, col_force = pair_forces(sizes, meta, listing, row_list, col_list, weights, row_y, col_y)
         row_parts = lax.all_to_all(row_force, "col", split_axis=0, concat_axis=0, tiled=True)
         force = jnp.sum(row_parts, axis=0) + col_force[0]

time: 119 us -> 118 us (level)
  blocking collectives: 0 us -> 10.3 us
  waiting for transfers between devices: 45.3 us -> 38.8 us
  starting transfers between devices: 47.6 us -> 41.9 us
    all_gather x0 -> x1, blocking collectives: none -> 10.3 us  [shards(): row_y = (lax.all_gather(embed, 'col', axis=0, tiled=False),)]
    ppermute x7, waiting for transfers between devices: 17.3 us -> 12 us  [from_shift(): return lax.ppermute(value, 'row', pairs)]
    ppermute x15 -> x11, waiting for transfers between devices: 17.3 us -> 13.6 us  [from_bits(): return lax.ppermute(value, 'col', pairs)]
    ppermute x15 -> x11, starting transfers between devices: 13.8 us -> 10.2 us  [from_bits(): return lax.ppermute(value, 'col', pairs)]
    all_to_all x2, waiting for transfers between devices: 6.66 us -> 9.15 us  [shards(): lax.all_to_all(row_force, 'col', split_axis=0, concat_axis=0, tiled=True)]
    ppermute x6, starting transfers between devices: 12.8 us -> 10.3 us  [to_shift(): return lax.ppermute(value, 'row', pairs)]
  transfers between devices with their start and end apart: 31 -> 27, of which waited for: 16 -> 11; matrix products, arithmetic and copies ran while one was open for 5% -> 5% of each run, Pallas kernels for 7% -> 7%
where the time goes in v11:
time: 118 us
  starting transfers between devices  41.9 us (36%)
  waiting for transfers between devices  38.8 us (33%)
  Pallas kernels  18.2 us (15%)
  blocking collectives  10.3 us (9%)
  local copies, waits for them, and re-layouts  3.5 us (3%)
  other arithmetic  3.47 us (3%)
  between operations  1.46 us (1%)
    ppermute x11, waiting for transfers between devices, from_bits(): return lax.ppermute(value, 'col', pairs)  13.6 us
    ppermute x7, waiting for transfers between devices, from_shift(): return lax.ppermute(value, 'row', pairs)  12 us
    ppermute x7, starting transfers between devices, from_shift(): return lax.ppermute(value, 'row', pairs)  11 us
    ppermute x6, starting transfers between devices, to_shift(): return lax.ppermute(value, 'row', pairs)  10.3 us
    all_gather x1, blocking collectives, shards(): row_y = (lax.all_gather(embed, 'col', axis=0, tiled=False),)  10.3 us
    ppermute x11, starting transfers between devices, from_bits(): return lax.ppermute(value, 'col', pairs)  10.2 us
    pallas_call x2, Pallas kernels, pair_forces(): pl.pallas_call(functools.partial(force_kernel, row_count, col_count, len(...  9.59 us
    all_to_all x2, waiting for transfers between devices, shards(): lax.all_to_all(row_force, 'col', split_axis=0, concat_axis=0, tiled=True)  9.15 us
  transfers between devices with their start and end apart: 27, of which 11 were waited for; matrix products, arithmetic and copies ran while one was open for 5% of the time, Pallas kernels for 7%

profile of v11, /device:TPU:0, one launch (start us, length us, event | category | flops | bytes accessed | tf_op | source)
XLA Modules:
  0.0 117.6 jit_solution(14113273445729585420)
XLA Ops:
  0.6 5.1 %collective-permute-start.2 = (f32[256,768]{1,0:T(8,128)}, f32[256,768]{1,0:T(8,128)S(1)}, u32[]{:S(2)}, u32[]{:S(2)}) collective-permute-start(f32[256,768]{1,0:T(8,128)} %rest_0_.1), channel_id=1, source_target_pairs={{8,0},{16,8},{24,16},{0,24},{9,1},{17,9},{25,17},{1,25},{10,2},{18... | collective-permute-start | bytes 2359304 | tf_op jit(solution)/shard_map/ppermute | solution.py:424
  5.7 1.5 %collective-permute-start.4 = (f32[256,768]{1,0:T(8,128)}, f32[256,768]{1,0:T(8,128)S(1)}, u32[]{:S(2)}, u32[]{:S(2)}) collective-permute-start(f32[256,768]{1,0:T(8,128)} %rest_0_.1), channel_id=1, source_target_pairs={{2,0},{3,1},{0,2},{1,3},{6,4},{7,5},{4,6},{5,7},{10,8},{11,9},{8,1... | collective-permute-start | bytes 2359304 | tf_op jit(solution)/shard_map/ppermute | solution.py:437
  7.2 1.5 %collective-permute-start.5 = (f32[256,768]{1,0:T(8,128)}, f32[256,768]{1,0:T(8,128)S(1)}, u32[]{:S(2)}, u32[]{:S(2)}) collective-permute-start(f32[256,768]{1,0:T(8,128)} %rest_0_.1), channel_id=1, source_target_pairs={{4,0},{5,1},{6,2},{7,3},{0,4},{1,5},{2,6},{3,7},{12,8},{13,9},{14,... | collective-permute-start | bytes 2359304 | tf_op jit(solution)/shard_map/ppermute | solution.py:437
  8.8 0.7 convert_element_type.19
  9.6 1.3 %multiply_reduce_fusion = f32[256]{0:T(256)S(1)} fusion(f32[256,768]{1,0:T(8,128)} %rest_0_.1), kind=kLoop, calls=%fused_computation | loop fusion | flops 392960 | bytes 787456 | tf_op jit(solution)/shard_map/reduce_sum | solution.py:457
  10.9 1.6 %concatenate.7.rest_3_.rest_2_ = f32[72,256]{1,0:T(8,128)S(1)} concatenate(f32[64,256]{1,0:T(8,128)} %param.13, f32[1,256]{1,0:T(1,128)} %bitcast.28, f32[1,256]{1,0:T(1,128)} %bitcast.29, f32[1,256]{1,0:T(1,128)S(1)} %bitcast.27, f32[1,256]{1,0:T(1,128)S(1)} %pad.12, f32[4,256]{1,0:T(4,128)S(1)} %broadcast_in_dim.4), dimensions={0} | concatenate | bytes 147456 | tf_op jit(solution)/shard_map/concatenate | solution.py:459
  13.0 0.8 copy.16
  14.4 0.8 copy.15
  15.4 9.7 %collective-permute-done.rest_4_.rest_3_ = f32[72,256]{1,0:T(8,128)S(1)} collective-permute-done((f32[72,256]{1,0:T(8,128)S(1)}, f32[72,256]{1,0:T(8,128)S(1)}, u32[]{:S(2)}, u32[]{:S(2)}) %collective-permute-start) | collective-permute-done | bytes 73760 | tf_op jit(solution)/shard_map/ppermute | solution.py:424
  25.2 2.2 %collective-permute-done.1.rest_5_.rest_4_ = f32[72,256]{1,0:T(8,128)S(1)} collective-permute-done((f32[72,256]{1,0:T(8,128)S(1)}, f32[72,256]{1,0:T(8,128)S(1)}, u32[]{:S(2)}, u32[]{:S(2)}) %collective-permute-start.1) | collective-permute-done | bytes 73760 | tf_op jit(solution)/shard_map/ppermute | solution.py:424
  28.1 2.4 %collective-permute-start.9 = (f32[256,768]{1,0:T(8,128)}, f32[256,768]{1,0:T(8,128)S(1)}, u32[]{:S(2)}, u32[]{:S(2)}) collective-permute-start(f32[256,768]{1,0:T(8,128)} %rest_0_.1), channel_id=1, source_target_pairs={{6,0},{7,1},{4,2},{5,3},{2,4},{3,5},{0,6},{1,7},{14,8},{15,9},{12,... | collective-permute-start | bytes 2359304 | tf_op jit(solution)/shard_map/ppermute | solution.py:437
  30.6 1.3 %collective-permute-start.8 = (f32[256,768]{1,0:T(8,128)S(1)}, f32[256,768]{1,0:T(8,128)S(1)}, u32[]{:S(2)}, u32[]{:S(2)}) collective-permute-start(f32[256,768]{1,0:T(8,128)S(1)} %copy-done), channel_id=1, source_target_pairs={{16,0},{8,24},{17,1},{9,25},{18,2},{10,26},{19,3},{11,27},{20,4},{... | collective-permute-start | bytes 2359304 | tf_op jit(solution)/shard_map/ppermute | solution.py:429
  31.9 2.4 %collective-permute-start.12 = (f32[72,256]{1,0:T(8,128)S(1)}, f32[72,256]{1,0:T(8,128)S(1)}, u32[]{:S(2)}, u32[]{:S(2)}) collective-permute-start(f32[72,256]{1,0:T(8,128)S(1)} %pad_add_fusion), channel_id=1, source_target_pairs={{6,0},{7,1},{4,2},{5,3},{2,4},{3,5},{0,6},{1,7},{14,8},{15,9},{12,... | collective-permute-start | bytes 221192 | tf_op jit(solution)/shard_map/ppermute | solution.py:437
  35.4 4.0 %grams.1 = (f32[6,2,128,128]{3,2,1,0:T(8,128)S(1)}, bf16[2,256,768]{2,1,0:T(8,128)(2,1)S(1)}, bf16[2,256,768]{2,1,0:T(8,128)(2,1)S(1)}, bf16[6,128,768]{2,1,0:T(8,128)(2,1)S(1)}, bf16[6,128,768]{2,1,0:T(8,128)(2,1)S(1)}) custom-call(s32[11]{0:T(128)S(1)} %pad_add_fusion.1.meta, s32[64]{0:T(128)S(1)} %reshape.27.listing, f32[256,768]{1,0:T(8,128)S(1)} %copy-done, ...), custom_call_target="tpu_custom_call" | custom-call | flops 905969664 | bytes 6291456 | tf_op jit(solution)/shard_map/grams/pallas_call | solution.py:109
  39.4 11.7 %collective-permute-done.12 = f32[72,256]{1,0:T(8,128)S(1)} collective-permute-done((f32[72,256]{1,0:T(8,128)S(1)}, f32[72,256]{1,0:T(8,128)S(1)}, u32[]{:S(2)}, u32[]{:S(2)}) %collective-permute-start.12) | collective-permute-done | bytes 73760 | tf_op jit(solution)/shard_map/ppermute | solution.py:437
  51.1 1.1 collective-permute-done.11
  52.9 1.6 %collective-permute-start.15 = (f32[64,256]{1,0:T(8,128)S(1)}, f32[64,256]{1,0:T(8,128)S(1)}, u32[]{:S(2)}, u32[]{:S(2)}) collective-permute-start(f32[64,256]{1,0:T(8,128)S(1)} %copy-done.3), channel_id=1, source_target_pairs={{24,0},{0,8},{8,16},{16,24},{25,1},{1,9},{9,17},{17,25},{26,2},{2,... | collective-permute-start | bytes 196616 | tf_op jit(solution)/shard_map/ppermute | solution.py:424
  55.1 4.6 %weights.1 = bf16[24,128,128]{2,1,0:T(8,128)(2,1)S(1)} custom-call(s32[11]{0:T(128)S(1)} %pad_add_fusion.1.meta, s32[64]{0:T(128)S(1)} %reshape.27.listing, s32[32]{0:T(128)S(1)} %reshape.28.seeds, f32[6,2,128,128]{3,2,1,0:T(8,128)S(1)} %get-tuple-element.34.grams, bf16[2,256,768]{2,1,0:T(8,128)(2,1)S(1)} %get-tuple-element.35.high_c, ...), custom_call_target="tpu_custom_call" | custom-call | flops 905969664 | bytes 2359296 | tf_op jit(solution)/shard_map/weights/pallas_call | solution.py:217
  59.8 4.8 %forces.2 = (f32[8,64,256]{2,1,0:T(8,128)}, f32[64,256]{1,0:T(8,128)S(1)}, f32[64,256]{1,0:T(8,128)S(1)}, f32[64,256]{1,0:T(8,128)S(1)}, f32[64,256]{1,0:T(8,128)S(1)}) custom-call(s32[11]{0:T(128)S(1)} %pad_add_fusion.1.meta, s32[64]{0:T(128)S(1)} %reshape.27.listing, s32[48]{0:T(128)S(1)} %bitcast.19, s32[48]{0:T(128)S(1)} %bitcast.21, ...), custom_call_target="tpu_custom_call" | custom-call | flops 1744830464 | bytes 1572864 | tf_op jit(solution)/shard_map/forces/pallas_call | solution.py:385
  64.6 4.6 %all-to-all-start = ((f32[8,64,256]{2,1,0:T(8,128)}), f32[8,64,256]{2,1,0:T(8,128)S(1)}, u32[]{:S(2)}, u32[]{:S(2)}) async-start(f32[8,64,256]{2,1,0:T(8,128)} %get-tuple-element.44), calls=%async_computation | async-start | bytes 1048576 | tf_op jit(solution)/shard_map/all_to_all | solution.py:500
  69.1 5.9 %collective-permute-start.18 = (f32[64,256]{1,0:T(8,128)S(1)}, f32[64,256]{1,0:T(8,128)S(1)}, u32[]{:S(2)}, u32[]{:S(2)}) collective-permute-start(f32[64,256]{1,0:T(8,128)S(1)} %get-tuple-element.48), channel_id=1, source_target_pairs={{0,24},{8,0},{16,8},{24,16},{1,25},{9,1},{17,9},{25,17},{2,26},{10... | collective-permute-start | bytes 196616 | tf_op jit(solution)/shard_map/ppermute | solution.py:433
  75.7 3.2 %all-to-all-done = f32[8,64,256]{2,1,0:T(8,128)S(1)} async-done(((f32[8,64,256]{2,1,0:T(8,128)}), f32[8,64,256]{2,1,0:T(8,128)S(1)}, u32[]{:S(2)}, u32[]{:S(2)}) %all-to-all-start) | async-done | bytes 524320 | tf_op jit(solution)/shard_map/all_to_all | solution.py:500
  78.9 3.0 %collective-permute-done.17 = f32[64,256]{1,0:T(8,128)S(1)} collective-permute-done((f32[64,256]{1,0:T(8,128)S(1)}, f32[64,256]{1,0:T(8,128)S(1)}, u32[]{:S(2)}, u32[]{:S(2)}) %collective-permute-start.17) | collective-permute-done | bytes 65568 | tf_op jit(solution)/shard_map/ppermute | solution.py:433
  82.0 2.9 %collective-permute-start.19 = (f32[64,256]{1,0:T(8,128)S(1)}, f32[64,256]{1,0:T(8,128)S(1)}, u32[]{:S(2)}, u32[]{:S(2)}) collective-permute-start(f32[64,256]{1,0:T(8,128)S(1)} %multiply_add_fusion.1.rest_1_), channel_id=1, source_target_pairs={{8,0},{16,8},{24,16},{0,24},{9,1},{17,9},{25,17},{1,25},{10,2},{18... | collective-permute-start | bytes 196616 | tf_op jit(solution)/shard_map/ppermute | solution.py:424
  84.9 0.9 collective-permute-start.21
  85.9 10.3 %all-gather = f32[512,256]{1,0:T(8,128)S(1)} all-gather(f32[64,256]{1,0:T(8,128)S(1)} %multiply_add_fusion.1.rest_1_), channel_id=2, replica_groups=mesh['row'=4,'col'=8] {'col'}, dimensions={0}, use_global_device_ids=true | all-gather | bytes 589824 | tf_op jit(solution)/shard_map/all_gather | solution.py:497
  96.2 4.8 %forces.3 = (f32[8,64,256]{2,1,0:T(8,128)}, f32[64,256]{1,0:T(8,128)S(1)}, f32[64,256]{1,0:T(8,128)S(1)}, f32[64,256]{1,0:T(8,128)S(1)}, f32[64,256]{1,0:T(8,128)S(1)}) custom-call(s32[11]{0:T(128)S(1)} %pad_add_fusion.1.meta, s32[64]{0:T(128)S(1)} %reshape.27.listing, s32[48]{0:T(128)S(1)} %bitcast.20, s32[48]{0:T(128)S(1)} %bitcast.22, ...), custom_call_target="tpu_custom_call" | custom-call | flops 1744830464 | bytes 1572864 | tf_op jit(solution)/shard_map/forces/pallas_call | solution.py:385
  100.9 4.5 %all-to-all-start.1 = ((f32[8,64,256]{2,1,0:T(8,128)}), f32[8,64,256]{2,1,0:T(8,128)S(1)}, u32[]{:S(2)}, u32[]{:S(2)}) async-start(f32[8,64,256]{2,1,0:T(8,128)} %get-tuple-element.49), calls=%async_computation.1 | async-start | bytes 1048576 | tf_op jit(solution)/shard_map/all_to_all | solution.py:500
  105.4 2.7 %collective-permute-start.24 = (f32[64,256]{1,0:T(8,128)S(1)}, f32[64,256]{1,0:T(8,128)S(1)}, u32[]{:S(2)}, u32[]{:S(2)}) collective-permute-start(f32[64,256]{1,0:T(8,128)S(1)} %get-tuple-element.53), channel_id=1, source_target_pairs={{0,24},{8,0},{16,8},{24,16},{1,25},{9,1},{17,9},{25,17},{2,26},{10... | collective-permute-start | bytes 196616 | tf_op jit(solution)/shard_map/ppermute | solution.py:433
  108.2 1.1 collective-permute-start.23
  109.3 5.9 %all-to-all-done.1 = f32[8,64,256]{2,1,0:T(8,128)S(1)} async-done(((f32[8,64,256]{2,1,0:T(8,128)}), f32[8,64,256]{2,1,0:T(8,128)S(1)}, u32[]{:S(2)}, u32[]{:S(2)}) %all-to-all-start.1) | async-done | bytes 524320 | tf_op jit(solution)/shard_map/all_to_all | solution.py:500
  115.2 1.1 collective-permute-done.23
  (57 shorter events, 6.1 us)
Async XLA Ops:
  0.6 29.9 %copy-start = (f32[256,768]{1,0:T(8,128)S(1)}, f32[256,768]{1,0:T(8,128)}, u32[]{:S(2)}) copy-start(f32[256,768]{1,0:T(8,128)} %rest_0_.1) | copy-start | bytes 2359300
  0.6 26.8 %collective-permute-start.2 = (f32[256,768]{1,0:T(8,128)}, f32[256,768]{1,0:T(8,128)S(1)}, u32[]{:S(2)}, u32[]{:S(2)}) collective-permute-start(f32[256,768]{1,0:T(8,128)} %rest_0_.1), channel_id=1, source_target_pairs={{8,0},{16,8},{24,16},{0,24},{9,1},{17,9},{25,17},{1,25},{10,2},{18... | collective-permute-start | bytes 2359304 | tf_op jit(solution)/shard_map/ppermute | solution.py:424
  5.7 21.7 %collective-permute-start.4 = (f32[256,768]{1,0:T(8,128)}, f32[256,768]{1,0:T(8,128)S(1)}, u32[]{:S(2)}, u32[]{:S(2)}) collective-permute-start(f32[256,768]{1,0:T(8,128)} %rest_0_.1), channel_id=1, source_target_pairs={{2,0},{3,1},{0,2},{1,3},{6,4},{7,5},{4,6},{5,7},{10,8},{11,9},{8,1... | collective-permute-start | bytes 2359304 | tf_op jit(solution)/shard_map/ppermute | solution.py:437
  7.2 20.2 %collective-permute-start.5 = (f32[256,768]{1,0:T(8,128)}, f32[256,768]{1,0:T(8,128)S(1)}, u32[]{:S(2)}, u32[]{:S(2)}) collective-permute-start(f32[256,768]{1,0:T(8,128)} %rest_0_.1), channel_id=1, source_target_pairs={{4,0},{5,1},{6,2},{7,3},{0,4},{1,5},{2,6},{3,7},{12,8},{13,9},{14,... | collective-permute-start | bytes 2359304 | tf_op jit(solution)/shard_map/ppermute | solution.py:437
  12.4 12.7 %collective-permute-start = (f32[72,256]{1,0:T(8,128)S(1)}, f32[72,256]{1,0:T(8,128)S(1)}, u32[]{:S(2)}, u32[]{:S(2)}) collective-permute-start(f32[72,256]{1,0:T(8,128)S(1)} %concatenate.7.rest_3_.rest_2_), channel_id=1, source_target_pairs={{8,0},{16,8},{24,16},{0,24},{9,1},{17,9},{25,17},{1,25},{10,2},{18... | collective-permute-start | bytes 221192 | tf_op jit(solution)/shard_map/ppermute | solution.py:424
  12.9 14.4 %collective-permute-start.1 = (f32[72,256]{1,0:T(8,128)S(1)}, f32[72,256]{1,0:T(8,128)S(1)}, u32[]{:S(2)}, u32[]{:S(2)}) collective-permute-start(f32[72,256]{1,0:T(8,128)S(1)} %concatenate.7.rest_3_.rest_2_), channel_id=1, source_target_pairs={{16,0},{24,8},{0,16},{8,24},{17,1},{25,9},{1,17},{9,25},{18,2},{26... | collective-permute-start | bytes 221192 | tf_op jit(solution)/shard_map/ppermute | solution.py:424
  27.4 3.2 %collective-permute-start.3 = (f32[256,768]{1,0:T(8,128)}, f32[256,768]{1,0:T(8,128)S(1)}, u32[]{:S(2)}, u32[]{:S(2)}) collective-permute-start(f32[256,768]{1,0:T(8,128)} %rest_0_.1), channel_id=1, source_target_pairs={{1,0},{0,1},{3,2},{2,3},{5,4},{4,5},{7,6},{6,7},{9,8},{8,9},{11,10... | collective-permute-start | bytes 2359304 | tf_op jit(solution)/shard_map/ppermute | solution.py:437
  27.4 4.4 %collective-permute-start.6 = (f32[256,768]{1,0:T(8,128)S(1)}, f32[256,768]{1,0:T(8,128)S(1)}, u32[]{:S(2)}, u32[]{:S(2)}) collective-permute-start(f32[256,768]{1,0:T(8,128)S(1)} %collective-permute-done.4.rest_3_), channel_id=1, source_target_pairs={{1,0},{0,1},{3,2},{2,3},{5,4},{4,5},{7,6},{6,7},{9,8},{8,9},{11,10... | collective-permute-start | bytes 2359304 | tf_op jit(solution)/shard_map/ppermute | solution.py:437
  28.0 3.9 %collective-permute-start.7 = (f32[256,768]{1,0:T(8,128)S(1)}, f32[256,768]{1,0:T(8,128)S(1)}, u32[]{:S(2)}, u32[]{:S(2)}) collective-permute-start(f32[256,768]{1,0:T(8,128)S(1)} %collective-permute-done.5.rest_5_), channel_id=1, source_target_pairs={{1,0},{0,1},{3,2},{2,3},{5,4},{4,5},{7,6},{6,7},{9,8},{8,9},{11,10... | collective-permute-start | bytes 2359304 | tf_op jit(solution)/shard_map/ppermute | solution.py:437
  28.1 24.3 %collective-permute-start.9 = (f32[256,768]{1,0:T(8,128)}, f32[256,768]{1,0:T(8,128)S(1)}, u32[]{:S(2)}, u32[]{:S(2)}) collective-permute-start(f32[256,768]{1,0:T(8,128)} %rest_0_.1), channel_id=1, source_target_pairs={{6,0},{7,1},{4,2},{5,3},{2,4},{3,5},{0,6},{1,7},{14,8},{15,9},{12,... | collective-permute-start | bytes 2359304 | tf_op jit(solution)/shard_map/ppermute | solution.py:437
  30.5 22.4 %copy-start.3 = (f32[64,256]{1,0:T(8,128)S(1)}, f32[64,256]{1,0:T(8,128)}, u32[]{:S(2)}) copy-start(f32[64,256]{1,0:T(8,128)} %param.13) | copy-start | bytes 196612
  30.6 23.9 %collective-permute-start.8 = (f32[256,768]{1,0:T(8,128)S(1)}, f32[256,768]{1,0:T(8,128)S(1)}, u32[]{:S(2)}, u32[]{:S(2)}) collective-permute-start(f32[256,768]{1,0:T(8,128)S(1)} %copy-done), channel_id=1, source_target_pairs={{16,0},{8,24},{17,1},{9,25},{18,2},{10,26},{19,3},{11,27},{20,4},{... | collective-permute-start | bytes 2359304 | tf_op jit(solution)/shard_map/ppermute | solution.py:429
  31.9 19.2 %collective-permute-start.12 = (f32[72,256]{1,0:T(8,128)S(1)}, f32[72,256]{1,0:T(8,128)S(1)}, u32[]{:S(2)}, u32[]{:S(2)}) collective-permute-start(f32[72,256]{1,0:T(8,128)S(1)} %pad_add_fusion), channel_id=1, source_target_pairs={{6,0},{7,1},{4,2},{5,3},{2,4},{3,5},{0,6},{1,7},{14,8},{15,9},{12,... | collective-permute-start | bytes 221192 | tf_op jit(solution)/shard_map/ppermute | solution.py:437
  34.4 17.8 %collective-permute-start.11 = (f32[72,256]{1,0:T(8,128)S(1)}, f32[72,256]{1,0:T(8,128)S(1)}, u32[]{:S(2)}, u32[]{:S(2)}) collective-permute-start(f32[72,256]{1,0:T(8,128)S(1)} %pad_add_fusion), channel_id=1, source_target_pairs={{4,0},{5,1},{6,2},{7,3},{0,4},{1,5},{2,6},{3,7},{12,8},{13,9},{14,... | collective-permute-start | bytes 221192 | tf_op jit(solution)/shard_map/ppermute | solution.py:437
  34.9 17.4 %collective-permute-start.10 = (f32[72,256]{1,0:T(8,128)S(1)}, f32[72,256]{1,0:T(8,128)S(1)}, u32[]{:S(2)}, u32[]{:S(2)}) collective-permute-start(f32[72,256]{1,0:T(8,128)S(1)} %pad_add_fusion), channel_id=1, source_target_pairs={{2,0},{3,1},{0,2},{1,3},{6,4},{7,5},{4,6},{5,7},{10,8},{11,9},{8,1... | collective-permute-start | bytes 221192 | tf_op jit(solution)/shard_map/ppermute | solution.py:437
  52.3 2.8 %collective-permute-start.13 = (f32[256,768]{1,0:T(8,128)S(1)}, f32[256,768]{1,0:T(8,128)S(1)}, u32[]{:S(2)}, u32[]{:S(2)}) collective-permute-start(f32[256,768]{1,0:T(8,128)S(1)} %collective-permute-done.9.rest_1_), channel_id=1, source_target_pairs={{1,0},{0,1},{3,2},{2,3},{5,4},{4,5},{7,6},{6,7},{9,8},{8,9},{11,10... | collective-permute-start | bytes 2359304 | tf_op jit(solution)/shard_map/ppermute | solution.py:437
  52.4 2.7 %collective-permute-start.14 = (f32[4,72,256]{2,1,0:T(8,128)S(1)}, f32[4,72,256]{2,1,0:T(8,128)S(1)}, u32[]{:S(2)}, u32[]{:S(2)}) collective-permute-start(f32[4,72,256]{2,1,0:T(8,128)S(1)} %pad_maximum_fusion.rest_6_.rest_0_), channel_id=1, source_target_pairs={{1,0},{0,1},{3,2},{2,3},{5,4},{4,5},{7,6},{6,7},{9,8},{8,9},{11,10... | collective-permute-start | bytes 884744 | tf_op jit(solution)/shard_map/ppermute | solution.py:437
  52.9 6.8 %collective-permute-start.15 = (f32[64,256]{1,0:T(8,128)S(1)}, f32[64,256]{1,0:T(8,128)S(1)}, u32[]{:S(2)}, u32[]{:S(2)}) collective-permute-start(f32[64,256]{1,0:T(8,128)S(1)} %copy-done.3), channel_id=1, source_target_pairs={{24,0},{0,8},{8,16},{16,24},{25,1},{1,9},{9,17},{17,25},{26,2},{2,... | collective-permute-start | bytes 196616 | tf_op jit(solution)/shard_map/ppermute | solution.py:424
  55.1 4.6 %copy-start.1 = (s32[1,1,48]{2,1,0:T(1,128)S(1)}, s32[1,1,48]{2,1,0:T(1,128)}, u32[]{:S(2)}) copy-start(s32[1,1,48]{2,1,0:T(1,128)} %param.16) | copy-start | bytes 580
  55.1 4.6 %copy-start.2 = (s32[1,1,48]{2,1,0:T(1,128)S(1)}, s32[1,1,48]{2,1,0:T(1,128)}, u32[]{:S(2)}) copy-start(s32[1,1,48]{2,1,0:T(1,128)} %param.17) | copy-start | bytes 580
  64.6 14.3 %all-to-all-start = ((f32[8,64,256]{2,1,0:T(8,128)}), f32[8,64,256]{2,1,0:T(8,128)S(1)}, u32[]{:S(2)}, u32[]{:S(2)}) async-start(f32[8,64,256]{2,1,0:T(8,128)} %get-tuple-element.44), calls=%async_computation | async-start | bytes 1048576 | tf_op jit(solution)/shard_map/all_to_all | solution.py:500
  69.1 9.8 %collective-permute-start.18 = (f32[64,256]{1,0:T(8,128)S(1)}, f32[64,256]{1,0:T(8,128)S(1)}, u32[]{:S(2)}, u32[]{:S(2)}) collective-permute-start(f32[64,256]{1,0:T(8,128)S(1)} %get-tuple-element.48), channel_id=1, source_target_pairs={{0,24},{8,0},{16,8},{24,16},{1,25},{9,1},{17,9},{25,17},{2,26},{10... | collective-permute-start | bytes 196616 | tf_op jit(solution)/shard_map/ppermute | solution.py:433
  75.0 7.0 %collective-permute-start.17 = (f32[64,256]{1,0:T(8,128)S(1)}, f32[64,256]{1,0:T(8,128)S(1)}, u32[]{:S(2)}, u32[]{:S(2)}) collective-permute-start(f32[64,256]{1,0:T(8,128)S(1)} %get-tuple-element.47), channel_id=1, source_target_pairs={{0,16},{8,24},{16,0},{24,8},{1,17},{9,25},{17,1},{25,9},{2,18},{10... | collective-permute-start | bytes 196616 | tf_op jit(solution)/shard_map/ppermute | solution.py:433
  75.0 7.0 %collective-permute-start.16 = (f32[64,256]{1,0:T(8,128)S(1)}, f32[64,256]{1,0:T(8,128)S(1)}, u32[]{:S(2)}, u32[]{:S(2)}) collective-permute-start(f32[64,256]{1,0:T(8,128)S(1)} %get-tuple-element.46), channel_id=1, source_target_pairs={{0,8},{8,16},{16,24},{24,0},{1,9},{9,17},{17,25},{25,1},{2,10},{10... | collective-permute-start | bytes 196616 | tf_op jit(solution)/shard_map/ppermute | solution.py:433
  82.0 14.1 %collective-permute-start.19 = (f32[64,256]{1,0:T(8,128)S(1)}, f32[64,256]{1,0:T(8,128)S(1)}, u32[]{:S(2)}, u32[]{:S(2)}) collective-permute-start(f32[64,256]{1,0:T(8,128)S(1)} %multiply_add_fusion.1.rest_1_), channel_id=1, source_target_pairs={{8,0},{16,8},{24,16},{0,24},{9,1},{17,9},{25,17},{1,25},{10,2},{18... | collective-permute-start | bytes 196616 | tf_op jit(solution)/shard_map/ppermute | solution.py:424
  84.9 11.2 %collective-permute-start.20 = (f32[64,256]{1,0:T(8,128)S(1)}, f32[64,256]{1,0:T(8,128)S(1)}, u32[]{:S(2)}, u32[]{:S(2)}) collective-permute-start(f32[64,256]{1,0:T(8,128)S(1)} %multiply_add_fusion.1.rest_1_), channel_id=1, source_target_pairs={{16,0},{24,8},{0,16},{8,24},{17,1},{25,9},{1,17},{9,25},{18,2},{26... | collective-permute-start | bytes 196616 | tf_op jit(solution)/shard_map/ppermute | solution.py:424
  84.9 11.2 %collective-permute-start.21 = (f32[64,256]{1,0:T(8,128)S(1)}, f32[64,256]{1,0:T(8,128)S(1)}, u32[]{:S(2)}, u32[]{:S(2)}) collective-permute-start(f32[64,256]{1,0:T(8,128)S(1)} %multiply_add_fusion.1.rest_1_), channel_id=1, source_target_pairs={{24,0},{0,8},{8,16},{16,24},{25,1},{1,9},{9,17},{17,25},{26,2},{2,... | collective-permute-start | bytes 196616 | tf_op jit(solution)/shard_map/ppermute | solution.py:424
  100.9 14.3 %all-to-all-start.1 = ((f32[8,64,256]{2,1,0:T(8,128)}), f32[8,64,256]{2,1,0:T(8,128)S(1)}, u32[]{:S(2)}, u32[]{:S(2)}) async-start(f32[8,64,256]{2,1,0:T(8,128)} %get-tuple-element.49), calls=%async_computation.1 | async-start | bytes 1048576 | tf_op jit(solution)/shard_map/all_to_all | solution.py:500
  105.4 9.8 %collective-permute-start.24 = (f32[64,256]{1,0:T(8,128)S(1)}, f32[64,256]{1,0:T(8,128)S(1)}, u32[]{:S(2)}, u32[]{:S(2)}) collective-permute-start(f32[64,256]{1,0:T(8,128)S(1)} %get-tuple-element.53), channel_id=1, source_target_pairs={{0,24},{8,0},{16,8},{24,16},{1,25},{9,1},{17,9},{25,17},{2,26},{10... | collective-permute-start | bytes 196616 | tf_op jit(solution)/shard_map/ppermute | solution.py:433
  108.2 8.1 %collective-permute-start.23 = (f32[64,256]{1,0:T(8,128)S(1)}, f32[64,256]{1,0:T(8,128)S(1)}, u32[]{:S(2)}, u32[]{:S(2)}) collective-permute-start(f32[64,256]{1,0:T(8,128)S(1)} %get-tuple-element.52), channel_id=1, source_target_pairs={{0,16},{8,24},{16,0},{24,8},{1,17},{9,25},{17,1},{25,9},{2,18},{10... | collective-permute-start | bytes 196616 | tf_op jit(solution)/shard_map/ppermute | solution.py:433
  109.3 7.0 %collective-permute-start.22 = (f32[64,256]{1,0:T(8,128)S(1)}, f32[64,256]{1,0:T(8,128)S(1)}, u32[]{:S(2)}, u32[]{:S(2)}) collective-permute-start(f32[64,256]{1,0:T(8,128)S(1)} %get-tuple-element.51), channel_id=1, source_target_pairs={{0,8},{8,16},{16,24},{24,0},{1,9},{9,17},{17,25},{25,1},{2,10},{10... | collective-permute-start | bytes 196616 | tf_op jit(solution)/shard_map/ppermute | solution.py:433
